TPU v7x, 32 devices: a whole 2x2x4 slice. The times are simulated.
32 devices in a mesh: dp: 8 (over z, y), phase: 2 (over core), mp: 2 (over x).
Axes of the slice: x: 2, y: 2, z: 4, core: 2. Of those that a mesh axis runs over, the one named last changes fastest.
Arguments:
- sec_acts: bfloat16 [2, 8, 512, 4096], P('phase', 'dp', None, 'mp'), may hold values from -40 to 40
- gain: bfloat16 [4096], P('mp'), may hold values from 0.5 to 1.5
- w_kv: bfloat16 [4096, 4096], P(('dp', 'phase'), 'mp'), may hold values from -0.09375 to 0.09375
- src_len: int32 [8], P('dp'), may hold values from 1 to 512, 2560 in all
- tgt_len: int32 [8], P('dp'), may hold values from 1 to 512, 3072 in all
Outputs:
- sec_grads: bfloat16 [2, 8, 512, 4096], P('phase', 'dp', None, 'mp')
- d_wkv: float32 [4096, 4096], P(('dp', 'phase'), 'mp')
- d_gain: float32 [4096], P('mp')
Inputs may be any that keep to these rules, and one draw needn't show every extreme that they name: Source positions 0 to src_len - 1 of a pair are real, the rest padding; some pair has exactly 512. Target positions 0 to tgt_len - 1 of a pair carry loss, the rest padding; some pair has exactly 512.
All inputs are finite; a program needn't handle non-finite values. No bound on the sum of `src_len` or of `tgt_len` on one device may be relied on, other than what follows from the above.
Results may differ from a plain program's by a relative error of at most 0.022.
Values may be sent and summed in bfloat16 or wider, within the bound.
No kernel may reach another device: no remote copies, remote signals or barrier semaphores. Data moves between devices by JAX's collectives and lax.ppermute only.
A program may use at most 128 MiB of HBM per device.

v0:
```python
import jax
import jax.numpy as jnp
from jax import lax
from jax.sharding import PartitionSpec as P

D = 4096
HEAD = 64


norm_epsilon = 1e-06


def shifted(value, axis, steps):
    count = lax.axis_size(axis)
    initial, last = (max(0, -steps), min(count, count - steps))
    return lax.ppermute(value, axis, [(source, source + steps) for source in range(initial, last)])


def attend_back(queries, grad_out, key_heads, values, key_mask):
    f32 = jnp.float32
    bf16 = jnp.bfloat16
    factor = 1.0 / HEAD**0.5
    scores = factor * jnp.einsum("pihd,pjhd->phij", queries, key_heads, preferred_element_type=f32)
    scores = jnp.where(key_mask[:, None, None, :], scores, -1e30)
    row_top = jnp.max(scores, axis=-1, keepdims=True)
    weights = jnp.exp(scores - row_top)
    probability = weights / jnp.sum(weights, axis=-1, keepdims=True)
    prob_low = probability.astype(bf16)
    attended = jnp.einsum("phij,pjhd->pihd", prob_low, values, preferred_element_type=f32)
    grad_prob = jnp.einsum("pihd,pjhd->phij", grad_out, values, preferred_element_type=f32)
    row_delta = jnp.einsum("pihd,pihd->phi", grad_out.astype(f32), attended)
    grad_score = (factor * probability * (grad_prob - row_delta[..., None])).astype(bf16)
    grad_query = jnp.einsum(
        "phij,pjhd->pihd", grad_score, key_heads, preferred_element_type=f32
    ).astype(bf16)
    grad_key = jnp.einsum(
        "phij,pihd->pjhd", grad_score, queries, preferred_element_type=f32
    ).astype(bf16)
    grad_value = jnp.einsum(
        "phij,pihd->pjhd", prob_low, grad_out, preferred_element_type=f32
    ).astype(bf16)
    return (grad_query, grad_key, grad_value)


def on_device(sec_acts, gain, w_kv, src_len, tgt_len):
    f32 = jnp.float32
    bf16 = jnp.bfloat16
    section = lax.axis_index("phase")
    packed = sec_acts[0]
    pair_dev, length, shard_width = packed.shape
    row_count = pair_dev * length
    pair_total = pair_dev * lax.axis_size("dp")
    pair_scale = 1.0 / pair_total
    hidden = packed.astype(f32)
    squares = lax.psum(jnp.sum(hidden * hidden, axis=-1), "mp")
    inv_rms = lax.rsqrt(squares / D + norm_epsilon)[..., None]
    normed = hidden * inv_rms
    gain_wide = gain.astype(f32)
    enc_shard = (normed * gain_wide).astype(bf16)
    enc_moved = shifted(enc_shard, "phase", 1)
    enc_full = lax.all_gather(enc_moved, "mp", axis=2, tiled=True)
    enc_rows = enc_full.reshape(row_count, D)
    whole_weight = lax.all_gather(w_kv, ("dp", "phase"), axis=0, tiled=True)
    key_value = jnp.dot(enc_rows, whole_weight, preferred_element_type=f32)
    heads_dev = shard_width // (2 * HEAD)
    kv_split = key_value.astype(bf16).reshape(pair_dev, length, heads_dev, 2, HEAD)
    dec_split = packed.reshape(pair_dev, length, heads_dev, 2, HEAD)
    positions = jnp.arange(length, dtype=jnp.int32)
    query_mask = positions[None, :] < tgt_len[:, None]
    key_mask = positions[None, :] < src_len[:, None]
    grad_out = jnp.where(query_mask[:, :, None, None], dec_split[:, :, :, 1], jnp.zeros((), bf16))
    grad_query, grad_key, grad_value = attend_back(
        dec_split[:, :, :, 0], grad_out, kv_split[:, :, :, 0], kv_split[:, :, :, 1], key_mask
    )
    dec_grads = jnp.stack([grad_query, grad_key], axis=3).reshape(pair_dev, length, shard_width)
    grad_kv = jnp.stack([grad_key, grad_value], axis=3).reshape(row_count, shard_width)
    reduced = lax.psum_scatter(
        (
            pair_scale
            * lax.dot_general(
                enc_rows, grad_kv, (((0,), (0,)), ((), ())), preferred_element_type=f32
            )
        ).astype(jnp.bfloat16),
        "dp",
        scatter_dimension=0,
        tiled=True,
    ).astype(jnp.float32)
    half_rows = reduced.shape[0] // 2
    lower_rows = shifted(reduced[:half_rows], "phase", -1)
    d_wkv = jnp.where(section == 0, lower_rows, reduced[half_rows:])
    partial_enc = lax.dot_general(
        grad_kv, whole_weight, (((1,), (1,)), ((), ())), preferred_element_type=f32
    ).astype(bf16)
    partial_enc = partial_enc.reshape(1, pair_dev, length, D)
    pieces = lax.all_to_all(partial_enc, "mp", split_axis=3, concat_axis=0, tiled=True)
    summed = jnp.sum(pieces.astype(f32), axis=0)
    grad_enc = shifted(summed, "phase", -1)
    grad_normed = grad_enc * gain_wide
    gain_term = pair_scale * jnp.sum(grad_enc * normed, axis=(0, 1))
    d_gain = lax.psum(gain_term, ("dp", "phase"))
    sec_grads = jnp.where(section == 0, grad_normed.astype(bf16), dec_grads)[None]
    return (sec_grads, d_wkv, d_gain)


def solution(mesh):
    placed = (P("phase", "dp", None, "mp"), P("mp"), P(("dp", "phase"), "mp"), P("dp"), P("dp"))
    return jax.shard_map(
        on_device,
        mesh=mesh,
        in_specs=placed,
        out_specs=(P("phase", "dp", None, "mp"), P(("dp", "phase"), "mp"), P("mp")),
        check_vma=False,
    )
```

profile of v0, /device:TPU:0, one launch (start us, length us, event | category | flops | bytes accessed | tf_op | source)
XLA Modules:
  0.0 625.9 jit_solution(5916800260280279327)
XLA Ops:
  10.0 6.0 psum.14
  16.0 2.1 fusion.12
  18.1 2.7 collective-permute-start
  20.8 2.5 collective-permute-done
  24.1 2.5 copy.33
  28.0 54.1 %all-gather.3.cloned.1.call-done = bf16[1,512,4096]{2,1,0:T(8,128)(2,1)} async-done(((bf16[1,512,2048]{2,1,0:T(8,128)(2,1)}), bf16[1,512,4096]{2,1,0:T(8,128)(2,1)}) %all-gather.3.cloned.1.call-update) | async-done | bytes 4194320 | tf_op jit(solution)/shard_map/all_gather | solution.py:61
  82.1 129.1 %all-gather.5.cloned.1.call-done = bf16[4096,2048]{1,0:T(8,128)(2,1)} async-done(((bf16[256,2048]{1,0:T(8,128)(2,1)}), bf16[4096,2048]{1,0:T(8,128)(2,1)}) %all-gather.5.cloned.1.call-update) | async-done | bytes 16777232 | tf_op jit(solution)/shard_map/all_gather | solution.py:63
  211.2 14.5 %fusion.18 = bf16[512,2048]{1,0:T(8,128)(2,1)} fusion(bf16[4096,2048]{1,0:T(8,128)(2,1)} %all-gather.5.cloned.1.call-done, bf16[1,512,4096]{2,1,0:T(8,128)(2,1)} %all-gather.3.cloned.1.call-done), kind=kOutput, calls=%fused_computation.26 | convolution fusion | flops 8590983168 | bytes 23068672 | tf_op jit(solution)/shard_map/dot_general | solution.py:64
  225.7 3.9 copy.31
  229.6 11.0 %fusion.39 = (f32[16,512]{1,0:T(8,128)S(1)}, f32[16,512,512]{1,2,0:T(8,128)}) fusion(pred[512]{0:T(512)(128)(4,1)S(1)} %iota_compare_fusion.1, bf16[1,512,16,2,64]{1,4,3,2,0:T(8,128)(2,1)} %bitcast.131, bf16[1,512,16,2,64]{1,4,3,2,0:T(8,128)(2,1)} %bitcast.126), kind=kOutput, calls=%fused_computation.57 | convolution fusion | flops 553648640 | bytes 18907648 | tf_op jit(solution)/shard_map/sub | solution.py:26
  240.7 6.8 %fusion.8 = bf16[16,512,512]{1,2,0:T(8,128)(2,1)S(1)} fusion(f32[16,512,512]{1,2,0:T(8,128)} %get-tuple-element.9, f32[16,512]{1,0:T(8,128)S(1)} %get-tuple-element.8), kind=kLoop, calls=%fused_computation.12 | loop fusion | flops 8388608 | bytes 25198592 | tf_op jit(solution)/shard_map/convert_element_type | solution.py:28
  247.5 3.6 fusion.27
  252.7 7.6 %multiply_convert_fusion.1 = bf16[16,512,512]{1,2,0:T(8,128)(2,1)S(1)} fusion(f32[16,512]{1,0:T(8,128)S(1)} %fusion.23, f32[16,512,512]{1,2,0:T(8,128)} %get-tuple-element.9, f32[16,512]{1,0:T(8,128)S(1)} %get-tuple-element.8, bf16[1,512,16,2,64]{1,4,3,2,0:T(8,128)(2,1)S(1)} %bitcast.133, bf16[1,512,16,2,64]{1,4,3,2,0:T(8,128)(2,1)S(1)} %bitcast.129, ...), kind=kOutput, calls=%fused_computation.6 | convolution fusion | flops 558366720 | bytes 27329024 | tf_op jit(solution)/shard_map/pihd,pjhd->phij/dot_general | solution.py:30
  260.3 2.6 fusion.26
  269.0 12.4 %multiply_convert_fusion = bf16[4096,2048]{1,0:T(8,128)(2,1)} fusion(bf16[512,2048]{0,1:T(8,128)(2,1)S(1)} %bitcast.137, bf16[1,512,4096]{2,1,0:T(8,128)(2,1)S(1)} %copy-done.6), kind=kOutput, calls=%fused_computation.1 | convolution fusion | flops 8606711808 | bytes 23068672 | tf_op jit(solution)/shard_map/dot_general | solution.py:80
  281.5 14.7 %fusion.9 = bf16[1,1,512,4096]{3,2,1,0:T(8,128)(2,1)} fusion(bf16[512,2048]{0,1:T(8,128)(2,1)} %bitcast.138, bf16[4096,2048]{1,0:T(8,128)(2,1)} %all-gather.5.cloned.1.call-done), kind=kOutput, calls=%fused_computation.14 | convolution fusion | flops 8592031744 | bytes 23068672 | tf_op jit(solution)/shard_map/dot_general | solution.py:91
  296.2 18.9 %copy.42 = bf16[1,1,512,4096]{2,1,0,3:T(2,128)(2,1)} copy(bf16[1,1,512,4096]{3,2,1,0:T(8,128)(2,1)} %fusion.9) | data formatting | bytes 8388608 | tf_op jit(solution)/shard_map/reshape | solution.py:94
  315.6 28.5 %reduce.11 = bf16[4096,512]{1,0:T(8,128)(2,1)} reduce(bf16[4096,1,1,512]{3,2,1,0:T(2,128)(2,1)} %bitcast.123, bf16[]{:T(256)} %broadcast.112), dimensions={1,2}, to_apply=%bitcast.101.reduce_sub_computation | reduce | bytes 8388610
  344.2 6.0 reshape.260
  350.1 55.7 %all_to_all.4 = bf16[2,2,524288]{2,1,0:T(2,128)(2,1)} all-to-all(bf16[2,2,524288]{2,1,0:T(2,128)(2,1)} %reshape.260), channel_id=1, replica_groups=mesh['dp'=8,'phase'=2,'mp'=2] {'mp'}, dimensions={0} | all-to-all | bytes 8388608 | tf_op jit(solution)/shard_map/all_to_all | solution.py:95
  405.8 7.1 %reshape.261 = bf16[4096,1,1,512]{3,2,1,0:T(2,128)(2,1)} reshape(bf16[2,2,524288]{2,1,0:T(2,128)(2,1)} %all_to_all.4) | data formatting | bytes 8388608
  412.9 7.7 %copy.59 = f32[1,1,512,4096]{2,3,0,1:T(8,128)} copy(bf16[1,1,512,4096]{2,1,0,3:T(2,128)(2,1)} %bitcast.125) | data formatting | bytes 12582912
  420.7 6.9 %reduce_sum.43 = f32[512,2048]{0,1:T(8,128)} reduce(f32[512,2,2048]{0,2,1:T(8,128)} %bitcast.124, f32[]{:T(128)} %constant.3.clone.1), dimensions={1}, to_apply=%region_4.5 | reduce | flops 1048576 | bytes 12582916 | tf_op jit(solution)/shard_map/reduce_sum | solution.py:96
  427.6 5.4 copy.60
  434.2 127.5 %reduce-scatter.2.cloned.1.call-done = bf16[512,2048]{1,0:T(8,128)(2,1)} async-done(((bf16[4096,2048]{1,0:T(8,128)(2,1)}), bf16[512,2048]{1,0:T(8,128)(2,1)}) %reduce-scatter.2.cloned.1.call-update) | async-done | bytes 2097168 | tf_op jit(solution)/shard_map/reduce_scatter | solution.py:77
  561.7 2.9 slice.28
  565.9 3.1 copy.45
  569.0 3.9 copy.46
  572.9 2.8 fusion.13
  575.8 35.0 %psum.15 = f32[2048]{0:T(1024)} all-reduce(f32[2048]{0:T(1024)S(1)} %broadcast_multiply_fusion), channel_id=1, replica_groups=mesh['dp'=8,'phase'=2,'mp'=2] {'dp','phase'}, use_global_device_ids=true, to_apply=%region_7.8 | all-reduce | flops 2048 | bytes 16384 | tf_op jit(solution)/shard_map/psum | solution.py:100
  610.7 4.4 fusion.22
  615.7 3.2 slice_select_fusion
  (36 shorter events, 14.8 us)
Async XLA Ops:
  7.2 74.9 %all-gather.3.cloned.1.call-start = ((), (), s32[]{:S(2)}) async-start(), calls=%async_computation.2 | async-start | bytes 6291456 | tf_op jit(solution)/shard_map/all_gather | solution.py:61
  10.0 14.2 %copy-start = (bf16[1,1,512,2048]{3,2,1,0:T(8,128)(2,1)S(1)}, bf16[1,1,512,2048]{3,2,1,0:T(8,128)(2,1)}, u32[]{:S(2)}) copy-start(bf16[1,1,512,2048]{3,2,1,0:T(8,128)(2,1)} %param.5) | copy-start | bytes 6291460
  18.1 5.2 collective-permute-start
  23.3 187.8 %all-gather.5.cloned.1.call-start = ((), (), s32[]{:S(2)}) async-start(), calls=%async_computation.3 | async-start | bytes 17825792 | tf_op jit(solution)/shard_map/all_gather | solution.py:63
  24.1 537.6 %reduce-scatter.2.cloned.1.call-start = ((), (), s32[]{:S(2)}) async-start(), calls=%async_computation.4 | async-start | bytes 18874368 | tf_op jit(solution)/shard_map/reduce_scatter | solution.py:77
  240.7 6.9 %copy-start.1 = (bf16[1,1,512,2048]{2,3,1,0:T(8,128)(2,1)S(1)}, bf16[1,1,512,2048]{2,3,1,0:T(8,128)(2,1)}, u32[]{:S(2)}) copy-start(bf16[1,1,512,2048]{2,3,1,0:T(8,128)(2,1)} %copy.33) | copy-start | bytes 6291460
  247.5 3.7 copy-start.2
  262.9 1.5 copy-start.4
  266.1 2.9 copy-start.6
  266.2 1.3 copy-start.5
  432.9 140.0 %collective-permute-start.1 = (f32[1,512,2048]{2,1,0:T(8,128)}, f32[1,512,2048]{2,1,0:T(8,128)}, u32[]{:S(2)}, u32[]{:S(2)}) collective-permute-start(f32[1,512,2048]{2,1,0:T(8,128)} %bitcast.136), channel_id=1, source_target_pairs={{2,0},{3,1},{6,4},{7,5},{10,8},{11,9},{14,12},{15,13},{18,16},{19,... | collective-permute-start | bytes 12582920 | tf_op jit(solution)/shard_map/ppermute | solution.py:16
  564.6 51.1 %collective-permute-start.2 = (f32[256,2048]{1,0:T(8,128)}, f32[256,2048]{1,0:T(8,128)}, u32[]{:S(2)}, u32[]{:S(2)}) collective-permute-start(f32[256,2048]{1,0:T(8,128)} %slice.28), channel_id=1, source_target_pairs={{2,0},{3,1},{6,4},{7,5},{10,8},{11,9},{14,12},{15,13},{18,16},{19,... | collective-permute-start | bytes 6291464 | tf_op jit(solution)/shard_map/ppermute | solution.py:16
  610.7 4.4 copy-start.3
Sparse Core Ops, SparseCore 0:
  23.5 58.5 all-gather.2
  84.2 126.8 all-gather.4
  281.6 280.0 reduce-scatter.1
where the time goes:
time: 636 us; the launch traced here: 626 us
  waiting for transfers between devices  314 us (49%)
  blocking collectives  96.6 us (15%)
  matrix products  69.5 us (11%)
  local copies, waits for them, and re-layouts  64.9 us (10%)
  other arithmetic  59.8 us (9%)
  between operations  15.7 us (2%)
    all_gather x1, waiting for transfers between devices, on_device(): whole_weight = lax.all_gather(w_kv, ('dp', 'phase'), axis=0, tiled=True)  129 us
    reduce_scatter x1, waiting for transfers between devices, on_device(): lax.psum_scatter((pair_scale * lax.dot_general(enc_rows, grad_kv, (((0,),...  128 us
    all_to_all x1, blocking collectives, on_device(): lax.all_to_all(partial_enc, 'mp', split_axis=3, concat_axis=0, tiled=True)  55.7 us
    all_gather x1, waiting for transfers between devices, on_device(): enc_full = lax.all_gather(enc_moved, 'mp', axis=2, tiled=True)  54.1 us
    psum x1, blocking collectives, on_device(): d_gain = lax.psum(gain_term, ('dp', 'phase'))  35 us
    unnamed x20, local copies, waits for them, and re-layouts  32 us
    unnamed x1, other arithmetic  28.5 us
    reshape x1, local copies, waits for them, and re-layouts, on_device(): partial_enc = partial_enc.reshape(1, pair_dev, length, D)  18.9 us
  transfers between devices with their start and end apart: 6, of which 4 were waited for; matrix products, arithmetic and copies ran while one was open for 19% of the time, Pallas kernels for 0%

commit v1 on v0

v1 whole, which is shorter than its diff:
```python
import jax
import jax.numpy as jnp
from jax import lax
from jax.experimental import pallas as pl
from jax.experimental.pallas import tpu as pltpu
from jax.sharding import Mesh, PartitionSpec as P

D = 4096
HEAD = 64
EPS = 1e-06
F32 = jnp.float32
BF16 = jnp.bfloat16

PLANE = ("y", "phase")
SWAP = [(0, 1), (1, 0)]


def attend_kernel(len_ref, qg_ref, kv_ref, dec_ref, gkv_ref):
    length = qg_ref.shape[0]
    qg = qg_ref[...]
    kv = kv_ref[...]
    low_lane = lax.broadcasted_iota(jnp.int32, qg.shape, 1) < HEAD
    factor = jnp.asarray(1.0 / HEAD**0.5, BF16)
    zero = jnp.zeros((), BF16)
    scaled = qg * factor
    queries = jnp.where(low_lane, scaled, zero)
    grads = jnp.where(low_lane, zero, scaled)
    keys = lax.broadcasted_iota(jnp.int32, (1, length), 1)
    bias = jnp.where(keys < len_ref[0], 0.0, -1e30).astype(F32)
    nt = (((1,), (1,)), ((), ()))
    nn = (((1,), (0,)), ((), ()))
    scores = lax.dot_general(queries, kv, nt, preferred_element_type=F32) + bias
    grad_prob = lax.dot_general(grads, kv, nt, preferred_element_type=F32)
    weights = jnp.exp(scores - jnp.max(scores, axis=-1, keepdims=True))
    probs = weights * (1.0 / jnp.sum(weights, axis=-1, keepdims=True))
    prob_low = probs.astype(BF16)
    attended = lax.dot_general(prob_low, kv, nn, preferred_element_type=F32)
    row_delta = jnp.sum(grads.astype(F32) * attended, axis=-1, keepdims=True)
    grad_score = (probs * (grad_prob - row_delta)).astype(BF16)
    grad_query = lax.dot_general(grad_score, kv, nn, preferred_element_type=F32)
    qg_t = qg.T
    key_t = lax.dot_general(qg_t[:HEAD], grad_score, nn, preferred_element_type=F32)
    value_t = lax.dot_general(qg_t[HEAD:], prob_low, nn, preferred_element_type=F32)
    gkv = jnp.concatenate([key_t, value_t], axis=0).T
    gkv_ref[...] = gkv.astype(BF16)
    rolled = pltpu.roll(gkv, HEAD, 1)
    dec_ref[...] = jnp.where(low_lane, grad_query, rolled).astype(BF16)


def attend(key_count, qg, kv):
    length, width = qg.shape
    block = pl.BlockSpec((length, 2 * HEAD), lambda h, n: (0, h))
    return pl.pallas_call(
        attend_kernel,
        grid_spec=pltpu.PrefetchScalarGridSpec(
            num_scalar_prefetch=1,
            grid=(width // (2 * HEAD),),
            in_specs=[block, block],
            out_specs=[block, block],
        ),
        out_shape=[jax.ShapeDtypeStruct((length, width), BF16)] * 2,
        compiler_params=pltpu.CompilerParams(vmem_limit_bytes=32 << 20),
        name="attend",
    )(key_count, qg, kv)


def cut(array, axis, index, size):
    return lax.dynamic_slice_in_dim(array, index * size, size, axis)


def ordered(first, own, other, axis):
    return jnp.where(
        first, jnp.concatenate([own, other], axis), jnp.concatenate([other, own], axis)
    )


def matmul(a, b, dims):
    return lax.dot_general(a, b, ((dims[:1], dims[1:]), ((), ())), preferred_element_type=F32)


def on_device(sec_acts, gain, w_kv, src_len, tgt_len):
    groups = lax.axis_size("z")
    shards = lax.axis_size("mp")
    y, core, x = lax.axis_index("y"), lax.axis_index("phase"), lax.axis_index("mp")
    straight = y == core
    packed = sec_acts[0, 0]
    length, width = packed.shape
    rows = w_kv.shape[0]
    half = width // 2
    pair_scale = 1.0 / (2 * groups)

    def across(value, turn, plane):
        moves = [
            (i * shards + s, i * shards + (s + turn) % shards) for i in plane for s in range(shards)
        ]
        return lax.ppermute(value, ("y", "phase", "mp"), moves)

    sent = lax.ppermute(cut(w_kv, 1, 1 - y, half), "y", SWAP)
    w_block = ordered(y == 0, cut(w_kv, 1, y, half), sent, 0)
    w_own = lax.all_gather(w_block, "z", axis=0, tiled=True)
    w_other = lax.ppermute(w_own, "phase", SWAP)

    here = lax.ppermute(packed, PLANE, [(0, 0), (2, 3)])
    there = lax.ppermute(packed, PLANE, [(0, 2), (2, 1)])
    raw = [jnp.where(straight, here, there)]
    gains = [gain]
    for turn in range(1, shards):
        raw.append(
            jnp.where(straight, across(here, turn, (0, 3)), across(there, turn, (1, 2)))
        )
        gains.append(lax.ppermute(gain, "mp", [(s, (s + turn) % shards) for s in range(shards)]))

    def natural(parts):
        if shards == 2:
            return [jnp.where(x == i, parts[0], parts[1]) for i in range(2)]
        stacked = jnp.stack(parts)
        return [
            lax.dynamic_index_in_dim(stacked, (x - i) % shards, 0, keepdims=False)
            for i in range(shards)
        ]

    hidden = jnp.concatenate(natural(raw), axis=1).astype(F32)
    gain_all = jnp.concatenate(natural(gains)).astype(F32)
    inv_rms = lax.rsqrt(jnp.sum(hidden * hidden, axis=-1, keepdims=True) / D + EPS)
    encoded = (hidden * inv_rms * gain_all).astype(BF16)
    by_core = encoded.reshape(length, 2 * groups, 2, rows)
    enc_0 = by_core[:, :, 0].reshape(length, -1)
    enc_1 = by_core[:, :, 1].reshape(length, -1)
    enc_own = jnp.where(core == 0, enc_0, enc_1)
    enc_other = jnp.where(core == 0, enc_1, enc_0)

    position = lax.broadcasted_iota(jnp.int32, (length, width), 0)
    is_grad = lax.broadcasted_iota(jnp.int32, (length, width), 1) % (2 * HEAD) >= HEAD
    masked = jnp.where(is_grad & (position >= tgt_len[0]), jnp.zeros((), BF16), packed)
    qg_here = lax.ppermute(cut(masked, 1, y, half), PLANE, [(1, 0), (3, 3)])
    qg_there = lax.ppermute(cut(masked, 1, 1 - y, half), PLANE, [(1, 2), (3, 1)])
    qg = jnp.where(straight, qg_here, qg_there)
    key_count = jnp.where(straight, src_len, lax.ppermute(src_len, "y", SWAP))

    kv = (matmul(enc_own, w_own, (1, 0)) + matmul(enc_other, w_other, (1, 0))).astype(BF16)
    dec, gkv = attend(key_count, qg, kv)

    dw_other = (pair_scale * matmul(enc_other, gkv, (0, 0))).astype(BF16)
    dw_own = pair_scale * matmul(enc_own, gkv, (0, 0))
    dw_chip = (dw_own + lax.ppermute(dw_other, "phase", SWAP).astype(F32)).astype(BF16)
    dw = lax.psum_scatter(dw_chip, "z", scatter_dimension=0, tiled=True)
    dw_sent = lax.ppermute(cut(dw, 0, 1 - y, rows), "y", SWAP)
    d_wkv = ordered(y == 0, cut(dw, 0, y, rows), dw_sent, 1).astype(F32)

    de_own = matmul(gkv, w_own, (1, 1)).astype(BF16)
    de_other = matmul(gkv, w_other, (1, 1)).astype(BF16)

    def features(shard):
        return jnp.concatenate(
            [cut(de_own, 1, shard, half), cut(de_other, 1, shard, half)], axis=1
        )

    total = features(x).astype(F32)
    for turn in range(1, shards):
        moved = lax.ppermute(
            features((x + turn) % shards), "mp", [(s, (s + turn) % shards) for s in range(shards)]
        )
        total = total + moved.astype(F32)
    total = total + lax.ppermute(total.astype(BF16), PLANE, [(2, 0), (1, 3)]).astype(F32)
    split = total.reshape(length, 2, -1, rows)
    first = jnp.where(core == 0, split[:, 0], split[:, 1])
    second = jnp.where(core == 0, split[:, 1], split[:, 0])
    grad_enc = jnp.stack([first, second], axis=2).reshape(length, width)
    grad_normed = (grad_enc * gain.astype(F32)).astype(BF16)
    enc_grads = lax.ppermute(grad_normed, PLANE, [(0, 0), (3, 2)])
    normed = raw[0].astype(F32) * inv_rms
    gain_term = pair_scale * jnp.sum(grad_enc * normed, axis=0)
    gain_term = jnp.where(straight, gain_term, 0.0)
    d_gain = lax.psum(gain_term, ("z", "y", "phase"))

    dec_here = lax.ppermute(dec, PLANE, [(0, 1), (3, 3)])
    dec_there = lax.ppermute(dec, PLANE, [(2, 1), (1, 3)])
    dec_grads = ordered(y == 0, dec_here, dec_there, 1)
    sec_grads = jnp.where(core == 0, enc_grads, dec_grads)[None, None]
    return (sec_grads, d_wkv, d_gain)


def solution(mesh):
    size = mesh.shape
    split = (size["dp"] // 2, 2, size["phase"], size["mp"])
    fine = Mesh(mesh.devices.reshape(split), ("z", "y", "phase", "mp"))
    pairs = ("z", "y")
    acts = P("phase", pairs, None, "mp")
    weights = P(("z", "y", "phase"), "mp")
    return jax.shard_map(
        on_device,
        mesh=fine,
        in_specs=(acts, P("mp"), weights, P(pairs), P(pairs)),
        out_specs=(acts, weights, P("mp")),
        check_vma=False,
    )
```

time: 636 us -> 383 us (0.60); the launches traced: 626 us -> 380 us
  waiting for transfers between devices: 314 us -> 140 us
  blocking collectives: 96.6 us -> 31.4 us
  starting transfers between devices: 5.33 us -> 61.5 us
  matrix products: 69.5 us -> 21.4 us
  local copies, waits for them, and re-layouts: 64.9 us -> 46.8 us
  Pallas kernels: 0 us -> 12.8 us
  other arithmetic: 59.8 us -> 50.3 us
    all_gather x2 -> x1, waiting for transfers between devices: 183 us -> 34.4 us  [on_device(): w_own = lax.all_gather(w_block, 'z', axis=0, tiled=True)]
    reduce_scatter x1, waiting for transfers between devices: 128 us -> 0.01 us  [on_device(): dw = lax.psum_scatter(dw_chip, 'z', scatter_dimension=0, tiled=True)]
    ppermute x3 -> x17, waiting for transfers between devices: 2.55 us -> 105 us  [the longest x1 38.2 us: on_device(): lax.ppermute(features((x + turn) % shards), 'mp', [(s, (s + turn) % shard...]
    ppermute x3 -> x17, starting transfers between devices: 5.21 us -> 61.4 us  [the longest x1 20.1 us: on_device(): lax.ppermute(dw_other, 'phase', SWAP).astype(F32)]
    all_to_all x1 -> x0, blocking collectives: 55.7 us -> none  [on_device(): lax.all_to_all(partial_enc, 'mp', split_axis=3, concat_axis=0, tiled=True)]
    dot_general x8 -> x6, matrix products: 58.5 us -> 21.4 us  [matmul(): lax.dot_general(a, b, ((dims[:1], dims[1:]), ((), ())), preferred_element...]
    unnamed x1 -> x0, other arithmetic: 28.5 us -> none
    unnamed x20 -> x24, local copies, waits for them, and re-layouts: 32 us -> 5.14 us
  transfers between devices with their start and end apart: 6 -> 19, of which waited for: 4 -> 7; matrix products, arithmetic and copies ran while one was open for 19% -> 25% of each run, Pallas kernels for 0% -> 0%
where the time goes in v1:
time: 383 us; the launch traced here: 380 us
  waiting for transfers between devices  140 us (37%)
  starting transfers between devices  61.5 us (16%)
  other arithmetic  50.3 us (13%)
  local copies, waits for them, and re-layouts  46.8 us (12%)
  blocking collectives  31.4 us (8%)
  matrix products  21.4 us (6%)
  between operations  16.3 us (4%)
  Pallas kernels  12.8 us (3%)
    ppermute x1, waiting for transfers between devices, on_device(): lax.ppermute(features((x + turn) % shards), 'mp', [(s, (s + turn) % shard...  38.2 us
    all_gather x1, waiting for transfers between devices, on_device(): w_own = lax.all_gather(w_block, 'z', axis=0, tiled=True)  34.4 us
    psum x1, blocking collectives, on_device(): d_gain = lax.psum(gain_term, ('z', 'y', 'phase'))  31.4 us
    ppermute x1, waiting for transfers between devices, on_device(): lax.ppermute(total.astype(BF16), PLANE, [(2, 0), (1, 3)]).astype(F32)  26.4 us
    dot_general x6, matrix products, matmul(): lax.dot_general(a, b, ((dims[:1], dims[1:]), ((), ())), preferred_element...  21.4 us
    ppermute x1, starting transfers between devices, on_device(): lax.ppermute(dw_other, 'phase', SWAP).astype(F32)  20.1 us
    concatenate x4, local copies, waits for them, and re-layouts, on_device(): hidden = jnp.concatenate(natural(raw), axis=1).astype(F32)  19.5 us
    ppermute x1, waiting for transfers between devices, on_device(): there = lax.ppermute(packed, PLANE, [(0, 2), (2, 1)])  17.9 us
  transfers between devices with their start and end apart: 19, of which 7 were waited for; matrix products, arithmetic and copies ran while one was open for 25% of the time, Pallas kernels for 0%

profile of v1, /device:TPU:0, one launch (start us, length us, event | category | flops | bytes accessed | tf_op | source)
XLA Modules:
  0.0 380.2 jit_solution(9459714761061337934)
XLA Ops:
  8.5 3.0 collective-permute-start.8
  11.5 11.9 %collective-permute-done.8 = bf16[256,1024]{1,0:T(8,128)(2,1)S(1)} collective-permute-done((bf16[256,1024]{1,0:T(8,128)(2,1)S(1)}, bf16[256,1024]{1,0:T(8,128)(2,1)S(1)}, u32[]{:S(2)}, u32[]{:S(2)}) %collective-permute-start.8) | collective-permute-done | bytes 524320 | tf_op jit(solution)/shard_map/ppermute | solution.py:98
  25.0 17.2 %collective-permute-start.3 = (bf16[512,2048]{1,0:T(8,128)(2,1)}, bf16[512,2048]{1,0:T(8,128)(2,1)}, u32[]{:S(2)}, u32[]{:S(2)}) collective-permute-start(bf16[512,2048]{1,0:T(8,128)(2,1)} %bitcast.2), channel_id=1, source_target_pairs={{0,0},{4,6},{1,1},{5,7},{8,8},{12,14},{9,9},{13,15},{16,16},{20,22... | collective-permute-start | bytes 6291464 | tf_op jit(solution)/shard_map/ppermute | solution.py:103
  42.2 2.6 collective-permute-start.4
  49.5 17.9 %collective-permute-done.4 = bf16[512,2048]{1,0:T(8,128)(2,1)} collective-permute-done((bf16[512,2048]{1,0:T(8,128)(2,1)}, bf16[512,2048]{1,0:T(8,128)(2,1)}, u32[]{:S(2)}, u32[]{:S(2)}) %collective-permute-start.4) | collective-permute-done | bytes 2097184 | tf_op jit(solution)/shard_map/ppermute | solution.py:104
  69.3 3.6 fusion.1
  72.9 34.4 %all-gather.2.cloned.1.call-done = bf16[2048,1024]{1,0:T(8,128)(2,1)} async-done(((bf16[512,1024]{1,0:T(8,128)(2,1)}), bf16[2048,1024]{1,0:T(8,128)(2,1)}) %all-gather.2.cloned.1.call-update) | async-done | bytes 4194320 | tf_op jit(solution)/shard_map/all_gather | solution.py:100
  107.3 2.7 constant_dynamic-slice_fusion.8
  119.0 2.8 broadcast_select_fusion.5
  124.8 4.5 %concatenate.45 = bf16[512,4,2,256]{3,2,1,0:T(2,128)(2,1)} reshape(bf16[512,2048]{1,0:T(8,128)(2,1)} %broadcast_select_fusion.2) | data formatting | bytes 4194304 | tf_op jit(solution)/shard_map/concatenate | solution.py:122
  129.3 6.1 %copy.15 = bf16[512,4,2,256]{0,3,1,2:T(8,128)(2,1)} copy(bf16[512,4,2,256]{3,2,1,0:T(2,128)(2,1)} %concatenate.45) | data formatting | bytes 4194304 | tf_op jit(solution)/shard_map/concatenate | solution.py:122
  135.4 2.7 concatenate.44
  138.1 6.2 %copy.14 = bf16[512,4,2,256]{0,3,1,2:T(8,128)(2,1)} copy(bf16[512,4,2,256]{3,2,1,0:T(2,128)(2,1)} %concatenate.44) | data formatting | bytes 4194304 | tf_op jit(solution)/shard_map/concatenate | solution.py:122
  148.5 5.4 %fusion.14 = f32[512,1024]{1,0:T(8,128)S(1)} fusion(bf16[512,2048]{0,1:T(8,128)(2,1)S(1)} %bitcast.27, bf16[2048,1024]{1,0:T(8,128)(2,1)} %collective-permute-done.9), kind=kOutput, calls=%fused_computation.58 | convolution fusion | flops 2147483648 | bytes 8388608 | tf_op jit(solution)/shard_map/dot_general | solution.py:78
  156.3 12.8 %attend.1 = (bf16[512,1024]{1,0:T(8,128)(2,1)S(1)}, bf16[512,1024]{1,0:T(8,128)(2,1)S(1)}) custom-call(s32[1]{0:T(128)S(6)} %select_n.178.len_ref, bf16[512,1024]{1,0:T(8,128)(2,1)S(1)} %broadcast_select_fusion.8.qg_ref, bf16[512,1024]{1,0:T(8,128)(2,1)S(1)} %add_convert_fusion.1.kv_ref), custom_call_target="tpu_custom_call" | custom-call | tf_op jit(solution)/shard_map/attend/pallas_call | solution.py:53
  169.1 4.3 %multiply_convert_fusion = bf16[2048,1024]{1,0:T(8,128)(2,1)} fusion(bf16[512,2048]{0,1:T(8,128)(2,1)S(1)} %bitcast.28, bf16[512,1024]{1,0:T(8,128)(2,1)S(1)} %get-tuple-element.5), kind=kOutput, calls=%fused_computation.1 | convolution fusion | flops 2151677952 | bytes 7340032 | tf_op jit(solution)/shard_map/dot_general | solution.py:78
  173.5 20.1 %collective-permute-start.15 = (bf16[2048,1024]{1,0:T(8,128)(2,1)}, bf16[2048,1024]{1,0:T(8,128)(2,1)}, u32[]{:S(2)}, u32[]{:S(2)}) collective-permute-start(bf16[2048,1024]{1,0:T(8,128)(2,1)} %multiply_convert_fusion), channel_id=1, source_target_pairs={{0,2},{2,0},{1,3},{3,1},{4,6},{6,4},{5,7},{7,5},{8,10},{10,8},{9,1... | collective-permute-start | bytes 12582920 | tf_op jit(solution)/shard_map/ppermute | solution.py:145
  193.5 4.6 %convolution_convert_fusion = bf16[512,2048]{1,0:T(8,128)(2,1)S(1)} fusion(bf16[512,1024]{1,0:T(8,128)(2,1)S(1)} %get-tuple-element.5, bf16[2048,1024]{1,0:T(8,128)(2,1)} %collective-permute-done.9), kind=kOutput, calls=%fused_computation.15 | convolution fusion | flops 2148532224 | bytes 7340032 | tf_op jit(solution)/shard_map/dot_general | solution.py:78
  209.2 5.8 %add_convert_fusion = bf16[2048,1024]{1,0:T(8,128)(2,1)} fusion(bf16[2048,1024]{1,0:T(8,128)(2,1)} %collective-permute-done.15, f32[2048,1024]{1,0:T(8,128)S(1)} %fusion.15), kind=kLoop, calls=%fused_computation | loop fusion | flops 8388608 | bytes 16777216 | tf_op jit(solution)/shard_map/convert_element_type | solution.py:145
  215.0 38.2 %collective-permute-done.10 = bf16[512,2048]{1,0:T(8,128)(2,1)} collective-permute-done((bf16[512,2048]{1,0:T(8,128)(2,1)}, bf16[512,2048]{1,0:T(8,128)(2,1)}, u32[]{:S(2)}, u32[]{:S(2)}) %collective-permute-start.10) | collective-permute-done | bytes 2097184 | tf_op jit(solution)/shard_map/ppermute | solution.py:160
  257.2 26.4 %collective-permute-done.11 = bf16[512,2048]{1,0:T(8,128)(2,1)S(1)} collective-permute-done((bf16[512,2048]{1,0:T(8,128)(2,1)S(1)}, bf16[512,2048]{1,0:T(8,128)(2,1)S(1)}, u32[]{:S(2)}, u32[]{:S(2)}) %collective-permute-start.11) | collective-permute-done | bytes 2097184 | tf_op jit(solution)/shard_map/ppermute | solution.py:164
  283.6 4.8 %convert_add_fusion = f32[512,2048]{1,0:T(8,128)} fusion(bf16[512,2048]{1,0:T(8,128)(2,1)S(1)} %collective-permute-done.11, bf16[512,2048]{1,0:T(8,128)(2,1)} %collective-permute-done.10, bf16[512,1024]{1,0:T(8,128)(2,1)S(1)} %get-tuple-element.19, bf16[512,1024]{1,0:T(8,128)(2,1)S(1)} %copy-done.2), kind=kLoop, calls=%fused_computation.7 | loop fusion | flops 8388608 | bytes 10485760 | tf_op jit(solution)/shard_map/add | solution.py:164
  288.4 6.0 %reshape.91 = f32[512,2,4,256]{3,2,1,0:T(4,128)} reshape(f32[512,2048]{1,0:T(8,128)} %convert_add_fusion) | data formatting | bytes 8388608 | tf_op jit(solution)/shard_map/reshape | solution.py:165
  294.5 2.9 fusion.13
  297.4 5.1 %fusion.3 = (f32[512,4,1,256]{3,2,1,0:T(1,128)S(1)}, f32[512,4,1,256]{3,2,1,0:T(1,128)S(1)}) fusion(pred[]{:T(512)S(6)} %eq.14, f32[512,1,4,256]{3,2,1,0:T(4,128)S(1)} %get-tuple-element.14, f32[512,1,4,256]{3,2,1,0:T(4,128)S(1)} %get-tuple-element.13), kind=kLoop, calls=%fused_computation.17 | loop fusion | flops 1048576 | bytes 8388609 | tf_op jit(solution)/shard_map/jit(_where)/select_n | solution.py:166
  302.5 5.7 %pad_maximum_fusion = f32[512,4,2,256]{3,2,1,0:T(2,128)} fusion(f32[512,4,1,256]{3,2,1,0:T(1,128)S(1)} %get-tuple-element.12, f32[512,4,1,256]{3,2,1,0:T(1,128)S(1)} %get-tuple-element.11), kind=kLoop, calls=%fused_computation.4 | loop fusion | flops 1048576 | bytes 8388608 | tf_op jit(solution)/shard_map/stack | solution.py:168
  308.2 6.6 %reshape.92 = f32[512,2048]{1,0:T(8,128)} reshape(f32[512,4,2,256]{3,2,1,0:T(2,128)} %pad_maximum_fusion) | data formatting | bytes 8388608 | tf_op jit(solution)/shard_map/reshape | solution.py:168
  314.8 4.6 %multiply_reduce_fusion.1 = (f32[2048]{0:T(1024)S(1)}, bf16[512,2048]{1,0:T(8,128)(2,1)}) fusion(f32[512,2048]{1,0:T(8,128)} %reshape.92, bf16[512,2048]{1,0:T(8,128)(2,1)S(1)} %copy-done.1, f32[512]{0:T(512)S(1)} %add_rsqrt_fusion, f32[2048]{0:T(1024)S(1)} %get-tuple-element.29), kind=kLoop, calls=%fused_computation.5 | loop fusion | flops 6289408 | bytes 8407040 | tf_op jit(solution)/shard_map/reduce_sum | solution.py:172
  323.3 2.7 collective-permute-start.13
  326.0 31.4 %psum.7 = f32[2048]{0:T(1024)} all-reduce(f32[2048]{0:T(1024)S(1)} %multiply_select_fusion), channel_id=1, replica_groups=mesh['z'=4,'y'=2,'phase'=2,'mp'=2] {'z','y','phase'}, use_global_device_ids=true, to_apply=%region_3.4 | all-reduce | flops 2048 | bytes 16384 | tf_op jit(solution)/shard_map/psum | solution.py:174
  358.8 4.1 %fusion.6 = bf16[1,1,512,2048]{3,2,1,0:T(8,128)(2,1)} fusion(bf16[512,2048]{1,0:T(8,128)(2,1)S(1)} %collective-permute-done.12, bf16[512,1024]{1,0:T(8,128)(2,1)} %collective-permute-done.14, bf16[512,1024]{1,0:T(8,128)(2,1)} %collective-permute-done.13, pred[]{:T(512)S(6)} %eq.31, pred[]{:T(512)S(6)} %eq.14), kind=kLoop, calls=%fused_computation.23 | loop fusion | flops 10485760 | bytes 6291458 | tf_op jit(solution)/shard_map/broadcast_in_dim | solution.py:179
  362.9 8.8 %collective-permute-done.16 = bf16[256,1024]{1,0:T(8,128)(2,1)S(1)} collective-permute-done((bf16[256,1024]{1,0:T(8,128)(2,1)S(1)}, bf16[256,1024]{1,0:T(8,128)(2,1)S(1)}, u32[]{:S(2)}, u32[]{:S(2)}) %collective-permute-start.16) | collective-permute-done | bytes 524320 | tf_op jit(solution)/shard_map/ppermute | solution.py:147
  (80 shorter events, 47.8 us)
Async XLA Ops:
  7.2 100.2 %all-gather.2.cloned.1.call-start = ((), (), s32[]{:S(2)}) async-start(), calls=%async_computation.1 | async-start | bytes 5242880 | tf_op jit(solution)/shard_map/all_gather | solution.py:100
  8.5 36.3 %copy-start.9 = (bf16[2048]{0:T(1024)(128)(2,1)S(1)}, bf16[2048]{0:T(1024)(128)(2,1)}, u32[]{:S(2)}) copy-start(bf16[2048]{0:T(1024)(128)(2,1)} %param.6) | copy-start | bytes 12292
  8.5 15.0 %collective-permute-start.8 = (bf16[256,1024]{1,0:T(8,128)(2,1)S(1)}, bf16[256,1024]{1,0:T(8,128)(2,1)S(1)}, u32[]{:S(2)}, u32[]{:S(2)}) collective-permute-start(bf16[256,1024]{1,0:T(8,128)(2,1)S(1)} %get-tuple-element.26), channel_id=1, source_target_pairs={{0,4},{4,0},{1,5},{5,1},{2,6},{6,2},{3,7},{7,3},{8,12},{12,8},{9,1... | collective-permute-start | bytes 1572872 | tf_op jit(solution)/shard_map/ppermute | solution.py:98
  25.0 332.4 %reduce-scatter.2.cloned.1.call-start = ((), (), s32[]{:S(2)}) async-start(), calls=%async_computation.2 | async-start | bytes 5242880 | tf_op jit(solution)/shard_map/reduce_scatter | solution.py:146
  25.0 22.2 %collective-permute-start.3 = (bf16[512,2048]{1,0:T(8,128)(2,1)}, bf16[512,2048]{1,0:T(8,128)(2,1)}, u32[]{:S(2)}, u32[]{:S(2)}) collective-permute-start(bf16[512,2048]{1,0:T(8,128)(2,1)} %bitcast.2), channel_id=1, source_target_pairs={{0,0},{4,6},{1,1},{5,7},{8,8},{12,14},{9,9},{13,15},{16,16},{20,22... | collective-permute-start | bytes 6291464 | tf_op jit(solution)/shard_map/ppermute | solution.py:103
  42.2 25.1 %collective-permute-start.4 = (bf16[512,2048]{1,0:T(8,128)(2,1)}, bf16[512,2048]{1,0:T(8,128)(2,1)}, u32[]{:S(2)}, u32[]{:S(2)}) collective-permute-start(bf16[512,2048]{1,0:T(8,128)(2,1)} %bitcast.2), channel_id=1, source_target_pairs={{0,4},{4,2},{1,5},{5,3},{8,12},{12,10},{9,13},{13,11},{16,20},{20,... | collective-permute-start | bytes 6291464 | tf_op jit(solution)/shard_map/ppermute | solution.py:104
  44.8 65.2 %collective-permute-start = (s32[1]{0:T(128)}, s32[1]{0:T(128)}, u32[]{:S(2)}, u32[]{:S(2)}) collective-permute-start(s32[1]{0:T(128)} %param.8), channel_id=1, source_target_pairs={{0,4},{4,0},{1,5},{5,1},{2,6},{6,2},{3,7},{7,3},{8,12},{12,8},{9,1... | collective-permute-start | bytes 20 | tf_op jit(solution)/shard_map/ppermute | solution.py:138
  44.8 66.5 %collective-permute-start.7 = (bf16[2048]{0:T(1024)(128)(2,1)S(1)}, bf16[2048]{0:T(1024)(128)(2,1)S(1)}, u32[]{:S(2)}, u32[]{:S(2)}) collective-permute-start(bf16[2048]{0:T(1024)(128)(2,1)S(1)} %copy-done.9), channel_id=1, source_target_pairs={{0,1},{1,0},{2,3},{3,2},{4,5},{5,4},{6,7},{7,6},{8,9},{9,8},{10,11... | collective-permute-start | bytes 12296 | tf_op jit(solution)/shard_map/ppermute | solution.py:111
  47.2 70.5 %collective-permute-start.5 = (bf16[512,2048]{1,0:T(8,128)(2,1)}, bf16[512,2048]{1,0:T(8,128)(2,1)S(1)}, u32[]{:S(2)}, u32[]{:S(2)}) collective-permute-start(bf16[512,2048]{1,0:T(8,128)(2,1)} %collective-permute-done.3), channel_id=1, source_target_pairs={{0,1},{1,0},{6,7},{7,6},{8,9},{9,8},{14,15},{15,14},{16,17},{17,16... | collective-permute-start | bytes 6291464 | tf_op jit(solution)/shard_map/ppermute | solution.py:96
  67.3 51.7 %collective-permute-start.6 = (bf16[512,2048]{1,0:T(8,128)(2,1)}, bf16[512,2048]{1,0:T(8,128)(2,1)}, u32[]{:S(2)}, u32[]{:S(2)}) collective-permute-start(bf16[512,2048]{1,0:T(8,128)(2,1)} %collective-permute-done.4), channel_id=1, source_target_pairs={{2,3},{3,2},{4,5},{5,4},{10,11},{11,10},{12,13},{13,12},{18,19},{1... | collective-permute-start | bytes 6291464 | tf_op jit(solution)/shard_map/ppermute | solution.py:96
  107.3 41.2 %collective-permute-start.9 = (bf16[2048,1024]{1,0:T(8,128)(2,1)}, bf16[2048,1024]{1,0:T(8,128)(2,1)}, u32[]{:S(2)}, u32[]{:S(2)}) collective-permute-start(bf16[2048,1024]{1,0:T(8,128)(2,1)} %all-gather.2.cloned.1.call-done), channel_id=1, source_target_pairs={{0,2},{2,0},{1,3},{3,1},{4,6},{6,4},{5,7},{7,5},{8,10},{10,8},{9,1... | collective-permute-start | bytes 12582920 | tf_op jit(solution)/shard_map/ppermute | solution.py:101
  110.0 6.3 %collective-permute-start.1 = (bf16[512,1024]{1,0:T(8,128)(2,1)}, bf16[512,1024]{1,0:T(8,128)(2,1)}, u32[]{:S(2)}, u32[]{:S(2)}) collective-permute-start(bf16[512,1024]{1,0:T(8,128)(2,1)} %get-tuple-element.22), channel_id=1, source_target_pairs={{2,0},{6,6},{3,1},{7,7},{10,8},{14,14},{11,9},{15,15},{18,16},{22,... | collective-permute-start | bytes 3145736 | tf_op jit(solution)/shard_map/ppermute | solution.py:135
  111.3 5.0 %collective-permute-start.2 = (bf16[512,1024]{1,0:T(8,128)(2,1)S(1)}, bf16[512,1024]{1,0:T(8,128)(2,1)}, u32[]{:S(2)}, u32[]{:S(2)}) collective-permute-start(bf16[512,1024]{1,0:T(8,128)(2,1)S(1)} %get-tuple-element.21), channel_id=1, source_target_pairs={{2,4},{6,2},{3,5},{7,3},{10,12},{14,10},{11,13},{15,11},{18,20},{2... | collective-permute-start | bytes 3145736 | tf_op jit(solution)/shard_map/ppermute | solution.py:136
  117.7 1.3 copy-start.3
  119.0 4.2 %copy-start.4 = (bf16[512,2048]{1,0:T(8,128)(2,1)S(1)}, bf16[512,2048]{1,0:T(8,128)(2,1)}, u32[]{:S(2)}) copy-start(bf16[512,2048]{1,0:T(8,128)(2,1)} %copy-done.3) | copy-start | bytes 6291460
  121.8 1.4 copy-start
  144.3 2.4 copy-start.5
  144.3 2.9 copy-start.6
  148.5 5.4 %copy-start.7 = (bf16[512,8,1,256]{0,3,1,2:T(8,128)(2,1)}, bf16[512,8,1,256]{0,3,1,2:T(8,128)(2,1)S(1)}, u32[]{:S(2)}) copy-start(bf16[512,8,1,256]{0,3,1,2:T(8,128)(2,1)S(1)} %get-tuple-element.15) | copy-start | bytes 6291460
  148.5 5.4 %copy-start.10 = (bf16[2048,1024]{1,0:T(8,128)(2,1)S(1)}, bf16[2048,1024]{1,0:T(8,128)(2,1)}, u32[]{:S(2)}) copy-start(bf16[2048,1024]{1,0:T(8,128)(2,1)} %all-gather.2.cloned.1.call-done) | copy-start | bytes 12582916
  173.5 35.7 %collective-permute-start.15 = (bf16[2048,1024]{1,0:T(8,128)(2,1)}, bf16[2048,1024]{1,0:T(8,128)(2,1)}, u32[]{:S(2)}, u32[]{:S(2)}) collective-permute-start(bf16[2048,1024]{1,0:T(8,128)(2,1)} %multiply_convert_fusion), channel_id=1, source_target_pairs={{0,2},{2,0},{1,3},{3,1},{4,6},{6,4},{5,7},{7,5},{8,10},{10,8},{9,1... | collective-permute-start | bytes 12582920 | tf_op jit(solution)/shard_map/ppermute | solution.py:145
  198.1 2.2 copy-start.11
  203.9 3.0 copy-start.8
  205.4 47.8 %collective-permute-start.10 = (bf16[512,2048]{1,0:T(8,128)(2,1)}, bf16[512,2048]{1,0:T(8,128)(2,1)}, u32[]{:S(2)}, u32[]{:S(2)}) collective-permute-start(bf16[512,2048]{1,0:T(8,128)(2,1)} %pad_maximum_fusion.2), channel_id=1, source_target_pairs={{0,1},{1,0},{2,3},{3,2},{4,5},{5,4},{6,7},{7,6},{8,9},{9,8},{10,11... | collective-permute-start | bytes 6291464 | tf_op jit(solution)/shard_map/ppermute | solution.py:160
  215.0 38.3 %copy-start.2 = (bf16[512,1024]{1,0:T(8,128)(2,1)S(1)}, bf16[512,1024]{1,0:T(8,128)(2,1)}, u32[]{:S(2)}) copy-start(bf16[512,1024]{1,0:T(8,128)(2,1)} %get-tuple-element.17) | copy-start | bytes 3145732
  255.7 27.9 %collective-permute-start.11 = (bf16[512,2048]{1,0:T(8,128)(2,1)S(1)}, bf16[512,2048]{1,0:T(8,128)(2,1)S(1)}, u32[]{:S(2)}, u32[]{:S(2)}) collective-permute-start(bf16[512,2048]{1,0:T(8,128)(2,1)S(1)} %fusion.2), channel_id=1, source_target_pairs={{4,0},{2,6},{5,1},{3,7},{12,8},{10,14},{13,9},{11,15},{20,16},{18,... | collective-permute-start | bytes 6291464 | tf_op jit(solution)/shard_map/ppermute | solution.py:164
  308.2 6.6 %copy-start.1 = (bf16[512,2048]{1,0:T(8,128)(2,1)S(1)}, bf16[512,2048]{1,0:T(8,128)(2,1)}, u32[]{:S(2)}) copy-start(bf16[512,2048]{1,0:T(8,128)(2,1)} %copy-done) | copy-start | bytes 6291460
  319.4 39.3 %collective-permute-start.12 = (bf16[512,2048]{1,0:T(8,128)(2,1)}, bf16[512,2048]{1,0:T(8,128)(2,1)S(1)}, u32[]{:S(2)}, u32[]{:S(2)}) collective-permute-start(bf16[512,2048]{1,0:T(8,128)(2,1)} %get-tuple-element.10), channel_id=1, source_target_pairs={{0,0},{6,4},{1,1},{7,5},{8,8},{14,12},{9,9},{15,13},{16,16},{22,20... | collective-permute-start | bytes 6291464 | tf_op jit(solution)/shard_map/ppermute | solution.py:170
  321.7 37.1 %collective-permute-start.14 = (bf16[512,1024]{1,0:T(8,128)(2,1)S(1)}, bf16[512,1024]{1,0:T(8,128)(2,1)}, u32[]{:S(2)}, u32[]{:S(2)}) collective-permute-start(bf16[512,1024]{1,0:T(8,128)(2,1)S(1)} %get-tuple-element.6), channel_id=1, source_target_pairs={{4,2},{2,6},{5,3},{3,7},{12,10},{10,14},{13,11},{11,15},{20,18},{1... | collective-permute-start | bytes 3145736 | tf_op jit(solution)/shard_map/ppermute | solution.py:177
  323.3 35.4 %collective-permute-start.13 = (bf16[512,1024]{1,0:T(8,128)(2,1)S(1)}, bf16[512,1024]{1,0:T(8,128)(2,1)}, u32[]{:S(2)}, u32[]{:S(2)}) collective-permute-start(bf16[512,1024]{1,0:T(8,128)(2,1)S(1)} %get-tuple-element.6), channel_id=1, source_target_pairs={{0,2},{6,6},{1,3},{7,7},{8,10},{14,14},{9,11},{15,15},{16,18},{22,... | collective-permute-start | bytes 3145736 | tf_op jit(solution)/shard_map/ppermute | solution.py:176
  358.7 13.0 %collective-permute-start.16 = (bf16[256,1024]{1,0:T(8,128)(2,1)S(1)}, bf16[256,1024]{1,0:T(8,128)(2,1)S(1)}, u32[]{:S(2)}, u32[]{:S(2)}) collective-permute-start(bf16[256,1024]{1,0:T(8,128)(2,1)S(1)} %get-tuple-element.24), channel_id=1, source_target_pairs={{0,4},{4,0},{1,5},{5,1},{2,6},{6,2},{3,7},{7,3},{8,12},{12,8},{9,1... | collective-permute-start | bytes 1572872 | tf_op jit(solution)/shard_map/ppermute | solution.py:147
Sparse Core Ops, SparseCore 0:
  25.1 82.2 all-gather.1
  215.1 73.7 reduce-scatter.1

commit v2 on v1

v2 whole, which is shorter than its diff:
```python
import jax
import jax.numpy as jnp
from jax import lax
from jax.experimental import pallas as pl
from jax.experimental.pallas import tpu as pltpu
from jax.sharding import Mesh, PartitionSpec as P

D = 4096
HEAD = 64
EPS = 1e-06
CHUNKS = 2
F32 = jnp.float32
BF16 = jnp.bfloat16
NN = (((1,), (0,)), ((), ()))
NT = (((1,), (1,)), ((), ()))
TN = (((0,), (0,)), ((), ()))

PLANE = ("y", "phase")
SWAP = [(0, 1), (1, 0)]


def dot(a, b, dims=NN):
    return lax.dot_general(a, b, dims, preferred_element_type=F32)


def params(mib):
    return pltpu.CompilerParams(vmem_limit_bytes=mib << 20)


def norm_kernel(groups, rows, at, here, there, far_here, far_there, gain, own, other, natural):
    straight, x, y, core, z = at[0] == 1, at[1], at[2], at[3], at[4]
    width = here.shape[1]
    near = jnp.where(straight, here[...], there[...]).astype(F32)
    far = jnp.where(straight, far_here[...], far_there[...]).astype(F32)
    total = jnp.sum(near * near, axis=-1, keepdims=True) + jnp.sum(far * far, axis=-1, keepdims=True)
    inv_rms = lax.rsqrt(total / D + EPS)
    near_at = pl.ds(pl.multiple_of(x * width, width), width)
    far_at = pl.ds(pl.multiple_of((1 - x) * width, width), width)
    natural[:, near_at] = (near * inv_rms * gain[:, near_at]).astype(BF16)
    natural[:, far_at] = (far * inv_rms * gain[:, far_at]).astype(BF16)
    for slot in range(groups):
        group = lax.rem(z + slot, groups)
        for k in range(2):
            row = 2 * group + (y if k == 0 else 1 - y)
            put = slice((2 * slot + k) * rows, (2 * slot + k + 1) * rows)
            for out, half in ((own, core), (other, 1 - core)):
                got = pl.multiple_of((2 * row + half) * rows, rows)
                out[:, put] = natural[:, pl.ds(got, rows)]


def norm(at, here, there, far_here, far_there, gain, groups, rows):
    length, width = here.shape
    step = 128

    def pick(want):
        return pl.BlockSpec((step, width), lambda i, s: (jnp.where(s[0] == want, i, 0), 0))

    out = pl.BlockSpec((step, D // 2), lambda i, s: (i, 0))
    return pl.pallas_call(
        lambda *refs: norm_kernel(groups, rows, *refs),
        grid_spec=pltpu.PrefetchScalarGridSpec(
            num_scalar_prefetch=1,
            grid=(length // step,),
            in_specs=[pick(1), pick(0), pick(1), pick(0), pl.BlockSpec((1, D), lambda i, s: (0, 0))],
            out_specs=[out, out],
            scratch_shapes=[pltpu.VMEM((step, D), BF16)],
        ),
        out_shape=[jax.ShapeDtypeStruct((length, D // 2), BF16)] * 2,
        compiler_params=params(32),
        name="norm",
    )(at, here, there, far_here, far_there, gain)


def attend_head(bias, qg, kv):
    low_lane = lax.broadcasted_iota(jnp.int32, qg.shape, 1) < HEAD
    zero = jnp.zeros((), BF16)
    scaled = qg * jnp.asarray(1.0 / HEAD**0.5, BF16)
    queries = jnp.where(low_lane, scaled, zero)
    grads = jnp.where(low_lane, zero, scaled)
    scores = dot(queries, kv, NT) + bias
    grad_prob = dot(grads, kv, NT)
    weights = jnp.exp(scores - jnp.max(scores, axis=-1, keepdims=True))
    probs = weights * (1.0 / jnp.sum(weights, axis=-1, keepdims=True))
    prob_low = probs.astype(BF16)
    attended = dot(prob_low, kv)
    row_delta = jnp.sum(grads.astype(F32) * attended, axis=-1, keepdims=True)
    grad_score = (probs * (grad_prob - row_delta)).astype(BF16)
    grad_query = dot(grad_score, kv)
    qg_t = qg.T
    key_t = dot(qg_t[:HEAD], grad_score)
    value_t = dot(qg_t[HEAD:], prob_low)
    gkv = jnp.concatenate([key_t, value_t], axis=0).T
    dec = jnp.where(low_lane, grad_query, pltpu.roll(gkv, HEAD, 1))
    return dec.astype(BF16), gkv.astype(BF16)


def attend_kernel(at, enc_own, enc_other, w_own, w_other, qg_here, qg_there, dec, gkv):
    kv = (dot(enc_own[...], w_own[...]) + dot(enc_other[...], w_other[...])).astype(BF16)
    keys = lax.broadcasted_iota(jnp.int32, (1, kv.shape[0]), 1)
    bias = jnp.where(keys < at[5], 0.0, -1e30).astype(F32)
    for head in range(kv.shape[1] // (2 * HEAD)):
        lanes = slice(head * 2 * HEAD, (head + 1) * 2 * HEAD)
        qg = jnp.where(at[0] == 1, qg_here[:, lanes], qg_there[:, lanes])
        dec[:, lanes], gkv[:, lanes] = attend_head(bias, qg, kv[:, lanes])


def attend(at, enc_own, enc_other, w_own, w_other, qg_here, qg_there, chunk):
    length = enc_own.shape[0]
    half, cols = w_own.shape
    step = min(256, cols)
    first = chunk * (cols // step)
    enc = pl.BlockSpec((length, half), lambda i, s: (0, 0))
    weight = pl.BlockSpec((half, step), lambda i, s: (0, i))
    out = pl.BlockSpec((length, step), lambda i, s: (0, i))

    def pick(want):
        return pl.BlockSpec((length, step), lambda i, s: (0, jnp.where(s[0] == want, first + i, first)))

    return pl.pallas_call(
        attend_kernel,
        grid_spec=pltpu.PrefetchScalarGridSpec(
            num_scalar_prefetch=1,
            grid=(cols // step,),
            in_specs=[enc, enc, weight, weight, pick(1), pick(0)],
            out_specs=[out, out],
        ),
        out_shape=[jax.ShapeDtypeStruct((length, cols), BF16)] * 2,
        compiler_params=params(48),
        name="attend",
    )(at, enc_own, enc_other, w_own, w_other, qg_here, qg_there)


def weight_grad_kernel(scale, at, enc_a, enc_b, gkv_a, gkv_b, weight, out, gain_term):
    grad = scale * (dot(enc_a[...], gkv_a[...], TN) + dot(enc_b[...], gkv_b[...], TN))
    out[...] = grad.astype(BF16)
    product = grad * weight[...].astype(F32)
    lanes = product[:, :128]
    for i in range(1, product.shape[1] // 128):
        lanes = lanes + product[:, i * 128 : (i + 1) * 128]
    gain_term[0] = jnp.sum(lanes.T, axis=0, keepdims=True)


def weight_grad(at, enc_a, enc_b, gkv_a, gkv_b, weight, groups, scale):
    length, half = enc_a.shape
    cols = weight.shape[1]
    step = half // groups

    def slot(i, s):
        return lax.rem(i + groups - s[4], groups)

    enc = pl.BlockSpec((length, step), lambda i, s: (0, slot(i, s)))
    gkv = pl.BlockSpec((length, cols), lambda i, s: (0, 0))
    return pl.pallas_call(
        lambda *refs: weight_grad_kernel(scale, *refs),
        grid_spec=pltpu.PrefetchScalarGridSpec(
            num_scalar_prefetch=1,
            grid=(groups,),
            in_specs=[enc, enc, gkv, gkv, pl.BlockSpec((step, cols), lambda i, s: (slot(i, s), 0))],
            out_specs=[
                pl.BlockSpec((step, cols), lambda i, s: (i, 0)),
                pl.BlockSpec((1, 1, step), lambda i, s: (i, 0, 0)),
            ],
        ),
        out_shape=[
            jax.ShapeDtypeStruct((half, cols), BF16),
            jax.ShapeDtypeStruct((groups, 1, step), F32),
        ],
        compiler_params=params(32),
        name="weight_grad",
    )(at, enc_a, enc_b, gkv_a, gkv_b, weight)


def enc_grad_kernel(at, gkv_0, gkv_1, own_0, own_1, other_0, other_1, out):
    rows = own_0.shape[0]
    own = dot(gkv_0[...], own_0[...], NT) + dot(gkv_1[...], own_1[...], NT)
    other = dot(gkv_0[...], other_0[...], NT) + dot(gkv_1[...], other_1[...], NT)
    first = at[3] == 0
    out[:, :rows] = jnp.where(first, own, other).astype(BF16)
    out[:, rows:] = jnp.where(first, other, own).astype(BF16)


def enc_grad(at, gkvs, owns, others, groups, rows, shard):
    length, cols = gkvs[0].shape
    per_shard = groups // 2

    def block(i, s):
        target = lax.rem(s[1] + shard, 2)
        group = target * per_shard + i // 2
        slot = lax.rem(group + groups - s[4], groups)
        return (2 * slot + lax.rem(i + s[2], 2), 0)

    gkv = pl.BlockSpec((length, cols), lambda i, s: (0, 0))
    weight = pl.BlockSpec((rows, cols), block)
    return pl.pallas_call(
        enc_grad_kernel,
        grid_spec=pltpu.PrefetchScalarGridSpec(
            num_scalar_prefetch=1,
            grid=(groups,),
            in_specs=[gkv, gkv, weight, weight, weight, weight],
            out_specs=pl.BlockSpec((length, 2 * rows), lambda i, s: (0, i)),
        ),
        out_shape=jax.ShapeDtypeStruct((length, D // 2), BF16),
        compiler_params=params(32),
        name="enc_grad",
    )(at, *gkvs, *owns, *others)


def cut(array, axis, index, size):
    return lax.dynamic_slice_in_dim(array, index * size, size, axis)


def ordered(first, own, other, axis):
    return jnp.where(
        first, jnp.concatenate([own, other], axis), jnp.concatenate([other, own], axis)
    )


def on_device(sec_acts, gain, w_kv, src_len, tgt_len):
    groups = lax.axis_size("z")
    shards = lax.axis_size("mp")
    z, y = lax.axis_index("z"), lax.axis_index("y")
    core, x = lax.axis_index("phase"), lax.axis_index("mp")
    straight = y == core
    packed = sec_acts[0, 0]
    length, width = packed.shape
    rows = w_kv.shape[0]
    half = width // 2
    cols = half // CHUNKS
    pair_scale = 1.0 / (2 * groups)
    tiled = shards == 2 and rows % 128 == 0

    def turned(count, by):
        return [(i, (i + by) % count) for i in range(count)]

    def across(value, turn, moves):
        return lax.ppermute(
            value,
            ("y", "phase", "mp"),
            [(a * shards + s, b * shards + (s + turn) % shards) for a, b in moves for s in range(shards)],
        )

    def chunk_of(side, k):
        return lax.dynamic_slice_in_dim(w_kv, side * half + k * cols, cols, 1)

    def slots(block):
        return [lax.ppermute(block, "z", turned(groups, -s)) for s in range(1, groups)]

    mine = [chunk_of(y, k) for k in range(CHUNKS)]
    swapped = [lax.ppermute(chunk_of(1 - y, k), "y", SWAP) for k in range(CHUNKS)]

    here = lax.ppermute(packed, PLANE, [(0, 0), (2, 3)])
    there = lax.ppermute(packed, PLANE, [(0, 2), (2, 1)])
    far_here = [across(here, turn, [(0, 0), (3, 3)]) for turn in range(1, shards)]
    far_there = [across(there, turn, [(1, 1), (2, 2)]) for turn in range(1, shards)]
    gains = [gain] + [lax.ppermute(gain, "mp", turned(shards, t)) for t in range(1, shards)]

    near_slots, far_slots = slots(mine[0]), slots(swapped[0])
    w_own = [
        jnp.concatenate(
            [p for pair in zip([mine[0]] + near_slots, [swapped[0]] + far_slots) for p in pair], 0
        )
    ]
    for k in range(1, CHUNKS):
        block = jnp.concatenate([mine[k], swapped[k]], 0)
        w_own.append(jnp.concatenate([block] + slots(block), 0))
    w_other = [lax.ppermute(w, "phase", SWAP) for w in w_own]

    position = lax.broadcasted_iota(jnp.int32, (length, width), 0)
    is_grad = lax.broadcasted_iota(jnp.int32, (length, width), 1) % (2 * HEAD) >= HEAD
    masked = jnp.where(is_grad & (position >= tgt_len[0]), jnp.zeros((), BF16), packed)
    qg_here = lax.ppermute(cut(masked, 1, y, half), PLANE, [(1, 0), (3, 3)])
    qg_there = lax.ppermute(cut(masked, 1, 1 - y, half), PLANE, [(1, 2), (3, 1)])
    key_count = jnp.where(straight, src_len, lax.ppermute(src_len, "y", SWAP))
    at = jnp.concatenate(
        [jnp.stack([straight.astype(jnp.int32), x, y, core, z]).astype(jnp.int32), key_count]
    )

    def natural(parts, axis):
        if shards == 2:
            return ordered(x == 0, parts[0], parts[1], axis)
        stacked = jnp.stack(parts)
        return jnp.concatenate(
            [
                lax.dynamic_index_in_dim(stacked, (x - i) % shards, 0, keepdims=False)
                for i in range(shards)
            ],
            axis,
        )

    block_group = (z + jnp.arange(groups)) % groups
    block_pair = 2 * block_group[:, None] + jnp.stack([y, 1 - y])[None, :]
    block_order = (2 * block_pair[None] + jnp.stack([core, 1 - core])[:, None, None]).reshape(-1)
    gain_all = natural(gains, 0).astype(F32)

    if tiled:
        enc_own, enc_other = norm(
            at, here, there, far_here[0], far_there[0], gain_all[None], groups, rows
        )
    else:
        raw = [jnp.where(straight, a, b) for a, b in zip([here] + far_here, [there] + far_there)]
        hidden = natural(raw, 1).astype(F32)
        inv_rms = lax.rsqrt(jnp.sum(hidden * hidden, axis=-1, keepdims=True) / D + EPS)
        encoded = (hidden * inv_rms * gain_all).astype(BF16)
        encoded = encoded.reshape(length, -1, rows)[:, block_order].reshape(length, 2, -1)
        enc_own, enc_other = encoded[:, 0], encoded[:, 1]
    enc_mate = lax.ppermute(enc_other, "phase", SWAP)

    decs, gkvs, weight_sums, gain_terms = [], [], [], []
    for k in range(CHUNKS):
        dec, gkv = attend(at, enc_own, enc_other, w_own[k], w_other[k], qg_here, qg_there, k)
        gkvs.append(gkv)
        decs.append(
            (
                lax.ppermute(dec, PLANE, [(0, 1), (3, 3)]),
                lax.ppermute(dec, PLANE, [(2, 1), (1, 3)]),
            )
        )
        gkv_mate = lax.ppermute(gkv, "phase", SWAP)
        if tiled:
            grad, term = weight_grad(
                at, enc_own, enc_mate, gkv, gkv_mate, w_own[k], groups, pair_scale
            )
            term = term.reshape(groups, 2, rows)
        else:
            grad = pair_scale * (dot(enc_own, gkv, TN) + dot(enc_mate, gkv_mate, TN))
            term = jnp.sum(grad * w_own[k].astype(F32), axis=1).reshape(groups, 2, rows)
            term = jnp.roll(term, z, 0)
            grad = jnp.roll(grad.astype(BF16).reshape(groups, -1, cols), z, 0).reshape(-1, cols)
        gain_terms.append(term)
        weight_sums.append(lax.psum_scatter(grad, "z", scatter_dimension=0, tiled=True))

    if tiled:
        terms = [enc_grad(at, gkvs, w_own, w_other, groups, rows, s) for s in (1, 0)][::-1]
    else:
        gkv_all = jnp.concatenate(gkvs, 1)
        full = dot(gkv_all, jnp.concatenate([jnp.concatenate(w, 0) for w in zip(w_own, w_other)], 1), NT)
        back = jnp.zeros_like(block_order).at[block_order].set(jnp.arange(block_order.shape[0]))
        full = full.astype(BF16).reshape(length, -1, rows)[:, back].reshape(length, D)
        terms = [cut(full, 1, (x + s) % shards, width) for s in range(shards)]
    grad_enc = terms[0].astype(F32)
    for turn in range(1, shards):
        grad_enc = grad_enc + across(terms[turn], turn, [(0, 0), (3, 3)]).astype(F32)
    for turn in range(shards):
        grad_enc = grad_enc + across(terms[turn], turn, [(2, 0), (1, 3)]).astype(F32)
    grad_normed = (grad_enc * gain.astype(F32)).astype(BF16)
    enc_grads = lax.ppermute(grad_normed, PLANE, [(0, 0), (3, 2)])

    term = sum(gain_terms)
    term = jnp.where(y == 0, term, term[:, ::-1])
    by_core = jnp.stack([jnp.where(core == 0, term, 0.0), jnp.where(core == 1, term, 0.0)], axis=2)
    gain_sums = lax.psum(by_core.reshape(D), ("z", "y", "phase", "mp"))
    d_gain = cut(gain_sums, 0, x, width) / gain.astype(F32)

    kept = jnp.concatenate([w[:rows] for w in weight_sums], 1)
    got = jnp.concatenate([lax.ppermute(w[rows:], "y", SWAP) for w in weight_sums], 1)
    d_wkv = ordered(y == 0, kept, got, 1).astype(F32)

    dec_here = jnp.concatenate([d[0] for d in decs], 1)
    dec_there = jnp.concatenate([d[1] for d in decs], 1)
    dec_grads = ordered(y == 0, dec_here, dec_there, 1)
    sec_grads = jnp.where(core == 0, enc_grads, dec_grads)[None, None]
    return (sec_grads, d_wkv, d_gain)


def solution(mesh):
    size = mesh.shape
    split = (size["dp"] // 2, 2, size["phase"], size["mp"])
    fine = Mesh(mesh.devices.reshape(split), ("z", "y", "phase", "mp"))
    pairs = ("z", "y")
    acts = P("phase", pairs, None, "mp")
    weights = P(("z", "y", "phase"), "mp")
    return jax.shard_map(
        on_device,
        mesh=fine,
        in_specs=(acts, P("mp"), weights, P(pairs), P(pairs)),
        out_specs=(acts, weights, P("mp")),
        check_vma=False,
    )
```

time: 383 us -> 402 us (1.050)
  Pallas kernels: 12.8 us -> 50.5 us
  other arithmetic: 50.3 us -> 13.2 us
  waiting for transfers between devices: 140 us -> 175 us
  local copies, waits for them, and re-layouts: 46.8 us -> 23.7 us
  matrix products: 21.4 us -> 0 us
  starting transfers between devices: 61.5 us -> 80.2 us
  blocking collectives: 31.4 us -> 40.9 us
    ppermute x11 -> x28, waiting for transfers between devices: 85.4 us -> 163 us  [the longest x9 72.5 us: slots(): lax.ppermute(block, 'z', turned(groups, -s))]
    all_gather x1 -> x0, waiting for transfers between devices: 34.4 us -> none  [on_device(): w_own = lax.all_gather(w_block, 'z', axis=0, tiled=True)]
    pallas_call x0 -> x5, Pallas kernels: none -> 23.4 us  [the longest x2 8.63 us: weight_grad(): pl.pallas_call(lambda *refs: weight_grad_kernel(scale, *refs), grid_spec=...]
    dot_general x6 -> x0, matrix products: 21.4 us -> none  [matmul(): lax.dot_general(a, b, ((dims[:1], dims[1:]), ((), ())), preferred_element...]
    concatenate x6 -> x5, local copies, waits for them, and re-layouts: 19.5 us -> 2.01 us  [the longest x1 1.89 us: on_device(): w_own.append(jnp.concatenate([block] + slots(block), 0))]
    ppermute x11 -> x28, starting transfers between devices: 36.4 us -> 51.8 us  [the longest x9 15.9 us: slots(): lax.ppermute(block, 'z', turned(groups, -s))]
    pallas_call x1 -> x2, Pallas kernels: 12.8 us -> 27.1 us  [attend(): pl.pallas_call(attend_kernel, grid_spec=pltpu.PrefetchScalarGridSpec(num_...]
    reshape x2 -> x0, local copies, waits for them, and re-layouts: 12.6 us -> none  [the longest x1 6.56 us: on_device(): grad_enc = jnp.stack([first, second], axis=2).reshape(length, width)]
  transfers between devices with their start and end apart: 19 -> 36, of which waited for: 7 -> 17; matrix products, arithmetic and copies ran while one was open for 25% -> 6% of each run, Pallas kernels for 0% -> 12%
where the time goes in v2:
time: 402 us; the launch traced here: 400 us
  waiting for transfers between devices  175 us (44%)
  starting transfers between devices  80.2 us (20%)
  Pallas kernels  50.5 us (13%)
  blocking collectives  40.9 us (10%)
  local copies, waits for them, and re-layouts  23.7 us (6%)
  between operations  16.5 us (4%)
  other arithmetic  13.2 us (3%)
    ppermute x9, waiting for transfers between devices, slots(): lax.ppermute(block, 'z', turned(groups, -s))  72.5 us
    ppermute x5, waiting for transfers between devices, across(): lax.ppermute(value, ('y', 'phase', 'mp'), [(a * shards + s, b * shards +...  42.6 us
    psum x1, blocking collectives, on_device(): gain_sums = lax.psum(by_core.reshape(D), ('z', 'y', 'phase', 'mp'))  40.9 us
    pallas_call x2, Pallas kernels, attend(): pl.pallas_call(attend_kernel, grid_spec=pltpu.PrefetchScalarGridSpec(num_...  27.1 us
    ppermute x1, waiting for transfers between devices, on_device(): lax.ppermute(gain, 'mp', turned(shards, t))  26.3 us
    ppermute x1, starting transfers between devices, on_device(): here = lax.ppermute(packed, PLANE, [(0, 0), (2, 3)])  17.2 us
    unnamed x56, local copies, waits for them, and re-layouts  17 us
    ppermute x9, starting transfers between devices, slots(): lax.ppermute(block, 'z', turned(groups, -s))  15.9 us
  transfers between devices with their start and end apart: 36, of which 17 were waited for; matrix products, arithmetic and copies ran while one was open for 6% of the time, Pallas kernels for 12%

profile of v2, /device:TPU:0, one launch (start us, length us, event | category | flops | bytes accessed | tf_op | source)
XLA Modules:
  0.0 400.5 jit_solution(2401751871670361524)
XLA Ops:
  7.2 6.3 %collective-permute-start.2 = (bf16[512,2048]{1,0:T(8,128)(2,1)}, bf16[512,2048]{1,0:T(8,128)(2,1)}, u32[]{:S(2)}, u32[]{:S(2)}) collective-permute-start(bf16[512,2048]{1,0:T(8,128)(2,1)} %bitcast.15), channel_id=1, source_target_pairs={{0,4},{4,2},{1,5},{5,3},{8,12},{12,10},{9,13},{13,11},{16,20},{20,... | collective-permute-start | bytes 6291464 | tf_op jit(solution)/shard_map/ppermute | solution.py:252
  13.5 17.2 %collective-permute-start.1 = (bf16[512,2048]{1,0:T(8,128)(2,1)}, bf16[512,2048]{1,0:T(8,128)(2,1)}, u32[]{:S(2)}, u32[]{:S(2)}) collective-permute-start(bf16[512,2048]{1,0:T(8,128)(2,1)} %bitcast.16), channel_id=1, source_target_pairs={{0,0},{4,6},{1,1},{5,7},{8,8},{12,14},{9,9},{13,15},{16,16},{20,22... | collective-permute-start | bytes 6291464 | tf_op jit(solution)/shard_map/ppermute | solution.py:251
  30.7 5.3 %collective-permute-done.2.refs_2_ = bf16[512,2048]{1,0:T(8,128)(2,1)} collective-permute-done((bf16[512,2048]{1,0:T(8,128)(2,1)}, bf16[512,2048]{1,0:T(8,128)(2,1)}, u32[]{:S(2)}, u32[]{:S(2)}) %collective-permute-start.2) | collective-permute-done | bytes 2097184 | tf_op jit(solution)/shard_map/ppermute | solution.py:252
  38.0 3.4 collective-permute-start.3
  46.0 5.7 %collective-permute-done.16 = bf16[256,512]{1,0:T(8,128)(2,1)S(1)} collective-permute-done((bf16[256,512]{1,0:T(8,128)(2,1)S(1)}, bf16[256,512]{1,0:T(8,128)(2,1)S(1)}, u32[]{:S(2)}, u32[]{:S(2)}) %collective-permute-start.16) | collective-permute-done | bytes 262176 | tf_op jit(solution)/shard_map/ppermute | solution.py:249
  51.8 3.7 collective-permute-start.17
  59.7 26.3 %collective-permute-done.5 = bf16[2048]{0:T(1024)(128)(2,1)S(1)} collective-permute-done((bf16[2048]{0:T(1024)(128)(2,1)S(1)}, bf16[2048]{0:T(1024)(128)(2,1)S(1)}, u32[]{:S(2)}, u32[]{:S(2)}) %collective-permute-start.5) | collective-permute-done | bytes 4128 | tf_op jit(solution)/shard_map/ppermute | solution.py:255
  93.6 5.7 %collective-permute-done.19 = bf16[512,512]{1,0:T(8,128)(2,1)} collective-permute-done((bf16[512,512]{1,0:T(8,128)(2,1)S(1)}, bf16[512,512]{1,0:T(8,128)(2,1)}, u32[]{:S(2)}, u32[]{:S(2)}) %collective-permute-start.19) | collective-permute-done | bytes 524320 | tf_op jit(solution)/shard_map/ppermute | solution.py:246
  101.2 6.6 %norm.1 = (bf16[512,2048]{1,0:T(8,128)(2,1)S(1)}, bf16[512,2048]{1,0:T(8,128)(2,1)}) custom-call(s32[6]{0:T(128)S(1)} %concatenate.57.refs_0_.at, bf16[512,2048]{1,0:T(8,128)(2,1)} %collective-permute-done.1.refs_1_, bf16[512,2048]{1,0:T(8,128)(2,1)} %collective-permute-done.2.refs_2_, bf16[512,2048]{1,0:T(8,128)(2,1)} %collective-permute-done.3.refs_3_, ...), custom_call_target="tpu_custom_call" | custom-call | tf_op jit(solution)/shard_map/norm/pallas_call | solution.py:59
  111.3 4.8 %collective-permute-done.14.qg_here = bf16[512,1024]{1,0:T(8,128)(2,1)S(1)} collective-permute-done((bf16[512,1024]{1,0:T(8,128)(2,1)S(1)}, bf16[512,1024]{1,0:T(8,128)(2,1)S(1)}, u32[]{:S(2)}, u32[]{:S(2)}) %collective-permute-start.14) | collective-permute-done | bytes 1048608 | tf_op jit(solution)/shard_map/ppermute | solution.py:271
  117.4 13.6 %attend.3 = (bf16[512,512]{1,0:T(8,128)(2,1)S(1)}, bf16[512,512]{1,0:T(8,128)(2,1)S(1)}) custom-call(s32[6]{0:T(128)S(1)} %concatenate.57.refs_0_.at, bf16[512,2048]{1,0:T(8,128)(2,1)S(1)} %get-tuple-element.13.enc_own.refs_1_, bf16[512,2048]{1,0:T(8,128)(2,1)} %get-tuple-element.14.enc_other, ...), custom_call_target="tpu_custom_call" | custom-call | tf_op jit(solution)/shard_map/attend/pallas_call | solution.py:119
  132.9 8.8 %collective-permute-start.31 = (bf16[512,512]{1,0:T(8,128)(2,1)S(1)}, bf16[512,512]{1,0:T(8,128)(2,1)S(1)}, u32[]{:S(2)}, u32[]{:S(2)}) collective-permute-start(bf16[512,512]{1,0:T(8,128)(2,1)S(1)} %get-tuple-element.16.gkv_1.refs_3_), channel_id=1, source_target_pairs={{0,2},{2,0},{1,3},{3,1},{4,6},{6,4},{5,7},{7,5},{8,10},{10,8},{9,1... | collective-permute-start | bytes 1572872 | tf_op jit(solution)/shard_map/ppermute | solution.py:318
  143.2 4.3 %weight_grad.3 = (bf16[2048,512]{1,0:T(8,128)(2,1)S(1)}, f32[4,1,512]{2,1,0:T(1,128)S(1)}) custom-call(s32[6]{0:T(128)S(1)} %concatenate.57.refs_0_.at, bf16[512,2048]{1,0:T(8,128)(2,1)S(1)} %get-tuple-element.13.enc_own.refs_1_, bf16[512,2048]{1,0:T(8,128)(2,1)S(1)} %collective-permute-done.29.refs_2_, ...), custom_call_target="tpu_custom_call" | custom-call | tf_op jit(solution)/shard_map/weight_grad/pallas_call | solution.py:153
  151.4 3.0 collective-permute-start.7
  154.3 3.9 collective-permute-done.6
  158.2 4.1 %collective-permute-start.8 = (bf16[256,512]{1,0:T(8,128)(2,1)S(1)}, bf16[256,512]{1,0:T(8,128)(2,1)S(1)}, u32[]{:S(2)}, u32[]{:S(2)}) collective-permute-start(bf16[256,512]{1,0:T(8,128)(2,1)S(1)} %collective-permute-done.6), channel_id=1, source_target_pairs={{0,24},{8,0},{16,8},{24,16},{1,25},{9,1},{17,9},{25,17},{2,26},{10... | collective-permute-start | bytes 786440 | tf_op jit(solution)/shard_map/ppermute | solution.py:246
  166.8 12.4 %collective-permute-done.8 = bf16[256,512]{1,0:T(8,128)(2,1)S(1)} collective-permute-done((bf16[256,512]{1,0:T(8,128)(2,1)S(1)}, bf16[256,512]{1,0:T(8,128)(2,1)S(1)}, u32[]{:S(2)}, u32[]{:S(2)}) %collective-permute-start.8) | collective-permute-done | bytes 262176 | tf_op jit(solution)/shard_map/ppermute | solution.py:246
  179.2 44.8 %collective-permute-done.9 = bf16[256,512]{1,0:T(8,128)(2,1)S(1)} collective-permute-done((bf16[256,512]{1,0:T(8,128)(2,1)S(1)}, bf16[256,512]{1,0:T(8,128)(2,1)S(1)}, u32[]{:S(2)}, u32[]{:S(2)}) %collective-permute-start.9) | collective-permute-done | bytes 262176 | tf_op jit(solution)/shard_map/ppermute | solution.py:246
  224.1 8.7 %collective-permute-done.10 = bf16[256,512]{1,0:T(8,128)(2,1)S(1)} collective-permute-done((bf16[256,512]{1,0:T(8,128)(2,1)S(1)}, bf16[256,512]{1,0:T(8,128)(2,1)S(1)}, u32[]{:S(2)}, u32[]{:S(2)}) %collective-permute-start.10) | collective-permute-done | bytes 262176 | tf_op jit(solution)/shard_map/ppermute | solution.py:246
  233.0 4.1 %collective-permute-done.13.w_other.other_0 = bf16[2048,512]{1,0:T(8,128)(2,1)S(1)} collective-permute-done((bf16[2048,512]{1,0:T(8,128)(2,1)S(1)}, bf16[2048,512]{1,0:T(8,128)(2,1)S(1)}, u32[]{:S(2)}, u32[]{:S(2)}) %collective-permute-start.13) | collective-permute-done | bytes 2097184 | tf_op jit(solution)/shard_map/ppermute | solution.py:266
  239.8 13.5 %attend.2 = (bf16[512,512]{1,0:T(8,128)(2,1)S(1)}, bf16[512,512]{1,0:T(8,128)(2,1)S(1)}) custom-call(s32[6]{0:T(128)S(1)} %concatenate.57.refs_0_.at, bf16[512,2048]{1,0:T(8,128)(2,1)S(1)} %copy-done.6, bf16[512,2048]{1,0:T(8,128)(2,1)} %get-tuple-element.14.enc_other, bf16[2048,512]{1,0:T(8,128)(2,1)} %copy-done, bf16[2048,512]{1,0:T(8,128)(2,1)} %copy-done.9, ...), custom_call_target="tpu_custom_call" | custom-call | tf_op jit(solution)/shard_map/attend/pallas_call | solution.py:119
  257.3 3.7 enc_grad.2
  262.7 4.4 %enc_grad.3 = bf16[512,2048]{1,0:T(8,128)(2,1)} custom-call(s32[6]{0:T(128)S(1)} %concatenate.57.refs_0_.at, bf16[512,512]{1,0:T(8,128)(2,1)S(1)} %get-tuple-element.15.gkv_0.refs_3_, bf16[512,512]{1,0:T(8,128)(2,1)S(1)} %get-tuple-element.16.gkv_1.refs_3_, bf16[2048,512]{1,0:T(8,128)(2,1)S(1)} %copy-done.1, bf16[2048,512]{1,0:T(8,128)(2,1)S(1)} %copy-done.4, ...), custom_call_target="tpu_custom_call" | custom-call | tf_op jit(solution)/shard_map/enc_grad/pallas_call | solution.py:194
  270.9 4.3 %weight_grad.2 = (bf16[2048,512]{1,0:T(8,128)(2,1)S(1)}, f32[4,1,512]{2,1,0:T(1,128)S(1)}) custom-call(s32[6]{0:T(128)S(1)} %concatenate.57.refs_0_.at, bf16[512,2048]{1,0:T(8,128)(2,1)S(1)} %copy-done.6, bf16[512,2048]{1,0:T(8,128)(2,1)S(1)} %copy-done.13, bf16[512,512]{1,0:T(8,128)(2,1)S(1)} %get-tuple-element.15.gkv_0.refs_3_, ...), custom_call_target="tpu_custom_call" | custom-call | tf_op jit(solution)/shard_map/weight_grad/pallas_call | solution.py:153
  276.5 28.1 %collective-permute-done.22 = bf16[512,2048]{1,0:T(8,128)(2,1)} collective-permute-done((bf16[512,2048]{1,0:T(8,128)(2,1)S(1)}, bf16[512,2048]{1,0:T(8,128)(2,1)}, u32[]{:S(2)}, u32[]{:S(2)}) %collective-permute-start.22) | collective-permute-done | bytes 2097184 | tf_op jit(solution)/shard_map/ppermute | solution.py:236
  304.6 14.5 %collective-permute-done.23 = bf16[512,2048]{1,0:T(8,128)(2,1)} collective-permute-done((bf16[512,2048]{1,0:T(8,128)(2,1)}, bf16[512,2048]{1,0:T(8,128)(2,1)}, u32[]{:S(2)}, u32[]{:S(2)}) %collective-permute-start.23) | collective-permute-done | bytes 2097184 | tf_op jit(solution)/shard_map/ppermute | solution.py:236
  319.1 6.0 %multiply_convert_fusion = bf16[512,2048]{1,0:T(8,128)(2,1)} fusion(bf16[512,2048]{1,0:T(8,128)(2,1)} %collective-permute-done.23, bf16[512,2048]{1,0:T(8,128)(2,1)} %collective-permute-done.22, bf16[512,2048]{1,0:T(8,128)(2,1)} %collective-permute-done.21, bf16[512,2048]{1,0:T(8,128)(2,1)S(1)} %enc_grad.2, f32[2048]{0:T(1024)S(1)} %convert_element_type.38), kind=kLoop, calls=%fused_computation | loop fusion | flops 9437184 | bytes 10493952 | tf_op jit(solution)/shard_map/convert_element_type | solution.py:345
  328.8 2.8 collective-permute-start.26
  335.4 40.9 %psum.7 = f32[4096]{0:T(1024)S(1)} all-reduce(f32[4096]{0:T(1024)S(1)} %bitcast.18), channel_id=1, replica_groups=mesh['z'=4,'y'=2,'phase'=2,'mp'=2] {'z','y','phase','mp'}, use_global_device_ids=true, to_apply=%region_2.3 | all-reduce | flops 4096 | bytes 32768 | tf_op jit(solution)/shard_map/psum | solution.py:351
  381.6 4.1 %fusion.3 = bf16[1,1,512,2048]{3,2,1,0:T(8,128)(2,1)} fusion(bf16[512,2048]{1,0:T(8,128)(2,1)S(1)} %collective-permute-done.24, bf16[512,512]{1,0:T(8,128)(2,1)} %collective-permute-done.28, bf16[512,512]{1,0:T(8,128)(2,1)} %collective-permute-done.27, bf16[512,512]{1,0:T(8,128)(2,1)} %collective-permute-done.26, ...), kind=kLoop, calls=%fused_computation.6 | loop fusion | flops 18874368 | bytes 6291458 | tf_op jit(solution)/shard_map/broadcast_in_dim | solution.py:361
  385.7 3.0 collective-permute-done.33
  388.7 3.3 collective-permute-done.32
  (133 shorter events, 62.8 us)
Async XLA Ops:
  7.2 369.7 %reduce-scatter.5.cloned.1.call-start = ((), (), s32[]{:S(2)}) async-start(), calls=%async_computation.3 | async-start | bytes 2621440 | tf_op jit(solution)/shard_map/reduce_scatter | solution.py:330
  7.2 28.7 %collective-permute-start.2 = (bf16[512,2048]{1,0:T(8,128)(2,1)}, bf16[512,2048]{1,0:T(8,128)(2,1)}, u32[]{:S(2)}, u32[]{:S(2)}) collective-permute-start(bf16[512,2048]{1,0:T(8,128)(2,1)} %bitcast.15), channel_id=1, source_target_pairs={{0,4},{4,2},{1,5},{5,3},{8,12},{12,10},{9,13},{13,11},{16,20},{20,... | collective-permute-start | bytes 6291464 | tf_op jit(solution)/shard_map/ppermute | solution.py:252
  13.5 24.5 %collective-permute-start.1 = (bf16[512,2048]{1,0:T(8,128)(2,1)}, bf16[512,2048]{1,0:T(8,128)(2,1)}, u32[]{:S(2)}, u32[]{:S(2)}) collective-permute-start(bf16[512,2048]{1,0:T(8,128)(2,1)} %bitcast.16), channel_id=1, source_target_pairs={{0,0},{4,6},{1,1},{5,7},{8,8},{12,14},{9,9},{13,15},{16,16},{20,22... | collective-permute-start | bytes 6291464 | tf_op jit(solution)/shard_map/ppermute | solution.py:251
  36.0 65.2 %collective-permute-start.4 = (bf16[512,2048]{1,0:T(8,128)(2,1)}, bf16[512,2048]{1,0:T(8,128)(2,1)}, u32[]{:S(2)}, u32[]{:S(2)}) collective-permute-start(bf16[512,2048]{1,0:T(8,128)(2,1)} %collective-permute-done.2.refs_2_), channel_id=1, source_target_pairs={{2,3},{3,2},{4,5},{5,4},{10,11},{11,10},{12,13},{13,12},{18,19},{1... | collective-permute-start | bytes 6291464 | tf_op jit(solution)/shard_map/ppermute | solution.py:236
  38.0 63.2 %collective-permute-start.3 = (bf16[512,2048]{1,0:T(8,128)(2,1)}, bf16[512,2048]{1,0:T(8,128)(2,1)}, u32[]{:S(2)}, u32[]{:S(2)}) collective-permute-start(bf16[512,2048]{1,0:T(8,128)(2,1)} %collective-permute-done.1.refs_1_), channel_id=1, source_target_pairs={{0,1},{1,0},{6,7},{7,6},{8,9},{9,8},{14,15},{15,14},{16,17},{17,16... | collective-permute-start | bytes 6291464 | tf_op jit(solution)/shard_map/ppermute | solution.py:236
  43.6 8.2 %collective-permute-start.16 = (bf16[256,512]{1,0:T(8,128)(2,1)S(1)}, bf16[256,512]{1,0:T(8,128)(2,1)S(1)}, u32[]{:S(2)}, u32[]{:S(2)}) collective-permute-start(bf16[256,512]{1,0:T(8,128)(2,1)S(1)} %get-tuple-element.29), channel_id=1, source_target_pairs={{0,4},{4,0},{1,5},{5,1},{2,6},{6,2},{3,7},{7,3},{8,12},{12,8},{9,1... | collective-permute-start | bytes 786440 | tf_op jit(solution)/shard_map/ppermute | solution.py:249
  51.8 38.0 %collective-permute-start.17 = (bf16[512,512]{1,0:T(8,128)(2,1)S(1)}, bf16[512,512]{1,0:T(8,128)(2,1)}, u32[]{:S(2)}, u32[]{:S(2)}) collective-permute-start(bf16[512,512]{1,0:T(8,128)(2,1)S(1)} %pad_maximum_fusion), channel_id=1, source_target_pairs={{0,24},{8,0},{16,8},{24,16},{1,25},{9,1},{17,9},{25,17},{2,26},{10... | collective-permute-start | bytes 1572872 | tf_op jit(solution)/shard_map/ppermute | solution.py:246
  56.1 29.9 %collective-permute-start.5 = (bf16[2048]{0:T(1024)(128)(2,1)S(1)}, bf16[2048]{0:T(1024)(128)(2,1)S(1)}, u32[]{:S(2)}, u32[]{:S(2)}) collective-permute-start(bf16[2048]{0:T(1024)(128)(2,1)S(1)} %copy-done.22), channel_id=1, source_target_pairs={{0,1},{1,0},{2,3},{3,2},{4,5},{5,4},{6,7},{7,6},{8,9},{9,8},{10,11... | collective-permute-start | bytes 12296 | tf_op jit(solution)/shard_map/ppermute | solution.py:255
  59.1 32.6 %collective-permute-start.18 = (bf16[512,512]{1,0:T(8,128)(2,1)S(1)}, bf16[512,512]{1,0:T(8,128)(2,1)}, u32[]{:S(2)}, u32[]{:S(2)}) collective-permute-start(bf16[512,512]{1,0:T(8,128)(2,1)S(1)} %pad_maximum_fusion), channel_id=1, source_target_pairs={{0,16},{8,24},{16,0},{24,8},{1,17},{9,25},{17,1},{25,9},{2,18},{10... | collective-permute-start | bytes 1572872 | tf_op jit(solution)/shard_map/ppermute | solution.py:246
  86.0 13.2 %collective-permute-start.19 = (bf16[512,512]{1,0:T(8,128)(2,1)S(1)}, bf16[512,512]{1,0:T(8,128)(2,1)}, u32[]{:S(2)}, u32[]{:S(2)}) collective-permute-start(bf16[512,512]{1,0:T(8,128)(2,1)S(1)} %pad_maximum_fusion), channel_id=1, source_target_pairs={{0,8},{8,16},{16,24},{24,0},{1,9},{9,17},{17,25},{25,1},{2,10},{10... | collective-permute-start | bytes 1572872 | tf_op jit(solution)/shard_map/ppermute | solution.py:246
  101.1 14.9 %collective-permute-start.20 = (bf16[2048,512]{1,0:T(8,128)(2,1)}, bf16[2048,512]{1,0:T(8,128)(2,1)S(1)}, u32[]{:S(2)}, u32[]{:S(2)}) collective-permute-start(bf16[2048,512]{1,0:T(8,128)(2,1)} %constant_dynamic-update-slice_fusion.8.w_own.own_1.refs_5_), channel_id=1, source_target_pairs={{0,2},{2,0},{1,3},{3,1},{4,6},{6,4},{5,7},{7,5},{8,10},{10,8},{9,1... | collective-permute-start | bytes 6291464 | tf_op jit(solution)/shard_map/ppermute | solution.py:266
  107.8 35.4 %collective-permute-start.29 = (bf16[512,2048]{1,0:T(8,128)(2,1)}, bf16[512,2048]{1,0:T(8,128)(2,1)S(1)}, u32[]{:S(2)}, u32[]{:S(2)}) collective-permute-start(bf16[512,2048]{1,0:T(8,128)(2,1)} %get-tuple-element.14.enc_other), channel_id=1, source_target_pairs={{0,2},{2,0},{1,3},{3,1},{4,6},{6,4},{5,7},{7,5},{8,10},{10,8},{9,1... | collective-permute-start | bytes 6291464 | tf_op jit(solution)/shard_map/ppermute | solution.py:306
  132.9 10.3 %collective-permute-start.31 = (bf16[512,512]{1,0:T(8,128)(2,1)S(1)}, bf16[512,512]{1,0:T(8,128)(2,1)S(1)}, u32[]{:S(2)}, u32[]{:S(2)}) collective-permute-start(bf16[512,512]{1,0:T(8,128)(2,1)S(1)} %get-tuple-element.16.gkv_1.refs_3_), channel_id=1, source_target_pairs={{0,2},{2,0},{1,3},{3,1},{4,6},{6,4},{5,7},{7,5},{8,10},{10,8},{9,1... | collective-permute-start | bytes 1572872 | tf_op jit(solution)/shard_map/ppermute | solution.py:318
  148.9 229.1 %reduce-scatter.3.cloned.1.call-start = ((), (), s32[]{:S(2)}) async-start(), calls=%async_computation.2 | async-start | bytes 2621440 | tf_op jit(solution)/shard_map/reduce_scatter | solution.py:330
  149.0 9.2 %collective-permute-start.6 = (bf16[256,512]{1,0:T(8,128)(2,1)}, bf16[256,512]{1,0:T(8,128)(2,1)S(1)}, u32[]{:S(2)}, u32[]{:S(2)}) collective-permute-start(bf16[256,512]{1,0:T(8,128)(2,1)} %get-tuple-element.30), channel_id=1, source_target_pairs={{0,4},{4,0},{1,5},{5,1},{2,6},{6,2},{3,7},{7,3},{8,12},{12,8},{9,1... | collective-permute-start | bytes 786440 | tf_op jit(solution)/shard_map/ppermute | solution.py:249
  151.4 15.3 %collective-permute-start.7 = (bf16[256,512]{1,0:T(8,128)(2,1)S(1)}, bf16[256,512]{1,0:T(8,128)(2,1)S(1)}, u32[]{:S(2)}, u32[]{:S(2)}) collective-permute-start(bf16[256,512]{1,0:T(8,128)(2,1)S(1)} %get-tuple-element.32), channel_id=1, source_target_pairs={{0,24},{8,0},{16,8},{24,16},{1,25},{9,1},{17,9},{25,17},{2,26},{10... | collective-permute-start | bytes 786440 | tf_op jit(solution)/shard_map/ppermute | solution.py:246
  158.2 21.0 %collective-permute-start.8 = (bf16[256,512]{1,0:T(8,128)(2,1)S(1)}, bf16[256,512]{1,0:T(8,128)(2,1)S(1)}, u32[]{:S(2)}, u32[]{:S(2)}) collective-permute-start(bf16[256,512]{1,0:T(8,128)(2,1)S(1)} %collective-permute-done.6), channel_id=1, source_target_pairs={{0,24},{8,0},{16,8},{24,16},{1,25},{9,1},{17,9},{25,17},{2,26},{10... | collective-permute-start | bytes 786440 | tf_op jit(solution)/shard_map/ppermute | solution.py:246
  162.3 61.8 %collective-permute-start.9 = (bf16[256,512]{1,0:T(8,128)(2,1)S(1)}, bf16[256,512]{1,0:T(8,128)(2,1)S(1)}, u32[]{:S(2)}, u32[]{:S(2)}) collective-permute-start(bf16[256,512]{1,0:T(8,128)(2,1)S(1)} %get-tuple-element.32), channel_id=1, source_target_pairs={{0,16},{8,24},{16,0},{24,8},{1,17},{9,25},{17,1},{25,9},{2,18},{10... | collective-permute-start | bytes 786440 | tf_op jit(solution)/shard_map/ppermute | solution.py:246
  162.3 70.5 %collective-permute-start.11 = (bf16[256,512]{1,0:T(8,128)(2,1)S(1)}, bf16[256,512]{1,0:T(8,128)(2,1)S(1)}, u32[]{:S(2)}, u32[]{:S(2)}) collective-permute-start(bf16[256,512]{1,0:T(8,128)(2,1)S(1)} %get-tuple-element.32), channel_id=1, source_target_pairs={{0,8},{8,16},{16,24},{24,0},{1,9},{9,17},{17,25},{25,1},{2,10},{10... | collective-permute-start | bytes 786440 | tf_op jit(solution)/shard_map/ppermute | solution.py:246
  163.4 69.4 %collective-permute-start.12 = (bf16[256,512]{1,0:T(8,128)(2,1)S(1)}, bf16[256,512]{1,0:T(8,128)(2,1)S(1)}, u32[]{:S(2)}, u32[]{:S(2)}) collective-permute-start(bf16[256,512]{1,0:T(8,128)(2,1)S(1)} %collective-permute-done.6), channel_id=1, source_target_pairs={{0,8},{8,16},{16,24},{24,0},{1,9},{9,17},{17,25},{25,1},{2,10},{10... | collective-permute-start | bytes 786440 | tf_op jit(solution)/shard_map/ppermute | solution.py:246
  166.6 66.2 %collective-permute-start.10 = (bf16[256,512]{1,0:T(8,128)(2,1)S(1)}, bf16[256,512]{1,0:T(8,128)(2,1)S(1)}, u32[]{:S(2)}, u32[]{:S(2)}) collective-permute-start(bf16[256,512]{1,0:T(8,128)(2,1)S(1)} %collective-permute-done.6), channel_id=1, source_target_pairs={{0,16},{8,24},{16,0},{24,8},{1,17},{9,25},{17,1},{25,9},{2,18},{10... | collective-permute-start | bytes 786440 | tf_op jit(solution)/shard_map/ppermute | solution.py:246
  253.4 17.5 %collective-permute-start.30 = (bf16[512,512]{1,0:T(8,128)(2,1)S(1)}, bf16[512,512]{1,0:T(8,128)(2,1)S(1)}, u32[]{:S(2)}, u32[]{:S(2)}) collective-permute-start(bf16[512,512]{1,0:T(8,128)(2,1)S(1)} %get-tuple-element.15.gkv_0.refs_3_), channel_id=1, source_target_pairs={{0,2},{2,0},{1,3},{3,1},{4,6},{6,4},{5,7},{7,5},{8,10},{10,8},{9,1... | collective-permute-start | bytes 1572872 | tf_op jit(solution)/shard_map/ppermute | solution.py:318
  261.1 43.5 %collective-permute-start.22 = (bf16[512,2048]{1,0:T(8,128)(2,1)S(1)}, bf16[512,2048]{1,0:T(8,128)(2,1)}, u32[]{:S(2)}, u32[]{:S(2)}) collective-permute-start(bf16[512,2048]{1,0:T(8,128)(2,1)S(1)} %enc_grad.2), channel_id=1, source_target_pairs={{4,0},{5,1},{2,6},{3,7},{12,8},{13,9},{10,14},{11,15},{20,16},{21,... | collective-permute-start | bytes 6291464 | tf_op jit(solution)/shard_map/ppermute | solution.py:236
  267.1 52.0 %collective-permute-start.23 = (bf16[512,2048]{1,0:T(8,128)(2,1)}, bf16[512,2048]{1,0:T(8,128)(2,1)}, u32[]{:S(2)}, u32[]{:S(2)}) collective-permute-start(bf16[512,2048]{1,0:T(8,128)(2,1)} %enc_grad.3), channel_id=1, source_target_pairs={{4,1},{5,0},{2,7},{3,6},{12,9},{13,8},{10,15},{11,14},{20,17},{21,... | collective-permute-start | bytes 6291464 | tf_op jit(solution)/shard_map/ppermute | solution.py:236
  268.4 50.7 %collective-permute-start.21 = (bf16[512,2048]{1,0:T(8,128)(2,1)}, bf16[512,2048]{1,0:T(8,128)(2,1)}, u32[]{:S(2)}, u32[]{:S(2)}) collective-permute-start(bf16[512,2048]{1,0:T(8,128)(2,1)} %enc_grad.3), channel_id=1, source_target_pairs={{0,1},{1,0},{6,7},{7,6},{8,9},{9,8},{14,15},{15,14},{16,17},{17,16... | collective-permute-start | bytes 6291464 | tf_op jit(solution)/shard_map/ppermute | solution.py:236
  325.1 56.5 %collective-permute-start.24 = (bf16[512,2048]{1,0:T(8,128)(2,1)}, bf16[512,2048]{1,0:T(8,128)(2,1)S(1)}, u32[]{:S(2)}, u32[]{:S(2)}) collective-permute-start(bf16[512,2048]{1,0:T(8,128)(2,1)} %multiply_convert_fusion), channel_id=1, source_target_pairs={{0,0},{6,4},{1,1},{7,5},{8,8},{14,12},{9,9},{15,13},{16,16},{22,20... | collective-permute-start | bytes 6291464 | tf_op jit(solution)/shard_map/ppermute | solution.py:346
  327.3 51.8 %collective-permute-start.28 = (bf16[512,512]{1,0:T(8,128)(2,1)S(1)}, bf16[512,512]{1,0:T(8,128)(2,1)}, u32[]{:S(2)}, u32[]{:S(2)}) collective-permute-start(bf16[512,512]{1,0:T(8,128)(2,1)S(1)} %get-tuple-element.18), channel_id=1, source_target_pairs={{4,2},{2,6},{5,3},{3,7},{12,10},{10,14},{13,11},{11,15},{20,18},{1... | collective-permute-start | bytes 1572872 | tf_op jit(solution)/shard_map/ppermute | solution.py:315
  328.8 52.7 %collective-permute-start.26 = (bf16[512,512]{1,0:T(8,128)(2,1)S(1)}, bf16[512,512]{1,0:T(8,128)(2,1)}, u32[]{:S(2)}, u32[]{:S(2)}) collective-permute-start(bf16[512,512]{1,0:T(8,128)(2,1)S(1)} %get-tuple-element.18), channel_id=1, source_target_pairs={{0,2},{6,6},{1,3},{7,7},{8,10},{14,14},{9,11},{15,15},{16,18},{22,... | collective-permute-start | bytes 1572872 | tf_op jit(solution)/shard_map/ppermute | solution.py:314
  331.6 50.0 %collective-permute-start.27 = (bf16[512,512]{1,0:T(8,128)(2,1)}, bf16[512,512]{1,0:T(8,128)(2,1)}, u32[]{:S(2)}, u32[]{:S(2)}) collective-permute-start(bf16[512,512]{1,0:T(8,128)(2,1)} %copy-done.20), channel_id=1, source_target_pairs={{4,2},{2,6},{5,3},{3,7},{12,10},{10,14},{13,11},{11,15},{20,18},{1... | collective-permute-start | bytes 1572872 | tf_op jit(solution)/shard_map/ppermute | solution.py:315
  333.1 48.5 %collective-permute-start.25 = (bf16[512,512]{1,0:T(8,128)(2,1)}, bf16[512,512]{1,0:T(8,128)(2,1)}, u32[]{:S(2)}, u32[]{:S(2)}) collective-permute-start(bf16[512,512]{1,0:T(8,128)(2,1)} %copy-done.20), channel_id=1, source_target_pairs={{0,2},{6,6},{1,3},{7,7},{8,10},{14,14},{9,11},{15,15},{16,18},{22,... | collective-permute-start | bytes 1572872 | tf_op jit(solution)/shard_map/ppermute | solution.py:314
  379.1 9.6 %collective-permute-start.33 = (bf16[256,512]{1,0:T(8,128)(2,1)S(1)}, bf16[256,512]{1,0:T(8,128)(2,1)S(1)}, u32[]{:S(2)}, u32[]{:S(2)}) collective-permute-start(bf16[256,512]{1,0:T(8,128)(2,1)S(1)} %get-tuple-element.38), channel_id=1, source_target_pairs={{0,4},{4,0},{1,5},{5,1},{2,6},{6,2},{3,7},{7,3},{8,12},{12,8},{9,1... | collective-permute-start | bytes 786440 | tf_op jit(solution)/shard_map/ppermute | solution.py:355
  381.5 10.6 %collective-permute-start.32 = (bf16[256,512]{1,0:T(8,128)(2,1)S(1)}, bf16[256,512]{1,0:T(8,128)(2,1)S(1)}, u32[]{:S(2)}, u32[]{:S(2)}) collective-permute-start(bf16[256,512]{1,0:T(8,128)(2,1)S(1)} %get-tuple-element.36), channel_id=1, source_target_pairs={{0,4},{4,0},{1,5},{5,1},{2,6},{6,2},{3,7},{7,3},{8,12},{12,8},{9,1... | collective-permute-start | bytes 786440 | tf_op jit(solution)/shard_map/ppermute | solution.py:355
  (27 other events, 401.0 us)
Sparse Core Ops, SparseCore 0:
  149.1 74.9 reduce-scatter.4
  276.6 48.4 reduce-scatter.2

commit v3 on v2

--- a/solution.py
+++ b/solution.py
@@ -23,15 +23,24 @@
     return lax.dot_general(a, b, dims, preferred_element_type=F32)
 
 
+def cost(flops, mib, exps=0):
+    return pl.CostEstimate(flops=flops, bytes_accessed=mib << 20, transcendentals=exps)
+
+
 def params(mib):
     return pltpu.CompilerParams(vmem_limit_bytes=mib << 20)
 
 
-def norm_kernel(groups, rows, at, here, there, far_here, far_there, gain, own, other, natural):
-    straight, x, y, core, z = at[0] == 1, at[1], at[2], at[3], at[4]
-    width = here.shape[1]
-    near = jnp.where(straight, here[...], there[...]).astype(F32)
-    far = jnp.where(straight, far_here[...], far_there[...]).astype(F32)
+def chosen(kind, local, here, there):
+    return jnp.where(kind == 0, local, jnp.where(kind == 1, here, there))
+
+
+def norm_kernel(groups, rows, at, *refs):
+    nears, fars, (gain, own, other, natural) = refs[:3], refs[3:6], refs[6:]
+    x, y, core, z = at[1], at[2], at[3], at[4]
+    width = nears[0].shape[1]
+    near = chosen(at[0], *[r[...] for r in nears]).astype(F32)
+    far = chosen(at[0], *[r[...] for r in fars]).astype(F32)
     total = jnp.sum(near * near, axis=-1, keepdims=True) + jnp.sum(far * far, axis=-1, keepdims=True)
     inv_rms = lax.rsqrt(total / D + EPS)
     near_at = pl.ds(pl.multiple_of(x * width, width), width)
@@ -48,8 +57,8 @@
                 out[:, put] = natural[:, pl.ds(got, rows)]
 
 
-def norm(at, here, there, far_here, far_there, gain, groups, rows):
-    length, width = here.shape
+def norm(at, nears, fars, gain, groups, rows):
+    length, width = nears[0].shape
     step = 128
 
     def pick(want):
@@ -61,14 +70,15 @@
         grid_spec=pltpu.PrefetchScalarGridSpec(
             num_scalar_prefetch=1,
             grid=(length // step,),
-            in_specs=[pick(1), pick(0), pick(1), pick(0), pl.BlockSpec((1, D), lambda i, s: (0, 0))],
+            in_specs=[pick(i % 3) for i in range(6)] + [pl.BlockSpec((1, D), lambda i, s: (0, 0))],
             out_specs=[out, out],
             scratch_shapes=[pltpu.VMEM((step, D), BF16)],
         ),
         out_shape=[jax.ShapeDtypeStruct((length, D // 2), BF16)] * 2,
         compiler_params=params(32),
+        cost_estimate=cost(8 * length * D, 8),
         name="norm",
-    )(at, here, there, far_here, far_there, gain)
+    )(at, *nears, *fars, gain)
 
 
 def attend_head(bias, qg, kv):
@@ -94,17 +104,18 @@
     return dec.astype(BF16), gkv.astype(BF16)
 
 
-def attend_kernel(at, enc_own, enc_other, w_own, w_other, qg_here, qg_there, dec, gkv):
+def attend_kernel(at, enc_own, enc_other, w_own, w_other, *refs):
+    qgs, (dec, gkv) = refs[:3], refs[3:]
     kv = (dot(enc_own[...], w_own[...]) + dot(enc_other[...], w_other[...])).astype(BF16)
     keys = lax.broadcasted_iota(jnp.int32, (1, kv.shape[0]), 1)
     bias = jnp.where(keys < at[5], 0.0, -1e30).astype(F32)
     for head in range(kv.shape[1] // (2 * HEAD)):
         lanes = slice(head * 2 * HEAD, (head + 1) * 2 * HEAD)
-        qg = jnp.where(at[0] == 1, qg_here[:, lanes], qg_there[:, lanes])
+        qg = chosen(at[6], *[r[:, lanes] for r in qgs])
         dec[:, lanes], gkv[:, lanes] = attend_head(bias, qg, kv[:, lanes])
 
 
-def attend(at, enc_own, enc_other, w_own, w_other, qg_here, qg_there, chunk):
+def attend(at, enc_own, enc_other, w_own, w_other, qgs, chunk):
     length = enc_own.shape[0]
     half, cols = w_own.shape
     step = min(256, cols)
@@ -114,20 +125,23 @@
     out = pl.BlockSpec((length, step), lambda i, s: (0, i))
 
     def pick(want):
-        return pl.BlockSpec((length, step), lambda i, s: (0, jnp.where(s[0] == want, first + i, first)))
+        return pl.BlockSpec((length, step), lambda i, s: (0, jnp.where(s[6] == want, first + i, first)))
 
     return pl.pallas_call(
         attend_kernel,
         grid_spec=pltpu.PrefetchScalarGridSpec(
             num_scalar_prefetch=1,
             grid=(cols // step,),
-            in_specs=[enc, enc, weight, weight, pick(1), pick(0)],
+            in_specs=[enc, enc, weight, weight, pick(0), pick(1), pick(2)],
             out_specs=[out, out],
         ),
         out_shape=[jax.ShapeDtypeStruct((length, cols), BF16)] * 2,
         compiler_params=params(48),
+        cost_estimate=cost(
+            length * cols * (4 * half + 14 * length), 8, length * length * cols // (2 * HEAD)
+        ),
         name="attend",
-    )(at, enc_own, enc_other, w_own, w_other, qg_here, qg_there)
+    )(at, enc_own, enc_other, w_own, w_other, *qgs)
 
 
 def weight_grad_kernel(scale, at, enc_a, enc_b, gkv_a, gkv_b, weight, out, gain_term):
@@ -166,6 +180,7 @@
             jax.ShapeDtypeStruct((groups, 1, step), F32),
         ],
         compiler_params=params(32),
+        cost_estimate=cost(4 * length * half * cols, 8),
         name="weight_grad",
     )(at, enc_a, enc_b, gkv_a, gkv_b, weight)
 
@@ -201,6 +216,7 @@
         ),
         out_shape=jax.ShapeDtypeStruct((length, D // 2), BF16),
         compiler_params=params(32),
+        cost_estimate=cost(4 * length * D * cols, 8),
         name="enc_grad",
     )(at, *gkvs, *owns, *others)
 
@@ -213,6 +229,10 @@
     return jnp.where(
         first, jnp.concatenate([own, other], axis), jnp.concatenate([other, own], axis)
     )
+
+
+def after(value, *others):
+    return lax.optimization_barrier((value,) + others)[0]
 
 
 def on_device(sec_acts, gain, w_kv, src_len, tgt_len):
@@ -246,12 +266,23 @@
         return [lax.ppermute(block, "z", turned(groups, -s)) for s in range(1, groups)]
 
     mine = [chunk_of(y, k) for k in range(CHUNKS)]
-    swapped = [lax.ppermute(chunk_of(1 - y, k), "y", SWAP) for k in range(CHUNKS)]
-
-    here = lax.ppermute(packed, PLANE, [(0, 0), (2, 3)])
+    swapped = []
+    for k in range(CHUNKS):
+        sent = chunk_of(1 - y, k)
+        swapped.append(lax.ppermute(after(sent, *swapped), "y", SWAP))
+
     there = lax.ppermute(packed, PLANE, [(0, 2), (2, 1)])
-    far_here = [across(here, turn, [(0, 0), (3, 3)]) for turn in range(1, shards)]
-    far_there = [across(there, turn, [(1, 1), (2, 2)]) for turn in range(1, shards)]
+    here = lax.ppermute(packed, PLANE, [(2, 3)])
+    nears = [packed, here, there]
+    fars = []
+    for turn in range(1, shards):
+        fars.append(
+            [
+                across(packed, turn, [(0, 0)]),
+                across(here, turn, [(3, 3)]),
+                across(there, turn, [(1, 1), (2, 2)]),
+            ]
+        )
     gains = [gain] + [lax.ppermute(gain, "mp", turned(shards, t)) for t in range(1, shards)]
 
     near_slots, far_slots = slots(mine[0]), slots(swapped[0])
@@ -260,19 +291,27 @@
             [p for pair in zip([mine[0]] + near_slots, [swapped[0]] + far_slots) for p in pair], 0
         )
     ]
+    slot_0, later = {}, {}
     for k in range(1, CHUNKS):
-        block = jnp.concatenate([mine[k], swapped[k]], 0)
-        w_own.append(jnp.concatenate([block] + slots(block), 0))
-    w_other = [lax.ppermute(w, "phase", SWAP) for w in w_own]
+        block = after(jnp.concatenate([mine[k], swapped[k]], 0), near_slots[0])
+        slot_0[k], later[k] = block, slots(block)
+    w_other = [lax.ppermute(w_own[0], "phase", SWAP)]
 
     position = lax.broadcasted_iota(jnp.int32, (length, width), 0)
     is_grad = lax.broadcasted_iota(jnp.int32, (length, width), 1) % (2 * HEAD) >= HEAD
     masked = jnp.where(is_grad & (position >= tgt_len[0]), jnp.zeros((), BF16), packed)
-    qg_here = lax.ppermute(cut(masked, 1, y, half), PLANE, [(1, 0), (3, 3)])
-    qg_there = lax.ppermute(cut(masked, 1, 1 - y, half), PLANE, [(1, 2), (3, 1)])
+    qg_near, qg_far = cut(masked, 1, y, half), cut(masked, 1, 1 - y, half)
+    qg_near, qg_far = lax.optimization_barrier((qg_near, qg_far, swapped[0]))[:2]
+    qgs = [
+        qg_near,
+        lax.ppermute(qg_near, PLANE, [(1, 0)]),
+        lax.ppermute(qg_far, PLANE, [(1, 2), (3, 1)]),
+    ]
     key_count = jnp.where(straight, src_len, lax.ppermute(src_len, "y", SWAP))
+    enc_kind = jnp.where(straight, y, 2)
+    qg_kind = jnp.where(straight, 1 - y, 2)
     at = jnp.concatenate(
-        [jnp.stack([straight.astype(jnp.int32), x, y, core, z]).astype(jnp.int32), key_count]
+        [jnp.stack([enc_kind, x, y, core, z]).astype(jnp.int32), key_count, qg_kind[None]]
     )
 
     def natural(parts, axis):
@@ -293,11 +332,10 @@
     gain_all = natural(gains, 0).astype(F32)
 
     if tiled:
-        enc_own, enc_other = norm(
-            at, here, there, far_here[0], far_there[0], gain_all[None], groups, rows
-        )
+        gain_row = after(gain_all[None], *swapped)
+        enc_own, enc_other = norm(at, nears, fars[0], gain_row, groups, rows)
     else:
-        raw = [jnp.where(straight, a, b) for a, b in zip([here] + far_here, [there] + far_there)]
+        raw = [chosen(enc_kind, *parts) for parts in [nears] + fars]
         hidden = natural(raw, 1).astype(F32)
         inv_rms = lax.rsqrt(jnp.sum(hidden * hidden, axis=-1, keepdims=True) / D + EPS)
         encoded = (hidden * inv_rms * gain_all).astype(BF16)
@@ -307,11 +345,15 @@
 
     decs, gkvs, weight_sums, gain_terms = [], [], [], []
     for k in range(CHUNKS):
-        dec, gkv = attend(at, enc_own, enc_other, w_own[k], w_other[k], qg_here, qg_there, k)
+        if k > 0:
+            slot_0[k] = after(slot_0[k], grad)
+            w_own.append(jnp.concatenate([slot_0[k]] + [after(p, grad) for p in later[k]], 0))
+            w_other.append(lax.ppermute(w_own[k], "phase", SWAP))
+        dec, gkv = attend(at, enc_own, enc_other, w_own[k], w_other[k], qgs, k)
         gkvs.append(gkv)
         decs.append(
             (
-                lax.ppermute(dec, PLANE, [(0, 1), (3, 3)]),
+                jnp.where(y == 0, lax.ppermute(dec, PLANE, [(0, 1)]), dec),
                 lax.ppermute(dec, PLANE, [(2, 1), (1, 3)]),
             )
         )
@@ -337,13 +379,8 @@
         back = jnp.zeros_like(block_order).at[block_order].set(jnp.arange(block_order.shape[0]))
         full = full.astype(BF16).reshape(length, -1, rows)[:, back].reshape(length, D)
         terms = [cut(full, 1, (x + s) % shards, width) for s in range(shards)]
-    grad_enc = terms[0].astype(F32)
-    for turn in range(1, shards):
-        grad_enc = grad_enc + across(terms[turn], turn, [(0, 0), (3, 3)]).astype(F32)
-    for turn in range(shards):
-        grad_enc = grad_enc + across(terms[turn], turn, [(2, 0), (1, 3)]).astype(F32)
-    grad_normed = (grad_enc * gain.astype(F32)).astype(BF16)
-    enc_grads = lax.ppermute(grad_normed, PLANE, [(0, 0), (3, 2)])
+    moved = [across(terms[turn], turn, [(0, 0), (3, 3)]) for turn in range(1, shards)]
+    moved += [across(terms[turn], turn, [(2, 0), (1, 3)]) for turn in range(shards)]
 
     term = sum(gain_terms)
     term = jnp.where(y == 0, term, term[:, ::-1])
@@ -352,7 +389,14 @@
     d_gain = cut(gain_sums, 0, x, width) / gain.astype(F32)
 
     kept = jnp.concatenate([w[:rows] for w in weight_sums], 1)
-    got = jnp.concatenate([lax.ppermute(w[rows:], "y", SWAP) for w in weight_sums], 1)
+    got = [lax.ppermute(w[rows:], "y", SWAP) for w in weight_sums]
+    terms[0] = after(terms[0], gain_sums, got[0])
+    grad_enc = terms[0].astype(F32)
+    for part in moved:
+        grad_enc = grad_enc + part.astype(F32)
+    grad_normed = (grad_enc * gain.astype(F32)).astype(BF16)
+    enc_grads = jnp.where(y == 0, grad_normed, lax.ppermute(grad_normed, PLANE, [(3, 2)]))
+    got = jnp.concatenate(got, 1)
     d_wkv = ordered(y == 0, kept, got, 1).astype(F32)
 
     dec_here = jnp.concatenate([d[0] for d in decs], 1)

time: 402 us -> 383 us (0.953)
  waiting for transfers between devices: 175 us -> 102 us
  blocking collectives: 40.9 us -> 88.8 us
  other arithmetic: 13.2 us -> 20.6 us
  Pallas kernels: 50.5 us -> 56.9 us
  starting transfers between devices: 80.2 us -> 75.3 us
    psum x1, blocking collectives: 40.9 us -> 88.8 us  [on_device(): gain_sums = lax.psum(by_core.reshape(D), ('z', 'y', 'phase', 'mp'))]
    ppermute x5 -> x6, waiting for transfers between devices: 42.6 us -> 0.02 us  [across(): lax.ppermute(value, ('y', 'phase', 'mp'), [(a * shards + s, b * shards +...]
    ppermute x1, waiting for transfers between devices: 26.3 us -> 0.01 us  [on_device(): lax.ppermute(gain, 'mp', turned(shards, t))]
    ppermute x12, waiting for transfers between devices: 24.8 us -> 39.7 us  [the longest x2 27 us: on_device(): swapped.append(lax.ppermute(after(sent, *swapped), 'y', SWAP))]
    ppermute x12, starting transfers between devices: 33.6 us -> 19.5 us  [the longest x2 10.3 us: on_device(): got = [lax.ppermute(w[rows:], 'y', SWAP) for w in weight_sums]]
    ppermute x9, waiting for transfers between devices: 72.5 us -> 62 us  [slots(): lax.ppermute(block, 'z', turned(groups, -s))]
    ppermute x9, starting transfers between devices: 15.9 us -> 22.8 us  [slots(): lax.ppermute(block, 'z', turned(groups, -s))]
    ppermute x1, waiting for transfers between devices: 5.29 us -> 0.01 us  [on_device(): there = lax.ppermute(packed, PLANE, [(0, 2), (2, 1)])]
  transfers between devices with their start and end apart: 36 -> 37, of which waited for: 17 -> 11; matrix products, arithmetic and copies ran while one was open for 6% -> 9% of each run, Pallas kernels for 12% -> 15%
where the time goes in v3:
time: 383 us; the launch traced here: 381 us
  waiting for transfers between devices  102 us (27%)
  blocking collectives  88.8 us (23%)
  starting transfers between devices  75.3 us (20%)
  Pallas kernels  56.9 us (15%)
  local copies, waits for them, and re-layouts  21 us (5%)
  other arithmetic  20.6 us (5%)
  between operations  16.4 us (4%)
    psum x1, blocking collectives, on_device(): gain_sums = lax.psum(by_core.reshape(D), ('z', 'y', 'phase', 'mp'))  88.8 us
    ppermute x9, waiting for transfers between devices, slots(): lax.ppermute(block, 'z', turned(groups, -s))  62 us
    pallas_call x2, Pallas kernels, attend(): pl.pallas_call(attend_kernel, grid_spec=pltpu.PrefetchScalarGridSpec(num_...  28.8 us
    ppermute x2, waiting for transfers between devices, on_device(): swapped.append(lax.ppermute(after(sent, *swapped), 'y', SWAP))  27 us
    ppermute x9, starting transfers between devices, slots(): lax.ppermute(block, 'z', turned(groups, -s))  22.8 us
    unnamed x49, local copies, waits for them, and re-layouts  16 us
    ppermute x6, starting transfers between devices, across(): lax.ppermute(value, ('y', 'phase', 'mp'), [(a * shards + s, b * shards +...  12.2 us
    pallas_call x2, Pallas kernels, weight_grad(): pl.pallas_call(lambda *refs: weight_grad_kernel(scale, *refs), grid_spec=...  11.3 us
  transfers between devices with their start and end apart: 37, of which 11 were waited for; matrix products, arithmetic and copies ran while one was open for 9% of the time, Pallas kernels for 15%

profile of v3, /device:TPU:0, one launch (start us, length us, event | category | flops | bytes accessed | tf_op | source)
XLA Modules:
  0.0 380.8 jit_solution(3887064744031158836)
XLA Ops:
  7.2 6.4 %collective-permute-start.2 = (bf16[512,2048]{1,0:T(8,128)(2,1)}, bf16[512,2048]{1,0:T(8,128)(2,1)}, u32[]{:S(2)}, u32[]{:S(2)}) collective-permute-start(bf16[512,2048]{1,0:T(8,128)(2,1)} %bitcast.17), channel_id=1, source_target_pairs={{0,4},{4,2},{1,5},{5,3},{8,12},{12,10},{9,13},{13,11},{16,20},{20,... | collective-permute-start | bytes 6291464 | tf_op jit(solution)/shard_map/ppermute | solution.py:274
  15.6 2.1 constant_dynamic-update-slice_fusion.7
  17.7 2.6 collective-permute-start.11
  20.3 3.4 collective-permute-start.3
  23.7 18.3 %collective-permute-done.7 = bf16[256,512]{1,0:T(8,128)(2,1)S(1)} collective-permute-done((bf16[256,512]{1,0:T(8,128)(2,1)S(1)}, bf16[256,512]{1,0:T(8,128)(2,1)S(1)}, u32[]{:S(2)}, u32[]{:S(2)}) %collective-permute-start.7) | collective-permute-done | bytes 262176 | tf_op jit(solution)/shard_map/ppermute | solution.py:272
  42.1 3.6 collective-permute-start.9
  52.9 4.8 %collective-permute-done.10 = bf16[256,512]{1,0:T(8,128)(2,1)S(1)} collective-permute-done((bf16[256,512]{1,0:T(8,128)(2,1)S(1)}, bf16[256,512]{1,0:T(8,128)(2,1)S(1)}, u32[]{:S(2)}, u32[]{:S(2)}) %collective-permute-start.10) | collective-permute-done | bytes 262176 | tf_op jit(solution)/shard_map/ppermute | solution.py:266
  57.7 11.6 %collective-permute-start.13 = (bf16[256,512]{1,0:T(8,128)(2,1)S(1)}, bf16[256,512]{1,0:T(8,128)(2,1)S(1)}, u32[]{:S(2)}, u32[]{:S(2)}) collective-permute-start(bf16[256,512]{1,0:T(8,128)(2,1)S(1)} %get-tuple-element.44), channel_id=1, source_target_pairs={{0,8},{8,16},{16,24},{24,0},{1,9},{9,17},{17,25},{25,1},{2,10},{10... | collective-permute-start | bytes 786440 | tf_op jit(solution)/shard_map/ppermute | solution.py:266
  73.4 2.2 collective-permute-done.13
  76.3 3.8 collective-permute-done.14
  85.8 8.6 %collective-permute-done.8 = bf16[256,512]{1,0:T(8,128)(2,1)S(1)} collective-permute-done((bf16[256,512]{1,0:T(8,128)(2,1)S(1)}, bf16[256,512]{1,0:T(8,128)(2,1)S(1)}, u32[]{:S(2)}, u32[]{:S(2)}) %collective-permute-start.8) | collective-permute-done | bytes 262176 | tf_op jit(solution)/shard_map/ppermute | solution.py:272
  94.4 5.7 %norm.1 = (bf16[512,2048]{1,0:T(8,128)(2,1)S(1)}, bf16[512,2048]{1,0:T(8,128)(2,1)S(1)}) custom-call(s32[7]{0:T(128)S(1)} %concatenate.56.refs_0_.at, bf16[512,2048]{1,0:T(8,128)(2,1)S(1)} %bitcast.20, bf16[512,2048]{1,0:T(8,128)(2,1)} %collective-permute-done.1.refs_2_, bf16[512,2048]{1,0:T(8,128)(2,1)} %collective-permute-done.2.refs_3_, ...), custom_call_target="tpu_custom_call" | custom-call | flops 16777216 | bytes 8388608 | tf_op jit(solution)/shard_map/norm/pallas_call | solution.py:68
  104.2 3.9 %collective-permute-done.16.refs_1_ = bf16[512,1024]{1,0:T(8,128)(2,1)S(1)} collective-permute-done((bf16[512,1024]{1,0:T(8,128)(2,1)S(1)}, bf16[512,1024]{1,0:T(8,128)(2,1)S(1)}, u32[]{:S(2)}, u32[]{:S(2)}) %collective-permute-start.16) | collective-permute-done | bytes 1048608 | tf_op jit(solution)/shard_map/ppermute | solution.py:307
  108.1 14.6 %attend.2 = (bf16[512,512]{1,0:T(8,128)(2,1)S(1)}, bf16[512,512]{1,0:T(8,128)(2,1)S(1)}) custom-call(s32[7]{0:T(128)S(1)} %concatenate.56.refs_0_.at, bf16[512,2048]{1,0:T(8,128)(2,1)} %copy-done.4, bf16[512,2048]{1,0:T(8,128)(2,1)} %copy-done.9, bf16[2048,512]{1,0:T(8,128)(2,1)} %constant_dynamic-update-slice_fusion.w_own.refs_5_.own_0, ...), custom_call_target="tpu_custom_call" | custom-call | flops 4026531840 | bytes 8388608 | tf_op jit(solution)/shard_map/attend/pallas_call | solution.py:130
  122.7 9.6 %collective-permute-start.19 = (bf16[512,512]{1,0:T(8,128)(2,1)S(1)}, bf16[512,512]{1,0:T(8,128)(2,1)S(1)}, u32[]{:S(2)}, u32[]{:S(2)}) collective-permute-start(bf16[512,512]{1,0:T(8,128)(2,1)S(1)} %get-tuple-element.29.refs_3_.gkv_0), channel_id=1, source_target_pairs={{0,2},{2,0},{1,3},{3,1},{4,6},{6,4},{5,7},{7,5},{8,10},{10,8},{9,1... | collective-permute-start | bytes 1572872 | tf_op jit(solution)/shard_map/ppermute | solution.py:360
  134.0 2.9 collective-permute-start.20
  137.0 6.2 %weight_grad.2 = (bf16[2048,512]{1,0:T(8,128)(2,1)}, f32[4,1,512]{2,1,0:T(1,128)S(1)}) custom-call(s32[7]{0:T(128)S(1)} %concatenate.56.refs_0_.at, bf16[512,2048]{1,0:T(8,128)(2,1)S(1)} %copy-done.5, bf16[512,2048]{1,0:T(8,128)(2,1)S(1)} %collective-permute-done.18.refs_2_, bf16[512,512]{1,0:T(8,128)(2,1)S(1)} %get-tuple-element.29.refs_3_.gkv_0, ...), custom_call_target="tpu_custom_call" | custom-call | flops 2147483648 | bytes 8388608 | tf_op jit(solution)/shard_map/weight_grad/pallas_call | solution.py:167
  143.5 6.6 %collective-permute-done.22 = bf16[512,512]{1,0:T(8,128)(2,1)} collective-permute-done((bf16[512,512]{1,0:T(8,128)(2,1)}, bf16[512,512]{1,0:T(8,128)(2,1)}, u32[]{:S(2)}, u32[]{:S(2)}) %collective-permute-start.22) | collective-permute-done | bytes 524320 | tf_op jit(solution)/shard_map/ppermute | solution.py:266
  150.1 42.7 %collective-permute-done.21 = bf16[512,512]{1,0:T(8,128)(2,1)} collective-permute-done((bf16[512,512]{1,0:T(8,128)(2,1)}, bf16[512,512]{1,0:T(8,128)(2,1)}, u32[]{:S(2)}, u32[]{:S(2)}) %collective-permute-start.21) | collective-permute-done | bytes 524320 | tf_op jit(solution)/shard_map/ppermute | solution.py:266
  197.2 4.1 %collective-permute-done.23.w_other.other_1 = bf16[2048,512]{1,0:T(8,128)(2,1)S(1)} collective-permute-done((bf16[2048,512]{1,0:T(8,128)(2,1)S(1)}, bf16[2048,512]{1,0:T(8,128)(2,1)S(1)}, u32[]{:S(2)}, u32[]{:S(2)}) %collective-permute-start.23) | collective-permute-done | bytes 2097184 | tf_op jit(solution)/shard_map/ppermute | solution.py:351
  202.8 14.2 %attend.3 = (bf16[512,512]{1,0:T(8,128)(2,1)S(1)}, bf16[512,512]{1,0:T(8,128)(2,1)S(1)}) custom-call(s32[7]{0:T(128)S(1)} %concatenate.56.refs_0_.at, bf16[512,2048]{1,0:T(8,128)(2,1)} %copy-done.4, bf16[512,2048]{1,0:T(8,128)(2,1)} %copy-done.9, bf16[2048,512]{1,0:T(8,128)(2,1)} %copy-done.1, bf16[2048,512]{1,0:T(8,128)(2,1)} %copy-done.10, ...), custom_call_target="tpu_custom_call" | custom-call | flops 4026531840 | bytes 8388608 | tf_op jit(solution)/shard_map/attend/pallas_call | solution.py:130
  220.4 5.1 %enc_grad.2 = bf16[512,2048]{1,0:T(8,128)(2,1)S(1)} custom-call(s32[7]{0:T(128)S(1)} %concatenate.56.refs_0_.at, bf16[512,512]{1,0:T(8,128)(2,1)S(1)} %copy-done.15, bf16[512,512]{1,0:T(8,128)(2,1)S(1)} %get-tuple-element.36.gkv_1.refs_3_, bf16[2048,512]{1,0:T(8,128)(2,1)} %constant_dynamic-update-slice_fusion.w_own.refs_5_.own_0, ...), custom_call_target="tpu_custom_call" | custom-call | flops 4294967296 | bytes 8388608 | tf_op jit(solution)/shard_map/enc_grad/pallas_call | solution.py:209
  227.1 6.0 %enc_grad.3 = bf16[512,2048]{1,0:T(8,128)(2,1)} custom-call(s32[7]{0:T(128)S(1)} %concatenate.56.refs_0_.at, bf16[512,512]{1,0:T(8,128)(2,1)S(1)} %copy-done.15, bf16[512,512]{1,0:T(8,128)(2,1)S(1)} %get-tuple-element.36.gkv_1.refs_3_, bf16[2048,512]{1,0:T(8,128)(2,1)} %constant_dynamic-update-slice_fusion.w_own.refs_5_.own_0, ...), custom_call_target="tpu_custom_call" | custom-call | flops 4294967296 | bytes 8388608 | tf_op jit(solution)/shard_map/enc_grad/pallas_call | solution.py:209
  236.3 5.1 %weight_grad.3 = (bf16[2048,512]{1,0:T(8,128)(2,1)}, f32[4,1,512]{2,1,0:T(1,128)S(1)}) custom-call(s32[7]{0:T(128)S(1)} %concatenate.56.refs_0_.at, bf16[512,2048]{1,0:T(8,128)(2,1)S(1)} %copy-done.6, bf16[512,2048]{1,0:T(8,128)(2,1)S(1)} %copy-done.8, bf16[512,512]{1,0:T(8,128)(2,1)S(1)} %get-tuple-element.36.gkv_1.refs_3_, ...), custom_call_target="tpu_custom_call" | custom-call | flops 2147483648 | bytes 8388608 | tf_op jit(solution)/shard_map/weight_grad/pallas_call | solution.py:167
  243.4 5.4 %collective-permute-start.25 = (bf16[256,512]{1,0:T(8,128)(2,1)}, bf16[256,512]{1,0:T(8,128)(2,1)}, u32[]{:S(2)}, u32[]{:S(2)}) collective-permute-start(bf16[256,512]{1,0:T(8,128)(2,1)} %get-tuple-element.51), channel_id=1, source_target_pairs={{0,4},{4,0},{1,5},{5,1},{2,6},{6,2},{3,7},{7,3},{8,12},{12,8},{9,1... | collective-permute-start | bytes 786440 | tf_op jit(solution)/shard_map/ppermute | solution.py:392
  249.0 88.8 %psum.7 = f32[4096]{0:T(1024)S(1)} all-reduce(f32[4096]{0:T(1024)S(1)} %bitcast.22), channel_id=1, replica_groups=mesh['z'=4,'y'=2,'phase'=2,'mp'=2] {'z','y','phase','mp'}, use_global_device_ids=true, to_apply=%region_0.1 | all-reduce | flops 4096 | bytes 32768 | tf_op jit(solution)/shard_map/psum | solution.py:388
  337.7 6.0 %multiply_convert_fusion = bf16[512,2048]{1,0:T(8,128)(2,1)} fusion(bf16[512,2048]{1,0:T(8,128)(2,1)} %collective-permute-done.28, bf16[512,2048]{1,0:T(8,128)(2,1)} %collective-permute-done.27, bf16[512,2048]{1,0:T(8,128)(2,1)} %collective-permute-done.26, bf16[512,2048]{1,0:T(8,128)(2,1)S(1)} %enc_grad.2, f32[2048]{0:T(1024)S(1)} %convert_element_type.37), kind=kLoop, calls=%fused_computation | loop fusion | flops 9437184 | bytes 10493952 | tf_op jit(solution)/shard_map/convert_element_type | solution.py:397
  346.6 2.1 collective-permute-start.31
  357.1 4.9 %collective-permute-start.34 = (bf16[256,512]{1,0:T(8,128)(2,1)S(1)}, bf16[256,512]{1,0:T(8,128)(2,1)S(1)}, u32[]{:S(2)}, u32[]{:S(2)}) collective-permute-start(bf16[256,512]{1,0:T(8,128)(2,1)S(1)} %get-tuple-element.53), channel_id=1, source_target_pairs={{0,4},{4,0},{1,5},{5,1},{2,6},{6,2},{3,7},{7,3},{8,12},{12,8},{9,1... | collective-permute-start | bytes 786440 | tf_op jit(solution)/shard_map/ppermute | solution.py:392
  362.0 4.7 %fusion.3 = bf16[1,1,512,2048]{3,2,1,0:T(8,128)(2,1)} fusion(bf16[512,512]{1,0:T(8,128)(2,1)} %collective-permute-done.33, bf16[512,512]{1,0:T(8,128)(2,1)} %collective-permute-done.32, bf16[512,512]{1,0:T(8,128)(2,1)} %broadcast_select_fusion, bf16[512,512]{1,0:T(8,128)(2,1)} %broadcast_select_fusion.1, bf16[512,2048]{1,0:T(8,128)(2,1)} %multiply_convert_fusion, ...), kind=kLoop, calls=%fused_computation.6 | loop fusion | flops 19922944 | bytes 8388610 | tf_op jit(solution)/shard_map/broadcast_in_dim | solution.py:405
  366.7 4.7 %collective-permute-done.34 = bf16[256,512]{1,0:T(8,128)(2,1)S(1)} collective-permute-done((bf16[256,512]{1,0:T(8,128)(2,1)S(1)}, bf16[256,512]{1,0:T(8,128)(2,1)S(1)}, u32[]{:S(2)}, u32[]{:S(2)}) %collective-permute-start.34) | collective-permute-done | bytes 262176 | tf_op jit(solution)/shard_map/ppermute | solution.py:392
  371.3 2.6 fusion.4
  (129 shorter events, 51.0 us)
Async XLA Ops:
  7.2 234.5 %reduce-scatter.3.cloned.1.call-start = ((), (), s32[]{:S(2)}) async-start(), calls=%async_computation.2 | async-start | bytes 2621440 | tf_op jit(solution)/shard_map/reduce_scatter | solution.py:372
  7.2 38.4 %collective-permute-start.2 = (bf16[512,2048]{1,0:T(8,128)(2,1)}, bf16[512,2048]{1,0:T(8,128)(2,1)}, u32[]{:S(2)}, u32[]{:S(2)}) collective-permute-start(bf16[512,2048]{1,0:T(8,128)(2,1)} %bitcast.17), channel_id=1, source_target_pairs={{0,4},{4,2},{1,5},{5,3},{8,12},{12,10},{9,13},{13,11},{16,20},{20,... | collective-permute-start | bytes 6291464 | tf_op jit(solution)/shard_map/ppermute | solution.py:274
  13.6 34.2 %collective-permute-start.1 = (bf16[512,2048]{1,0:T(8,128)(2,1)}, bf16[512,2048]{1,0:T(8,128)(2,1)}, u32[]{:S(2)}, u32[]{:S(2)}) collective-permute-start(bf16[512,2048]{1,0:T(8,128)(2,1)} %bitcast.18), channel_id=1, source_target_pairs={{4,6},{5,7},{12,14},{13,15},{20,22},{21,23},{28,30},{29,31}} | collective-permute-start | bytes 6291464 | tf_op jit(solution)/shard_map/ppermute | solution.py:275
  17.7 24.4 %collective-permute-start.7 = (bf16[256,512]{1,0:T(8,128)(2,1)S(1)}, bf16[256,512]{1,0:T(8,128)(2,1)S(1)}, u32[]{:S(2)}, u32[]{:S(2)}) collective-permute-start(bf16[256,512]{1,0:T(8,128)(2,1)S(1)} %get-tuple-element.48), channel_id=1, source_target_pairs={{0,4},{4,0},{1,5},{5,1},{2,6},{6,2},{3,7},{7,3},{8,12},{12,8},{9,1... | collective-permute-start | bytes 786440 | tf_op jit(solution)/shard_map/ppermute | solution.py:272
  17.7 32.7 %collective-permute-start.11 = (bf16[256,512]{1,0:T(8,128)(2,1)S(1)}, bf16[256,512]{1,0:T(8,128)(2,1)S(1)}, u32[]{:S(2)}, u32[]{:S(2)}) collective-permute-start(bf16[256,512]{1,0:T(8,128)(2,1)S(1)} %get-tuple-element.44), channel_id=1, source_target_pairs={{0,16},{8,24},{16,0},{24,8},{1,17},{9,25},{17,1},{25,9},{2,18},{10... | collective-permute-start | bytes 786440 | tf_op jit(solution)/shard_map/ppermute | solution.py:266
  20.3 74.1 %collective-permute-start.3 = (bf16[512,2048]{1,0:T(8,128)(2,1)S(1)}, bf16[512,2048]{1,0:T(8,128)(2,1)}, u32[]{:S(2)}, u32[]{:S(2)}) collective-permute-start(bf16[512,2048]{1,0:T(8,128)(2,1)S(1)} %bitcast.19), channel_id=1, source_target_pairs={{0,1},{1,0},{8,9},{9,8},{16,17},{17,16},{24,25},{25,24}} | collective-permute-start | bytes 6291464 | tf_op jit(solution)/shard_map/ppermute | solution.py:256
  42.1 8.8 %collective-permute-start.9 = (bf16[256,512]{1,0:T(8,128)(2,1)S(1)}, bf16[256,512]{1,0:T(8,128)(2,1)S(1)}, u32[]{:S(2)}, u32[]{:S(2)}) collective-permute-start(bf16[256,512]{1,0:T(8,128)(2,1)S(1)} %get-tuple-element.44), channel_id=1, source_target_pairs={{0,24},{8,0},{16,8},{24,16},{1,25},{9,1},{17,9},{25,17},{2,26},{10... | collective-permute-start | bytes 786440 | tf_op jit(solution)/shard_map/ppermute | solution.py:266
  45.7 48.7 %collective-permute-start.5 = (bf16[512,2048]{1,0:T(8,128)(2,1)}, bf16[512,2048]{1,0:T(8,128)(2,1)}, u32[]{:S(2)}, u32[]{:S(2)}) collective-permute-start(bf16[512,2048]{1,0:T(8,128)(2,1)} %collective-permute-done.2.refs_3_), channel_id=1, source_target_pairs={{2,3},{3,2},{4,5},{5,4},{10,11},{11,10},{12,13},{13,12},{18,19},{1... | collective-permute-start | bytes 6291464 | tf_op jit(solution)/shard_map/ppermute | solution.py:256
  47.7 46.7 %collective-permute-start.4 = (bf16[512,2048]{1,0:T(8,128)(2,1)}, bf16[512,2048]{1,0:T(8,128)(2,1)}, u32[]{:S(2)}, u32[]{:S(2)}) collective-permute-start(bf16[512,2048]{1,0:T(8,128)(2,1)} %collective-permute-done.1.refs_2_), channel_id=1, source_target_pairs={{6,7},{7,6},{14,15},{15,14},{22,23},{23,22},{30,31},{31,30}} | collective-permute-start | bytes 6291464 | tf_op jit(solution)/shard_map/ppermute | solution.py:256
  50.4 7.4 %collective-permute-start.10 = (bf16[256,512]{1,0:T(8,128)(2,1)S(1)}, bf16[256,512]{1,0:T(8,128)(2,1)S(1)}, u32[]{:S(2)}, u32[]{:S(2)}) collective-permute-start(bf16[256,512]{1,0:T(8,128)(2,1)S(1)} %collective-permute-done.7), channel_id=1, source_target_pairs={{0,24},{8,0},{16,8},{24,16},{1,25},{9,1},{17,9},{25,17},{2,26},{10... | collective-permute-start | bytes 786440 | tf_op jit(solution)/shard_map/ppermute | solution.py:266
  50.9 21.0 %collective-permute-start.12 = (bf16[256,512]{1,0:T(8,128)(2,1)S(1)}, bf16[256,512]{1,0:T(8,128)(2,1)S(1)}, u32[]{:S(2)}, u32[]{:S(2)}) collective-permute-start(bf16[256,512]{1,0:T(8,128)(2,1)S(1)} %collective-permute-done.7), channel_id=1, source_target_pairs={{0,16},{8,24},{16,0},{24,8},{1,17},{9,25},{17,1},{25,9},{2,18},{10... | collective-permute-start | bytes 786440 | tf_op jit(solution)/shard_map/ppermute | solution.py:266
  57.7 17.8 %collective-permute-start.13 = (bf16[256,512]{1,0:T(8,128)(2,1)S(1)}, bf16[256,512]{1,0:T(8,128)(2,1)S(1)}, u32[]{:S(2)}, u32[]{:S(2)}) collective-permute-start(bf16[256,512]{1,0:T(8,128)(2,1)S(1)} %get-tuple-element.44), channel_id=1, source_target_pairs={{0,8},{8,16},{16,24},{24,0},{1,9},{9,17},{17,25},{25,1},{2,10},{10... | collective-permute-start | bytes 786440 | tf_op jit(solution)/shard_map/ppermute | solution.py:266
  71.9 8.2 %collective-permute-start.14 = (bf16[256,512]{1,0:T(8,128)(2,1)S(1)}, bf16[256,512]{1,0:T(8,128)(2,1)S(1)}, u32[]{:S(2)}, u32[]{:S(2)}) collective-permute-start(bf16[256,512]{1,0:T(8,128)(2,1)S(1)} %collective-permute-done.7), channel_id=1, source_target_pairs={{0,8},{8,16},{16,24},{24,0},{1,9},{9,17},{17,25},{25,1},{2,10},{10... | collective-permute-start | bytes 786440 | tf_op jit(solution)/shard_map/ppermute | solution.py:266
  75.6 6.7 %collective-permute-start = (s32[1]{0:T(128)}, s32[1]{0:T(128)}, u32[]{:S(2)}, u32[]{:S(2)}) collective-permute-start(s32[1]{0:T(128)} %param.8), channel_id=1, source_target_pairs={{0,4},{4,0},{1,5},{5,1},{2,6},{6,2},{3,7},{7,3},{8,12},{12,8},{9,1... | collective-permute-start | bytes 20 | tf_op jit(solution)/shard_map/ppermute | solution.py:310
  82.3 25.8 %collective-permute-start.15 = (bf16[2048,512]{1,0:T(8,128)(2,1)}, bf16[2048,512]{1,0:T(8,128)(2,1)}, u32[]{:S(2)}, u32[]{:S(2)}) collective-permute-start(bf16[2048,512]{1,0:T(8,128)(2,1)} %constant_dynamic-update-slice_fusion.w_own.refs_5_.own_0), channel_id=1, source_target_pairs={{0,2},{2,0},{1,3},{3,1},{4,6},{6,4},{5,7},{7,5},{8,10},{10,8},{9,1... | collective-permute-start | bytes 6291464 | tf_op jit(solution)/shard_map/ppermute | solution.py:298
  85.6 8.8 %collective-permute-start.8 = (bf16[256,512]{1,0:T(8,128)(2,1)S(1)}, bf16[256,512]{1,0:T(8,128)(2,1)S(1)}, u32[]{:S(2)}, u32[]{:S(2)}) collective-permute-start(bf16[256,512]{1,0:T(8,128)(2,1)S(1)} %copy-done.17), channel_id=1, source_target_pairs={{0,4},{4,0},{1,5},{5,1},{2,6},{6,2},{3,7},{7,3},{8,12},{12,8},{9,1... | collective-permute-start | bytes 786440 | tf_op jit(solution)/shard_map/ppermute | solution.py:272
  100.2 36.8 %collective-permute-start.18 = (bf16[512,2048]{1,0:T(8,128)(2,1)S(1)}, bf16[512,2048]{1,0:T(8,128)(2,1)S(1)}, u32[]{:S(2)}, u32[]{:S(2)}) collective-permute-start(bf16[512,2048]{1,0:T(8,128)(2,1)S(1)} %get-tuple-element.26.enc_other), channel_id=1, source_target_pairs={{0,2},{2,0},{1,3},{3,1},{4,6},{6,4},{5,7},{7,5},{8,10},{10,8},{9,1... | collective-permute-start | bytes 6291464 | tf_op jit(solution)/shard_map/ppermute | solution.py:344
  122.7 14.3 %collective-permute-start.19 = (bf16[512,512]{1,0:T(8,128)(2,1)S(1)}, bf16[512,512]{1,0:T(8,128)(2,1)S(1)}, u32[]{:S(2)}, u32[]{:S(2)}) collective-permute-start(bf16[512,512]{1,0:T(8,128)(2,1)S(1)} %get-tuple-element.29.refs_3_.gkv_0), channel_id=1, source_target_pairs={{0,2},{2,0},{1,3},{3,1},{4,6},{6,4},{5,7},{7,5},{8,10},{10,8},{9,1... | collective-permute-start | bytes 1572872 | tf_op jit(solution)/shard_map/ppermute | solution.py:360
  133.1 17.0 %collective-permute-start.22 = (bf16[512,512]{1,0:T(8,128)(2,1)}, bf16[512,512]{1,0:T(8,128)(2,1)}, u32[]{:S(2)}, u32[]{:S(2)}) collective-permute-start(bf16[512,512]{1,0:T(8,128)(2,1)} %pad_maximum_fusion), channel_id=1, source_target_pairs={{0,8},{8,16},{16,24},{24,0},{1,9},{9,17},{17,25},{25,1},{2,10},{10... | collective-permute-start | bytes 1572872 | tf_op jit(solution)/shard_map/ppermute | solution.py:266
  133.9 59.0 %collective-permute-start.21 = (bf16[512,512]{1,0:T(8,128)(2,1)}, bf16[512,512]{1,0:T(8,128)(2,1)}, u32[]{:S(2)}, u32[]{:S(2)}) collective-permute-start(bf16[512,512]{1,0:T(8,128)(2,1)} %pad_maximum_fusion), channel_id=1, source_target_pairs={{0,16},{8,24},{16,0},{24,8},{1,17},{9,25},{17,1},{25,9},{2,18},{10... | collective-permute-start | bytes 1572872 | tf_op jit(solution)/shard_map/ppermute | solution.py:266
  134.0 58.8 %collective-permute-start.20 = (bf16[512,512]{1,0:T(8,128)(2,1)}, bf16[512,512]{1,0:T(8,128)(2,1)}, u32[]{:S(2)}, u32[]{:S(2)}) collective-permute-start(bf16[512,512]{1,0:T(8,128)(2,1)} %pad_maximum_fusion), channel_id=1, source_target_pairs={{0,24},{8,0},{16,8},{24,16},{1,25},{9,1},{17,9},{25,17},{2,26},{10... | collective-permute-start | bytes 1572872 | tf_op jit(solution)/shard_map/ppermute | solution.py:266
  143.3 212.7 %reduce-scatter.5.cloned.1.call-start = ((), (), s32[]{:S(2)}) async-start(), calls=%async_computation.3 | async-start | bytes 2621440 | tf_op jit(solution)/shard_map/reduce_scatter | solution.py:372
  217.0 19.3 %collective-permute-start.24 = (bf16[512,512]{1,0:T(8,128)(2,1)S(1)}, bf16[512,512]{1,0:T(8,128)(2,1)S(1)}, u32[]{:S(2)}, u32[]{:S(2)}) collective-permute-start(bf16[512,512]{1,0:T(8,128)(2,1)S(1)} %get-tuple-element.36.gkv_1.refs_3_), channel_id=1, source_target_pairs={{0,2},{2,0},{1,3},{3,1},{4,6},{6,4},{5,7},{7,5},{8,10},{10,8},{9,1... | collective-permute-start | bytes 1572872 | tf_op jit(solution)/shard_map/ppermute | solution.py:360
  225.6 112.2 %collective-permute-start.27 = (bf16[512,2048]{1,0:T(8,128)(2,1)S(1)}, bf16[512,2048]{1,0:T(8,128)(2,1)}, u32[]{:S(2)}, u32[]{:S(2)}) collective-permute-start(bf16[512,2048]{1,0:T(8,128)(2,1)S(1)} %enc_grad.2), channel_id=1, source_target_pairs={{4,0},{5,1},{2,6},{3,7},{12,8},{13,9},{10,14},{11,15},{20,16},{21,... | collective-permute-start | bytes 6291464 | tf_op jit(solution)/shard_map/ppermute | solution.py:256
  233.1 104.6 %collective-permute-start.28 = (bf16[512,2048]{1,0:T(8,128)(2,1)}, bf16[512,2048]{1,0:T(8,128)(2,1)}, u32[]{:S(2)}, u32[]{:S(2)}) collective-permute-start(bf16[512,2048]{1,0:T(8,128)(2,1)} %enc_grad.3), channel_id=1, source_target_pairs={{4,1},{5,0},{2,7},{3,6},{12,9},{13,8},{10,15},{11,14},{20,17},{21,... | collective-permute-start | bytes 6291464 | tf_op jit(solution)/shard_map/ppermute | solution.py:256
  234.4 103.4 %collective-permute-start.26 = (bf16[512,2048]{1,0:T(8,128)(2,1)}, bf16[512,2048]{1,0:T(8,128)(2,1)}, u32[]{:S(2)}, u32[]{:S(2)}) collective-permute-start(bf16[512,2048]{1,0:T(8,128)(2,1)} %enc_grad.3), channel_id=1, source_target_pairs={{0,1},{1,0},{6,7},{7,6},{8,9},{9,8},{14,15},{15,14},{16,17},{17,16... | collective-permute-start | bytes 6291464 | tf_op jit(solution)/shard_map/ppermute | solution.py:256
  243.4 94.3 %collective-permute-start.25 = (bf16[256,512]{1,0:T(8,128)(2,1)}, bf16[256,512]{1,0:T(8,128)(2,1)}, u32[]{:S(2)}, u32[]{:S(2)}) collective-permute-start(bf16[256,512]{1,0:T(8,128)(2,1)} %get-tuple-element.51), channel_id=1, source_target_pairs={{0,4},{4,0},{1,5},{5,1},{2,6},{6,2},{3,7},{7,3},{8,12},{12,8},{9,1... | collective-permute-start | bytes 786440 | tf_op jit(solution)/shard_map/ppermute | solution.py:392
  343.7 18.3 %collective-permute-start.29 = (bf16[512,2048]{1,0:T(8,128)(2,1)}, bf16[512,2048]{1,0:T(8,128)(2,1)S(1)}, u32[]{:S(2)}, u32[]{:S(2)}) collective-permute-start(bf16[512,2048]{1,0:T(8,128)(2,1)} %multiply_convert_fusion), channel_id=1, source_target_pairs={{6,4},{7,5},{14,12},{15,13},{22,20},{23,21},{30,28},{31,29}} | collective-permute-start | bytes 6291464 | tf_op jit(solution)/shard_map/ppermute | solution.py:398
  346.6 7.5 %collective-permute-start.31 = (bf16[512,512]{1,0:T(8,128)(2,1)S(1)}, bf16[512,512]{1,0:T(8,128)(2,1)}, u32[]{:S(2)}, u32[]{:S(2)}) collective-permute-start(bf16[512,512]{1,0:T(8,128)(2,1)S(1)} %get-tuple-element.41), channel_id=1, source_target_pairs={{0,2},{1,3},{8,10},{9,11},{16,18},{17,19},{24,26},{25,27}} | collective-permute-start | bytes 1572872 | tf_op jit(solution)/shard_map/ppermute | solution.py:356
  348.7 13.3 %collective-permute-start.32 = (bf16[512,512]{1,0:T(8,128)(2,1)S(1)}, bf16[512,512]{1,0:T(8,128)(2,1)}, u32[]{:S(2)}, u32[]{:S(2)}) collective-permute-start(bf16[512,512]{1,0:T(8,128)(2,1)S(1)} %get-tuple-element.40), channel_id=1, source_target_pairs={{4,2},{2,6},{5,3},{3,7},{12,10},{10,14},{13,11},{11,15},{20,18},{1... | collective-permute-start | bytes 1572872 | tf_op jit(solution)/shard_map/ppermute | solution.py:357
  352.0 9.9 %collective-permute-start.33 = (bf16[512,512]{1,0:T(8,128)(2,1)S(1)}, bf16[512,512]{1,0:T(8,128)(2,1)}, u32[]{:S(2)}, u32[]{:S(2)}) collective-permute-start(bf16[512,512]{1,0:T(8,128)(2,1)S(1)} %get-tuple-element.41), channel_id=1, source_target_pairs={{4,2},{2,6},{5,3},{3,7},{12,10},{10,14},{13,11},{11,15},{20,18},{1... | collective-permute-start | bytes 1572872 | tf_op jit(solution)/shard_map/ppermute | solution.py:357
  357.1 14.3 %collective-permute-start.34 = (bf16[256,512]{1,0:T(8,128)(2,1)S(1)}, bf16[256,512]{1,0:T(8,128)(2,1)S(1)}, u32[]{:S(2)}, u32[]{:S(2)}) collective-permute-start(bf16[256,512]{1,0:T(8,128)(2,1)S(1)} %get-tuple-element.53), channel_id=1, source_target_pairs={{0,4},{4,0},{1,5},{5,1},{2,6},{6,2},{3,7},{7,3},{8,12},{12,8},{9,1... | collective-permute-start | bytes 786440 | tf_op jit(solution)/shard_map/ppermute | solution.py:392
  (24 other events, 310.1 us)
Sparse Core Ops, SparseCore 0:
  143.4 68.4 reduce-scatter.2
  241.6 68.3 reduce-scatter.4

commit v4 on v3

--- a/solution.py
+++ b/solution.py
@@ -9,6 +9,7 @@
 HEAD = 64
 EPS = 1e-06
 CHUNKS = 2
+DIRECT = ()
 F32 = jnp.float32
 BF16 = jnp.bfloat16
 NN = (((1,), (0,)), ((), ()))
@@ -31,27 +32,23 @@
     return pltpu.CompilerParams(vmem_limit_bytes=mib << 20)
 
 
-def chosen(kind, local, here, there):
-    return jnp.where(kind == 0, local, jnp.where(kind == 1, here, there))
-
-
 def norm_kernel(groups, rows, at, *refs):
-    nears, fars, (gain, own, other, natural) = refs[:3], refs[3:6], refs[6:]
-    x, y, core, z = at[1], at[2], at[3], at[4]
+    nears, fars, (gain, own, other, inv_out, natural) = refs[:2], refs[2:4], refs[4:]
+    x, y, core = at[1], at[2], at[3]
     width = nears[0].shape[1]
-    near = chosen(at[0], *[r[...] for r in nears]).astype(F32)
-    far = chosen(at[0], *[r[...] for r in fars]).astype(F32)
+    near = jnp.where(at[0] == 1, *[r[...] for r in nears]).astype(F32)
+    far = jnp.where(at[0] == 1, *[r[...] for r in fars]).astype(F32)
     total = jnp.sum(near * near, axis=-1, keepdims=True) + jnp.sum(far * far, axis=-1, keepdims=True)
     inv_rms = lax.rsqrt(total / D + EPS)
+    inv_out[...] = jnp.broadcast_to(inv_rms, inv_out.shape)
     near_at = pl.ds(pl.multiple_of(x * width, width), width)
     far_at = pl.ds(pl.multiple_of((1 - x) * width, width), width)
     natural[:, near_at] = (near * inv_rms * gain[:, near_at]).astype(BF16)
     natural[:, far_at] = (far * inv_rms * gain[:, far_at]).astype(BF16)
-    for slot in range(groups):
-        group = lax.rem(z + slot, groups)
+    for group in range(groups):
         for k in range(2):
             row = 2 * group + (y if k == 0 else 1 - y)
-            put = slice((2 * slot + k) * rows, (2 * slot + k + 1) * rows)
+            put = slice((2 * group + k) * rows, (2 * group + k + 1) * rows)
             for out, half in ((own, core), (other, 1 - core)):
                 got = pl.multiple_of((2 * row + half) * rows, rows)
                 out[:, put] = natural[:, pl.ds(got, rows)]
@@ -70,11 +67,12 @@
         grid_spec=pltpu.PrefetchScalarGridSpec(
             num_scalar_prefetch=1,
             grid=(length // step,),
-            in_specs=[pick(i % 3) for i in range(6)] + [pl.BlockSpec((1, D), lambda i, s: (0, 0))],
-            out_specs=[out, out],
+            in_specs=[pick(1), pick(0), pick(1), pick(0)] + [pl.BlockSpec((1, D), lambda i, s: (0, 0))],
+            out_specs=[out, out, pl.BlockSpec((step, 128), lambda i, s: (i, 0))],
             scratch_shapes=[pltpu.VMEM((step, D), BF16)],
         ),
-        out_shape=[jax.ShapeDtypeStruct((length, D // 2), BF16)] * 2,
+        out_shape=[jax.ShapeDtypeStruct((length, D // 2), BF16)] * 2
+        + [jax.ShapeDtypeStruct((length, 128), F32)],
         compiler_params=params(32),
         cost_estimate=cost(8 * length * D, 8),
         name="norm",
@@ -105,13 +103,13 @@
 
 
 def attend_kernel(at, enc_own, enc_other, w_own, w_other, *refs):
-    qgs, (dec, gkv) = refs[:3], refs[3:]
+    qgs, (dec, gkv) = refs[:2], refs[2:]
     kv = (dot(enc_own[...], w_own[...]) + dot(enc_other[...], w_other[...])).astype(BF16)
     keys = lax.broadcasted_iota(jnp.int32, (1, kv.shape[0]), 1)
-    bias = jnp.where(keys < at[5], 0.0, -1e30).astype(F32)
+    bias = jnp.where(keys < at[4], 0.0, -1e30).astype(F32)
     for head in range(kv.shape[1] // (2 * HEAD)):
         lanes = slice(head * 2 * HEAD, (head + 1) * 2 * HEAD)
-        qg = chosen(at[6], *[r[:, lanes] for r in qgs])
+        qg = jnp.where(at[0] == 1, *[r[:, lanes] for r in qgs])
         dec[:, lanes], gkv[:, lanes] = attend_head(bias, qg, kv[:, lanes])
 
 
@@ -125,14 +123,14 @@
     out = pl.BlockSpec((length, step), lambda i, s: (0, i))
 
     def pick(want):
-        return pl.BlockSpec((length, step), lambda i, s: (0, jnp.where(s[6] == want, first + i, first)))
+        return pl.BlockSpec((length, step), lambda i, s: (0, jnp.where(s[0] == want, first + i, first)))
 
     return pl.pallas_call(
         attend_kernel,
         grid_spec=pltpu.PrefetchScalarGridSpec(
             num_scalar_prefetch=1,
             grid=(cols // step,),
-            in_specs=[enc, enc, weight, weight, pick(0), pick(1), pick(2)],
+            in_specs=[enc, enc, weight, weight, pick(1), pick(0)],
             out_specs=[out, out],
         ),
         out_shape=[jax.ShapeDtypeStruct((length, cols), BF16)] * 2,
@@ -144,45 +142,66 @@
     )(at, enc_own, enc_other, w_own, w_other, *qgs)
 
 
-def weight_grad_kernel(scale, at, enc_a, enc_b, gkv_a, gkv_b, weight, out, gain_term):
+def weight_grad_kernel(scale, at, enc_a, enc_b, gkv_a, gkv_b, out):
     grad = scale * (dot(enc_a[...], gkv_a[...], TN) + dot(enc_b[...], gkv_b[...], TN))
     out[...] = grad.astype(BF16)
-    product = grad * weight[...].astype(F32)
-    lanes = product[:, :128]
-    for i in range(1, product.shape[1] // 128):
-        lanes = lanes + product[:, i * 128 : (i + 1) * 128]
-    gain_term[0] = jnp.sum(lanes.T, axis=0, keepdims=True)
-
-
-def weight_grad(at, enc_a, enc_b, gkv_a, gkv_b, weight, groups, scale):
+
+
+def weight_grad(at, enc_a, enc_b, gkv_a, gkv_b, groups, scale):
     length, half = enc_a.shape
-    cols = weight.shape[1]
+    cols = gkv_a.shape[1]
     step = half // groups
-
-    def slot(i, s):
-        return lax.rem(i + groups - s[4], groups)
-
-    enc = pl.BlockSpec((length, step), lambda i, s: (0, slot(i, s)))
+    enc = pl.BlockSpec((length, step), lambda i, s: (0, i))
     gkv = pl.BlockSpec((length, cols), lambda i, s: (0, 0))
     return pl.pallas_call(
         lambda *refs: weight_grad_kernel(scale, *refs),
         grid_spec=pltpu.PrefetchScalarGridSpec(
             num_scalar_prefetch=1,
             grid=(groups,),
-            in_specs=[enc, enc, gkv, gkv, pl.BlockSpec((step, cols), lambda i, s: (slot(i, s), 0))],
-            out_specs=[
-                pl.BlockSpec((step, cols), lambda i, s: (i, 0)),
-                pl.BlockSpec((1, 1, step), lambda i, s: (i, 0, 0)),
+            in_specs=[enc, enc, gkv, gkv],
+            out_specs=pl.BlockSpec((step, cols), lambda i, s: (i, 0)),
+        ),
+        out_shape=jax.ShapeDtypeStruct((half, cols), BF16),
+        cost_estimate=cost(4 * length * half * cols // 64, 0),
+        compiler_params=params(32),
+        name="weight_grad",
+    )(at, enc_a, enc_b, gkv_a, gkv_b)
+
+
+def collect_kernel(scale, at, *refs):
+    terms, (raw, inv, gain, out, gain_term) = refs[:4], refs[4:]
+    total = terms[0][...].astype(F32)
+    for term in terms[1:]:
+        total = total + term[...].astype(F32)
+    out[...] = (total * gain[...]).astype(BF16)
+    product = total * (raw[...].astype(F32) * inv[:, :1])
+    gain_term[0] = scale * jnp.sum(product, axis=0, keepdims=True)
+
+
+def collect(at, terms, raw, inv_rms, gain, scale):
+    length, width = raw.shape
+    step = 128
+    block = pl.BlockSpec((step, width), lambda i, s: (i, 0))
+    return pl.pallas_call(
+        lambda *refs: collect_kernel(scale, *refs),
+        grid_spec=pltpu.PrefetchScalarGridSpec(
+            num_scalar_prefetch=1,
+            grid=(length // step,),
+            in_specs=[block] * 5
+            + [
+                pl.BlockSpec((step, 128), lambda i, s: (i, 0)),
+                pl.BlockSpec((1, width), lambda i, s: (0, 0)),
             ],
+            out_specs=[block, pl.BlockSpec((1, 1, width), lambda i, s: (i, 0, 0))],
         ),
         out_shape=[
-            jax.ShapeDtypeStruct((half, cols), BF16),
-            jax.ShapeDtypeStruct((groups, 1, step), F32),
+            jax.ShapeDtypeStruct((length, width), BF16),
+            jax.ShapeDtypeStruct((length // step, 1, width), F32),
         ],
+        cost_estimate=cost(8 * length * width, 12),
         compiler_params=params(32),
-        cost_estimate=cost(4 * length * half * cols, 8),
-        name="weight_grad",
-    )(at, enc_a, enc_b, gkv_a, gkv_b, weight)
+        name="collect",
+    )(at, *terms, raw, inv_rms, gain)
 
 
 def enc_grad_kernel(at, gkv_0, gkv_1, own_0, own_1, other_0, other_1, out):
@@ -201,8 +220,7 @@
     def block(i, s):
         target = lax.rem(s[1] + shard, 2)
         group = target * per_shard + i // 2
-        slot = lax.rem(group + groups - s[4], groups)
-        return (2 * slot + lax.rem(i + s[2], 2), 0)
+        return (2 * group + lax.rem(i + s[2], 2), 0)
 
     gkv = pl.BlockSpec((length, cols), lambda i, s: (0, 0))
     weight = pl.BlockSpec((rows, cols), block)
@@ -266,52 +284,34 @@
         return [lax.ppermute(block, "z", turned(groups, -s)) for s in range(1, groups)]
 
     mine = [chunk_of(y, k) for k in range(CHUNKS)]
-    swapped = []
-    for k in range(CHUNKS):
-        sent = chunk_of(1 - y, k)
-        swapped.append(lax.ppermute(after(sent, *swapped), "y", SWAP))
-
-    there = lax.ppermute(packed, PLANE, [(0, 2), (2, 1)])
-    here = lax.ppermute(packed, PLANE, [(2, 3)])
-    nears = [packed, here, there]
+    swap = lax.ppermute(cut(w_kv, 1, 1 - y, half), "y", SWAP)
+    swapped = [swap[:, k * cols : (k + 1) * cols] for k in range(CHUNKS)]
+
+    there = lax.ppermute(after(packed, swap), PLANE, [(0, 2), (2, 1)])
+    here = jnp.where(y == 0, packed, lax.ppermute(packed, PLANE, [(2, 3)]))
+    nears = [here, there]
     fars = []
     for turn in range(1, shards):
         fars.append(
-            [
-                across(packed, turn, [(0, 0)]),
-                across(here, turn, [(3, 3)]),
-                across(there, turn, [(1, 1), (2, 2)]),
-            ]
+            [across(here, turn, [(0, 0), (3, 3)]), across(there, turn, [(1, 1), (2, 2)])]
         )
     gains = [gain] + [lax.ppermute(gain, "mp", turned(shards, t)) for t in range(1, shards)]
 
-    near_slots, far_slots = slots(mine[0]), slots(swapped[0])
-    w_own = [
-        jnp.concatenate(
-            [p for pair in zip([mine[0]] + near_slots, [swapped[0]] + far_slots) for p in pair], 0
-        )
-    ]
-    slot_0, later = {}, {}
-    for k in range(1, CHUNKS):
-        block = after(jnp.concatenate([mine[k], swapped[k]], 0), near_slots[0])
-        slot_0[k], later[k] = block, slots(block)
-    w_other = [lax.ppermute(w_own[0], "phase", SWAP)]
+    blocks = [jnp.concatenate([mine[k], swapped[k]], 0) for k in range(CHUNKS)]
+    w_own, w_other = [], []
 
     position = lax.broadcasted_iota(jnp.int32, (length, width), 0)
     is_grad = lax.broadcasted_iota(jnp.int32, (length, width), 1) % (2 * HEAD) >= HEAD
     masked = jnp.where(is_grad & (position >= tgt_len[0]), jnp.zeros((), BF16), packed)
     qg_near, qg_far = cut(masked, 1, y, half), cut(masked, 1, 1 - y, half)
-    qg_near, qg_far = lax.optimization_barrier((qg_near, qg_far, swapped[0]))[:2]
+    qg_near, qg_far = lax.optimization_barrier((qg_near, qg_far, there))[:2]
     qgs = [
-        qg_near,
-        lax.ppermute(qg_near, PLANE, [(1, 0)]),
+        jnp.where(y == 1, qg_near, lax.ppermute(qg_near, PLANE, [(1, 0)])),
         lax.ppermute(qg_far, PLANE, [(1, 2), (3, 1)]),
     ]
     key_count = jnp.where(straight, src_len, lax.ppermute(src_len, "y", SWAP))
-    enc_kind = jnp.where(straight, y, 2)
-    qg_kind = jnp.where(straight, 1 - y, 2)
     at = jnp.concatenate(
-        [jnp.stack([enc_kind, x, y, core, z]).astype(jnp.int32), key_count, qg_kind[None]]
+        [jnp.stack([straight.astype(jnp.int32), x, y, core]).astype(jnp.int32), key_count]
     )
 
     def natural(parts, axis):
@@ -326,16 +326,17 @@
             axis,
         )
 
-    block_group = (z + jnp.arange(groups)) % groups
+    block_group = jnp.arange(groups)
     block_pair = 2 * block_group[:, None] + jnp.stack([y, 1 - y])[None, :]
     block_order = (2 * block_pair[None] + jnp.stack([core, 1 - core])[:, None, None]).reshape(-1)
     gain_all = natural(gains, 0).astype(F32)
 
     if tiled:
-        gain_row = after(gain_all[None], *swapped)
-        enc_own, enc_other = norm(at, nears, fars[0], gain_row, groups, rows)
+        enc_own, enc_other, inv_rms = norm(
+            at, nears, fars[0], after(gain_all[None], *qgs), groups, rows
+        )
     else:
-        raw = [chosen(enc_kind, *parts) for parts in [nears] + fars]
+        raw = [jnp.where(straight, *parts) for parts in [nears] + fars]
         hidden = natural(raw, 1).astype(F32)
         inv_rms = lax.rsqrt(jnp.sum(hidden * hidden, axis=-1, keepdims=True) / D + EPS)
         encoded = (hidden * inv_rms * gain_all).astype(BF16)
@@ -343,12 +344,22 @@
         enc_own, enc_other = encoded[:, 0], encoded[:, 1]
     enc_mate = lax.ppermute(enc_other, "phase", SWAP)
 
-    decs, gkvs, weight_sums, gain_terms = [], [], [], []
+    decs, gkvs, weight_sums = [], [], []
     for k in range(CHUNKS):
-        if k > 0:
-            slot_0[k] = after(slot_0[k], grad)
-            w_own.append(jnp.concatenate([slot_0[k]] + [after(p, grad) for p in later[k]], 0))
-            w_other.append(lax.ppermute(w_own[k], "phase", SWAP))
+        if k in DIRECT:
+            pieces = [blocks[k]] + slots(after(blocks[k], w_own[0]))
+            pieces = lax.optimization_barrier((*pieces, grad))[:-1]
+            gathered = jnp.zeros((groups * 2 * rows, cols), BF16)
+            for turn, piece in enumerate(pieces):
+                start = (z + turn) % groups * 2 * rows
+                gathered = lax.dynamic_update_slice_in_dim(gathered, piece, start, 0)
+            w_own.append(gathered)
+        else:
+            block = blocks[k] if k == 0 else after(blocks[k], there)
+            w_own.append(lax.all_gather(block, "z", axis=0, tiled=True))
+            if k > 0:
+                w_own[k] = after(w_own[k], grad)
+        w_other.append(lax.ppermute(w_own[k], "phase", SWAP))
         dec, gkv = attend(at, enc_own, enc_other, w_own[k], w_other[k], qgs, k)
         gkvs.append(gkv)
         decs.append(
@@ -357,18 +368,13 @@
                 lax.ppermute(dec, PLANE, [(2, 1), (1, 3)]),
             )
         )
-        gkv_mate = lax.ppermute(gkv, "phase", SWAP)
+        parts = jnp.split(gkv, 2, axis=1)
+        gkv_mate = jnp.concatenate([lax.ppermute(p, "phase", SWAP) for p in parts], 1)
         if tiled:
-            grad, term = weight_grad(
-                at, enc_own, enc_mate, gkv, gkv_mate, w_own[k], groups, pair_scale
-            )
-            term = term.reshape(groups, 2, rows)
+            grad = weight_grad(at, enc_own, enc_mate, gkv, gkv_mate, groups, pair_scale)
         else:
             grad = pair_scale * (dot(enc_own, gkv, TN) + dot(enc_mate, gkv_mate, TN))
-            term = jnp.sum(grad * w_own[k].astype(F32), axis=1).reshape(groups, 2, rows)
-            term = jnp.roll(term, z, 0)
-            grad = jnp.roll(grad.astype(BF16).reshape(groups, -1, cols), z, 0).reshape(-1, cols)
-        gain_terms.append(term)
+            grad = grad.astype(BF16)
         weight_sums.append(lax.psum_scatter(grad, "z", scatter_dimension=0, tiled=True))
 
     if tiled:
@@ -382,20 +388,30 @@
     moved = [across(terms[turn], turn, [(0, 0), (3, 3)]) for turn in range(1, shards)]
     moved += [across(terms[turn], turn, [(2, 0), (1, 3)]) for turn in range(shards)]
 
-    term = sum(gain_terms)
-    term = jnp.where(y == 0, term, term[:, ::-1])
-    by_core = jnp.stack([jnp.where(core == 0, term, 0.0), jnp.where(core == 1, term, 0.0)], axis=2)
-    gain_sums = lax.psum(by_core.reshape(D), ("z", "y", "phase", "mp"))
-    d_gain = cut(gain_sums, 0, x, width) / gain.astype(F32)
-
     kept = jnp.concatenate([w[:rows] for w in weight_sums], 1)
     got = [lax.ppermute(w[rows:], "y", SWAP) for w in weight_sums]
-    terms[0] = after(terms[0], gain_sums, got[0])
-    grad_enc = terms[0].astype(F32)
-    for part in moved:
-        grad_enc = grad_enc + part.astype(F32)
-    grad_normed = (grad_enc * gain.astype(F32)).astype(BF16)
+    if tiled:
+        terms[0] = after(terms[0], got[0])
+        grad_normed, gain_term = collect(
+            at, [terms[0]] + moved, here, inv_rms, gain.astype(F32)[None], pair_scale
+        )
+        gain_term = jnp.sum(gain_term, axis=(0, 1))
+    else:
+        grad_enc = terms[0].astype(F32)
+        for part in moved:
+            grad_enc = grad_enc + part.astype(F32)
+        grad_normed = (grad_enc * gain.astype(F32)).astype(BF16)
+        normed = raw[0].astype(F32) * inv_rms
+        gain_term = pair_scale * jnp.sum(grad_enc * normed, axis=0)
     enc_grads = jnp.where(y == 0, grad_normed, lax.ppermute(grad_normed, PLANE, [(3, 2)]))
+
+    gain_term = jnp.where(straight, gain_term, 0.0)
+    gain_term = gain_term + lax.ppermute(gain_term, PLANE, [(0, 3), (3, 0), (1, 2), (2, 1)])
+    turn = 1
+    while turn < groups:
+        gain_term = gain_term + lax.ppermute(gain_term, "z", [(i, i ^ turn) for i in range(groups)])
+        turn *= 2
+    d_gain = jnp.where(straight, gain_term, lax.ppermute(gain_term, "phase", SWAP))
     got = jnp.concatenate(got, 1)
     d_wkv = ordered(y == 0, kept, got, 1).astype(F32)
 

time: 383 us -> 273 us (0.71)
  blocking collectives: 88.8 us -> 0 us
  starting transfers between devices: 75.3 us -> 52.5 us
  local copies, waits for them, and re-layouts: 21 us -> 30.3 us
  waiting for transfers between devices: 102 us -> 97.5 us
    psum x1 -> x0, blocking collectives: 88.8 us -> none  [on_device(): gain_sums = lax.psum(by_core.reshape(D), ('z', 'y', 'phase', 'mp'))]
    ppermute x16 -> x11, waiting for transfers between devices: 89 us -> 28.9 us  [the longest x1 12.3 us: on_device(): there = lax.ppermute(after(packed, swap), PLANE, [(0, 2), (2, 1)])]
    ppermute x16 -> x11, starting transfers between devices: 41 us -> 11.4 us  [the longest x1 5.05 us: on_device(): there = lax.ppermute(after(packed, swap), PLANE, [(0, 2), (2, 1)])]
    ppermute x6 -> x5, waiting for transfers between devices: 0.02 us -> 26.5 us  [across(): lax.ppermute(value, ('y', 'phase', 'mp'), [(a * shards + s, b * shards +...]
    ppermute x2, waiting for transfers between devices: 4.67 us -> 19.5 us  [on_device(): got = [lax.ppermute(w[rows:], 'y', SWAP) for w in weight_sums]]
    all_gather x0 -> x2, waiting for transfers between devices: none -> 10.7 us  [on_device(): w_own.append(lax.all_gather(block, 'z', axis=0, tiled=True))]
    ppermute x1 -> x2, starting transfers between devices: 0.07 us -> 9.04 us  [on_device(): w_other.append(lax.ppermute(w_own[k], 'phase', SWAP))]
    unnamed x49 -> x58, local copies, waits for them, and re-layouts: 16 us -> 22.9 us
  transfers between devices with their start and end apart: 37 -> 34, of which waited for: 11 -> 16; matrix products, arithmetic and copies ran while one was open for 9% -> 8% of each run, Pallas kernels for 15% -> 22%
where the time goes in v4:
time: 273 us; the launch traced here: 272 us
  waiting for transfers between devices  97.5 us (36%)
  Pallas kernels  58.4 us (21%)
  starting transfers between devices  52.5 us (19%)
  local copies, waits for them, and re-layouts  30.3 us (11%)
  other arithmetic  16.8 us (6%)
  between operations  16.1 us (6%)
    pallas_call x2, Pallas kernels, attend(): pl.pallas_call(attend_kernel, grid_spec=pltpu.PrefetchScalarGridSpec(num_...  27 us
    ppermute x5, waiting for transfers between devices, across(): lax.ppermute(value, ('y', 'phase', 'mp'), [(a * shards + s, b * shards +...  26.5 us
    unnamed x58, local copies, waits for them, and re-layouts  22.9 us
    ppermute x2, waiting for transfers between devices, on_device(): got = [lax.ppermute(w[rows:], 'y', SWAP) for w in weight_sums]  19.5 us
    ppermute x1, waiting for transfers between devices, on_device(): there = lax.ppermute(after(packed, swap), PLANE, [(0, 2), (2, 1)])  12.3 us
    pallas_call x2, Pallas kernels, enc_grad(): pl.pallas_call(enc_grad_kernel, grid_spec=pltpu.PrefetchScalarGridSpec(nu...  11.6 us
    ppermute x5, starting transfers between devices, across(): lax.ppermute(value, ('y', 'phase', 'mp'), [(a * shards + s, b * shards +...  11.2 us
    all_gather x2, waiting for transfers between devices, on_device(): w_own.append(lax.all_gather(block, 'z', axis=0, tiled=True))  10.7 us
  transfers between devices with their start and end apart: 34, of which 16 were waited for; matrix products, arithmetic and copies ran while one was open for 8% of the time, Pallas kernels for 22%

profile of v4, /device:TPU:0, one launch (start us, length us, event | category | flops | bytes accessed | tf_op | source)
XLA Modules:
  0.0 271.5 jit_solution(5494402682768344279)
XLA Ops:
  8.3 3.0 %collective-permute-start.2 = (bf16[256,1024]{1,0:T(8,128)(2,1)S(1)}, bf16[256,1024]{1,0:T(8,128)(2,1)S(1)}, u32[]{:S(2)}, u32[]{:S(2)}) collective-permute-start(bf16[256,1024]{1,0:T(8,128)(2,1)S(1)} %constant_dynamic-slice_fusion.4), channel_id=1, source_target_pairs={{0,4},{4,0},{1,5},{5,1},{2,6},{6,2},{3,7},{7,3},{8,12},{12,8},{9,1... | collective-permute-start | bytes 1572872 | tf_op jit(solution)/shard_map/ppermute | solution.py:287
  13.2 10.1 %collective-permute-done.2 = bf16[256,1024]{1,0:T(8,128)(2,1)S(1)} collective-permute-done((bf16[256,1024]{1,0:T(8,128)(2,1)S(1)}, bf16[256,1024]{1,0:T(8,128)(2,1)S(1)}, u32[]{:S(2)}, u32[]{:S(2)}) %collective-permute-start.2) | collective-permute-done | bytes 524320 | tf_op jit(solution)/shard_map/ppermute | solution.py:287
  23.3 5.1 %collective-permute-start.3 = (bf16[512,2048]{1,0:T(8,128)(2,1)}, bf16[512,2048]{1,0:T(8,128)(2,1)}, u32[]{:S(2)}, u32[]{:S(2)}) collective-permute-start(bf16[512,2048]{1,0:T(8,128)(2,1)} %bitcast.4), channel_id=1, source_target_pairs={{0,4},{4,2},{1,5},{5,3},{8,12},{12,10},{9,13},{13,11},{16,20},{20,... | collective-permute-start | bytes 6291464 | tf_op jit(solution)/shard_map/ppermute | solution.py:290
  32.0 3.0 %fusion.1 = (bf16[512,2048]{1,0:T(8,128)(2,1)S(1)}, bf16[512,2048]{1,0:T(8,128)(2,1)S(1)}) fusion(s32[2048]{0:T(1024)S(1)} %get-tuple-element.51, s32[2048]{0:T(1024)S(1)} %get-tuple-element.52, pred[512]{0:T(512)(128)(4,1)S(1)} %iota_compare_fusion, pred[2048]{0:T(1024)(128)(4,1)S(1)} %fusion.9, bf16[1,1,512,2048]{3,2,1,0:T(8,128)(2,1)} %param.5, ...), kind=kLoop, calls=%fused_computation.2 | loop fusion | flops 5242880 | bytes 8407553 | tf_op jit(solution)/shard_map/jit(_where)/select_n | solution.py:305
  35.0 3.4 %collective-permute-start.4 = (bf16[512,2048]{1,0:T(8,128)(2,1)S(1)}, bf16[512,2048]{1,0:T(8,128)(2,1)}, u32[]{:S(2)}, u32[]{:S(2)}) collective-permute-start(bf16[512,2048]{1,0:T(8,128)(2,1)S(1)} %get-tuple-element.38.refs_1_.refs_5_), channel_id=1, source_target_pairs={{0,1},{1,0},{6,7},{7,6},{8,9},{9,8},{14,15},{15,14},{16,17},{17,16... | collective-permute-start | bytes 6291464 | tf_op jit(solution)/shard_map/ppermute | solution.py:274
  38.4 12.3 %collective-permute-done.3.refs_2_ = bf16[512,2048]{1,0:T(8,128)(2,1)} collective-permute-done((bf16[512,2048]{1,0:T(8,128)(2,1)}, bf16[512,2048]{1,0:T(8,128)(2,1)}, u32[]{:S(2)}, u32[]{:S(2)}) %collective-permute-start.3) | collective-permute-done | bytes 2097184 | tf_op jit(solution)/shard_map/ppermute | solution.py:290
  50.8 2.0 collective-permute-start.5
  57.2 4.8 %collective-permute-start = (s32[1]{0:T(128)}, s32[1]{0:T(128)}, u32[]{:S(2)}, u32[]{:S(2)}) collective-permute-start(s32[1]{0:T(128)} %param.8), channel_id=1, source_target_pairs={{0,4},{4,0},{1,5},{5,1},{2,6},{6,2},{3,7},{7,3},{8,12},{12,8},{9,1... | collective-permute-start | bytes 20 | tf_op jit(solution)/shard_map/ppermute | solution.py:312
  64.4 5.5 %collective-permute-done.6 = bf16[2048]{0:T(1024)(128)(2,1)S(1)} collective-permute-done((bf16[2048]{0:T(1024)(128)(2,1)S(1)}, bf16[2048]{0:T(1024)(128)(2,1)S(1)}, u32[]{:S(2)}, u32[]{:S(2)}) %collective-permute-start.6) | collective-permute-done | bytes 4128 | tf_op jit(solution)/shard_map/ppermute | solution.py:298
  69.9 6.4 %all-gather.3.cloned.1.call-done.w_own.own_0 = bf16[2048,512]{1,0:T(8,128)(2,1)} async-done(((bf16[512,512]{1,0:T(8,128)(2,1)}), bf16[2048,512]{1,0:T(8,128)(2,1)}) %all-gather.3.cloned.1.call-update) | async-done | bytes 2097168 | tf_op jit(solution)/shard_map/all_gather | solution.py:359
  76.3 9.0 %collective-permute-start.9 = (bf16[2048,512]{1,0:T(8,128)(2,1)}, bf16[2048,512]{1,0:T(8,128)(2,1)}, u32[]{:S(2)}, u32[]{:S(2)}) collective-permute-start(bf16[2048,512]{1,0:T(8,128)(2,1)} %all-gather.3.cloned.1.call-done.w_own.own_0), channel_id=1, source_target_pairs={{0,2},{2,0},{1,3},{3,1},{4,6},{6,4},{5,7},{7,5},{8,10},{10,8},{9,1... | collective-permute-start | bytes 6291464 | tf_op jit(solution)/shard_map/ppermute | solution.py:362
  89.2 5.2 %norm.1 = (bf16[512,2048]{1,0:T(8,128)(2,1)S(1)}, bf16[512,2048]{1,0:T(8,128)(2,1)S(1)}, f32[512,128]{1,0:T(8,128)S(1)}) custom-call(s32[5]{0:T(128)S(1)} %concatenate.59.refs_0_.at, bf16[512,2048]{1,0:T(8,128)(2,1)S(1)} %get-tuple-element.38.refs_1_.refs_5_, bf16[512,2048]{1,0:T(8,128)(2,1)} %collective-permute-done.3.refs_2_, ...), custom_call_target="tpu_custom_call" | custom-call | flops 16777216 | bytes 8388608 | tf_op jit(solution)/shard_map/norm/pallas_call | solution.py:65
  95.8 13.5 %attend.2 = (bf16[512,512]{1,0:T(8,128)(2,1)S(1)}, bf16[512,512]{1,0:T(8,128)(2,1)S(1)}) custom-call(s32[5]{0:T(128)S(1)} %concatenate.59.refs_0_.at, bf16[512,2048]{1,0:T(8,128)(2,1)S(1)} %get-tuple-element.23.enc_own.refs_1_, bf16[512,2048]{1,0:T(8,128)(2,1)} %copy-done.16, bf16[2048,512]{1,0:T(8,128)(2,1)} %all-gather.3.cloned.1.call-done.w_own.own_0, ...), custom_call_target="tpu_custom_call" | custom-call | flops 4026531840 | bytes 8388608 | tf_op jit(solution)/shard_map/attend/pallas_call | solution.py:128
  111.4 3.9 %weight_grad.2 = bf16[2048,512]{1,0:T(8,128)(2,1)S(1)} custom-call(s32[5]{0:T(128)S(1)} %concatenate.59.refs_0_.at, bf16[512,2048]{1,0:T(8,128)(2,1)S(1)} %get-tuple-element.23.enc_own.refs_1_, bf16[512,2048]{1,0:T(8,128)(2,1)S(1)} %collective-permute-done.10.refs_2_, bf16[512,512]{1,0:T(8,128)(2,1)S(1)} %get-tuple-element.25.refs_3_.gkv_0, ...), custom_call_target="tpu_custom_call" | custom-call | flops 33554432 | tf_op jit(solution)/shard_map/weight_grad/pallas_call | solution.py:156
  118.3 4.3 %all-gather.5.cloned.1.call-done.w_own.own_1 = bf16[2048,512]{1,0:T(8,128)(2,1)} async-done(((bf16[512,512]{1,0:T(8,128)(2,1)}), bf16[2048,512]{1,0:T(8,128)(2,1)}) %all-gather.5.cloned.1.call-update) | async-done | bytes 2097168 | tf_op jit(solution)/shard_map/all_gather | solution.py:359
  122.6 4.4 %collective-permute-done.13.w_other.other_1 = bf16[2048,512]{1,0:T(8,128)(2,1)S(1)} collective-permute-done((bf16[2048,512]{1,0:T(8,128)(2,1)}, bf16[2048,512]{1,0:T(8,128)(2,1)S(1)}, u32[]{:S(2)}, u32[]{:S(2)}) %collective-permute-start.13) | collective-permute-done | bytes 2097184 | tf_op jit(solution)/shard_map/ppermute | solution.py:362
  132.6 13.5 %attend.3 = (bf16[512,512]{1,0:T(8,128)(2,1)S(1)}, bf16[512,512]{1,0:T(8,128)(2,1)S(1)}) custom-call(s32[5]{0:T(128)S(1)} %concatenate.59.refs_0_.at, bf16[512,2048]{1,0:T(8,128)(2,1)S(1)} %copy-done.3, bf16[512,2048]{1,0:T(8,128)(2,1)} %copy-done.16, bf16[2048,512]{1,0:T(8,128)(2,1)} %all-gather.5.cloned.1.call-done.w_own.own_1, ...), custom_call_target="tpu_custom_call" | custom-call | flops 4026531840 | bytes 8388608 | tf_op jit(solution)/shard_map/attend/pallas_call | solution.py:128
  151.6 5.8 %enc_grad.2.refs_1_ = bf16[512,2048]{1,0:T(8,128)(2,1)} custom-call(s32[5]{0:T(128)S(1)} %concatenate.59.refs_0_.at, bf16[512,512]{1,0:T(8,128)(2,1)S(1)} %get-tuple-element.25.refs_3_.gkv_0, bf16[512,512]{1,0:T(8,128)(2,1)S(1)} %get-tuple-element.28.gkv_1.refs_3_, bf16[2048,512]{1,0:T(8,128)(2,1)S(1)} %copy-done.12, bf16[2048,512]{1,0:T(8,128)(2,1)S(1)} %copy-done.14, ...), custom_call_target="tpu_custom_call" | custom-call | flops 4294967296 | bytes 8388608 | tf_op jit(solution)/shard_map/enc_grad/pallas_call | solution.py:227
  158.8 3.9 %weight_grad.3 = bf16[2048,512]{1,0:T(8,128)(2,1)S(1)} custom-call(s32[5]{0:T(128)S(1)} %concatenate.59.refs_0_.at, bf16[512,2048]{1,0:T(8,128)(2,1)S(1)} %copy-done.3, bf16[512,2048]{1,0:T(8,128)(2,1)S(1)} %copy-done.5, bf16[512,512]{1,0:T(8,128)(2,1)S(1)} %get-tuple-element.28.gkv_1.refs_3_, bf16[512,512]{1,0:T(8,128)(2,1)S(1)} %pad_maximum_fusion.3.refs_4_), custom_call_target="tpu_custom_call" | custom-call | flops 33554432 | tf_op jit(solution)/shard_map/weight_grad/pallas_call | solution.py:156
  168.9 5.8 %enc_grad.3 = bf16[512,2048]{1,0:T(8,128)(2,1)} custom-call(s32[5]{0:T(128)S(1)} %concatenate.59.refs_0_.at, bf16[512,512]{1,0:T(8,128)(2,1)S(1)} %get-tuple-element.25.refs_3_.gkv_0, bf16[512,512]{1,0:T(8,128)(2,1)S(1)} %get-tuple-element.28.gkv_1.refs_3_, bf16[2048,512]{1,0:T(8,128)(2,1)S(1)} %copy-done.13, bf16[2048,512]{1,0:T(8,128)(2,1)S(1)} %copy-done.15, ...), custom_call_target="tpu_custom_call" | custom-call | flops 4294967296 | bytes 8388608 | tf_op jit(solution)/shard_map/enc_grad/pallas_call | solution.py:227
  175.9 3.2 %collective-permute-start.15 = (bf16[512,2048]{1,0:T(8,128)(2,1)}, bf16[512,2048]{1,0:T(8,128)(2,1)}, u32[]{:S(2)}, u32[]{:S(2)}) collective-permute-start(bf16[512,2048]{1,0:T(8,128)(2,1)} %enc_grad.3), channel_id=1, source_target_pairs={{0,1},{1,0},{6,7},{7,6},{8,9},{9,8},{14,15},{15,14},{16,17},{17,16... | collective-permute-start | bytes 6291464 | tf_op jit(solution)/shard_map/ppermute | solution.py:274
  181.0 4.0 %collective-permute-start.14 = (bf16[256,512]{1,0:T(8,128)(2,1)S(1)}, bf16[256,512]{1,0:T(8,128)(2,1)S(1)}, u32[]{:S(2)}, u32[]{:S(2)}) collective-permute-start(bf16[256,512]{1,0:T(8,128)(2,1)S(1)} %get-tuple-element.42), channel_id=1, source_target_pairs={{0,4},{4,0},{1,5},{5,1},{2,6},{6,2},{3,7},{7,3},{8,12},{12,8},{9,1... | collective-permute-start | bytes 786440 | tf_op jit(solution)/shard_map/ppermute | solution.py:392
  185.0 15.0 %collective-permute-done.14 = bf16[256,512]{1,0:T(8,128)(2,1)S(1)} collective-permute-done((bf16[256,512]{1,0:T(8,128)(2,1)S(1)}, bf16[256,512]{1,0:T(8,128)(2,1)S(1)}, u32[]{:S(2)}, u32[]{:S(2)}) %collective-permute-start.14) | collective-permute-done | bytes 262176 | tf_op jit(solution)/shard_map/ppermute | solution.py:392
  200.0 26.4 %collective-permute-done.17.refs_4_ = bf16[512,2048]{1,0:T(8,128)(2,1)} collective-permute-done((bf16[512,2048]{1,0:T(8,128)(2,1)}, bf16[512,2048]{1,0:T(8,128)(2,1)}, u32[]{:S(2)}, u32[]{:S(2)}) %collective-permute-start.17) | collective-permute-done | bytes 2097184 | tf_op jit(solution)/shard_map/ppermute | solution.py:274
  226.5 6.8 %collect.1 = (bf16[512,2048]{1,0:T(8,128)(2,1)}, f32[4,1,2048]{2,1,0:T(1,128)S(1)}) custom-call(s32[5]{0:T(128)S(1)} %concatenate.59.refs_0_.at, bf16[512,2048]{1,0:T(8,128)(2,1)} %enc_grad.2.refs_1_, bf16[512,2048]{1,0:T(8,128)(2,1)} %collective-permute-done.15.refs_2_, bf16[512,2048]{1,0:T(8,128)(2,1)} %collective-permute-done.16.refs_3_, ...), custom_call_target="tpu_custom_call" | custom-call | flops 8388608 | bytes 12582912 | tf_op jit(solution)/shard_map/collect/pallas_call | solution.py:185
  234.1 2.1 collective-permute-start.19
  236.3 2.1 collective-permute-start.20
  238.6 2.9 %collective-permute-done.26 = f32[2048]{0:T(1024)S(1)} collective-permute-done((f32[2048]{0:T(1024)S(1)}, f32[2048]{0:T(1024)S(1)}, u32[]{:S(2)}, u32[]{:S(2)}) %collective-permute-start.26) | collective-permute-done | bytes 8224 | tf_op jit(solution)/shard_map/ppermute | solution.py:409
  243.1 2.1 collective-permute-done.27
  249.8 1.9 broadcast_select_fusion.2
  254.4 4.5 %fusion.3 = bf16[1,1,512,2048]{3,2,1,0:T(8,128)(2,1)} fusion(bf16[512,512]{1,0:T(8,128)(2,1)} %collective-permute-done.22, bf16[512,512]{1,0:T(8,128)(2,1)} %collective-permute-done.21, bf16[512,512]{1,0:T(8,128)(2,1)} %broadcast_select_fusion.2, bf16[512,512]{1,0:T(8,128)(2,1)} %broadcast_select_fusion.3, bf16[512,2048]{1,0:T(8,128)(2,1)} %get-tuple-element.31, ...), kind=kLoop, calls=%fused_computation.5 | loop fusion | flops 19922944 | bytes 8388610 | tf_op jit(solution)/shard_map/broadcast_in_dim | solution.py:421
  258.9 4.5 %collective-permute-done.25 = bf16[256,512]{1,0:T(8,128)(2,1)S(1)} collective-permute-done((bf16[256,512]{1,0:T(8,128)(2,1)S(1)}, bf16[256,512]{1,0:T(8,128)(2,1)S(1)}, u32[]{:S(2)}, u32[]{:S(2)}) %collective-permute-start.25) | collective-permute-done | bytes 262176 | tf_op jit(solution)/shard_map/ppermute | solution.py:392
  (138 shorter events, 54.8 us)
Async XLA Ops:
  7.2 69.2 %all-gather.3.cloned.1.call-start = ((), (), s32[]{:S(2)}) async-start(), calls=%async_computation.2 | async-start | bytes 2621440 | tf_op jit(solution)/shard_map/all_gather | solution.py:359
  8.3 15.0 %collective-permute-start.2 = (bf16[256,1024]{1,0:T(8,128)(2,1)S(1)}, bf16[256,1024]{1,0:T(8,128)(2,1)S(1)}, u32[]{:S(2)}, u32[]{:S(2)}) collective-permute-start(bf16[256,1024]{1,0:T(8,128)(2,1)S(1)} %constant_dynamic-slice_fusion.4), channel_id=1, source_target_pairs={{0,4},{4,0},{1,5},{5,1},{2,6},{6,2},{3,7},{7,3},{8,12},{12,8},{9,1... | collective-permute-start | bytes 1572872 | tf_op jit(solution)/shard_map/ppermute | solution.py:287
  11.3 19.4 %collective-permute-start.1 = (bf16[512,2048]{1,0:T(8,128)(2,1)}, bf16[512,2048]{1,0:T(8,128)(2,1)S(1)}, u32[]{:S(2)}, u32[]{:S(2)}) collective-permute-start(bf16[512,2048]{1,0:T(8,128)(2,1)} %bitcast.4), channel_id=1, source_target_pairs={{4,6},{5,7},{12,14},{13,15},{20,22},{21,23},{28,30},{29,31}} | collective-permute-start | bytes 6291464 | tf_op jit(solution)/shard_map/ppermute | solution.py:291
  23.3 27.5 %collective-permute-start.3 = (bf16[512,2048]{1,0:T(8,128)(2,1)}, bf16[512,2048]{1,0:T(8,128)(2,1)}, u32[]{:S(2)}, u32[]{:S(2)}) collective-permute-start(bf16[512,2048]{1,0:T(8,128)(2,1)} %bitcast.4), channel_id=1, source_target_pairs={{0,4},{4,2},{1,5},{5,3},{8,12},{12,10},{9,13},{13,11},{16,20},{20,... | collective-permute-start | bytes 6291464 | tf_op jit(solution)/shard_map/ppermute | solution.py:290
  30.0 92.6 %all-gather.5.cloned.1.call-start = ((), (), s32[]{:S(2)}) async-start(), calls=%async_computation.3 | async-start | bytes 2621440 | tf_op jit(solution)/shard_map/all_gather | solution.py:359
  35.0 54.2 %collective-permute-start.4 = (bf16[512,2048]{1,0:T(8,128)(2,1)S(1)}, bf16[512,2048]{1,0:T(8,128)(2,1)}, u32[]{:S(2)}, u32[]{:S(2)}) collective-permute-start(bf16[512,2048]{1,0:T(8,128)(2,1)S(1)} %get-tuple-element.38.refs_1_.refs_5_), channel_id=1, source_target_pairs={{0,1},{1,0},{6,7},{7,6},{8,9},{9,8},{14,15},{15,14},{16,17},{17,16... | collective-permute-start | bytes 6291464 | tf_op jit(solution)/shard_map/ppermute | solution.py:274
  50.8 38.5 %collective-permute-start.5 = (bf16[512,2048]{1,0:T(8,128)(2,1)}, bf16[512,2048]{1,0:T(8,128)(2,1)}, u32[]{:S(2)}, u32[]{:S(2)}) collective-permute-start(bf16[512,2048]{1,0:T(8,128)(2,1)} %collective-permute-done.3.refs_2_), channel_id=1, source_target_pairs={{2,3},{3,2},{4,5},{5,4},{10,11},{11,10},{12,13},{13,12},{18,19},{1... | collective-permute-start | bytes 6291464 | tf_op jit(solution)/shard_map/ppermute | solution.py:274
  54.3 32.5 %collective-permute-start.7 = (bf16[512,1024]{1,0:T(8,128)(2,1)}, bf16[512,1024]{1,0:T(8,128)(2,1)}, u32[]{:S(2)}, u32[]{:S(2)}) collective-permute-start(bf16[512,1024]{1,0:T(8,128)(2,1)} %get-tuple-element.20), channel_id=1, source_target_pairs={{2,0},{3,1},{10,8},{11,9},{18,16},{19,17},{26,24},{27,25}} | collective-permute-start | bytes 3145736 | tf_op jit(solution)/shard_map/ppermute | solution.py:309
  55.6 32.6 %collective-permute-start.8 = (bf16[512,1024]{1,0:T(8,128)(2,1)}, bf16[512,1024]{1,0:T(8,128)(2,1)S(1)}, u32[]{:S(2)}, u32[]{:S(2)}) collective-permute-start(bf16[512,1024]{1,0:T(8,128)(2,1)} %get-tuple-element.21), channel_id=1, source_target_pairs={{2,4},{6,2},{3,5},{7,3},{10,12},{14,10},{11,13},{15,11},{18,20},{2... | collective-permute-start | bytes 3145736 | tf_op jit(solution)/shard_map/ppermute | solution.py:310
  57.2 122.0 %reduce-scatter.3.cloned.1.call-start = ((), (), s32[]{:S(2)}) async-start(), calls=%async_computation.4 | async-start | bytes 2621440 | tf_op jit(solution)/shard_map/reduce_scatter | solution.py:378
  57.2 6.6 %collective-permute-start = (s32[1]{0:T(128)}, s32[1]{0:T(128)}, u32[]{:S(2)}, u32[]{:S(2)}) collective-permute-start(s32[1]{0:T(128)} %param.8), channel_id=1, source_target_pairs={{0,4},{4,0},{1,5},{5,1},{2,6},{6,2},{3,7},{7,3},{8,12},{12,8},{9,1... | collective-permute-start | bytes 20 | tf_op jit(solution)/shard_map/ppermute | solution.py:312
  63.8 6.1 %collective-permute-start.6 = (bf16[2048]{0:T(1024)(128)(2,1)S(1)}, bf16[2048]{0:T(1024)(128)(2,1)S(1)}, u32[]{:S(2)}, u32[]{:S(2)}) collective-permute-start(bf16[2048]{0:T(1024)(128)(2,1)S(1)} %copy-done.28), channel_id=1, source_target_pairs={{0,1},{1,0},{2,3},{3,2},{4,5},{5,4},{6,7},{7,6},{8,9},{9,8},{10,11... | collective-permute-start | bytes 12296 | tf_op jit(solution)/shard_map/ppermute | solution.py:298
  76.3 18.4 %collective-permute-start.9 = (bf16[2048,512]{1,0:T(8,128)(2,1)}, bf16[2048,512]{1,0:T(8,128)(2,1)}, u32[]{:S(2)}, u32[]{:S(2)}) collective-permute-start(bf16[2048,512]{1,0:T(8,128)(2,1)} %all-gather.3.cloned.1.call-done.w_own.own_0), channel_id=1, source_target_pairs={{0,2},{2,0},{1,3},{3,1},{4,6},{6,4},{5,7},{7,5},{8,10},{10,8},{9,1... | collective-permute-start | bytes 6291464 | tf_op jit(solution)/shard_map/ppermute | solution.py:362
  94.5 16.9 %collective-permute-start.10 = (bf16[512,2048]{1,0:T(8,128)(2,1)S(1)}, bf16[512,2048]{1,0:T(8,128)(2,1)S(1)}, u32[]{:S(2)}, u32[]{:S(2)}) collective-permute-start(bf16[512,2048]{1,0:T(8,128)(2,1)S(1)} %get-tuple-element.24.enc_other), channel_id=1, source_target_pairs={{0,2},{2,0},{1,3},{3,1},{4,6},{6,4},{5,7},{7,5},{8,10},{10,8},{9,1... | collective-permute-start | bytes 6291464 | tf_op jit(solution)/shard_map/ppermute | solution.py:345
  118.1 134.2 %reduce-scatter.5.cloned.1.call-start = ((), (), s32[]{:S(2)}) async-start(), calls=%async_computation.5 | async-start | bytes 2621440 | tf_op jit(solution)/shard_map/reduce_scatter | solution.py:378
  122.6 4.4 %collective-permute-start.13 = (bf16[2048,512]{1,0:T(8,128)(2,1)}, bf16[2048,512]{1,0:T(8,128)(2,1)S(1)}, u32[]{:S(2)}, u32[]{:S(2)}) collective-permute-start(bf16[2048,512]{1,0:T(8,128)(2,1)} %all-gather.5.cloned.1.call-done.w_own.own_1), channel_id=1, source_target_pairs={{0,2},{2,0},{1,3},{3,1},{4,6},{6,4},{5,7},{7,5},{8,10},{10,8},{9,1... | collective-permute-start | bytes 6291464 | tf_op jit(solution)/shard_map/ppermute | solution.py:362
  146.2 12.5 %collective-permute-start.23 = (bf16[512,256]{1,0:T(8,128)(2,1)S(1)}, bf16[512,256]{1,0:T(8,128)(2,1)S(1)}, u32[]{:S(2)}, u32[]{:S(2)}) collective-permute-start(bf16[512,256]{1,0:T(8,128)(2,1)S(1)} %get-tuple-element.45), channel_id=1, source_target_pairs={{0,2},{2,0},{1,3},{3,1},{4,6},{6,4},{5,7},{7,5},{8,10},{10,8},{9,1... | collective-permute-start | bytes 786440 | tf_op jit(solution)/shard_map/ppermute | solution.py:372
  146.2 12.5 %collective-permute-start.24 = (bf16[512,256]{1,0:T(8,128)(2,1)S(1)}, bf16[512,256]{1,0:T(8,128)(2,1)S(1)}, u32[]{:S(2)}, u32[]{:S(2)}) collective-permute-start(bf16[512,256]{1,0:T(8,128)(2,1)S(1)} %get-tuple-element.46), channel_id=1, source_target_pairs={{0,2},{2,0},{1,3},{3,1},{4,6},{6,4},{5,7},{7,5},{8,10},{10,8},{9,1... | collective-permute-start | bytes 786440 | tf_op jit(solution)/shard_map/ppermute | solution.py:372
  157.4 42.6 %collective-permute-start.16 = (bf16[512,2048]{1,0:T(8,128)(2,1)}, bf16[512,2048]{1,0:T(8,128)(2,1)}, u32[]{:S(2)}, u32[]{:S(2)}) collective-permute-start(bf16[512,2048]{1,0:T(8,128)(2,1)} %enc_grad.2.refs_1_), channel_id=1, source_target_pairs={{4,0},{5,1},{2,6},{3,7},{12,8},{13,9},{10,14},{11,15},{20,16},{21,... | collective-permute-start | bytes 6291464 | tf_op jit(solution)/shard_map/ppermute | solution.py:274
  174.7 51.8 %collective-permute-start.17 = (bf16[512,2048]{1,0:T(8,128)(2,1)}, bf16[512,2048]{1,0:T(8,128)(2,1)}, u32[]{:S(2)}, u32[]{:S(2)}) collective-permute-start(bf16[512,2048]{1,0:T(8,128)(2,1)} %enc_grad.3), channel_id=1, source_target_pairs={{4,1},{5,0},{2,7},{3,6},{12,9},{13,8},{10,15},{11,14},{20,17},{21,... | collective-permute-start | bytes 6291464 | tf_op jit(solution)/shard_map/ppermute | solution.py:274
  175.9 50.6 %collective-permute-start.15 = (bf16[512,2048]{1,0:T(8,128)(2,1)}, bf16[512,2048]{1,0:T(8,128)(2,1)}, u32[]{:S(2)}, u32[]{:S(2)}) collective-permute-start(bf16[512,2048]{1,0:T(8,128)(2,1)} %enc_grad.3), channel_id=1, source_target_pairs={{0,1},{1,0},{6,7},{7,6},{8,9},{9,8},{14,15},{15,14},{16,17},{17,16... | collective-permute-start | bytes 6291464 | tf_op jit(solution)/shard_map/ppermute | solution.py:274
  181.0 19.0 %collective-permute-start.14 = (bf16[256,512]{1,0:T(8,128)(2,1)S(1)}, bf16[256,512]{1,0:T(8,128)(2,1)S(1)}, u32[]{:S(2)}, u32[]{:S(2)}) collective-permute-start(bf16[256,512]{1,0:T(8,128)(2,1)S(1)} %get-tuple-element.42), channel_id=1, source_target_pairs={{0,4},{4,0},{1,5},{5,1},{2,6},{6,2},{3,7},{7,3},{8,12},{12,8},{9,1... | collective-permute-start | bytes 786440 | tf_op jit(solution)/shard_map/ppermute | solution.py:392
  233.3 21.0 %collective-permute-start.18 = (bf16[512,2048]{1,0:T(8,128)(2,1)}, bf16[512,2048]{1,0:T(8,128)(2,1)S(1)}, u32[]{:S(2)}, u32[]{:S(2)}) collective-permute-start(bf16[512,2048]{1,0:T(8,128)(2,1)} %get-tuple-element.31), channel_id=1, source_target_pairs={{6,4},{7,5},{14,12},{15,13},{22,20},{23,21},{30,28},{31,29}} | collective-permute-start | bytes 6291464 | tf_op jit(solution)/shard_map/ppermute | solution.py:406
  234.1 12.2 %collective-permute-start.19 = (bf16[512,512]{1,0:T(8,128)(2,1)S(1)}, bf16[512,512]{1,0:T(8,128)(2,1)}, u32[]{:S(2)}, u32[]{:S(2)}) collective-permute-start(bf16[512,512]{1,0:T(8,128)(2,1)S(1)} %copy-done.9), channel_id=1, source_target_pairs={{0,2},{1,3},{8,10},{9,11},{16,18},{17,19},{24,26},{25,27}} | collective-permute-start | bytes 1572872 | tf_op jit(solution)/shard_map/ppermute | solution.py:367
  236.3 13.5 %collective-permute-start.20 = (bf16[512,512]{1,0:T(8,128)(2,1)S(1)}, bf16[512,512]{1,0:T(8,128)(2,1)}, u32[]{:S(2)}, u32[]{:S(2)}) collective-permute-start(bf16[512,512]{1,0:T(8,128)(2,1)S(1)} %copy-done.11), channel_id=1, source_target_pairs={{0,2},{1,3},{8,10},{9,11},{16,18},{17,19},{24,26},{25,27}} | collective-permute-start | bytes 1572872 | tf_op jit(solution)/shard_map/ppermute | solution.py:367
  238.4 3.1 %collective-permute-start.26 = (f32[2048]{0:T(1024)S(1)}, f32[2048]{0:T(1024)S(1)}, u32[]{:S(2)}, u32[]{:S(2)}) collective-permute-start(f32[2048]{0:T(1024)S(1)} %broadcast_select_fusion.5), channel_id=1, source_target_pairs={{0,6},{6,0},{2,4},{4,2},{1,7},{7,1},{3,5},{5,3},{8,14},{14,8},{10,... | collective-permute-start | bytes 24584 | tf_op jit(solution)/shard_map/ppermute | solution.py:409
  241.6 3.7 %collective-permute-start.27 = (f32[2048]{0:T(1024)S(1)}, f32[2048]{0:T(1024)S(1)}, u32[]{:S(2)}, u32[]{:S(2)}) collective-permute-start(f32[2048]{0:T(1024)S(1)} %fusion.15), channel_id=1, source_target_pairs={{0,8},{8,0},{16,24},{24,16},{1,9},{9,1},{17,25},{25,17},{2,10},{10... | collective-permute-start | bytes 24584 | tf_op jit(solution)/shard_map/ppermute | solution.py:412
  241.6 12.7 %collective-permute-start.21 = (bf16[512,512]{1,0:T(8,128)(2,1)S(1)}, bf16[512,512]{1,0:T(8,128)(2,1)}, u32[]{:S(2)}, u32[]{:S(2)}) collective-permute-start(bf16[512,512]{1,0:T(8,128)(2,1)S(1)} %copy-done.9), channel_id=1, source_target_pairs={{4,2},{2,6},{5,3},{3,7},{12,10},{10,14},{13,11},{11,15},{20,18},{1... | collective-permute-start | bytes 1572872 | tf_op jit(solution)/shard_map/ppermute | solution.py:368
  245.2 4.5 %collective-permute-start.28 = (f32[2048]{0:T(1024)S(1)}, f32[2048]{0:T(1024)S(1)}, u32[]{:S(2)}, u32[]{:S(2)}) collective-permute-start(f32[2048]{0:T(1024)S(1)} %add.42), channel_id=1, source_target_pairs={{0,16},{8,24},{16,0},{24,8},{1,17},{9,25},{17,1},{25,9},{2,18},{10... | collective-permute-start | bytes 24584 | tf_op jit(solution)/shard_map/ppermute | solution.py:412
  248.2 6.1 %collective-permute-start.22 = (bf16[512,512]{1,0:T(8,128)(2,1)S(1)}, bf16[512,512]{1,0:T(8,128)(2,1)}, u32[]{:S(2)}, u32[]{:S(2)}) collective-permute-start(bf16[512,512]{1,0:T(8,128)(2,1)S(1)} %copy-done.11), channel_id=1, source_target_pairs={{4,2},{2,6},{5,3},{3,7},{12,10},{10,14},{13,11},{11,15},{20,18},{1... | collective-permute-start | bytes 1572872 | tf_op jit(solution)/shard_map/ppermute | solution.py:368
  249.8 1.9 collective-permute-start.29
  253.4 10.0 %collective-permute-start.25 = (bf16[256,512]{1,0:T(8,128)(2,1)S(1)}, bf16[256,512]{1,0:T(8,128)(2,1)S(1)}, u32[]{:S(2)}, u32[]{:S(2)}) collective-permute-start(bf16[256,512]{1,0:T(8,128)(2,1)S(1)} %get-tuple-element.44), channel_id=1, source_target_pairs={{0,4},{4,0},{1,5},{5,1},{2,6},{6,2},{3,7},{7,3},{8,12},{12,8},{9,1... | collective-permute-start | bytes 786440 | tf_op jit(solution)/shard_map/ppermute | solution.py:392
  (31 other events, 155.5 us)
Sparse Core Ops, SparseCore 0:
  30.1 46.2 all-gather.2
  77.9 44.6 all-gather.4
  124.9 42.5 reduce-scatter.2
  169.7 43.1 reduce-scatter.4

commit v5 on v4

--- a/solution.py
+++ b/solution.py
@@ -26,6 +26,10 @@
 
 def cost(flops, mib, exps=0):
     return pl.CostEstimate(flops=flops, bytes_accessed=mib << 20, transcendentals=exps)
+
+
+def in_hbm(*arrays):
+    return [pltpu.with_memory_space_constraint(a, pltpu.HBM) for a in arrays]
 
 
 def params(mib):
@@ -71,12 +75,12 @@
             out_specs=[out, out, pl.BlockSpec((step, 128), lambda i, s: (i, 0))],
             scratch_shapes=[pltpu.VMEM((step, D), BF16)],
         ),
-        out_shape=[jax.ShapeDtypeStruct((length, D // 2), BF16)] * 2
+        out_shape=[pltpu.HBM((length, D // 2), BF16)] * 2
         + [jax.ShapeDtypeStruct((length, 128), F32)],
         compiler_params=params(32),
         cost_estimate=cost(8 * length * D, 8),
         name="norm",
-    )(at, *nears, *fars, gain)
+    )(at, *in_hbm(*nears, *fars), gain)
 
 
 def attend_head(bias, qg, kv):
@@ -133,13 +137,13 @@
             in_specs=[enc, enc, weight, weight, pick(1), pick(0)],
             out_specs=[out, out],
         ),
-        out_shape=[jax.ShapeDtypeStruct((length, cols), BF16)] * 2,
+        out_shape=[pltpu.HBM((length, cols), BF16)] * 2,
         compiler_params=params(48),
         cost_estimate=cost(
             length * cols * (4 * half + 14 * length), 8, length * length * cols // (2 * HEAD)
         ),
         name="attend",
-    )(at, enc_own, enc_other, w_own, w_other, *qgs)
+    )(at, *in_hbm(enc_own, enc_other, w_own, w_other, *qgs))
 
 
 def weight_grad_kernel(scale, at, enc_a, enc_b, gkv_a, gkv_b, out):
@@ -161,11 +165,11 @@
             in_specs=[enc, enc, gkv, gkv],
             out_specs=pl.BlockSpec((step, cols), lambda i, s: (i, 0)),
         ),
-        out_shape=jax.ShapeDtypeStruct((half, cols), BF16),
+        out_shape=pltpu.HBM((half, cols), BF16),
         cost_estimate=cost(4 * length * half * cols // 64, 0),
         compiler_params=params(32),
         name="weight_grad",
-    )(at, enc_a, enc_b, gkv_a, gkv_b)
+    )(at, *in_hbm(enc_a, enc_b, gkv_a, gkv_b))
 
 
 def collect_kernel(scale, at, *refs):
@@ -201,7 +205,7 @@
         cost_estimate=cost(8 * length * width, 12),
         compiler_params=params(32),
         name="collect",
-    )(at, *terms, raw, inv_rms, gain)
+    )(at, *in_hbm(*terms, raw), inv_rms, gain)
 
 
 def enc_grad_kernel(at, gkv_0, gkv_1, own_0, own_1, other_0, other_1, out):
@@ -232,11 +236,11 @@
             in_specs=[gkv, gkv, weight, weight, weight, weight],
             out_specs=pl.BlockSpec((length, 2 * rows), lambda i, s: (0, i)),
         ),
-        out_shape=jax.ShapeDtypeStruct((length, D // 2), BF16),
+        out_shape=pltpu.HBM((length, D // 2), BF16),
         compiler_params=params(32),
         cost_estimate=cost(4 * length * D * cols, 8),
         name="enc_grad",
-    )(at, *gkvs, *owns, *others)
+    )(at, *in_hbm(*gkvs, *owns, *others))
 
 
 def cut(array, axis, index, size):
@@ -283,21 +287,22 @@
     def slots(block):
         return [lax.ppermute(block, "z", turned(groups, -s)) for s in range(1, groups)]
 
-    mine = [chunk_of(y, k) for k in range(CHUNKS)]
-    swap = lax.ppermute(cut(w_kv, 1, 1 - y, half), "y", SWAP)
-    swapped = [swap[:, k * cols : (k + 1) * cols] for k in range(CHUNKS)]
-
-    there = lax.ppermute(after(packed, swap), PLANE, [(0, 2), (2, 1)])
+    gains = [gain] + [lax.ppermute(gain, "mp", turned(shards, t)) for t in range(1, shards)]
+    key_count = jnp.where(straight, src_len, lax.ppermute(src_len, "y", SWAP))
+
     here = jnp.where(y == 0, packed, lax.ppermute(packed, PLANE, [(2, 3)]))
+    swapped = [lax.ppermute(chunk_of(1 - y, 0), "y", SWAP)]
+    there = after(packed, swapped[0], key_count, here, *gains)
+    there = lax.ppermute(there, PLANE, [(0, 2), (2, 1)])
+    for k in range(1, CHUNKS):
+        swapped.append(lax.ppermute(after(chunk_of(1 - y, k), there), "y", SWAP))
     nears = [here, there]
     fars = []
     for turn in range(1, shards):
         fars.append(
             [across(here, turn, [(0, 0), (3, 3)]), across(there, turn, [(1, 1), (2, 2)])]
         )
-    gains = [gain] + [lax.ppermute(gain, "mp", turned(shards, t)) for t in range(1, shards)]
-
-    blocks = [jnp.concatenate([mine[k], swapped[k]], 0) for k in range(CHUNKS)]
+    blocks = [jnp.concatenate([chunk_of(y, k), swapped[k]], 0) for k in range(CHUNKS)]
     w_own, w_other = [], []
 
     position = lax.broadcasted_iota(jnp.int32, (length, width), 0)
@@ -309,7 +314,6 @@
         jnp.where(y == 1, qg_near, lax.ppermute(qg_near, PLANE, [(1, 0)])),
         lax.ppermute(qg_far, PLANE, [(1, 2), (3, 1)]),
     ]
-    key_count = jnp.where(straight, src_len, lax.ppermute(src_len, "y", SWAP))
     at = jnp.concatenate(
         [jnp.stack([straight.astype(jnp.int32), x, y, core]).astype(jnp.int32), key_count]
     )
@@ -333,7 +337,7 @@
 
     if tiled:
         enc_own, enc_other, inv_rms = norm(
-            at, nears, fars[0], after(gain_all[None], *qgs), groups, rows
+            at, nears, fars[0], after(gain_all[None], *qgs, *blocks), groups, rows
         )
     else:
         raw = [jnp.where(straight, *parts) for parts in [nears] + fars]
@@ -355,7 +359,7 @@
                 gathered = lax.dynamic_update_slice_in_dim(gathered, piece, start, 0)
             w_own.append(gathered)
         else:
-            block = blocks[k] if k == 0 else after(blocks[k], there)
+            block = blocks[k]
             w_own.append(lax.all_gather(block, "z", axis=0, tiled=True))
             if k > 0:
                 w_own[k] = after(w_own[k], grad)
@@ -371,15 +375,16 @@
         parts = jnp.split(gkv, 2, axis=1)
         gkv_mate = jnp.concatenate([lax.ppermute(p, "phase", SWAP) for p in parts], 1)
         if tiled:
+            if k == CHUNKS - 1:
+                terms = [enc_grad(at, gkvs, w_own, w_other, groups, rows, s) for s in (1, 0)][::-1]
+                gkv_mate = after(gkv_mate, *terms)
             grad = weight_grad(at, enc_own, enc_mate, gkv, gkv_mate, groups, pair_scale)
         else:
             grad = pair_scale * (dot(enc_own, gkv, TN) + dot(enc_mate, gkv_mate, TN))
             grad = grad.astype(BF16)
         weight_sums.append(lax.psum_scatter(grad, "z", scatter_dimension=0, tiled=True))
 
-    if tiled:
-        terms = [enc_grad(at, gkvs, w_own, w_other, groups, rows, s) for s in (1, 0)][::-1]
-    else:
+    if not tiled:
         gkv_all = jnp.concatenate(gkvs, 1)
         full = dot(gkv_all, jnp.concatenate([jnp.concatenate(w, 0) for w in zip(w_own, w_other)], 1), NT)
         back = jnp.zeros_like(block_order).at[block_order].set(jnp.arange(block_order.shape[0]))
@@ -388,10 +393,15 @@
     moved = [across(terms[turn], turn, [(0, 0), (3, 3)]) for turn in range(1, shards)]
     moved += [across(terms[turn], turn, [(2, 0), (1, 3)]) for turn in range(shards)]
 
+    dec_here = jnp.concatenate([d[0] for d in decs], 1)
+    dec_there = jnp.concatenate([d[1] for d in decs], 1)
+    dec_grads = ordered(y == 0, dec_here, dec_there, 1)
     kept = jnp.concatenate([w[:rows] for w in weight_sums], 1)
     got = [lax.ppermute(w[rows:], "y", SWAP) for w in weight_sums]
+    got = jnp.concatenate(got, 1)
+    d_wkv = ordered(y == 0, kept, got, 1).astype(F32)
     if tiled:
-        terms[0] = after(terms[0], got[0])
+        terms[0], d_wkv, dec_grads = lax.optimization_barrier((terms[0], d_wkv, dec_grads))
         grad_normed, gain_term = collect(
             at, [terms[0]] + moved, here, inv_rms, gain.astype(F32)[None], pair_scale
         )
@@ -412,12 +422,7 @@
         gain_term = gain_term + lax.ppermute(gain_term, "z", [(i, i ^ turn) for i in range(groups)])
         turn *= 2
     d_gain = jnp.where(straight, gain_term, lax.ppermute(gain_term, "phase", SWAP))
-    got = jnp.concatenate(got, 1)
-    d_wkv = ordered(y == 0, kept, got, 1).astype(F32)
-
-    dec_here = jnp.concatenate([d[0] for d in decs], 1)
-    dec_there = jnp.concatenate([d[1] for d in decs], 1)
-    dec_grads = ordered(y == 0, dec_here, dec_there, 1)
+
     sec_grads = jnp.where(core == 0, enc_grads, dec_grads)[None, None]
     return (sec_grads, d_wkv, d_gain)
 

time: 273 us -> 275 us (level)
  local copies, waits for them, and re-layouts: 30.3 us -> 13.8 us
  starting transfers between devices: 52.5 us -> 65.9 us
  Pallas kernels: 58.4 us -> 71.4 us
  waiting for transfers between devices: 97.5 us -> 88.2 us
    reduce_scatter x2, waiting for transfers between devices: 0.02 us -> 28.4 us  [on_device(): lax.psum_scatter(grad, 'z', scatter_dimension=0, tiled=True)]
    ppermute x5, waiting for transfers between devices: 26.5 us -> 0.01 us  [across(): lax.ppermute(value, ('y', 'phase', 'mp'), [(a * shards + s, b * shards +...]
    unnamed x58 -> x14, local copies, waits for them, and re-layouts: 22.9 us -> 3.94 us
    ppermute x2, starting transfers between devices: 4.98 us -> 19 us  [on_device(): got = [lax.ppermute(w[rows:], 'y', SWAP) for w in weight_sums]]
    ppermute x2, waiting for transfers between devices: 19.5 us -> 5.49 us  [on_device(): got = [lax.ppermute(w[rows:], 'y', SWAP) for w in weight_sums]]
    ppermute x2, starting transfers between devices: 9.04 us -> 0.01 us  [on_device(): w_other.append(lax.ppermute(w_own[k], 'phase', SWAP))]
    all_gather x2, waiting for transfers between devices: 10.7 us -> 18.6 us  [on_device(): w_own.append(lax.all_gather(block, 'z', axis=0, tiled=True))]
    pallas_call x2, Pallas kernels: 7.74 us -> 13.3 us  [weight_grad(): pl.pallas_call(lambda *refs: weight_grad_kernel(scale, *refs), grid_spec=...]
  transfers between devices with their start and end apart: 34 -> 35, of which waited for: 16 -> 15; matrix products, arithmetic and copies ran while one was open for 8% -> 9% of each run, Pallas kernels for 22% -> 24%
where the time goes in v5:
time: 275 us; the launch traced here: 273 us
  waiting for transfers between devices  88.2 us (32%)
  Pallas kernels  71.4 us (26%)
  starting transfers between devices  65.9 us (24%)
  other arithmetic  17.3 us (6%)
  between operations  16 us (6%)
  local copies, waits for them, and re-layouts  13.8 us (5%)
    pallas_call x2, Pallas kernels, attend(): pl.pallas_call(attend_kernel, grid_spec=pltpu.PrefetchScalarGridSpec(num_...  30.9 us
    reduce_scatter x2, waiting for transfers between devices, on_device(): lax.psum_scatter(grad, 'z', scatter_dimension=0, tiled=True)  28.4 us
    ppermute x1, waiting for transfers between devices, on_device(): there = lax.ppermute(there, PLANE, [(0, 2), (2, 1)])  19.2 us
    ppermute x2, starting transfers between devices, on_device(): got = [lax.ppermute(w[rows:], 'y', SWAP) for w in weight_sums]  19 us
    all_gather x2, waiting for transfers between devices, on_device(): w_own.append(lax.all_gather(block, 'z', axis=0, tiled=True))  18.6 us
    pallas_call x2, Pallas kernels, enc_grad(): pl.pallas_call(enc_grad_kernel, grid_spec=pltpu.PrefetchScalarGridSpec(nu...  13.6 us
    pallas_call x2, Pallas kernels, weight_grad(): pl.pallas_call(lambda *refs: weight_grad_kernel(scale, *refs), grid_spec=...  13.3 us
    ppermute x5, starting transfers between devices, across(): lax.ppermute(value, ('y', 'phase', 'mp'), [(a * shards + s, b * shards +...  10.4 us
  transfers between devices with their start and end apart: 35, of which 15 were waited for; matrix products, arithmetic and copies ran while one was open for 9% of the time, Pallas kernels for 24%

profile of v5, /device:TPU:0, one launch (start us, length us, event | category | flops | bytes accessed | tf_op | source)
XLA Modules:
  0.0 272.6 jit_solution(4187235487767257239)
XLA Ops:
  8.0 4.1 %collective-permute-start = (s32[1]{0:T(128)}, s32[1]{0:T(128)}, u32[]{:S(2)}, u32[]{:S(2)}) collective-permute-start(s32[1]{0:T(128)} %param.8), channel_id=1, source_target_pairs={{0,4},{4,0},{1,5},{5,1},{2,6},{6,2},{3,7},{7,3},{8,12},{12,8},{9,1... | collective-permute-start | bytes 20 | tf_op jit(solution)/shard_map/ppermute | solution.py:291
  19.0 4.3 %fusion.1 = (bf16[512,2048]{1,0:T(8,128)(2,1)}, bf16[512,2048]{1,0:T(8,128)(2,1)S(1)}) fusion(s32[2048]{0:T(1024)S(1)} %get-tuple-element.57, s32[2048]{0:T(1024)S(1)} %get-tuple-element.58, pred[512]{0:T(512)(128)(4,1)S(1)} %iota_compare_fusion, pred[2048]{0:T(1024)(128)(4,1)S(1)} %fusion.7, bf16[1,1,512,2048]{3,2,1,0:T(8,128)(2,1)} %param.5, ...), kind=kLoop, calls=%fused_computation.2 | loop fusion | flops 5242880 | bytes 8407553 | tf_op jit(solution)/shard_map/jit(_where)/select_n | solution.py:310
  23.4 5.8 %collective-permute-start.4 = (bf16[512,2048]{1,0:T(8,128)(2,1)}, bf16[512,2048]{1,0:T(8,128)(2,1)}, u32[]{:S(2)}, u32[]{:S(2)}) collective-permute-start(bf16[512,2048]{1,0:T(8,128)(2,1)} %bitcast.4), channel_id=1, source_target_pairs={{0,4},{4,2},{1,5},{5,3},{8,12},{12,10},{9,13},{13,11},{16,20},{20,... | collective-permute-start | bytes 6291464 | tf_op jit(solution)/shard_map/ppermute | solution.py:296
  30.1 2.4 collective-permute-start.5
  32.5 19.2 %collective-permute-done.4.refs_2_ = bf16[512,2048]{1,0:T(8,128)(2,1)} collective-permute-done((bf16[512,2048]{1,0:T(8,128)(2,1)}, bf16[512,2048]{1,0:T(8,128)(2,1)}, u32[]{:S(2)}, u32[]{:S(2)}) %collective-permute-start.4) | collective-permute-done | bytes 2097184 | tf_op jit(solution)/shard_map/ppermute | solution.py:296
  51.7 2.0 collective-permute-start.6
  53.7 3.0 %collective-permute-start.9 = (bf16[256,512]{1,0:T(8,128)(2,1)}, bf16[256,512]{1,0:T(8,128)(2,1)S(1)}, u32[]{:S(2)}, u32[]{:S(2)}) collective-permute-start(bf16[256,512]{1,0:T(8,128)(2,1)} %get-tuple-element.25), channel_id=1, source_target_pairs={{0,4},{4,0},{1,5},{5,1},{2,6},{6,2},{3,7},{7,3},{8,12},{12,8},{9,1... | collective-permute-start | bytes 786440 | tf_op jit(solution)/shard_map/ppermute | solution.py:298
  56.7 2.7 %constant_dynamic-slice_fusion.3 = (bf16[512,1024]{1,0:T(8,128)(2,1)}, bf16[512,1024]{1,0:T(8,128)(2,1)S(1)}) fusion(bf16[512,2048]{1,0:T(8,128)(2,1)} %get-tuple-element.43, s32[]{:T(128)S(6)} %select_n.114, s32[]{:T(128)S(6)} %select_n.120), kind=kLoop, calls=%fused_computation.29 | loop fusion | bytes 4194312 | tf_op jit(solution)/shard_map/dynamic_slice | solution.py:247
  63.8 11.7 %all-gather.3.cloned.1.call-done.w_own.own_0 = bf16[2048,512]{1,0:T(8,128)(2,1)} async-done(((bf16[512,512]{1,0:T(8,128)(2,1)}), bf16[2048,512]{1,0:T(8,128)(2,1)}) %all-gather.3.cloned.1.call-update) | async-done | bytes 2097168 | tf_op jit(solution)/shard_map/all_gather | solution.py:363
  75.7 2.3 broadcast_select_fusion.1.refs_0_
  78.0 7.0 %norm.1 = (bf16[512,2048]{1,0:T(8,128)(2,1)}, bf16[512,2048]{1,0:T(8,128)(2,1)}, f32[512,128]{1,0:T(8,128)S(1)}) custom-call(s32[5]{0:T(128)S(1)} %concatenate.59.refs_0_.at, bf16[512,2048]{1,0:T(8,128)(2,1)} %copy-done, bf16[512,2048]{1,0:T(8,128)(2,1)} %collective-permute-done.4.refs_2_, bf16[512,2048]{1,0:T(8,128)(2,1)} %collective-permute-done.5.refs_3_, ...), custom_call_target="tpu_custom_call" | custom-call | flops 16777216 | bytes 8388608 | tf_op jit(solution)/shard_map/norm/pallas_call | solution.py:69
  85.0 2.4 collective-permute-start.11
  87.4 15.3 %attend.2 = (bf16[512,512]{1,0:T(8,128)(2,1)}, bf16[512,512]{1,0:T(8,128)(2,1)}) custom-call(s32[5]{0:T(128)S(1)} %concatenate.59.refs_0_.at, bf16[512,2048]{1,0:T(8,128)(2,1)} %get-tuple-element.27.enc_own.refs_1_, bf16[512,2048]{1,0:T(8,128)(2,1)} %get-tuple-element.28.enc_other, bf16[2048,512]{1,0:T(8,128)(2,1)} %all-gather.3.cloned.1.call-done.w_own.own_0, ...), custom_call_target="tpu_custom_call" | custom-call | flops 4026531840 | bytes 8388608 | tf_op jit(solution)/shard_map/attend/pallas_call | solution.py:132
  107.9 6.7 %weight_grad.2 = bf16[2048,512]{1,0:T(8,128)(2,1)} custom-call(s32[5]{0:T(128)S(1)} %concatenate.59.refs_0_.at, bf16[512,2048]{1,0:T(8,128)(2,1)} %get-tuple-element.27.enc_own.refs_1_, bf16[512,2048]{1,0:T(8,128)(2,1)} %copy-done.1, bf16[512,512]{1,0:T(8,128)(2,1)} %get-tuple-element.29.refs_3_.gkv_0, bf16[512,512]{1,0:T(8,128)(2,1)} %pad_maximum_fusion.2.refs_4_), custom_call_target="tpu_custom_call" | custom-call | flops 33554432 | tf_op jit(solution)/shard_map/weight_grad/pallas_call | solution.py:160
  114.8 6.9 %all-gather.5.cloned.1.call-done.w_own.own_1 = bf16[2048,512]{1,0:T(8,128)(2,1)} async-done(((bf16[512,512]{1,0:T(8,128)(2,1)}), bf16[2048,512]{1,0:T(8,128)(2,1)}) %all-gather.5.cloned.1.call-update) | async-done | bytes 2097168 | tf_op jit(solution)/shard_map/all_gather | solution.py:363
  121.8 4.4 %collective-permute-done.14.w_other.other_1 = bf16[2048,512]{1,0:T(8,128)(2,1)S(1)} collective-permute-done((bf16[2048,512]{1,0:T(8,128)(2,1)}, bf16[2048,512]{1,0:T(8,128)(2,1)S(1)}, u32[]{:S(2)}, u32[]{:S(2)}) %collective-permute-start.14) | collective-permute-done | bytes 2097184 | tf_op jit(solution)/shard_map/ppermute | solution.py:366
  127.4 15.6 %attend.3 = (bf16[512,512]{1,0:T(8,128)(2,1)}, bf16[512,512]{1,0:T(8,128)(2,1)}) custom-call(s32[5]{0:T(128)S(1)} %concatenate.59.refs_0_.at, bf16[512,2048]{1,0:T(8,128)(2,1)} %get-tuple-element.27.enc_own.refs_1_, bf16[512,2048]{1,0:T(8,128)(2,1)} %get-tuple-element.28.enc_other, bf16[2048,512]{1,0:T(8,128)(2,1)} %all-gather.5.cloned.1.call-done.w_own.own_1, ...), custom_call_target="tpu_custom_call" | custom-call | flops 4026531840 | bytes 8388608 | tf_op jit(solution)/shard_map/attend/pallas_call | solution.py:132
  144.7 6.8 %enc_grad.3 = bf16[512,2048]{1,0:T(8,128)(2,1)} custom-call(s32[5]{0:T(128)S(1)} %concatenate.59.refs_0_.at, bf16[512,512]{1,0:T(8,128)(2,1)} %get-tuple-element.29.refs_3_.gkv_0, bf16[512,512]{1,0:T(8,128)(2,1)} %get-tuple-element.31.gkv_1.refs_3_, bf16[2048,512]{1,0:T(8,128)(2,1)} %all-gather.3.cloned.1.call-done.w_own.own_0, ...), custom_call_target="tpu_custom_call" | custom-call | flops 4294967296 | bytes 8388608 | tf_op jit(solution)/shard_map/enc_grad/pallas_call | solution.py:231
  151.5 6.8 %enc_grad.2.refs_1_ = bf16[512,2048]{1,0:T(8,128)(2,1)} custom-call(s32[5]{0:T(128)S(1)} %concatenate.59.refs_0_.at, bf16[512,512]{1,0:T(8,128)(2,1)} %get-tuple-element.29.refs_3_.gkv_0, bf16[512,512]{1,0:T(8,128)(2,1)} %get-tuple-element.31.gkv_1.refs_3_, bf16[2048,512]{1,0:T(8,128)(2,1)} %all-gather.3.cloned.1.call-done.w_own.own_0, ...), custom_call_target="tpu_custom_call" | custom-call | flops 4294967296 | bytes 8388608 | tf_op jit(solution)/shard_map/enc_grad/pallas_call | solution.py:231
  159.1 6.6 %weight_grad.3 = bf16[2048,512]{1,0:T(8,128)(2,1)} custom-call(s32[5]{0:T(128)S(1)} %concatenate.59.refs_0_.at, bf16[512,2048]{1,0:T(8,128)(2,1)} %get-tuple-element.27.enc_own.refs_1_, bf16[512,2048]{1,0:T(8,128)(2,1)} %copy-done.1, bf16[512,512]{1,0:T(8,128)(2,1)} %get-tuple-element.31.gkv_1.refs_3_, bf16[512,512]{1,0:T(8,128)(2,1)} %pad_maximum_fusion.3.refs_4_), custom_call_target="tpu_custom_call" | custom-call | flops 33554432 | tf_op jit(solution)/shard_map/weight_grad/pallas_call | solution.py:160
  165.8 2.3 collective-permute-start.19
  170.7 3.4 %collective-permute-start.23 = (bf16[512,2048]{1,0:T(8,128)(2,1)}, bf16[512,2048]{1,0:T(8,128)(2,1)}, u32[]{:S(2)}, u32[]{:S(2)}) collective-permute-start(bf16[512,2048]{1,0:T(8,128)(2,1)} %enc_grad.3), channel_id=1, source_target_pairs={{0,1},{1,0},{6,7},{7,6},{8,9},{9,8},{14,15},{15,14},{16,17},{17,16... | collective-permute-start | bytes 6291464 | tf_op jit(solution)/shard_map/ppermute | solution.py:278
  174.2 4.5 %collective-permute-start.20 = (bf16[512,512]{1,0:T(8,128)(2,1)}, bf16[512,512]{1,0:T(8,128)(2,1)S(1)}, u32[]{:S(2)}, u32[]{:S(2)}) collective-permute-start(bf16[512,512]{1,0:T(8,128)(2,1)} %get-tuple-element.34), channel_id=1, source_target_pairs={{0,2},{1,3},{8,10},{9,11},{16,18},{17,19},{24,26},{25,27}} | collective-permute-start | bytes 1572872 | tf_op jit(solution)/shard_map/ppermute | solution.py:371
  183.8 28.3 %reduce-scatter.5.cloned.1.call-done = bf16[512,512]{1,0:T(8,128)(2,1)} async-done(((bf16[2048,512]{1,0:T(8,128)(2,1)}), bf16[512,512]{1,0:T(8,128)(2,1)}) %reduce-scatter.5.cloned.1.call-update) | async-done | bytes 524304 | tf_op jit(solution)/shard_map/reduce_scatter | solution.py:385
  213.2 10.6 %collective-permute-start.17 = (bf16[256,512]{1,0:T(8,128)(2,1)}, bf16[256,512]{1,0:T(8,128)(2,1)S(1)}, u32[]{:S(2)}, u32[]{:S(2)}) collective-permute-start(bf16[256,512]{1,0:T(8,128)(2,1)} %get-tuple-element.50), channel_id=1, source_target_pairs={{0,4},{4,0},{1,5},{5,1},{2,6},{6,2},{3,7},{7,3},{8,12},{12,8},{9,1... | collective-permute-start | bytes 786440 | tf_op jit(solution)/shard_map/ppermute | solution.py:400
  223.8 8.4 %collective-permute-start.18 = (bf16[256,512]{1,0:T(8,128)(2,1)S(1)}, bf16[256,512]{1,0:T(8,128)(2,1)S(1)}, u32[]{:S(2)}, u32[]{:S(2)}) collective-permute-start(bf16[256,512]{1,0:T(8,128)(2,1)S(1)} %get-tuple-element.52), channel_id=1, source_target_pairs={{0,4},{4,0},{1,5},{5,1},{2,6},{6,2},{3,7},{7,3},{8,12},{12,8},{9,1... | collective-permute-start | bytes 786440 | tf_op jit(solution)/shard_map/ppermute | solution.py:400
  232.2 3.3 %maximum_select_fusion = bf16[512,2048]{1,0:T(8,128)(2,1)} fusion(bf16[512,512]{1,0:T(8,128)(2,1)} %collective-permute-done.22, bf16[512,512]{1,0:T(8,128)(2,1)} %collective-permute-done.21, bf16[512,512]{1,0:T(8,128)(2,1)S(1)} %broadcast_select_fusion.2, bf16[512,512]{1,0:T(8,128)(2,1)S(1)} %broadcast_select_fusion.3, pred[]{:T(512)S(6)} %eq.23), kind=kLoop, calls=%fused_computation.3 | loop fusion | flops 17825792 | bytes 4194305 | tf_op jit(solution)/shard_map/jit(_where)/select_n | solution.py:251
  235.6 5.4 %collective-permute-done.18 = bf16[256,512]{1,0:T(8,128)(2,1)S(1)} collective-permute-done((bf16[256,512]{1,0:T(8,128)(2,1)S(1)}, bf16[256,512]{1,0:T(8,128)(2,1)S(1)}, u32[]{:S(2)}, u32[]{:S(2)}) %collective-permute-start.18) | collective-permute-done | bytes 262176 | tf_op jit(solution)/shard_map/ppermute | solution.py:400
  242.6 6.6 %collect.1 = (bf16[512,2048]{1,0:T(8,128)(2,1)S(1)}, f32[4,1,2048]{2,1,0:T(1,128)S(1)}) custom-call(s32[5]{0:T(128)S(1)} %concatenate.59.refs_0_.at, bf16[512,2048]{1,0:T(8,128)(2,1)} %enc_grad.2.refs_1_, bf16[512,2048]{1,0:T(8,128)(2,1)} %collective-permute-done.23.refs_2_, bf16[512,2048]{1,0:T(8,128)(2,1)} %collective-permute-done.24.refs_3_, ...), custom_call_target="tpu_custom_call" | custom-call | flops 8388608 | bytes 12582912 | tf_op jit(solution)/shard_map/collect/pallas_call | solution.py:189
  249.3 2.0 collective-permute-start.26
  254.5 3.6 %collective-permute-done.28 = f32[2048]{0:T(1024)S(1)} collective-permute-done((f32[2048]{0:T(1024)S(1)}, f32[2048]{0:T(1024)S(1)}, u32[]{:S(2)}, u32[]{:S(2)}) %collective-permute-start.28) | collective-permute-done | bytes 8224 | tf_op jit(solution)/shard_map/ppermute | solution.py:422
  259.1 3.5 %collective-permute-done.29 = f32[2048]{0:T(1024)S(1)} collective-permute-done((f32[2048]{0:T(1024)S(1)}, f32[2048]{0:T(1024)S(1)}, u32[]{:S(2)}, u32[]{:S(2)}) %collective-permute-start.29) | collective-permute-done | bytes 8224 | tf_op jit(solution)/shard_map/ppermute | solution.py:422
  (95 shorter events, 38.4 us)
Async XLA Ops:
  7.2 68.3 %all-gather.3.cloned.1.call-start = ((), (), s32[]{:S(2)}) async-start(), calls=%async_computation.2 | async-start | bytes 2621440 | tf_op jit(solution)/shard_map/all_gather | solution.py:363
  7.2 10.5 %collective-permute-start.1 = (bf16[512,2048]{1,0:T(8,128)(2,1)}, bf16[512,2048]{1,0:T(8,128)(2,1)S(1)}, u32[]{:S(2)}, u32[]{:S(2)}) collective-permute-start(bf16[512,2048]{1,0:T(8,128)(2,1)} %bitcast.4), channel_id=1, source_target_pairs={{4,6},{5,7},{12,14},{13,15},{20,22},{21,23},{28,30},{29,31}} | collective-permute-start | bytes 6291464 | tf_op jit(solution)/shard_map/ppermute | solution.py:293
  8.0 9.0 %collective-permute-start = (s32[1]{0:T(128)}, s32[1]{0:T(128)}, u32[]{:S(2)}, u32[]{:S(2)}) collective-permute-start(s32[1]{0:T(128)} %param.8), channel_id=1, source_target_pairs={{0,4},{4,0},{1,5},{5,1},{2,6},{6,2},{3,7},{7,3},{8,12},{12,8},{9,1... | collective-permute-start | bytes 20 | tf_op jit(solution)/shard_map/ppermute | solution.py:291
  12.1 11.2 %collective-permute-start.3 = (bf16[2048]{0:T(1024)(128)(2,1)}, bf16[2048]{0:T(1024)(128)(2,1)S(1)}, u32[]{:S(2)}, u32[]{:S(2)}) collective-permute-start(bf16[2048]{0:T(1024)(128)(2,1)} %param.6), channel_id=1, source_target_pairs={{0,1},{1,0},{2,3},{3,2},{4,5},{5,4},{6,7},{7,6},{8,9},{9,8},{10,11... | collective-permute-start | bytes 12296 | tf_op jit(solution)/shard_map/ppermute | solution.py:290
  15.6 7.8 %collective-permute-start.2 = (bf16[256,512]{1,0:T(8,128)(2,1)S(1)}, bf16[256,512]{1,0:T(8,128)(2,1)S(1)}, u32[]{:S(2)}, u32[]{:S(2)}) collective-permute-start(bf16[256,512]{1,0:T(8,128)(2,1)S(1)} %get-tuple-element.47), channel_id=1, source_target_pairs={{0,4},{4,0},{1,5},{5,1},{2,6},{6,2},{3,7},{7,3},{8,12},{12,8},{9,1... | collective-permute-start | bytes 786440 | tf_op jit(solution)/shard_map/ppermute | solution.py:294
  23.4 28.3 %collective-permute-start.4 = (bf16[512,2048]{1,0:T(8,128)(2,1)}, bf16[512,2048]{1,0:T(8,128)(2,1)}, u32[]{:S(2)}, u32[]{:S(2)}) collective-permute-start(bf16[512,2048]{1,0:T(8,128)(2,1)} %bitcast.4), channel_id=1, source_target_pairs={{0,4},{4,2},{1,5},{5,3},{8,12},{12,10},{9,13},{13,11},{16,20},{20,... | collective-permute-start | bytes 6291464 | tf_op jit(solution)/shard_map/ppermute | solution.py:296
  30.0 91.7 %all-gather.5.cloned.1.call-start = ((), (), s32[]{:S(2)}) async-start(), calls=%async_computation.3 | async-start | bytes 2621440 | tf_op jit(solution)/shard_map/all_gather | solution.py:363
  30.1 47.9 %collective-permute-start.5 = (bf16[512,2048]{1,0:T(8,128)(2,1)S(1)}, bf16[512,2048]{1,0:T(8,128)(2,1)}, u32[]{:S(2)}, u32[]{:S(2)}) collective-permute-start(bf16[512,2048]{1,0:T(8,128)(2,1)S(1)} %get-tuple-element.44.refs_1_.refs_5_), channel_id=1, source_target_pairs={{0,1},{1,0},{6,7},{7,6},{8,9},{9,8},{14,15},{15,14},{16,17},{17,16... | collective-permute-start | bytes 6291464 | tf_op jit(solution)/shard_map/ppermute | solution.py:278
  51.7 26.3 %collective-permute-start.6 = (bf16[512,2048]{1,0:T(8,128)(2,1)}, bf16[512,2048]{1,0:T(8,128)(2,1)}, u32[]{:S(2)}, u32[]{:S(2)}) collective-permute-start(bf16[512,2048]{1,0:T(8,128)(2,1)} %collective-permute-done.4.refs_2_), channel_id=1, source_target_pairs={{2,3},{3,2},{4,5},{5,4},{10,11},{11,10},{12,13},{13,12},{18,19},{1... | collective-permute-start | bytes 6291464 | tf_op jit(solution)/shard_map/ppermute | solution.py:278
  53.7 9.3 %collective-permute-start.9 = (bf16[256,512]{1,0:T(8,128)(2,1)}, bf16[256,512]{1,0:T(8,128)(2,1)S(1)}, u32[]{:S(2)}, u32[]{:S(2)}) collective-permute-start(bf16[256,512]{1,0:T(8,128)(2,1)} %get-tuple-element.25), channel_id=1, source_target_pairs={{0,4},{4,0},{1,5},{5,1},{2,6},{6,2},{3,7},{7,3},{8,12},{12,8},{9,1... | collective-permute-start | bytes 786440 | tf_op jit(solution)/shard_map/ppermute | solution.py:298
  59.4 16.2 %collective-permute-start.7 = (bf16[512,1024]{1,0:T(8,128)(2,1)S(1)}, bf16[512,1024]{1,0:T(8,128)(2,1)}, u32[]{:S(2)}, u32[]{:S(2)}) collective-permute-start(bf16[512,1024]{1,0:T(8,128)(2,1)S(1)} %get-tuple-element.23), channel_id=1, source_target_pairs={{2,0},{3,1},{10,8},{11,9},{18,16},{19,17},{26,24},{27,25}} | collective-permute-start | bytes 3145736 | tf_op jit(solution)/shard_map/ppermute | solution.py:314
  60.7 17.3 %collective-permute-start.8 = (bf16[512,1024]{1,0:T(8,128)(2,1)}, bf16[512,1024]{1,0:T(8,128)(2,1)}, u32[]{:S(2)}, u32[]{:S(2)}) collective-permute-start(bf16[512,1024]{1,0:T(8,128)(2,1)} %get-tuple-element.24), channel_id=1, source_target_pairs={{2,4},{6,2},{3,5},{7,3},{10,12},{14,10},{11,13},{15,11},{18,20},{2... | collective-permute-start | bytes 3145736 | tf_op jit(solution)/shard_map/ppermute | solution.py:315
  63.8 118.2 %reduce-scatter.3.cloned.1.call-start = ((), (), s32[]{:S(2)}) async-start(), calls=%async_computation.4 | async-start | bytes 2621440 | tf_op jit(solution)/shard_map/reduce_scatter | solution.py:385
  75.5 11.9 %collective-permute-start.10 = (bf16[2048,512]{1,0:T(8,128)(2,1)}, bf16[2048,512]{1,0:T(8,128)(2,1)}, u32[]{:S(2)}, u32[]{:S(2)}) collective-permute-start(bf16[2048,512]{1,0:T(8,128)(2,1)} %all-gather.3.cloned.1.call-done.w_own.own_0), channel_id=1, source_target_pairs={{0,2},{2,0},{1,3},{3,1},{4,6},{6,4},{5,7},{7,5},{8,10},{10,8},{9,1... | collective-permute-start | bytes 6291464 | tf_op jit(solution)/shard_map/ppermute | solution.py:366
  85.0 21.6 %collective-permute-start.11 = (bf16[512,2048]{1,0:T(8,128)(2,1)}, bf16[512,2048]{1,0:T(8,128)(2,1)S(1)}, u32[]{:S(2)}, u32[]{:S(2)}) collective-permute-start(bf16[512,2048]{1,0:T(8,128)(2,1)} %get-tuple-element.28.enc_other), channel_id=1, source_target_pairs={{0,2},{2,0},{1,3},{3,1},{4,6},{6,4},{5,7},{7,5},{8,10},{10,8},{9,1... | collective-permute-start | bytes 6291464 | tf_op jit(solution)/shard_map/ppermute | solution.py:349
  114.6 97.5 %reduce-scatter.5.cloned.1.call-start = ((), (), s32[]{:S(2)}) async-start(), calls=%async_computation.5 | async-start | bytes 2621440 | tf_op jit(solution)/shard_map/reduce_scatter | solution.py:385
  121.8 4.4 %collective-permute-start.14 = (bf16[2048,512]{1,0:T(8,128)(2,1)}, bf16[2048,512]{1,0:T(8,128)(2,1)S(1)}, u32[]{:S(2)}, u32[]{:S(2)}) collective-permute-start(bf16[2048,512]{1,0:T(8,128)(2,1)} %all-gather.5.cloned.1.call-done.w_own.own_1), channel_id=1, source_target_pairs={{0,2},{2,0},{1,3},{3,1},{4,6},{6,4},{5,7},{7,5},{8,10},{10,8},{9,1... | collective-permute-start | bytes 6291464 | tf_op jit(solution)/shard_map/ppermute | solution.py:366
  144.1 14.2 %collective-permute-start.15 = (bf16[512,256]{1,0:T(8,128)(2,1)S(1)}, bf16[512,256]{1,0:T(8,128)(2,1)S(1)}, u32[]{:S(2)}, u32[]{:S(2)}) collective-permute-start(bf16[512,256]{1,0:T(8,128)(2,1)S(1)} %get-tuple-element.53), channel_id=1, source_target_pairs={{0,2},{2,0},{1,3},{3,1},{4,6},{6,4},{5,7},{7,5},{8,10},{10,8},{9,1... | collective-permute-start | bytes 786440 | tf_op jit(solution)/shard_map/ppermute | solution.py:376
  144.3 14.0 %collective-permute-start.16 = (bf16[512,256]{1,0:T(8,128)(2,1)S(1)}, bf16[512,256]{1,0:T(8,128)(2,1)S(1)}, u32[]{:S(2)}, u32[]{:S(2)}) collective-permute-start(bf16[512,256]{1,0:T(8,128)(2,1)S(1)} %get-tuple-element.54), channel_id=1, source_target_pairs={{0,2},{2,0},{1,3},{3,1},{4,6},{6,4},{5,7},{7,5},{8,10},{10,8},{9,1... | collective-permute-start | bytes 786440 | tf_op jit(solution)/shard_map/ppermute | solution.py:376
  165.8 12.9 %collective-permute-start.19 = (bf16[512,512]{1,0:T(8,128)(2,1)}, bf16[512,512]{1,0:T(8,128)(2,1)S(1)}, u32[]{:S(2)}, u32[]{:S(2)}) collective-permute-start(bf16[512,512]{1,0:T(8,128)(2,1)} %get-tuple-element.33), channel_id=1, source_target_pairs={{0,2},{1,3},{8,10},{9,11},{16,18},{17,19},{24,26},{25,27}} | collective-permute-start | bytes 1572872 | tf_op jit(solution)/shard_map/ppermute | solution.py:371
  168.1 74.5 %collective-permute-start.24 = (bf16[512,2048]{1,0:T(8,128)(2,1)S(1)}, bf16[512,2048]{1,0:T(8,128)(2,1)}, u32[]{:S(2)}, u32[]{:S(2)}) collective-permute-start(bf16[512,2048]{1,0:T(8,128)(2,1)S(1)} %copy-done.3), channel_id=1, source_target_pairs={{4,0},{5,1},{2,6},{3,7},{12,8},{13,9},{10,14},{11,15},{20,16},{21,... | collective-permute-start | bytes 6291464 | tf_op jit(solution)/shard_map/ppermute | solution.py:278
  169.4 73.2 %collective-permute-start.25 = (bf16[512,2048]{1,0:T(8,128)(2,1)}, bf16[512,2048]{1,0:T(8,128)(2,1)}, u32[]{:S(2)}, u32[]{:S(2)}) collective-permute-start(bf16[512,2048]{1,0:T(8,128)(2,1)} %enc_grad.3), channel_id=1, source_target_pairs={{4,1},{5,0},{2,7},{3,6},{12,9},{13,8},{10,15},{11,14},{20,17},{21,... | collective-permute-start | bytes 6291464 | tf_op jit(solution)/shard_map/ppermute | solution.py:278
  170.7 71.9 %collective-permute-start.23 = (bf16[512,2048]{1,0:T(8,128)(2,1)}, bf16[512,2048]{1,0:T(8,128)(2,1)}, u32[]{:S(2)}, u32[]{:S(2)}) collective-permute-start(bf16[512,2048]{1,0:T(8,128)(2,1)} %enc_grad.3), channel_id=1, source_target_pairs={{0,1},{1,0},{6,7},{7,6},{8,9},{9,8},{14,15},{15,14},{16,17},{17,16... | collective-permute-start | bytes 6291464 | tf_op jit(solution)/shard_map/ppermute | solution.py:278
  174.2 6.2 %collective-permute-start.20 = (bf16[512,512]{1,0:T(8,128)(2,1)}, bf16[512,512]{1,0:T(8,128)(2,1)S(1)}, u32[]{:S(2)}, u32[]{:S(2)}) collective-permute-start(bf16[512,512]{1,0:T(8,128)(2,1)} %get-tuple-element.34), channel_id=1, source_target_pairs={{0,2},{1,3},{8,10},{9,11},{16,18},{17,19},{24,26},{25,27}} | collective-permute-start | bytes 1572872 | tf_op jit(solution)/shard_map/ppermute | solution.py:371
  178.7 34.5 %collective-permute-start.21 = (bf16[512,512]{1,0:T(8,128)(2,1)}, bf16[512,512]{1,0:T(8,128)(2,1)}, u32[]{:S(2)}, u32[]{:S(2)}) collective-permute-start(bf16[512,512]{1,0:T(8,128)(2,1)} %get-tuple-element.33), channel_id=1, source_target_pairs={{4,2},{2,6},{5,3},{3,7},{12,10},{10,14},{13,11},{11,15},{20,18},{1... | collective-permute-start | bytes 1572872 | tf_op jit(solution)/shard_map/ppermute | solution.py:372
  180.4 43.4 %collective-permute-start.22 = (bf16[512,512]{1,0:T(8,128)(2,1)}, bf16[512,512]{1,0:T(8,128)(2,1)}, u32[]{:S(2)}, u32[]{:S(2)}) collective-permute-start(bf16[512,512]{1,0:T(8,128)(2,1)} %get-tuple-element.34), channel_id=1, source_target_pairs={{4,2},{2,6},{5,3},{3,7},{12,10},{10,14},{13,11},{11,15},{20,18},{1... | collective-permute-start | bytes 1572872 | tf_op jit(solution)/shard_map/ppermute | solution.py:372
  213.2 22.4 %collective-permute-start.17 = (bf16[256,512]{1,0:T(8,128)(2,1)}, bf16[256,512]{1,0:T(8,128)(2,1)S(1)}, u32[]{:S(2)}, u32[]{:S(2)}) collective-permute-start(bf16[256,512]{1,0:T(8,128)(2,1)} %get-tuple-element.50), channel_id=1, source_target_pairs={{0,4},{4,0},{1,5},{5,1},{2,6},{6,2},{3,7},{7,3},{8,12},{12,8},{9,1... | collective-permute-start | bytes 786440 | tf_op jit(solution)/shard_map/ppermute | solution.py:400
  223.8 17.2 %collective-permute-start.18 = (bf16[256,512]{1,0:T(8,128)(2,1)S(1)}, bf16[256,512]{1,0:T(8,128)(2,1)S(1)}, u32[]{:S(2)}, u32[]{:S(2)}) collective-permute-start(bf16[256,512]{1,0:T(8,128)(2,1)S(1)} %get-tuple-element.52), channel_id=1, source_target_pairs={{0,4},{4,0},{1,5},{5,1},{2,6},{6,2},{3,7},{7,3},{8,12},{12,8},{9,1... | collective-permute-start | bytes 786440 | tf_op jit(solution)/shard_map/ppermute | solution.py:400
  249.3 15.2 %collective-permute-start.26 = (bf16[512,2048]{1,0:T(8,128)(2,1)S(1)}, bf16[512,2048]{1,0:T(8,128)(2,1)}, u32[]{:S(2)}, u32[]{:S(2)}) collective-permute-start(bf16[512,2048]{1,0:T(8,128)(2,1)S(1)} %get-tuple-element.37), channel_id=1, source_target_pairs={{6,4},{7,5},{14,12},{15,13},{22,20},{23,21},{30,28},{31,29}} | collective-permute-start | bytes 6291464 | tf_op jit(solution)/shard_map/ppermute | solution.py:416
  251.3 3.2 %collective-permute-start.27 = (f32[2048]{0:T(1024)S(1)}, f32[2048]{0:T(1024)S(1)}, u32[]{:S(2)}, u32[]{:S(2)}) collective-permute-start(f32[2048]{0:T(1024)S(1)} %broadcast_select_fusion.5), channel_id=1, source_target_pairs={{0,6},{6,0},{2,4},{4,2},{1,7},{7,1},{3,5},{5,3},{8,14},{14,8},{10,... | collective-permute-start | bytes 24584 | tf_op jit(solution)/shard_map/ppermute | solution.py:419
  254.5 3.7 %collective-permute-start.28 = (f32[2048]{0:T(1024)S(1)}, f32[2048]{0:T(1024)S(1)}, u32[]{:S(2)}, u32[]{:S(2)}) collective-permute-start(f32[2048]{0:T(1024)S(1)} %fusion.12), channel_id=1, source_target_pairs={{0,8},{8,0},{16,24},{24,16},{1,9},{9,1},{17,25},{25,17},{2,10},{10... | collective-permute-start | bytes 24584 | tf_op jit(solution)/shard_map/ppermute | solution.py:422
  258.1 4.5 %collective-permute-start.29 = (f32[2048]{0:T(1024)S(1)}, f32[2048]{0:T(1024)S(1)}, u32[]{:S(2)}, u32[]{:S(2)}) collective-permute-start(f32[2048]{0:T(1024)S(1)} %add.52), channel_id=1, source_target_pairs={{0,16},{8,24},{16,0},{24,8},{1,17},{9,25},{17,1},{25,9},{2,18},{10... | collective-permute-start | bytes 24584 | tf_op jit(solution)/shard_map/ppermute | solution.py:422
  (10 other events, 83.0 us)
Sparse Core Ops, SparseCore 0:
  30.2 45.2 all-gather.2
  77.0 44.6 all-gather.4
  124.1 42.5 reduce-scatter.2
  168.9 43.1 reduce-scatter.4

commit v6 on v5

--- a/solution.py
+++ b/solution.py
@@ -36,12 +36,16 @@
     return pltpu.CompilerParams(vmem_limit_bytes=mib << 20)
 
 
+def chosen(kind, *values):
+    return jnp.where(kind == 0, values[0], jnp.where(kind == 1, values[1], values[2]))
+
+
 def norm_kernel(groups, rows, at, *refs):
-    nears, fars, (gain, own, other, inv_out, natural) = refs[:2], refs[2:4], refs[4:]
+    nears, fars, (gain, own, other, inv_out, natural) = refs[:3], refs[3:6], refs[6:]
     x, y, core = at[1], at[2], at[3]
     width = nears[0].shape[1]
-    near = jnp.where(at[0] == 1, *[r[...] for r in nears]).astype(F32)
-    far = jnp.where(at[0] == 1, *[r[...] for r in fars]).astype(F32)
+    near = chosen(at[0], *[r[...] for r in nears]).astype(F32)
+    far = chosen(at[0], *[r[...] for r in fars]).astype(F32)
     total = jnp.sum(near * near, axis=-1, keepdims=True) + jnp.sum(far * far, axis=-1, keepdims=True)
     inv_rms = lax.rsqrt(total / D + EPS)
     inv_out[...] = jnp.broadcast_to(inv_rms, inv_out.shape)
@@ -71,16 +75,16 @@
         grid_spec=pltpu.PrefetchScalarGridSpec(
             num_scalar_prefetch=1,
             grid=(length // step,),
-            in_specs=[pick(1), pick(0), pick(1), pick(0)] + [pl.BlockSpec((1, D), lambda i, s: (0, 0))],
+            in_specs=[pick(i % 3) for i in range(6)] + [pl.BlockSpec((1, D), lambda i, s: (0, 0))],
             out_specs=[out, out, pl.BlockSpec((step, 128), lambda i, s: (i, 0))],
             scratch_shapes=[pltpu.VMEM((step, D), BF16)],
         ),
         out_shape=[pltpu.HBM((length, D // 2), BF16)] * 2
         + [jax.ShapeDtypeStruct((length, 128), F32)],
-        compiler_params=params(32),
+        compiler_params=params(14),
         cost_estimate=cost(8 * length * D, 8),
         name="norm",
-    )(at, *in_hbm(*nears, *fars), gain)
+    )(at, *nears, *fars, gain)
 
 
 def attend_head(bias, qg, kv):
@@ -94,8 +98,7 @@
     weights = jnp.exp(scores - jnp.max(scores, axis=-1, keepdims=True))
     probs = weights * (1.0 / jnp.sum(weights, axis=-1, keepdims=True))
     prob_low = probs.astype(BF16)
-    attended = dot(prob_low, kv)
-    row_delta = jnp.sum(grads.astype(F32) * attended, axis=-1, keepdims=True)
+    row_delta = jnp.sum(prob_low.astype(F32) * grad_prob, axis=-1, keepdims=True)
     grad_score = (probs * (grad_prob - row_delta)).astype(BF16)
     grad_query = dot(grad_score, kv)
     qg_t = qg.T
@@ -107,13 +110,13 @@
 
 
 def attend_kernel(at, enc_own, enc_other, w_own, w_other, *refs):
-    qgs, (dec, gkv) = refs[:2], refs[2:]
+    qgs, (dec, gkv) = refs[:3], refs[3:]
     kv = (dot(enc_own[...], w_own[...]) + dot(enc_other[...], w_other[...])).astype(BF16)
     keys = lax.broadcasted_iota(jnp.int32, (1, kv.shape[0]), 1)
     bias = jnp.where(keys < at[4], 0.0, -1e30).astype(F32)
     for head in range(kv.shape[1] // (2 * HEAD)):
         lanes = slice(head * 2 * HEAD, (head + 1) * 2 * HEAD)
-        qg = jnp.where(at[0] == 1, *[r[:, lanes] for r in qgs])
+        qg = chosen(at[5], *[r[:, lanes] for r in qgs])
         dec[:, lanes], gkv[:, lanes] = attend_head(bias, qg, kv[:, lanes])
 
 
@@ -127,18 +130,18 @@
     out = pl.BlockSpec((length, step), lambda i, s: (0, i))
 
     def pick(want):
-        return pl.BlockSpec((length, step), lambda i, s: (0, jnp.where(s[0] == want, first + i, first)))
+        return pl.BlockSpec((length, step), lambda i, s: (0, jnp.where(s[5] == want, first + i, first)))
 
     return pl.pallas_call(
         attend_kernel,
         grid_spec=pltpu.PrefetchScalarGridSpec(
             num_scalar_prefetch=1,
             grid=(cols // step,),
-            in_specs=[enc, enc, weight, weight, pick(1), pick(0)],
+            in_specs=[enc, enc, weight, weight, pick(0), pick(1), pick(2)],
             out_specs=[out, out],
         ),
-        out_shape=[pltpu.HBM((length, cols), BF16)] * 2,
-        compiler_params=params(48),
+        out_shape=[jax.ShapeDtypeStruct((length, cols), BF16)] * 2,
+        compiler_params=params(26),
         cost_estimate=cost(
             length * cols * (4 * half + 14 * length), 8, length * length * cols // (2 * HEAD)
         ),
@@ -167,31 +170,37 @@
         ),
         out_shape=pltpu.HBM((half, cols), BF16),
         cost_estimate=cost(4 * length * half * cols // 64, 0),
-        compiler_params=params(32),
+        compiler_params=params(12),
         name="weight_grad",
-    )(at, *in_hbm(enc_a, enc_b, gkv_a, gkv_b))
+    )(at, *in_hbm(enc_a, enc_b), gkv_a, gkv_b)
 
 
 def collect_kernel(scale, at, *refs):
-    terms, (raw, inv, gain, out, gain_term) = refs[:4], refs[4:]
+    terms, (local, here, inv, gain, out, gain_term) = refs[:3], refs[3:]
     total = terms[0][...].astype(F32)
     for term in terms[1:]:
         total = total + term[...].astype(F32)
     out[...] = (total * gain[...]).astype(BF16)
-    product = total * (raw[...].astype(F32) * inv[:, :1])
+    raw = jnp.where(at[0] == 0, local[...], here[...]).astype(F32)
+    product = total * (raw * inv[:, :1])
     gain_term[0] = scale * jnp.sum(product, axis=0, keepdims=True)
 
 
-def collect(at, terms, raw, inv_rms, gain, scale):
-    length, width = raw.shape
+def collect(at, terms, local, here, inv_rms, gain, scale):
+    length, width = local.shape
     step = 128
     block = pl.BlockSpec((step, width), lambda i, s: (i, 0))
+
+    def pick(want):
+        return pl.BlockSpec((step, width), lambda i, s: (jnp.where(s[0] == want, i, 0), 0))
+
     return pl.pallas_call(
         lambda *refs: collect_kernel(scale, *refs),
         grid_spec=pltpu.PrefetchScalarGridSpec(
             num_scalar_prefetch=1,
             grid=(length // step,),
-            in_specs=[block] * 5
+            in_specs=[block] * 3
+            + [pick(0), pick(1)]
             + [
                 pl.BlockSpec((step, 128), lambda i, s: (i, 0)),
                 pl.BlockSpec((1, width), lambda i, s: (0, 0)),
@@ -203,9 +212,9 @@
             jax.ShapeDtypeStruct((length // step, 1, width), F32),
         ],
         cost_estimate=cost(8 * length * width, 12),
-        compiler_params=params(32),
+        compiler_params=params(16),
         name="collect",
-    )(at, *in_hbm(*terms, raw), inv_rms, gain)
+    )(at, *terms, local, here, inv_rms, gain)
 
 
 def enc_grad_kernel(at, gkv_0, gkv_1, own_0, own_1, other_0, other_1, out):
@@ -237,7 +246,7 @@
             out_specs=pl.BlockSpec((length, 2 * rows), lambda i, s: (0, i)),
         ),
         out_shape=pltpu.HBM((length, D // 2), BF16),
-        compiler_params=params(32),
+        compiler_params=params(12),
         cost_estimate=cost(4 * length * D * cols, 8),
         name="enc_grad",
     )(at, *in_hbm(*gkvs, *owns, *others))
@@ -287,20 +296,23 @@
     def slots(block):
         return [lax.ppermute(block, "z", turned(groups, -s)) for s in range(1, groups)]
 
-    gains = [gain] + [lax.ppermute(gain, "mp", turned(shards, t)) for t in range(1, shards)]
-    key_count = jnp.where(straight, src_len, lax.ppermute(src_len, "y", SWAP))
-
-    here = jnp.where(y == 0, packed, lax.ppermute(packed, PLANE, [(2, 3)]))
     swapped = [lax.ppermute(chunk_of(1 - y, 0), "y", SWAP)]
-    there = after(packed, swapped[0], key_count, here, *gains)
-    there = lax.ppermute(there, PLANE, [(0, 2), (2, 1)])
+    here = lax.ppermute(packed, PLANE, [(2, 3)])
+    gain_sent, len_sent = lax.optimization_barrier((gain, src_len, here))[:2]
+    gains = [gain] + [lax.ppermute(gain_sent, "mp", turned(shards, t)) for t in range(1, shards)]
+    key_count = jnp.where(straight, src_len, lax.ppermute(len_sent, "y", SWAP))
+    there = lax.ppermute(after(packed, swapped[0], key_count, *gains), PLANE, [(0, 2), (2, 1)])
     for k in range(1, CHUNKS):
         swapped.append(lax.ppermute(after(chunk_of(1 - y, k), there), "y", SWAP))
-    nears = [here, there]
+    nears = [packed, here, there]
     fars = []
     for turn in range(1, shards):
         fars.append(
-            [across(here, turn, [(0, 0), (3, 3)]), across(there, turn, [(1, 1), (2, 2)])]
+            [
+                across(packed, turn, [(0, 0)]),
+                across(here, turn, [(3, 3)]),
+                across(there, turn, [(1, 1), (2, 2)]),
+            ]
         )
     blocks = [jnp.concatenate([chunk_of(y, k), swapped[k]], 0) for k in range(CHUNKS)]
     w_own, w_other = [], []
@@ -311,11 +323,14 @@
     qg_near, qg_far = cut(masked, 1, y, half), cut(masked, 1, 1 - y, half)
     qg_near, qg_far = lax.optimization_barrier((qg_near, qg_far, there))[:2]
     qgs = [
-        jnp.where(y == 1, qg_near, lax.ppermute(qg_near, PLANE, [(1, 0)])),
+        qg_near,
+        lax.ppermute(qg_near, PLANE, [(1, 0)]),
         lax.ppermute(qg_far, PLANE, [(1, 2), (3, 1)]),
     ]
+    enc_kind = jnp.where(straight, y, 2)
+    qg_kind = jnp.where(straight, 1 - y, 2)
     at = jnp.concatenate(
-        [jnp.stack([straight.astype(jnp.int32), x, y, core]).astype(jnp.int32), key_count]
+        [jnp.stack([enc_kind, x, y, core]).astype(jnp.int32), key_count, qg_kind[None]]
     )
 
     def natural(parts, axis):
@@ -340,7 +355,7 @@
             at, nears, fars[0], after(gain_all[None], *qgs, *blocks), groups, rows
         )
     else:
-        raw = [jnp.where(straight, *parts) for parts in [nears] + fars]
+        raw = [chosen(enc_kind, *parts) for parts in [nears] + fars]
         hidden = natural(raw, 1).astype(F32)
         inv_rms = lax.rsqrt(jnp.sum(hidden * hidden, axis=-1, keepdims=True) / D + EPS)
         encoded = (hidden * inv_rms * gain_all).astype(BF16)
@@ -368,16 +383,19 @@
         gkvs.append(gkv)
         decs.append(
             (
-                jnp.where(y == 0, lax.ppermute(dec, PLANE, [(0, 1)]), dec),
+                lax.ppermute(dec, PLANE, [(0, 1)]),
+                dec,
                 lax.ppermute(dec, PLANE, [(2, 1), (1, 3)]),
             )
         )
-        parts = jnp.split(gkv, 2, axis=1)
+        if tiled and k == CHUNKS - 1:
+            terms = [enc_grad(at, gkvs, w_own, w_other, groups, rows, s) for s in (1, 0)][::-1]
+            gkv_sent = after(gkv, *terms)
+        else:
+            gkv_sent = gkv
+        parts = jnp.split(gkv_sent, 2, axis=1)
         gkv_mate = jnp.concatenate([lax.ppermute(p, "phase", SWAP) for p in parts], 1)
         if tiled:
-            if k == CHUNKS - 1:
-                terms = [enc_grad(at, gkvs, w_own, w_other, groups, rows, s) for s in (1, 0)][::-1]
-                gkv_mate = after(gkv_mate, *terms)
             grad = weight_grad(at, enc_own, enc_mate, gkv, gkv_mate, groups, pair_scale)
         else:
             grad = pair_scale * (dot(enc_own, gkv, TN) + dot(enc_mate, gkv_mate, TN))
@@ -390,20 +408,22 @@
         back = jnp.zeros_like(block_order).at[block_order].set(jnp.arange(block_order.shape[0]))
         full = full.astype(BF16).reshape(length, -1, rows)[:, back].reshape(length, D)
         terms = [cut(full, 1, (x + s) % shards, width) for s in range(shards)]
+    far_terms = terms[0].astype(F32)
+    for turn in range(1, shards):
+        far_terms = far_terms + across(terms[turn], turn, [(1, 1), (2, 2)]).astype(F32)
     moved = [across(terms[turn], turn, [(0, 0), (3, 3)]) for turn in range(1, shards)]
-    moved += [across(terms[turn], turn, [(2, 0), (1, 3)]) for turn in range(shards)]
-
-    dec_here = jnp.concatenate([d[0] for d in decs], 1)
-    dec_there = jnp.concatenate([d[1] for d in decs], 1)
+    moved.append(lax.ppermute(far_terms.astype(BF16), PLANE, [(2, 0), (1, 3)]))
+
+    dec_here = jnp.concatenate([jnp.where(y == 0, d[0], d[1]) for d in decs], 1)
+    dec_there = jnp.concatenate([d[2] for d in decs], 1)
     dec_grads = ordered(y == 0, dec_here, dec_there, 1)
     kept = jnp.concatenate([w[:rows] for w in weight_sums], 1)
     got = [lax.ppermute(w[rows:], "y", SWAP) for w in weight_sums]
     got = jnp.concatenate(got, 1)
     d_wkv = ordered(y == 0, kept, got, 1).astype(F32)
     if tiled:
-        terms[0], d_wkv, dec_grads = lax.optimization_barrier((terms[0], d_wkv, dec_grads))
         grad_normed, gain_term = collect(
-            at, [terms[0]] + moved, here, inv_rms, gain.astype(F32)[None], pair_scale
+            at, [terms[0]] + moved, packed, here, inv_rms, gain.astype(F32)[None], pair_scale
         )
         gain_term = jnp.sum(gain_term, axis=(0, 1))
     else:

time: 275 us -> 261 us (0.949)
  starting transfers between devices: 65.9 us -> 55.5 us
  waiting for transfers between devices: 88.2 us -> 97.1 us
  local copies, waits for them, and re-layouts: 13.8 us -> 8.39 us
  Pallas kernels: 71.4 us -> 68.4 us
    reduce_scatter x2, waiting for transfers between devices: 28.4 us -> 0.01 us  [on_device(): lax.psum_scatter(grad, 'z', scatter_dimension=0, tiled=True)]
    ppermute x5, waiting for transfers between devices: 0.01 us -> 24.7 us  [across(): lax.ppermute(value, ('y', 'phase', 'mp'), [(a * shards + s, b * shards +...]
    ppermute x2, starting transfers between devices: 19 us -> 2.09 us  [on_device(): got = [lax.ppermute(w[rows:], 'y', SWAP) for w in weight_sums]]
    ppermute x4 -> x5, waiting for transfers between devices: 19.2 us -> 30.5 us  [the longest x1 14.6 us: on_device(): lax.ppermute(after(packed, swapped[0], key_count, *gains), PLANE, [(0, 2)...]
    ppermute x1, waiting for transfers between devices: 0.54 us -> 6.66 us  [on_device(): swapped.append(lax.ppermute(after(chunk_of(1 - y, k), there), 'y', SWAP))]
    ppermute x2, waiting for transfers between devices: 5.49 us -> 10.8 us  [on_device(): got = [lax.ppermute(w[rows:], 'y', SWAP) for w in weight_sums]]
    ppermute x2, waiting for transfers between devices: 7.19 us -> 2.06 us  [on_device(): lax.ppermute(gain_term, 'z', [(i, i ^ turn) for i in range(groups)])]
    ppermute x1, starting transfers between devices: 0.08 us -> 4.05 us  [on_device(): swapped = [lax.ppermute(chunk_of(1 - y, 0), 'y', SWAP)]]
  transfers between devices with their start and end apart: 35 -> 36, of which waited for: 15 -> 16; matrix products, arithmetic and copies ran while one was open for 9% -> 6% of each run, Pallas kernels for 24% -> 26%
where the time goes in v6:
time: 261 us; the launch traced here: 260 us
  waiting for transfers between devices  97.1 us (37%)
  Pallas kernels  68.4 us (26%)
  starting transfers between devices  55.5 us (21%)
  between operations  16.1 us (6%)
  other arithmetic  14.6 us (6%)
  local copies, waits for them, and re-layouts  8.39 us (3%)
    pallas_call x2, Pallas kernels, attend(): pl.pallas_call(attend_kernel, grid_spec=pltpu.PrefetchScalarGridSpec(num_...  30.1 us
    ppermute x5, waiting for transfers between devices, across(): lax.ppermute(value, ('y', 'phase', 'mp'), [(a * shards + s, b * shards +...  24.7 us
    all_gather x2, waiting for transfers between devices, on_device(): w_own.append(lax.all_gather(block, 'z', axis=0, tiled=True))  15.2 us
    ppermute x1, waiting for transfers between devices, on_device(): lax.ppermute(after(packed, swapped[0], key_count, *gains), PLANE, [(0, 2)...  14.6 us
    pallas_call x2, Pallas kernels, enc_grad(): pl.pallas_call(enc_grad_kernel, grid_spec=pltpu.PrefetchScalarGridSpec(nu...  13.7 us
    ppermute x1, waiting for transfers between devices, on_device(): moved.append(lax.ppermute(far_terms.astype(BF16), PLANE, [(2, 0), (1, 3)]))  12.8 us
    pallas_call x2, Pallas kernels, weight_grad(): pl.pallas_call(lambda *refs: weight_grad_kernel(scale, *refs), grid_spec=...  12.6 us
    ppermute x5, starting transfers between devices, across(): lax.ppermute(value, ('y', 'phase', 'mp'), [(a * shards + s, b * shards +...  12.1 us
  transfers between devices with their start and end apart: 36, of which 16 were waited for; matrix products, arithmetic and copies ran while one was open for 6% of the time, Pallas kernels for 26%

profile of v6, /device:TPU:0, one launch (start us, length us, event | category | flops | bytes accessed | tf_op | source)
XLA Modules:
  0.0 260.0 jit_solution(2163656868097462894)
XLA Ops:
  7.2 2.2 collective-permute-start
  9.4 2.0 constant_dynamic-slice_fusion.1
  11.4 4.0 %collective-permute-start.2 = (bf16[256,512]{1,0:T(8,128)(2,1)S(1)}, bf16[256,512]{1,0:T(8,128)(2,1)S(1)}, u32[]{:S(2)}, u32[]{:S(2)}) collective-permute-start(bf16[256,512]{1,0:T(8,128)(2,1)S(1)} %get-tuple-element.43), channel_id=1, source_target_pairs={{0,4},{4,0},{1,5},{5,1},{2,6},{6,2},{3,7},{7,3},{8,12},{12,8},{9,1... | collective-permute-start | bytes 786440 | tf_op jit(solution)/shard_map/ppermute | solution.py:299
  18.4 3.0 %collective-permute-done.1 = s32[1]{0:T(128)} collective-permute-done((s32[1]{0:T(128)}, s32[1]{0:T(128)}, u32[]{:S(2)}, u32[]{:S(2)}) %collective-permute-start.1) | collective-permute-done | bytes 36 | tf_op jit(solution)/shard_map/ppermute | solution.py:303
  22.1 4.1 %collective-permute-start.4 = (bf16[512,2048]{1,0:T(8,128)(2,1)S(1)}, bf16[512,2048]{1,0:T(8,128)(2,1)}, u32[]{:S(2)}, u32[]{:S(2)}) collective-permute-start(bf16[512,2048]{1,0:T(8,128)(2,1)S(1)} %bitcast.13), channel_id=1, source_target_pairs={{0,4},{4,2},{1,5},{5,3},{8,12},{12,10},{9,13},{13,11},{16,20},{20,... | collective-permute-start | bytes 6291464 | tf_op jit(solution)/shard_map/ppermute | solution.py:304
  27.0 3.2 %collective-permute-start.5 = (bf16[512,2048]{1,0:T(8,128)(2,1)S(1)}, bf16[512,2048]{1,0:T(8,128)(2,1)}, u32[]{:S(2)}, u32[]{:S(2)}) collective-permute-start(bf16[512,2048]{1,0:T(8,128)(2,1)S(1)} %bitcast.14), channel_id=1, source_target_pairs={{0,1},{1,0},{8,9},{9,8},{16,17},{17,16},{24,25},{25,24}} | collective-permute-start | bytes 6291464 | tf_op jit(solution)/shard_map/ppermute | solution.py:287
  31.6 2.1 collective-permute-start.6
  33.7 14.6 %collective-permute-done.4.refs_3_ = bf16[512,2048]{1,0:T(8,128)(2,1)} collective-permute-done((bf16[512,2048]{1,0:T(8,128)(2,1)S(1)}, bf16[512,2048]{1,0:T(8,128)(2,1)}, u32[]{:S(2)}, u32[]{:S(2)}) %collective-permute-start.4) | collective-permute-done | bytes 2097184 | tf_op jit(solution)/shard_map/ppermute | solution.py:304
  52.7 4.1 %collective-permute-start.10 = (bf16[256,512]{1,0:T(8,128)(2,1)S(1)}, bf16[256,512]{1,0:T(8,128)(2,1)S(1)}, u32[]{:S(2)}, u32[]{:S(2)}) collective-permute-start(bf16[256,512]{1,0:T(8,128)(2,1)S(1)} %copy-done.8), channel_id=1, source_target_pairs={{0,4},{4,0},{1,5},{5,1},{2,6},{6,2},{3,7},{7,3},{8,12},{12,8},{9,1... | collective-permute-start | bytes 786440 | tf_op jit(solution)/shard_map/ppermute | solution.py:306
  56.9 6.7 %collective-permute-done.10 = bf16[256,512]{1,0:T(8,128)(2,1)S(1)} collective-permute-done((bf16[256,512]{1,0:T(8,128)(2,1)S(1)}, bf16[256,512]{1,0:T(8,128)(2,1)S(1)}, u32[]{:S(2)}, u32[]{:S(2)}) %collective-permute-start.10) | collective-permute-done | bytes 262176 | tf_op jit(solution)/shard_map/ppermute | solution.py:306
  66.1 7.1 %all-gather.3.cloned.1.call-done.w_own.own_0 = bf16[2048,512]{1,0:T(8,128)(2,1)} async-done(((bf16[512,512]{1,0:T(8,128)(2,1)}), bf16[2048,512]{1,0:T(8,128)(2,1)}) %all-gather.3.cloned.1.call-update) | async-done | bytes 2097168 | tf_op jit(solution)/shard_map/all_gather | solution.py:378
  73.4 7.0 %norm.1 = (bf16[512,2048]{1,0:T(8,128)(2,1)}, bf16[512,2048]{1,0:T(8,128)(2,1)}, f32[512,128]{1,0:T(8,128)S(1)}) custom-call(s32[6]{0:T(128)S(1)} %concatenate.59.refs_0_.at, bf16[512,2048]{1,0:T(8,128)(2,1)S(1)} %bitcast.15, bf16[512,2048]{1,0:T(8,128)(2,1)} %collective-permute-done.refs_2_.refs_5_, bf16[512,2048]{1,0:T(8,128)(2,1)} %collective-permute-done.4.refs_3_, ...), custom_call_target="tpu_custom_call" | custom-call | flops 16777216 | bytes 8388608 | tf_op jit(solution)/shard_map/norm/pallas_call | solution.py:73
  80.3 6.2 %collective-permute-start.12 = (bf16[512,2048]{1,0:T(8,128)(2,1)}, bf16[512,2048]{1,0:T(8,128)(2,1)S(1)}, u32[]{:S(2)}, u32[]{:S(2)}) collective-permute-start(bf16[512,2048]{1,0:T(8,128)(2,1)} %get-tuple-element.29.enc_other), channel_id=1, source_target_pairs={{0,2},{2,0},{1,3},{3,1},{4,6},{6,4},{5,7},{7,5},{8,10},{10,8},{9,1... | collective-permute-start | bytes 6291464 | tf_op jit(solution)/shard_map/ppermute | solution.py:364
  86.6 14.9 %attend.2 = (bf16[512,512]{1,0:T(8,128)(2,1)S(1)}, bf16[512,512]{1,0:T(8,128)(2,1)S(1)}) custom-call(s32[6]{0:T(128)S(1)} %concatenate.59.refs_0_.at, bf16[512,2048]{1,0:T(8,128)(2,1)} %get-tuple-element.28.enc_own.refs_1_, bf16[512,2048]{1,0:T(8,128)(2,1)} %get-tuple-element.29.enc_other, bf16[2048,512]{1,0:T(8,128)(2,1)} %all-gather.3.cloned.1.call-done.w_own.own_0, ...), custom_call_target="tpu_custom_call" | custom-call | flops 4026531840 | bytes 8388608 | tf_op jit(solution)/shard_map/attend/pallas_call | solution.py:135
  104.9 6.3 %weight_grad.2 = bf16[2048,512]{1,0:T(8,128)(2,1)} custom-call(s32[6]{0:T(128)S(1)} %concatenate.59.refs_0_.at, bf16[512,2048]{1,0:T(8,128)(2,1)} %get-tuple-element.28.enc_own.refs_1_, bf16[512,2048]{1,0:T(8,128)(2,1)} %copy-done.5, bf16[512,512]{1,0:T(8,128)(2,1)S(1)} %get-tuple-element.30.refs_3_.gkv_0, bf16[512,512]{1,0:T(8,128)(2,1)S(1)} %pad_maximum_fusion.2.refs_4_), custom_call_target="tpu_custom_call" | custom-call | flops 33554432 | tf_op jit(solution)/shard_map/weight_grad/pallas_call | solution.py:163
  111.2 8.2 %all-gather.5.cloned.1.call-done.w_own.own_1 = bf16[2048,512]{1,0:T(8,128)(2,1)} async-done(((bf16[512,512]{1,0:T(8,128)(2,1)}), bf16[2048,512]{1,0:T(8,128)(2,1)}) %all-gather.5.cloned.1.call-update) | async-done | bytes 2097168 | tf_op jit(solution)/shard_map/all_gather | solution.py:378
  119.6 4.2 %collective-permute-done.15.w_other.other_1 = bf16[2048,512]{1,0:T(8,128)(2,1)} collective-permute-done((bf16[2048,512]{1,0:T(8,128)(2,1)}, bf16[2048,512]{1,0:T(8,128)(2,1)}, u32[]{:S(2)}, u32[]{:S(2)}) %collective-permute-start.15) | collective-permute-done | bytes 2097184 | tf_op jit(solution)/shard_map/ppermute | solution.py:381
  123.9 15.2 %attend.3 = (bf16[512,512]{1,0:T(8,128)(2,1)S(1)}, bf16[512,512]{1,0:T(8,128)(2,1)S(1)}) custom-call(s32[6]{0:T(128)S(1)} %concatenate.59.refs_0_.at, bf16[512,2048]{1,0:T(8,128)(2,1)} %get-tuple-element.28.enc_own.refs_1_, bf16[512,2048]{1,0:T(8,128)(2,1)} %get-tuple-element.29.enc_other, bf16[2048,512]{1,0:T(8,128)(2,1)} %all-gather.5.cloned.1.call-done.w_own.own_1, ...), custom_call_target="tpu_custom_call" | custom-call | flops 4026531840 | bytes 8388608 | tf_op jit(solution)/shard_map/attend/pallas_call | solution.py:135
  139.9 6.9 %enc_grad.3 = bf16[512,2048]{1,0:T(8,128)(2,1)} custom-call(s32[6]{0:T(128)S(1)} %concatenate.59.refs_0_.at, bf16[512,512]{1,0:T(8,128)(2,1)} %copy-done.2, bf16[512,512]{1,0:T(8,128)(2,1)} %copy-done.3, bf16[2048,512]{1,0:T(8,128)(2,1)} %all-gather.3.cloned.1.call-done.w_own.own_0, bf16[2048,512]{1,0:T(8,128)(2,1)} %all-gather.5.cloned.1.call-done.w_own.own_1, ...), custom_call_target="tpu_custom_call" | custom-call | flops 4294967296 | bytes 8388608 | tf_op jit(solution)/shard_map/enc_grad/pallas_call | solution.py:240
  146.8 2.1 collective-permute-start.17
  148.9 6.8 %enc_grad.2.refs_1_ = bf16[512,2048]{1,0:T(8,128)(2,1)} custom-call(s32[6]{0:T(128)S(1)} %concatenate.59.refs_0_.at, bf16[512,512]{1,0:T(8,128)(2,1)} %copy-done.2, bf16[512,512]{1,0:T(8,128)(2,1)} %copy-done.3, bf16[2048,512]{1,0:T(8,128)(2,1)} %all-gather.3.cloned.1.call-done.w_own.own_0, bf16[2048,512]{1,0:T(8,128)(2,1)} %all-gather.5.cloned.1.call-done.w_own.own_1, ...), custom_call_target="tpu_custom_call" | custom-call | flops 4294967296 | bytes 8388608 | tf_op jit(solution)/shard_map/enc_grad/pallas_call | solution.py:240
  158.5 6.3 %weight_grad.3 = bf16[2048,512]{1,0:T(8,128)(2,1)} custom-call(s32[6]{0:T(128)S(1)} %concatenate.59.refs_0_.at, bf16[512,2048]{1,0:T(8,128)(2,1)} %get-tuple-element.28.enc_own.refs_1_, bf16[512,2048]{1,0:T(8,128)(2,1)} %copy-done.5, bf16[512,512]{1,0:T(8,128)(2,1)S(1)} %copy-done.4, bf16[512,512]{1,0:T(8,128)(2,1)S(1)} %pad_maximum_fusion.3.refs_4_), custom_call_target="tpu_custom_call" | custom-call | flops 33554432 | tf_op jit(solution)/shard_map/weight_grad/pallas_call | solution.py:163
  164.8 2.8 %collective-permute-start.16 = (bf16[512,2048]{1,0:T(8,128)(2,1)}, bf16[512,2048]{1,0:T(8,128)(2,1)S(1)}, u32[]{:S(2)}, u32[]{:S(2)}) collective-permute-start(bf16[512,2048]{1,0:T(8,128)(2,1)} %enc_grad.3), channel_id=1, source_target_pairs={{0,1},{1,0},{6,7},{7,6},{8,9},{9,8},{14,15},{15,14},{16,17},{17,16... | collective-permute-start | bytes 6291464 | tf_op jit(solution)/shard_map/ppermute | solution.py:287
  167.6 3.0 %add_convert_fusion = bf16[512,2048]{1,0:T(8,128)(2,1)S(1)} fusion(bf16[512,2048]{1,0:T(8,128)(2,1)} %collective-permute-done.17, bf16[512,2048]{1,0:T(8,128)(2,1)} %enc_grad.2.refs_1_), kind=kLoop, calls=%fused_computation | loop fusion | flops 4194304 | bytes 6291456 | tf_op jit(solution)/shard_map/convert_element_type | solution.py:415
  172.0 24.7 %collective-permute-done.16.refs_2_ = bf16[512,2048]{1,0:T(8,128)(2,1)S(1)} collective-permute-done((bf16[512,2048]{1,0:T(8,128)(2,1)}, bf16[512,2048]{1,0:T(8,128)(2,1)S(1)}, u32[]{:S(2)}, u32[]{:S(2)}) %collective-permute-start.16) | collective-permute-done | bytes 2097184 | tf_op jit(solution)/shard_map/ppermute | solution.py:287
  196.6 12.8 %collective-permute-done.18.refs_3_ = bf16[512,2048]{1,0:T(8,128)(2,1)S(1)} collective-permute-done((bf16[512,2048]{1,0:T(8,128)(2,1)S(1)}, bf16[512,2048]{1,0:T(8,128)(2,1)S(1)}, u32[]{:S(2)}, u32[]{:S(2)}) %collective-permute-start.18) | collective-permute-done | bytes 2097184 | tf_op jit(solution)/shard_map/ppermute | solution.py:415
  209.5 5.1 %collect.1 = (bf16[512,2048]{1,0:T(8,128)(2,1)}, f32[4,1,2048]{2,1,0:T(1,128)S(1)}) custom-call(s32[6]{0:T(128)S(1)} %concatenate.59.refs_0_.at, bf16[512,2048]{1,0:T(8,128)(2,1)S(1)} %copy-done.1, bf16[512,2048]{1,0:T(8,128)(2,1)S(1)} %collective-permute-done.16.refs_2_, bf16[512,2048]{1,0:T(8,128)(2,1)S(1)} %collective-permute-done.18.refs_3_, ...), custom_call_target="tpu_custom_call" | custom-call | flops 8388608 | bytes 12582912 | tf_op jit(solution)/shard_map/collect/pallas_call | solution.py:197
  215.4 2.1 collective-permute-start.20
  219.3 4.8 %collective-permute-start.21 = (bf16[512,512]{1,0:T(8,128)(2,1)S(1)}, bf16[512,512]{1,0:T(8,128)(2,1)}, u32[]{:S(2)}, u32[]{:S(2)}) collective-permute-start(bf16[512,512]{1,0:T(8,128)(2,1)S(1)} %get-tuple-element.36), channel_id=1, source_target_pairs={{0,2},{1,3},{8,10},{9,11},{16,18},{17,19},{24,26},{25,27}} | collective-permute-start | bytes 1572872 | tf_op jit(solution)/shard_map/ppermute | solution.py:386
  237.2 5.6 %collective-permute-done.26 = bf16[256,512]{1,0:T(8,128)(2,1)S(1)} collective-permute-done((bf16[256,512]{1,0:T(8,128)(2,1)}, bf16[256,512]{1,0:T(8,128)(2,1)S(1)}, u32[]{:S(2)}, u32[]{:S(2)}) %collective-permute-start.26) | collective-permute-done | bytes 262176 | tf_op jit(solution)/shard_map/ppermute | solution.py:421
  242.8 5.2 %collective-permute-done.27 = bf16[256,512]{1,0:T(8,128)(2,1)S(1)} collective-permute-done((bf16[256,512]{1,0:T(8,128)(2,1)S(1)}, bf16[256,512]{1,0:T(8,128)(2,1)S(1)}, u32[]{:S(2)}, u32[]{:S(2)}) %collective-permute-start.27) | collective-permute-done | bytes 262176 | tf_op jit(solution)/shard_map/ppermute | solution.py:421
  249.6 3.8 %fusion.3 = bf16[1,1,512,2048]{3,2,1,0:T(8,128)(2,1)} fusion(bf16[512,512]{1,0:T(8,128)(2,1)} %collective-permute-done.23, bf16[512,512]{1,0:T(8,128)(2,1)} %collective-permute-done.22, bf16[512,512]{1,0:T(8,128)(2,1)S(1)} %broadcast_select_fusion, bf16[512,512]{1,0:T(8,128)(2,1)S(1)} %copy-done.6, bf16[512,2048]{1,0:T(8,128)(2,1)} %get-tuple-element.34, ...), kind=kLoop, calls=%fused_computation.6 | loop fusion | flops 19922944 | bytes 8388610 | tf_op jit(solution)/shard_map/broadcast_in_dim | solution.py:446
  (102 shorter events, 37.0 us)
Async XLA Ops:
  7.2 66.0 %all-gather.3.cloned.1.call-start = ((), (), s32[]{:S(2)}) async-start(), calls=%async_computation.2 | async-start | bytes 2621440 | tf_op jit(solution)/shard_map/all_gather | solution.py:378
  7.2 8.2 %collective-permute-start = (bf16[512,2048]{1,0:T(8,128)(2,1)}, bf16[512,2048]{1,0:T(8,128)(2,1)}, u32[]{:S(2)}, u32[]{:S(2)}) collective-permute-start(bf16[512,2048]{1,0:T(8,128)(2,1)} %bitcast.12), channel_id=1, source_target_pairs={{4,6},{5,7},{12,14},{13,15},{20,22},{21,23},{28,30},{29,31}} | collective-permute-start | bytes 6291464 | tf_op jit(solution)/shard_map/ppermute | solution.py:300
  11.4 10.7 %collective-permute-start.2 = (bf16[256,512]{1,0:T(8,128)(2,1)S(1)}, bf16[256,512]{1,0:T(8,128)(2,1)S(1)}, u32[]{:S(2)}, u32[]{:S(2)}) collective-permute-start(bf16[256,512]{1,0:T(8,128)(2,1)S(1)} %get-tuple-element.43), channel_id=1, source_target_pairs={{0,4},{4,0},{1,5},{5,1},{2,6},{6,2},{3,7},{7,3},{8,12},{12,8},{9,1... | collective-permute-start | bytes 786440 | tf_op jit(solution)/shard_map/ppermute | solution.py:299
  15.4 6.6 %collective-permute-start.3 = (bf16[2048]{0:T(1024)(128)(2,1)S(1)}, bf16[2048]{0:T(1024)(128)(2,1)S(1)}, u32[]{:S(2)}, u32[]{:S(2)}) collective-permute-start(bf16[2048]{0:T(1024)(128)(2,1)S(1)} %copy-done.9), channel_id=1, source_target_pairs={{0,1},{1,0},{2,3},{3,2},{4,5},{5,4},{6,7},{7,6},{8,9},{9,8},{10,11... | collective-permute-start | bytes 12296 | tf_op jit(solution)/shard_map/ppermute | solution.py:302
  17.6 3.8 %collective-permute-start.1 = (s32[1]{0:T(128)}, s32[1]{0:T(128)}, u32[]{:S(2)}, u32[]{:S(2)}) collective-permute-start(s32[1]{0:T(128)} %param.8), channel_id=1, source_target_pairs={{0,4},{4,0},{1,5},{5,1},{2,6},{6,2},{3,7},{7,3},{8,12},{12,8},{9,1... | collective-permute-start | bytes 20 | tf_op jit(solution)/shard_map/ppermute | solution.py:303
  22.1 26.2 %collective-permute-start.4 = (bf16[512,2048]{1,0:T(8,128)(2,1)S(1)}, bf16[512,2048]{1,0:T(8,128)(2,1)}, u32[]{:S(2)}, u32[]{:S(2)}) collective-permute-start(bf16[512,2048]{1,0:T(8,128)(2,1)S(1)} %bitcast.13), channel_id=1, source_target_pairs={{0,4},{4,2},{1,5},{5,3},{8,12},{12,10},{9,13},{13,11},{16,20},{20,... | collective-permute-start | bytes 6291464 | tf_op jit(solution)/shard_map/ppermute | solution.py:304
  27.0 92.4 %all-gather.5.cloned.1.call-start = ((), (), s32[]{:S(2)}) async-start(), calls=%async_computation.3 | async-start | bytes 2621440 | tf_op jit(solution)/shard_map/all_gather | solution.py:378
  27.0 46.3 %collective-permute-start.5 = (bf16[512,2048]{1,0:T(8,128)(2,1)S(1)}, bf16[512,2048]{1,0:T(8,128)(2,1)}, u32[]{:S(2)}, u32[]{:S(2)}) collective-permute-start(bf16[512,2048]{1,0:T(8,128)(2,1)S(1)} %bitcast.14), channel_id=1, source_target_pairs={{0,1},{1,0},{8,9},{9,8},{16,17},{17,16},{24,25},{25,24}} | collective-permute-start | bytes 6291464 | tf_op jit(solution)/shard_map/ppermute | solution.py:287
  31.6 41.8 %collective-permute-start.6 = (bf16[512,2048]{1,0:T(8,128)(2,1)}, bf16[512,2048]{1,0:T(8,128)(2,1)}, u32[]{:S(2)}, u32[]{:S(2)}) collective-permute-start(bf16[512,2048]{1,0:T(8,128)(2,1)} %collective-permute-done.refs_2_.refs_5_), channel_id=1, source_target_pairs={{6,7},{7,6},{14,15},{15,14},{22,23},{23,22},{30,31},{31,30}} | collective-permute-start | bytes 6291464 | tf_op jit(solution)/shard_map/ppermute | solution.py:287
  48.3 25.0 %collective-permute-start.7 = (bf16[512,2048]{1,0:T(8,128)(2,1)}, bf16[512,2048]{1,0:T(8,128)(2,1)}, u32[]{:S(2)}, u32[]{:S(2)}) collective-permute-start(bf16[512,2048]{1,0:T(8,128)(2,1)} %collective-permute-done.4.refs_3_), channel_id=1, source_target_pairs={{2,3},{3,2},{4,5},{5,4},{10,11},{11,10},{12,13},{13,12},{18,19},{1... | collective-permute-start | bytes 6291464 | tf_op jit(solution)/shard_map/ppermute | solution.py:287
  51.4 21.7 %collective-permute-start.8 = (bf16[512,1024]{1,0:T(8,128)(2,1)S(1)}, bf16[512,1024]{1,0:T(8,128)(2,1)}, u32[]{:S(2)}, u32[]{:S(2)}) collective-permute-start(bf16[512,1024]{1,0:T(8,128)(2,1)S(1)} %get-tuple-element.24.refs_0_), channel_id=1, source_target_pairs={{2,0},{3,1},{10,8},{11,9},{18,16},{19,17},{26,24},{27,25}} | collective-permute-start | bytes 3145736 | tf_op jit(solution)/shard_map/ppermute | solution.py:327
  52.7 10.8 %collective-permute-start.10 = (bf16[256,512]{1,0:T(8,128)(2,1)S(1)}, bf16[256,512]{1,0:T(8,128)(2,1)S(1)}, u32[]{:S(2)}, u32[]{:S(2)}) collective-permute-start(bf16[256,512]{1,0:T(8,128)(2,1)S(1)} %copy-done.8), channel_id=1, source_target_pairs={{0,4},{4,0},{1,5},{5,1},{2,6},{6,2},{3,7},{7,3},{8,12},{12,8},{9,1... | collective-permute-start | bytes 786440 | tf_op jit(solution)/shard_map/ppermute | solution.py:306
  63.5 9.8 %collective-permute-start.9 = (bf16[512,1024]{1,0:T(8,128)(2,1)}, bf16[512,1024]{1,0:T(8,128)(2,1)}, u32[]{:S(2)}, u32[]{:S(2)}) collective-permute-start(bf16[512,1024]{1,0:T(8,128)(2,1)} %get-tuple-element.25), channel_id=1, source_target_pairs={{2,4},{6,2},{3,5},{7,3},{10,12},{14,10},{11,13},{15,11},{18,20},{2... | collective-permute-start | bytes 3145736 | tf_op jit(solution)/shard_map/ppermute | solution.py:328
  66.0 162.7 %reduce-scatter.3.cloned.1.call-start = ((), (), s32[]{:S(2)}) async-start(), calls=%async_computation.4 | async-start | bytes 2621440 | tf_op jit(solution)/shard_map/reduce_scatter | solution.py:403
  73.1 13.4 %collective-permute-start.11 = (bf16[2048,512]{1,0:T(8,128)(2,1)}, bf16[2048,512]{1,0:T(8,128)(2,1)}, u32[]{:S(2)}, u32[]{:S(2)}) collective-permute-start(bf16[2048,512]{1,0:T(8,128)(2,1)} %all-gather.3.cloned.1.call-done.w_own.own_0), channel_id=1, source_target_pairs={{0,2},{2,0},{1,3},{3,1},{4,6},{6,4},{5,7},{7,5},{8,10},{10,8},{9,1... | collective-permute-start | bytes 6291464 | tf_op jit(solution)/shard_map/ppermute | solution.py:381
  80.3 23.2 %collective-permute-start.12 = (bf16[512,2048]{1,0:T(8,128)(2,1)}, bf16[512,2048]{1,0:T(8,128)(2,1)S(1)}, u32[]{:S(2)}, u32[]{:S(2)}) collective-permute-start(bf16[512,2048]{1,0:T(8,128)(2,1)} %get-tuple-element.29.enc_other), channel_id=1, source_target_pairs={{0,2},{2,0},{1,3},{3,1},{4,6},{6,4},{5,7},{7,5},{8,10},{10,8},{9,1... | collective-permute-start | bytes 6291464 | tf_op jit(solution)/shard_map/ppermute | solution.py:364
  119.4 4.5 %collective-permute-start.15 = (bf16[2048,512]{1,0:T(8,128)(2,1)}, bf16[2048,512]{1,0:T(8,128)(2,1)}, u32[]{:S(2)}, u32[]{:S(2)}) collective-permute-start(bf16[2048,512]{1,0:T(8,128)(2,1)} %all-gather.5.cloned.1.call-done.w_own.own_1), channel_id=1, source_target_pairs={{0,2},{2,0},{1,3},{3,1},{4,6},{6,4},{5,7},{7,5},{8,10},{10,8},{9,1... | collective-permute-start | bytes 6291464 | tf_op jit(solution)/shard_map/ppermute | solution.py:381
  119.4 112.9 %reduce-scatter.5.cloned.1.call-start = ((), (), s32[]{:S(2)}) async-start(), calls=%async_computation.5 | async-start | bytes 2621440 | tf_op jit(solution)/shard_map/reduce_scatter | solution.py:403
  146.8 20.8 %collective-permute-start.17 = (bf16[512,2048]{1,0:T(8,128)(2,1)}, bf16[512,2048]{1,0:T(8,128)(2,1)}, u32[]{:S(2)}, u32[]{:S(2)}) collective-permute-start(bf16[512,2048]{1,0:T(8,128)(2,1)} %enc_grad.3), channel_id=1, source_target_pairs={{2,3},{3,2},{4,5},{5,4},{10,11},{11,10},{12,13},{13,12},{18,19},{1... | collective-permute-start | bytes 6291464 | tf_op jit(solution)/shard_map/ppermute | solution.py:287
  164.8 31.8 %collective-permute-start.16 = (bf16[512,2048]{1,0:T(8,128)(2,1)}, bf16[512,2048]{1,0:T(8,128)(2,1)S(1)}, u32[]{:S(2)}, u32[]{:S(2)}) collective-permute-start(bf16[512,2048]{1,0:T(8,128)(2,1)} %enc_grad.3), channel_id=1, source_target_pairs={{0,1},{1,0},{6,7},{7,6},{8,9},{9,8},{14,15},{15,14},{16,17},{17,16... | collective-permute-start | bytes 6291464 | tf_op jit(solution)/shard_map/ppermute | solution.py:287
  170.6 38.8 %collective-permute-start.18 = (bf16[512,2048]{1,0:T(8,128)(2,1)S(1)}, bf16[512,2048]{1,0:T(8,128)(2,1)S(1)}, u32[]{:S(2)}, u32[]{:S(2)}) collective-permute-start(bf16[512,2048]{1,0:T(8,128)(2,1)S(1)} %add_convert_fusion), channel_id=1, source_target_pairs={{4,0},{2,6},{5,1},{3,7},{12,8},{10,14},{13,9},{11,15},{20,16},{18,... | collective-permute-start | bytes 6291464 | tf_op jit(solution)/shard_map/ppermute | solution.py:415
  214.6 35.0 %collective-permute-start.19 = (bf16[512,2048]{1,0:T(8,128)(2,1)}, bf16[512,2048]{1,0:T(8,128)(2,1)S(1)}, u32[]{:S(2)}, u32[]{:S(2)}) collective-permute-start(bf16[512,2048]{1,0:T(8,128)(2,1)} %get-tuple-element.34), channel_id=1, source_target_pairs={{6,4},{7,5},{14,12},{15,13},{22,20},{23,21},{30,28},{31,29}} | collective-permute-start | bytes 6291464 | tf_op jit(solution)/shard_map/ppermute | solution.py:436
  215.4 8.7 %collective-permute-start.20 = (bf16[512,512]{1,0:T(8,128)(2,1)S(1)}, bf16[512,512]{1,0:T(8,128)(2,1)}, u32[]{:S(2)}, u32[]{:S(2)}) collective-permute-start(bf16[512,512]{1,0:T(8,128)(2,1)S(1)} %get-tuple-element.35), channel_id=1, source_target_pairs={{0,2},{1,3},{8,10},{9,11},{16,18},{17,19},{24,26},{25,27}} | collective-permute-start | bytes 1572872 | tf_op jit(solution)/shard_map/ppermute | solution.py:386
  217.5 6.6 %collective-permute-start.28 = (f32[2048]{0:T(1024)S(1)}, f32[2048]{0:T(1024)S(1)}, u32[]{:S(2)}, u32[]{:S(2)}) collective-permute-start(f32[2048]{0:T(1024)S(1)} %broadcast_select_fusion.3), channel_id=1, source_target_pairs={{0,6},{6,0},{2,4},{4,2},{1,7},{7,1},{3,5},{5,3},{8,14},{14,8},{10,... | collective-permute-start | bytes 24584 | tf_op jit(solution)/shard_map/ppermute | solution.py:439
  217.9 31.7 %collective-permute-start.22 = (bf16[512,512]{1,0:T(8,128)(2,1)S(1)}, bf16[512,512]{1,0:T(8,128)(2,1)}, u32[]{:S(2)}, u32[]{:S(2)}) collective-permute-start(bf16[512,512]{1,0:T(8,128)(2,1)S(1)} %get-tuple-element.35), channel_id=1, source_target_pairs={{4,2},{2,6},{5,3},{3,7},{12,10},{10,14},{13,11},{11,15},{20,18},{1... | collective-permute-start | bytes 1572872 | tf_op jit(solution)/shard_map/ppermute | solution.py:388
  219.3 14.1 %collective-permute-start.21 = (bf16[512,512]{1,0:T(8,128)(2,1)S(1)}, bf16[512,512]{1,0:T(8,128)(2,1)}, u32[]{:S(2)}, u32[]{:S(2)}) collective-permute-start(bf16[512,512]{1,0:T(8,128)(2,1)S(1)} %get-tuple-element.36), channel_id=1, source_target_pairs={{0,2},{1,3},{8,10},{9,11},{16,18},{17,19},{24,26},{25,27}} | collective-permute-start | bytes 1572872 | tf_op jit(solution)/shard_map/ppermute | solution.py:386
  224.1 3.7 %collective-permute-start.29 = (f32[2048]{0:T(1024)S(1)}, f32[2048]{0:T(1024)S(1)}, u32[]{:S(2)}, u32[]{:S(2)}) collective-permute-start(f32[2048]{0:T(1024)S(1)} %fusion.14), channel_id=1, source_target_pairs={{0,8},{8,0},{16,24},{24,16},{1,9},{9,1},{17,25},{25,17},{2,10},{10... | collective-permute-start | bytes 24584 | tf_op jit(solution)/shard_map/ppermute | solution.py:442
  226.0 23.6 %collective-permute-start.23 = (bf16[512,512]{1,0:T(8,128)(2,1)S(1)}, bf16[512,512]{1,0:T(8,128)(2,1)}, u32[]{:S(2)}, u32[]{:S(2)}) collective-permute-start(bf16[512,512]{1,0:T(8,128)(2,1)S(1)} %get-tuple-element.36), channel_id=1, source_target_pairs={{4,2},{2,6},{5,3},{3,7},{12,10},{10,14},{13,11},{11,15},{20,18},{1... | collective-permute-start | bytes 1572872 | tf_op jit(solution)/shard_map/ppermute | solution.py:388
  227.7 4.5 %collective-permute-start.30 = (f32[2048]{0:T(1024)S(1)}, f32[2048]{0:T(1024)S(1)}, u32[]{:S(2)}, u32[]{:S(2)}) collective-permute-start(f32[2048]{0:T(1024)S(1)} %add.56), channel_id=1, source_target_pairs={{0,16},{8,24},{16,0},{24,8},{1,17},{9,25},{17,1},{25,9},{2,18},{10... | collective-permute-start | bytes 24584 | tf_op jit(solution)/shard_map/ppermute | solution.py:442
  232.3 2.4 collective-permute-start.31
  233.4 9.4 %collective-permute-start.26 = (bf16[256,512]{1,0:T(8,128)(2,1)}, bf16[256,512]{1,0:T(8,128)(2,1)S(1)}, u32[]{:S(2)}, u32[]{:S(2)}) collective-permute-start(bf16[256,512]{1,0:T(8,128)(2,1)} %get-tuple-element.46), channel_id=1, source_target_pairs={{0,4},{4,0},{1,5},{5,1},{2,6},{6,2},{3,7},{7,3},{8,12},{12,8},{9,1... | collective-permute-start | bytes 786440 | tf_op jit(solution)/shard_map/ppermute | solution.py:421
  234.8 13.2 %collective-permute-start.27 = (bf16[256,512]{1,0:T(8,128)(2,1)S(1)}, bf16[256,512]{1,0:T(8,128)(2,1)S(1)}, u32[]{:S(2)}, u32[]{:S(2)}) collective-permute-start(bf16[256,512]{1,0:T(8,128)(2,1)S(1)} %get-tuple-element.48), channel_id=1, source_target_pairs={{0,4},{4,0},{1,5},{5,1},{2,6},{6,2},{3,7},{7,3},{8,12},{12,8},{9,1... | collective-permute-start | bytes 786440 | tf_op jit(solution)/shard_map/ppermute | solution.py:421
  (14 other events, 161.1 us)
Sparse Core Ops, SparseCore 0:
  27.1 45.9 all-gather.2
  74.7 44.6 all-gather.4
  121.7 42.5 reduce-scatter.2
  166.5 43.1 reduce-scatter.4

commit v7 on v6

--- a/solution.py
+++ b/solution.py
@@ -109,9 +109,9 @@
     return dec.astype(BF16), gkv.astype(BF16)
 
 
-def attend_kernel(at, enc_own, enc_other, w_own, w_other, *refs):
+def attend_kernel(at, part, enc_other, w_other, *refs):
     qgs, (dec, gkv) = refs[:3], refs[3:]
-    kv = (dot(enc_own[...], w_own[...]) + dot(enc_other[...], w_other[...])).astype(BF16)
+    kv = (part[...] + dot(enc_other[...], w_other[...])).astype(BF16)
     keys = lax.broadcasted_iota(jnp.int32, (1, kv.shape[0]), 1)
     bias = jnp.where(keys < at[4], 0.0, -1e30).astype(F32)
     for head in range(kv.shape[1] // (2 * HEAD)):
@@ -120,9 +120,9 @@
         dec[:, lanes], gkv[:, lanes] = attend_head(bias, qg, kv[:, lanes])
 
 
-def attend(at, enc_own, enc_other, w_own, w_other, qgs, chunk):
-    length = enc_own.shape[0]
-    half, cols = w_own.shape
+def attend(at, part, enc_other, w_other, qgs, chunk):
+    length = part.shape[0]
+    half, cols = w_other.shape
     step = min(256, cols)
     first = chunk * (cols // step)
     enc = pl.BlockSpec((length, half), lambda i, s: (0, 0))
@@ -137,7 +137,7 @@
         grid_spec=pltpu.PrefetchScalarGridSpec(
             num_scalar_prefetch=1,
             grid=(cols // step,),
-            in_specs=[enc, enc, weight, weight, pick(0), pick(1), pick(2)],
+            in_specs=[out, enc, weight, pick(0), pick(1), pick(2)],
             out_specs=[out, out],
         ),
         out_shape=[jax.ShapeDtypeStruct((length, cols), BF16)] * 2,
@@ -146,7 +146,7 @@
             length * cols * (4 * half + 14 * length), 8, length * length * cols // (2 * HEAD)
         ),
         name="attend",
-    )(at, *in_hbm(enc_own, enc_other, w_own, w_other, *qgs))
+    )(at, part, *in_hbm(enc_other, w_other, *qgs))
 
 
 def weight_grad_kernel(scale, at, enc_a, enc_b, gkv_a, gkv_b, out):
@@ -379,7 +379,7 @@
             if k > 0:
                 w_own[k] = after(w_own[k], grad)
         w_other.append(lax.ppermute(w_own[k], "phase", SWAP))
-        dec, gkv = attend(at, enc_own, enc_other, w_own[k], w_other[k], qgs, k)
+        dec, gkv = attend(at, dot(enc_own, w_own[k]), enc_other, w_other[k], qgs, k)
         gkvs.append(gkv)
         decs.append(
             (
@@ -388,15 +388,17 @@
                 lax.ppermute(dec, PLANE, [(2, 1), (1, 3)]),
             )
         )
-        if tiled and k == CHUNKS - 1:
-            terms = [enc_grad(at, gkvs, w_own, w_other, groups, rows, s) for s in (1, 0)][::-1]
-            gkv_sent = after(gkv, *terms)
-        else:
-            gkv_sent = gkv
-        parts = jnp.split(gkv_sent, 2, axis=1)
+        parts = jnp.split(gkv, 2, axis=1)
         gkv_mate = jnp.concatenate([lax.ppermute(p, "phase", SWAP) for p in parts], 1)
         if tiled:
+            last = k == CHUNKS - 1
+            if last:
+                away = enc_grad(at, gkvs, w_own, w_other, groups, rows, 1)
+                gkv_mate = after(gkv_mate, away)
             grad = weight_grad(at, enc_own, enc_mate, gkv, gkv_mate, groups, pair_scale)
+            if last:
+                kept = [after(gkvs[0], grad)] + gkvs[1:]
+                terms = [enc_grad(at, kept, w_own, w_other, groups, rows, 0), away]
         else:
             grad = pair_scale * (dot(enc_own, gkv, TN) + dot(enc_mate, gkv_mate, TN))
             grad = grad.astype(BF16)
@@ -409,9 +411,11 @@
         full = full.astype(BF16).reshape(length, -1, rows)[:, back].reshape(length, D)
         terms = [cut(full, 1, (x + s) % shards, width) for s in range(shards)]
     far_terms = terms[0].astype(F32)
+    moved = []
     for turn in range(1, shards):
-        far_terms = far_terms + across(terms[turn], turn, [(1, 1), (2, 2)]).astype(F32)
-    moved = [across(terms[turn], turn, [(0, 0), (3, 3)]) for turn in range(1, shards)]
+        got = across(terms[turn], turn, [(1, 1), (2, 2)])
+        far_terms = far_terms + got.astype(F32)
+        moved.append(across(after(terms[turn], got), turn, [(0, 0), (3, 3)]))
     moved.append(lax.ppermute(far_terms.astype(BF16), PLANE, [(2, 0), (1, 3)]))
 
     dec_here = jnp.concatenate([jnp.where(y == 0, d[0], d[1]) for d in decs], 1)
@@ -419,9 +423,8 @@
     dec_grads = ordered(y == 0, dec_here, dec_there, 1)
     kept = jnp.concatenate([w[:rows] for w in weight_sums], 1)
     got = [lax.ppermute(w[rows:], "y", SWAP) for w in weight_sums]
-    got = jnp.concatenate(got, 1)
-    d_wkv = ordered(y == 0, kept, got, 1).astype(F32)
     if tiled:
+        moved[0], dec_grads, got[0] = lax.optimization_barrier((moved[0], dec_grads, got[0]))
         grad_normed, gain_term = collect(
             at, [terms[0]] + moved, packed, here, inv_rms, gain.astype(F32)[None], pair_scale
         )
@@ -443,6 +446,8 @@
         turn *= 2
     d_gain = jnp.where(straight, gain_term, lax.ppermute(gain_term, "phase", SWAP))
 
+    got = jnp.concatenate(got, 1)
+    d_wkv = ordered(y == 0, kept, got, 1).astype(F32)
     sec_grads = jnp.where(core == 0, enc_grads, dec_grads)[None, None]
     return (sec_grads, d_wkv, d_gain)
 

time: 261 us -> 266 us (1.019)
  waiting for transfers between devices: 97.1 us -> 85.1 us
  starting transfers between devices: 55.5 us -> 67.3 us
  Pallas kernels: 68.4 us -> 60.3 us
  matrix products: 0 us -> 6.4 us
  other arithmetic: 14.6 us -> 21 us
    ppermute x5, waiting for transfers between devices: 24.7 us -> 0.01 us  [across(): lax.ppermute(value, ('y', 'phase', 'mp'), [(a * shards + s, b * shards +...]
    ppermute x2, waiting for transfers between devices: 10.8 us -> 25.3 us  [on_device(): got = [lax.ppermute(w[rows:], 'y', SWAP) for w in weight_sums]]
    ppermute x1, waiting for transfers between devices: 12.8 us -> 0.01 us  [on_device(): moved.append(lax.ppermute(far_terms.astype(BF16), PLANE, [(2, 0), (1, 3)]))]
    ppermute x2, starting transfers between devices: 6.87 us -> 18.6 us  [on_device(): lax.ppermute(dec, PLANE, [(0, 1)])]
    pallas_call x2, Pallas kernels: 30.1 us -> 21 us  [attend(): pl.pallas_call(attend_kernel, grid_spec=pltpu.PrefetchScalarGridSpec(num_...]
    all_gather x2, waiting for transfers between devices: 15.2 us -> 23.2 us  [on_device(): w_own.append(lax.all_gather(block, 'z', axis=0, tiled=True))]
    dot_general x0 -> x2, matrix products: none -> 6.4 us  [dot(): return lax.dot_general(a, b, dims, preferred_element_type=F32)]
    ppermute x1, starting transfers between devices: 6.21 us -> 0.34 us  [on_device(): enc_mate = lax.ppermute(enc_other, 'phase', SWAP)]
  transfers between devices with their start and end apart: 36 -> 36, of which waited for: 16 -> 15; matrix products, arithmetic and copies ran while one was open for 6% -> 11% of each run, Pallas kernels for 26% -> 23%
where the time goes in v7:
time: 266 us; the launch traced here: 264 us
  waiting for transfers between devices  85.1 us (32%)
  starting transfers between devices  67.3 us (25%)
  Pallas kernels  60.3 us (23%)
  other arithmetic  21 us (8%)
  between operations  16.1 us (6%)
  local copies, waits for them, and re-layouts  8.33 us (3%)
  matrix products  6.4 us (2%)
    ppermute x2, waiting for transfers between devices, on_device(): got = [lax.ppermute(w[rows:], 'y', SWAP) for w in weight_sums]  25.3 us
    all_gather x2, waiting for transfers between devices, on_device(): w_own.append(lax.all_gather(block, 'z', axis=0, tiled=True))  23.2 us
    pallas_call x2, Pallas kernels, attend(): pl.pallas_call(attend_kernel, grid_spec=pltpu.PrefetchScalarGridSpec(num_...  21 us
    ppermute x2, starting transfers between devices, on_device(): lax.ppermute(dec, PLANE, [(0, 1)])  18.6 us
    ppermute x1, waiting for transfers between devices, on_device(): lax.ppermute(after(packed, swapped[0], key_count, *gains), PLANE, [(0, 2)...  14.6 us
    pallas_call x2, Pallas kernels, enc_grad(): pl.pallas_call(enc_grad_kernel, grid_spec=pltpu.PrefetchScalarGridSpec(nu...  13.7 us
    pallas_call x2, Pallas kernels, weight_grad(): pl.pallas_call(lambda *refs: weight_grad_kernel(scale, *refs), grid_spec=...  12.6 us
    ppermute x5, starting transfers between devices, across(): lax.ppermute(value, ('y', 'phase', 'mp'), [(a * shards + s, b * shards +...  12 us
  transfers between devices with their start and end apart: 36, of which 15 were waited for; matrix products, arithmetic and copies ran while one was open for 11% of the time, Pallas kernels for 23%

profile of v7, /device:TPU:0, one launch (start us, length us, event | category | flops | bytes accessed | tf_op | source)
XLA Modules:
  0.0 264.4 jit_solution(3982052369436758780)
XLA Ops:
  7.2 2.2 collective-permute-start
  11.4 4.0 %collective-permute-start.2 = (bf16[256,512]{1,0:T(8,128)(2,1)S(1)}, bf16[256,512]{1,0:T(8,128)(2,1)S(1)}, u32[]{:S(2)}, u32[]{:S(2)}) collective-permute-start(bf16[256,512]{1,0:T(8,128)(2,1)S(1)} %get-tuple-element.53), channel_id=1, source_target_pairs={{0,4},{4,0},{1,5},{5,1},{2,6},{6,2},{3,7},{7,3},{8,12},{12,8},{9,1... | collective-permute-start | bytes 786440 | tf_op jit(solution)/shard_map/ppermute | solution.py:299
  18.4 2.8 %collective-permute-done.1 = s32[1]{0:T(128)} collective-permute-done((s32[1]{0:T(128)}, s32[1]{0:T(128)}, u32[]{:S(2)}, u32[]{:S(2)}) %collective-permute-start.1) | collective-permute-done | bytes 36 | tf_op jit(solution)/shard_map/ppermute | solution.py:303
  22.0 4.1 %collective-permute-start.4 = (bf16[512,2048]{1,0:T(8,128)(2,1)S(1)}, bf16[512,2048]{1,0:T(8,128)(2,1)}, u32[]{:S(2)}, u32[]{:S(2)}) collective-permute-start(bf16[512,2048]{1,0:T(8,128)(2,1)S(1)} %bitcast.17), channel_id=1, source_target_pairs={{0,4},{4,2},{1,5},{5,3},{8,12},{12,10},{9,13},{13,11},{16,20},{20,... | collective-permute-start | bytes 6291464 | tf_op jit(solution)/shard_map/ppermute | solution.py:304
  26.9 3.1 %collective-permute-start.5 = (bf16[512,2048]{1,0:T(8,128)(2,1)S(1)}, bf16[512,2048]{1,0:T(8,128)(2,1)}, u32[]{:S(2)}, u32[]{:S(2)}) collective-permute-start(bf16[512,2048]{1,0:T(8,128)(2,1)S(1)} %bitcast.18), channel_id=1, source_target_pairs={{0,1},{1,0},{8,9},{9,8},{16,17},{17,16},{24,25},{25,24}} | collective-permute-start | bytes 6291464 | tf_op jit(solution)/shard_map/ppermute | solution.py:287
  31.5 2.1 collective-permute-start.6
  33.6 14.6 %collective-permute-done.4.refs_3_ = bf16[512,2048]{1,0:T(8,128)(2,1)} collective-permute-done((bf16[512,2048]{1,0:T(8,128)(2,1)S(1)}, bf16[512,2048]{1,0:T(8,128)(2,1)}, u32[]{:S(2)}, u32[]{:S(2)}) %collective-permute-start.4) | collective-permute-done | bytes 2097184 | tf_op jit(solution)/shard_map/ppermute | solution.py:304
  53.0 3.5 %collective-permute-start.10 = (bf16[256,512]{1,0:T(8,128)(2,1)S(1)}, bf16[256,512]{1,0:T(8,128)(2,1)S(1)}, u32[]{:S(2)}, u32[]{:S(2)}) collective-permute-start(bf16[256,512]{1,0:T(8,128)(2,1)S(1)} %copy-done.11), channel_id=1, source_target_pairs={{0,4},{4,0},{1,5},{5,1},{2,6},{6,2},{3,7},{7,3},{8,12},{12,8},{9,1... | collective-permute-start | bytes 786440 | tf_op jit(solution)/shard_map/ppermute | solution.py:306
  56.5 7.1 %collective-permute-done.10 = bf16[256,512]{1,0:T(8,128)(2,1)S(1)} collective-permute-done((bf16[256,512]{1,0:T(8,128)(2,1)S(1)}, bf16[256,512]{1,0:T(8,128)(2,1)S(1)}, u32[]{:S(2)}, u32[]{:S(2)}) %collective-permute-start.10) | collective-permute-done | bytes 262176 | tf_op jit(solution)/shard_map/ppermute | solution.py:306
  65.8 7.3 %all-gather.3.cloned.1.call-done.own_0 = bf16[2048,512]{1,0:T(8,128)(2,1)} async-done(((bf16[512,512]{1,0:T(8,128)(2,1)}), bf16[2048,512]{1,0:T(8,128)(2,1)}) %all-gather.3.cloned.1.call-update) | async-done | bytes 2097168 | tf_op jit(solution)/shard_map/all_gather | solution.py:378
  73.0 4.8 %collective-permute-start.11 = (bf16[2048,512]{1,0:T(8,128)(2,1)}, bf16[2048,512]{1,0:T(8,128)(2,1)}, u32[]{:S(2)}, u32[]{:S(2)}) collective-permute-start(bf16[2048,512]{1,0:T(8,128)(2,1)} %all-gather.3.cloned.1.call-done.own_0), channel_id=1, source_target_pairs={{0,2},{2,0},{1,3},{3,1},{4,6},{6,4},{5,7},{7,5},{8,10},{10,8},{9,1... | collective-permute-start | bytes 6291464 | tf_op jit(solution)/shard_map/ppermute | solution.py:381
  78.1 7.0 %norm.1 = (bf16[512,2048]{1,0:T(8,128)(2,1)}, bf16[512,2048]{1,0:T(8,128)(2,1)}, f32[512,128]{1,0:T(8,128)S(1)}) custom-call(s32[6]{0:T(128)S(1)} %concatenate.59.refs_0_.at, bf16[512,2048]{1,0:T(8,128)(2,1)S(1)} %bitcast.19, bf16[512,2048]{1,0:T(8,128)(2,1)} %collective-permute-done.refs_2_.refs_5_, bf16[512,2048]{1,0:T(8,128)(2,1)} %collective-permute-done.4.refs_3_, ...), custom_call_target="tpu_custom_call" | custom-call | flops 16777216 | bytes 8388608 | tf_op jit(solution)/shard_map/norm/pallas_call | solution.py:73
  85.4 2.9 %fusion.12.part = f32[512,512]{1,0:T(8,128)S(1)} fusion(bf16[512,2048]{1,0:T(8,128)(2,1)} %get-tuple-element.33.refs_1_, bf16[2048,512]{1,0:T(8,128)(2,1)S(1)} %copy-done.14), kind=kOutput, calls=%fused_computation.35 | convolution fusion | flops 1073741824 | bytes 5242880 | tf_op jit(solution)/shard_map/dot_general | solution.py:24
  88.4 10.4 %attend.2 = (bf16[512,512]{1,0:T(8,128)(2,1)S(1)}, bf16[512,512]{1,0:T(8,128)(2,1)S(1)}) custom-call(s32[6]{0:T(128)S(1)} %concatenate.59.refs_0_.at, f32[512,512]{1,0:T(8,128)S(1)} %fusion.12.part, bf16[512,2048]{1,0:T(8,128)(2,1)} %get-tuple-element.34.enc_other, bf16[2048,512]{1,0:T(8,128)(2,1)} %collective-permute-done.11.w_other.other_0, ...), custom_call_target="tpu_custom_call" | custom-call | flops 4026531840 | bytes 8388608 | tf_op jit(solution)/shard_map/attend/pallas_call | solution.py:135
  102.2 6.3 %weight_grad.2 = bf16[2048,512]{1,0:T(8,128)(2,1)} custom-call(s32[6]{0:T(128)S(1)} %concatenate.59.refs_0_.at, bf16[512,2048]{1,0:T(8,128)(2,1)} %get-tuple-element.33.refs_1_, bf16[512,2048]{1,0:T(8,128)(2,1)} %copy-done.8, bf16[512,512]{1,0:T(8,128)(2,1)S(1)} %get-tuple-element.39.refs_3_.gkv_0, bf16[512,512]{1,0:T(8,128)(2,1)S(1)} %pad_maximum_fusion.2.refs_4_), custom_call_target="tpu_custom_call" | custom-call | flops 33554432 | tf_op jit(solution)/shard_map/weight_grad/pallas_call | solution.py:163
  108.5 15.9 %all-gather.5.cloned.1.call-done.own_1 = bf16[2048,512]{1,0:T(8,128)(2,1)} async-done(((bf16[512,512]{1,0:T(8,128)(2,1)}), bf16[2048,512]{1,0:T(8,128)(2,1)}) %all-gather.5.cloned.1.call-update) | async-done | bytes 2097168 | tf_op jit(solution)/shard_map/all_gather | solution.py:378
  124.7 3.5 %fusion.13.part = f32[512,512]{1,0:T(8,128)S(1)} fusion(bf16[512,2048]{1,0:T(8,128)(2,1)} %get-tuple-element.33.refs_1_, bf16[2048,512]{1,0:T(8,128)(2,1)} %all-gather.5.cloned.1.call-done.own_1), kind=kOutput, calls=%fused_computation.36 | convolution fusion | flops 1073741824 | bytes 5242880 | tf_op jit(solution)/shard_map/dot_general | solution.py:24
  128.9 10.6 %attend.3 = (bf16[512,512]{1,0:T(8,128)(2,1)S(1)}, bf16[512,512]{1,0:T(8,128)(2,1)S(1)}) custom-call(s32[6]{0:T(128)S(1)} %concatenate.59.refs_0_.at, f32[512,512]{1,0:T(8,128)S(1)} %fusion.13.part, bf16[512,2048]{1,0:T(8,128)(2,1)} %get-tuple-element.34.enc_other, bf16[2048,512]{1,0:T(8,128)(2,1)} %collective-permute-done.15.w_other.other_1, ...), custom_call_target="tpu_custom_call" | custom-call | flops 4026531840 | bytes 8388608 | tf_op jit(solution)/shard_map/attend/pallas_call | solution.py:135
  140.3 6.9 %enc_grad.2 = bf16[512,2048]{1,0:T(8,128)(2,1)} custom-call(s32[6]{0:T(128)S(1)} %concatenate.59.refs_0_.at, bf16[512,512]{1,0:T(8,128)(2,1)} %copy-done.2, bf16[512,512]{1,0:T(8,128)(2,1)} %copy-done.3, bf16[2048,512]{1,0:T(8,128)(2,1)} %all-gather.3.cloned.1.call-done.own_0, bf16[2048,512]{1,0:T(8,128)(2,1)} %all-gather.5.cloned.1.call-done.own_1, ...), custom_call_target="tpu_custom_call" | custom-call | flops 4294967296 | bytes 8388608 | tf_op jit(solution)/shard_map/enc_grad/pallas_call | solution.py:240
  151.9 6.3 %weight_grad.3 = bf16[2048,512]{1,0:T(8,128)(2,1)} custom-call(s32[6]{0:T(128)S(1)} %concatenate.59.refs_0_.at, bf16[512,2048]{1,0:T(8,128)(2,1)} %get-tuple-element.33.refs_1_, bf16[512,2048]{1,0:T(8,128)(2,1)} %copy-done.8, bf16[512,512]{1,0:T(8,128)(2,1)S(1)} %copy-done.4, bf16[512,512]{1,0:T(8,128)(2,1)S(1)} %pad_maximum_fusion.3.refs_4_), custom_call_target="tpu_custom_call" | custom-call | flops 33554432 | tf_op jit(solution)/shard_map/weight_grad/pallas_call | solution.py:163
  158.2 6.8 %enc_grad.3.refs_1_ = bf16[512,2048]{1,0:T(8,128)(2,1)} custom-call(s32[6]{0:T(128)S(1)} %concatenate.59.refs_0_.at, bf16[512,512]{1,0:T(8,128)(2,1)} %copy-done.2, bf16[512,512]{1,0:T(8,128)(2,1)} %copy-done.3, bf16[2048,512]{1,0:T(8,128)(2,1)} %all-gather.3.cloned.1.call-done.own_0, bf16[2048,512]{1,0:T(8,128)(2,1)} %all-gather.5.cloned.1.call-done.own_1, ...), custom_call_target="tpu_custom_call" | custom-call | flops 4294967296 | bytes 8388608 | tf_op jit(solution)/shard_map/enc_grad/pallas_call | solution.py:240
  165.0 2.8 %collective-permute-start.19 = (bf16[512,2048]{1,0:T(8,128)(2,1)}, bf16[512,2048]{1,0:T(8,128)(2,1)}, u32[]{:S(2)}, u32[]{:S(2)}) collective-permute-start(bf16[512,2048]{1,0:T(8,128)(2,1)} %enc_grad.2), channel_id=1, source_target_pairs={{0,1},{1,0},{6,7},{7,6},{8,9},{9,8},{14,15},{15,14},{16,17},{17,16... | collective-permute-start | bytes 6291464 | tf_op jit(solution)/shard_map/ppermute | solution.py:287
  167.7 4.4 %add_convert_fusion = bf16[512,2048]{1,0:T(8,128)(2,1)} fusion(bf16[512,2048]{1,0:T(8,128)(2,1)} %collective-permute-done.18, bf16[512,2048]{1,0:T(8,128)(2,1)} %enc_grad.3.refs_1_), kind=kLoop, calls=%fused_computation | loop fusion | flops 4194304 | bytes 6291456 | tf_op jit(solution)/shard_map/convert_element_type | solution.py:419
  173.5 16.5 %collective-permute-start.20 = (bf16[512,512]{1,0:T(8,128)(2,1)S(1)}, bf16[512,512]{1,0:T(8,128)(2,1)}, u32[]{:S(2)}, u32[]{:S(2)}) collective-permute-start(bf16[512,512]{1,0:T(8,128)(2,1)S(1)} %get-tuple-element.41), channel_id=1, source_target_pairs={{0,2},{1,3},{8,10},{9,11},{16,18},{17,19},{24,26},{25,27}} | collective-permute-start | bytes 1572872 | tf_op jit(solution)/shard_map/ppermute | solution.py:386
  190.0 2.1 collective-permute-start.21
  201.3 3.7 %maximum_select_fusion = bf16[512,2048]{1,0:T(8,128)(2,1)} fusion(bf16[512,512]{1,0:T(8,128)(2,1)} %collective-permute-done.23, bf16[512,512]{1,0:T(8,128)(2,1)} %collective-permute-done.22, bf16[512,512]{1,0:T(8,128)(2,1)} %broadcast_select_fusion, bf16[512,512]{1,0:T(8,128)(2,1)} %broadcast_select_fusion.1, pred[]{:T(512)S(6)} %eq.19), kind=kLoop, calls=%fused_computation.4 | loop fusion | flops 17825792 | bytes 4194305 | tf_op jit(solution)/shard_map/jit(_where)/select_n | solution.py:260
  205.0 25.3 %collective-permute-done.24 = bf16[256,512]{1,0:T(8,128)(2,1)S(1)} collective-permute-done((bf16[256,512]{1,0:T(8,128)(2,1)S(1)}, bf16[256,512]{1,0:T(8,128)(2,1)S(1)}, u32[]{:S(2)}, u32[]{:S(2)}) %collective-permute-start.24) | collective-permute-done | bytes 262176 | tf_op jit(solution)/shard_map/ppermute | solution.py:425
  230.3 6.0 %collect.1 = (bf16[512,2048]{1,0:T(8,128)(2,1)}, f32[4,1,2048]{2,1,0:T(1,128)S(1)}) custom-call(s32[6]{0:T(128)S(1)} %concatenate.59.refs_0_.at, bf16[512,2048]{1,0:T(8,128)(2,1)S(1)} %copy-done.1, bf16[512,2048]{1,0:T(8,128)(2,1)} %collective-permute-done.19.refs_2_, bf16[512,2048]{1,0:T(8,128)(2,1)} %collective-permute-done.25.refs_3_, ...), custom_call_target="tpu_custom_call" | custom-call | flops 8388608 | bytes 12582912 | tf_op jit(solution)/shard_map/collect/pallas_call | solution.py:197
  242.1 3.6 %collective-permute-done.29 = f32[2048]{0:T(1024)S(1)} collective-permute-done((f32[2048]{0:T(1024)S(1)}, f32[2048]{0:T(1024)S(1)}, u32[]{:S(2)}, u32[]{:S(2)}) %collective-permute-start.29) | collective-permute-done | bytes 8224 | tf_op jit(solution)/shard_map/ppermute | solution.py:445
  246.8 3.5 %collective-permute-done.30 = f32[2048]{0:T(1024)S(1)} collective-permute-done((f32[2048]{0:T(1024)S(1)}, f32[2048]{0:T(1024)S(1)}, u32[]{:S(2)}, u32[]{:S(2)}) %collective-permute-start.30) | collective-permute-done | bytes 8224 | tf_op jit(solution)/shard_map/ppermute | solution.py:445
  252.1 2.6 %fusion.2 = f32[256,2048]{1,0:T(8,128)} fusion(bf16[256,512]{1,0:T(8,128)(2,1)S(1)} %collective-permute-done.27, bf16[256,512]{1,0:T(8,128)(2,1)} %copy-done.12, bf16[256,512]{1,0:T(8,128)(2,1)S(1)} %get-tuple-element.57, bf16[256,512]{1,0:T(8,128)(2,1)S(1)} %copy-done.10, pred[]{:T(512)S(6)} %eq.19), kind=kLoop, calls=%fused_computation.7 | loop fusion | flops 9437184 | bytes 3145729 | tf_op jit(solution)/shard_map/convert_element_type | solution.py:450
  254.7 3.2 %select_bitcast_fusion = bf16[1,1,512,2048]{3,2,1,0:T(8,128)(2,1)} fusion(bf16[512,2048]{1,0:T(8,128)(2,1)S(1)} %copy-done.7, bf16[512,2048]{1,0:T(8,128)(2,1)} %get-tuple-element.45, bf16[512,2048]{1,0:T(8,128)(2,1)} %collective-permute-done.26, pred[]{:T(512)S(6)} %eq.19, pred[]{:T(512)S(6)} %eq.18), kind=kLoop, calls=%fused_computation.5 | loop fusion | flops 2097152 | bytes 8388610 | tf_op jit(solution)/shard_map/broadcast_in_dim | solution.py:451
  (115 shorter events, 42.4 us)
Async XLA Ops:
  7.2 65.8 %all-gather.3.cloned.1.call-start = ((), (), s32[]{:S(2)}) async-start(), calls=%async_computation.2 | async-start | bytes 2621440 | tf_op jit(solution)/shard_map/all_gather | solution.py:378
  7.2 8.2 %collective-permute-start = (bf16[512,2048]{1,0:T(8,128)(2,1)}, bf16[512,2048]{1,0:T(8,128)(2,1)}, u32[]{:S(2)}, u32[]{:S(2)}) collective-permute-start(bf16[512,2048]{1,0:T(8,128)(2,1)} %bitcast.16), channel_id=1, source_target_pairs={{4,6},{5,7},{12,14},{13,15},{20,22},{21,23},{28,30},{29,31}} | collective-permute-start | bytes 6291464 | tf_op jit(solution)/shard_map/ppermute | solution.py:300
  11.4 10.6 %collective-permute-start.2 = (bf16[256,512]{1,0:T(8,128)(2,1)S(1)}, bf16[256,512]{1,0:T(8,128)(2,1)S(1)}, u32[]{:S(2)}, u32[]{:S(2)}) collective-permute-start(bf16[256,512]{1,0:T(8,128)(2,1)S(1)} %get-tuple-element.53), channel_id=1, source_target_pairs={{0,4},{4,0},{1,5},{5,1},{2,6},{6,2},{3,7},{7,3},{8,12},{12,8},{9,1... | collective-permute-start | bytes 786440 | tf_op jit(solution)/shard_map/ppermute | solution.py:299
  15.4 6.6 %collective-permute-start.3 = (bf16[2048]{0:T(1024)(128)(2,1)S(1)}, bf16[2048]{0:T(1024)(128)(2,1)S(1)}, u32[]{:S(2)}, u32[]{:S(2)}) collective-permute-start(bf16[2048]{0:T(1024)(128)(2,1)S(1)} %copy-done.13), channel_id=1, source_target_pairs={{0,1},{1,0},{2,3},{3,2},{4,5},{5,4},{6,7},{7,6},{8,9},{9,8},{10,11... | collective-permute-start | bytes 12296 | tf_op jit(solution)/shard_map/ppermute | solution.py:302
  17.6 3.7 %collective-permute-start.1 = (s32[1]{0:T(128)}, s32[1]{0:T(128)}, u32[]{:S(2)}, u32[]{:S(2)}) collective-permute-start(s32[1]{0:T(128)} %param.8), channel_id=1, source_target_pairs={{0,4},{4,0},{1,5},{5,1},{2,6},{6,2},{3,7},{7,3},{8,12},{12,8},{9,1... | collective-permute-start | bytes 20 | tf_op jit(solution)/shard_map/ppermute | solution.py:303
  22.0 26.2 %collective-permute-start.4 = (bf16[512,2048]{1,0:T(8,128)(2,1)S(1)}, bf16[512,2048]{1,0:T(8,128)(2,1)}, u32[]{:S(2)}, u32[]{:S(2)}) collective-permute-start(bf16[512,2048]{1,0:T(8,128)(2,1)S(1)} %bitcast.17), channel_id=1, source_target_pairs={{0,4},{4,2},{1,5},{5,3},{8,12},{12,10},{9,13},{13,11},{16,20},{20,... | collective-permute-start | bytes 6291464 | tf_op jit(solution)/shard_map/ppermute | solution.py:304
  26.9 97.5 %all-gather.5.cloned.1.call-start = ((), (), s32[]{:S(2)}) async-start(), calls=%async_computation.3 | async-start | bytes 2621440 | tf_op jit(solution)/shard_map/all_gather | solution.py:378
  26.9 51.1 %collective-permute-start.5 = (bf16[512,2048]{1,0:T(8,128)(2,1)S(1)}, bf16[512,2048]{1,0:T(8,128)(2,1)}, u32[]{:S(2)}, u32[]{:S(2)}) collective-permute-start(bf16[512,2048]{1,0:T(8,128)(2,1)S(1)} %bitcast.18), channel_id=1, source_target_pairs={{0,1},{1,0},{8,9},{9,8},{16,17},{17,16},{24,25},{25,24}} | collective-permute-start | bytes 6291464 | tf_op jit(solution)/shard_map/ppermute | solution.py:287
  31.5 46.6 %collective-permute-start.6 = (bf16[512,2048]{1,0:T(8,128)(2,1)}, bf16[512,2048]{1,0:T(8,128)(2,1)}, u32[]{:S(2)}, u32[]{:S(2)}) collective-permute-start(bf16[512,2048]{1,0:T(8,128)(2,1)} %collective-permute-done.refs_2_.refs_5_), channel_id=1, source_target_pairs={{6,7},{7,6},{14,15},{15,14},{22,23},{23,22},{30,31},{31,30}} | collective-permute-start | bytes 6291464 | tf_op jit(solution)/shard_map/ppermute | solution.py:287
  48.2 29.9 %collective-permute-start.7 = (bf16[512,2048]{1,0:T(8,128)(2,1)}, bf16[512,2048]{1,0:T(8,128)(2,1)}, u32[]{:S(2)}, u32[]{:S(2)}) collective-permute-start(bf16[512,2048]{1,0:T(8,128)(2,1)} %collective-permute-done.4.refs_3_), channel_id=1, source_target_pairs={{2,3},{3,2},{4,5},{5,4},{10,11},{11,10},{12,13},{13,12},{18,19},{1... | collective-permute-start | bytes 6291464 | tf_op jit(solution)/shard_map/ppermute | solution.py:287
  51.3 21.7 %collective-permute-start.9 = (bf16[512,1024]{1,0:T(8,128)(2,1)}, bf16[512,1024]{1,0:T(8,128)(2,1)}, u32[]{:S(2)}, u32[]{:S(2)}) collective-permute-start(bf16[512,1024]{1,0:T(8,128)(2,1)} %get-tuple-element.30), channel_id=1, source_target_pairs={{2,4},{6,2},{3,5},{7,3},{10,12},{14,10},{11,13},{15,11},{18,20},{2... | collective-permute-start | bytes 3145736 | tf_op jit(solution)/shard_map/ppermute | solution.py:328
  53.0 10.6 %collective-permute-start.10 = (bf16[256,512]{1,0:T(8,128)(2,1)S(1)}, bf16[256,512]{1,0:T(8,128)(2,1)S(1)}, u32[]{:S(2)}, u32[]{:S(2)}) collective-permute-start(bf16[256,512]{1,0:T(8,128)(2,1)S(1)} %copy-done.11), channel_id=1, source_target_pairs={{0,4},{4,0},{1,5},{5,1},{2,6},{6,2},{3,7},{7,3},{8,12},{12,8},{9,1... | collective-permute-start | bytes 786440 | tf_op jit(solution)/shard_map/ppermute | solution.py:306
  63.5 14.5 %collective-permute-start.8 = (bf16[512,1024]{1,0:T(8,128)(2,1)S(1)}, bf16[512,1024]{1,0:T(8,128)(2,1)}, u32[]{:S(2)}, u32[]{:S(2)}) collective-permute-start(bf16[512,1024]{1,0:T(8,128)(2,1)S(1)} %get-tuple-element.29.refs_0_), channel_id=1, source_target_pairs={{2,0},{3,1},{10,8},{11,9},{18,16},{19,17},{26,24},{27,25}} | collective-permute-start | bytes 3145736 | tf_op jit(solution)/shard_map/ppermute | solution.py:327
  65.7 133.2 %reduce-scatter.3.cloned.1.call-start = ((), (), s32[]{:S(2)}) async-start(), calls=%async_computation.4 | async-start | bytes 2621440 | tf_op jit(solution)/shard_map/reduce_scatter | solution.py:405
  73.0 15.3 %collective-permute-start.11 = (bf16[2048,512]{1,0:T(8,128)(2,1)}, bf16[2048,512]{1,0:T(8,128)(2,1)}, u32[]{:S(2)}, u32[]{:S(2)}) collective-permute-start(bf16[2048,512]{1,0:T(8,128)(2,1)} %all-gather.3.cloned.1.call-done.own_0), channel_id=1, source_target_pairs={{0,2},{2,0},{1,3},{3,1},{4,6},{6,4},{5,7},{7,5},{8,10},{10,8},{9,1... | collective-permute-start | bytes 6291464 | tf_op jit(solution)/shard_map/ppermute | solution.py:381
  85.1 15.8 %collective-permute-start.12 = (bf16[512,2048]{1,0:T(8,128)(2,1)}, bf16[512,2048]{1,0:T(8,128)(2,1)S(1)}, u32[]{:S(2)}, u32[]{:S(2)}) collective-permute-start(bf16[512,2048]{1,0:T(8,128)(2,1)} %get-tuple-element.34.enc_other), channel_id=1, source_target_pairs={{0,2},{2,0},{1,3},{3,1},{4,6},{6,4},{5,7},{7,5},{8,10},{10,8},{9,1... | collective-permute-start | bytes 6291464 | tf_op jit(solution)/shard_map/ppermute | solution.py:364
  124.4 4.5 %collective-permute-start.15 = (bf16[2048,512]{1,0:T(8,128)(2,1)}, bf16[2048,512]{1,0:T(8,128)(2,1)}, u32[]{:S(2)}, u32[]{:S(2)}) collective-permute-start(bf16[2048,512]{1,0:T(8,128)(2,1)} %all-gather.5.cloned.1.call-done.own_1), channel_id=1, source_target_pairs={{0,2},{2,0},{1,3},{3,1},{4,6},{6,4},{5,7},{7,5},{8,10},{10,8},{9,1... | collective-permute-start | bytes 6291464 | tf_op jit(solution)/shard_map/ppermute | solution.py:381
  124.5 115.8 %reduce-scatter.5.cloned.1.call-start = ((), (), s32[]{:S(2)}) async-start(), calls=%async_computation.5 | async-start | bytes 2621440 | tf_op jit(solution)/shard_map/reduce_scatter | solution.py:405
  147.2 17.7 %collective-permute-start.18 = (bf16[512,2048]{1,0:T(8,128)(2,1)}, bf16[512,2048]{1,0:T(8,128)(2,1)}, u32[]{:S(2)}, u32[]{:S(2)}) collective-permute-start(bf16[512,2048]{1,0:T(8,128)(2,1)} %enc_grad.2), channel_id=1, source_target_pairs={{2,3},{3,2},{4,5},{5,4},{10,11},{11,10},{12,13},{13,12},{18,19},{1... | collective-permute-start | bytes 6291464 | tf_op jit(solution)/shard_map/ppermute | solution.py:287
  149.3 2.2 collective-permute-start.16
  165.0 65.3 %collective-permute-start.19 = (bf16[512,2048]{1,0:T(8,128)(2,1)}, bf16[512,2048]{1,0:T(8,128)(2,1)}, u32[]{:S(2)}, u32[]{:S(2)}) collective-permute-start(bf16[512,2048]{1,0:T(8,128)(2,1)} %enc_grad.2), channel_id=1, source_target_pairs={{0,1},{1,0},{6,7},{7,6},{8,9},{9,8},{14,15},{15,14},{16,17},{17,16... | collective-permute-start | bytes 6291464 | tf_op jit(solution)/shard_map/ppermute | solution.py:287
  172.2 58.1 %collective-permute-start.25 = (bf16[512,2048]{1,0:T(8,128)(2,1)}, bf16[512,2048]{1,0:T(8,128)(2,1)}, u32[]{:S(2)}, u32[]{:S(2)}) collective-permute-start(bf16[512,2048]{1,0:T(8,128)(2,1)} %add_convert_fusion), channel_id=1, source_target_pairs={{4,0},{2,6},{5,1},{3,7},{12,8},{10,14},{13,9},{11,15},{20,16},{18,... | collective-permute-start | bytes 6291464 | tf_op jit(solution)/shard_map/ppermute | solution.py:419
  173.5 20.1 %collective-permute-start.20 = (bf16[512,512]{1,0:T(8,128)(2,1)S(1)}, bf16[512,512]{1,0:T(8,128)(2,1)}, u32[]{:S(2)}, u32[]{:S(2)}) collective-permute-start(bf16[512,512]{1,0:T(8,128)(2,1)S(1)} %get-tuple-element.41), channel_id=1, source_target_pairs={{0,2},{1,3},{8,10},{9,11},{16,18},{17,19},{24,26},{25,27}} | collective-permute-start | bytes 1572872 | tf_op jit(solution)/shard_map/ppermute | solution.py:386
  190.0 6.9 %collective-permute-start.21 = (bf16[512,512]{1,0:T(8,128)(2,1)S(1)}, bf16[512,512]{1,0:T(8,128)(2,1)}, u32[]{:S(2)}, u32[]{:S(2)}) collective-permute-start(bf16[512,512]{1,0:T(8,128)(2,1)S(1)} %copy-done.6), channel_id=1, source_target_pairs={{0,2},{1,3},{8,10},{9,11},{16,18},{17,19},{24,26},{25,27}} | collective-permute-start | bytes 1572872 | tf_op jit(solution)/shard_map/ppermute | solution.py:386
  192.1 9.2 %collective-permute-start.22 = (bf16[512,512]{1,0:T(8,128)(2,1)S(1)}, bf16[512,512]{1,0:T(8,128)(2,1)}, u32[]{:S(2)}, u32[]{:S(2)}) collective-permute-start(bf16[512,512]{1,0:T(8,128)(2,1)S(1)} %get-tuple-element.41), channel_id=1, source_target_pairs={{4,2},{2,6},{5,3},{3,7},{12,10},{10,14},{13,11},{11,15},{20,18},{1... | collective-permute-start | bytes 1572872 | tf_op jit(solution)/shard_map/ppermute | solution.py:388
  193.6 7.8 %collective-permute-start.23 = (bf16[512,512]{1,0:T(8,128)(2,1)S(1)}, bf16[512,512]{1,0:T(8,128)(2,1)}, u32[]{:S(2)}, u32[]{:S(2)}) collective-permute-start(bf16[512,512]{1,0:T(8,128)(2,1)S(1)} %copy-done.6), channel_id=1, source_target_pairs={{4,2},{2,6},{5,3},{3,7},{12,10},{10,14},{13,11},{11,15},{20,18},{1... | collective-permute-start | bytes 1572872 | tf_op jit(solution)/shard_map/ppermute | solution.py:388
  200.7 29.6 %collective-permute-start.24 = (bf16[256,512]{1,0:T(8,128)(2,1)S(1)}, bf16[256,512]{1,0:T(8,128)(2,1)S(1)}, u32[]{:S(2)}, u32[]{:S(2)}) collective-permute-start(bf16[256,512]{1,0:T(8,128)(2,1)S(1)} %get-tuple-element.56), channel_id=1, source_target_pairs={{0,4},{4,0},{1,5},{5,1},{2,6},{6,2},{3,7},{7,3},{8,12},{12,8},{9,1... | collective-permute-start | bytes 786440 | tf_op jit(solution)/shard_map/ppermute | solution.py:425
  236.3 18.4 %collective-permute-start.26 = (bf16[512,2048]{1,0:T(8,128)(2,1)}, bf16[512,2048]{1,0:T(8,128)(2,1)}, u32[]{:S(2)}, u32[]{:S(2)}) collective-permute-start(bf16[512,2048]{1,0:T(8,128)(2,1)} %get-tuple-element.45), channel_id=1, source_target_pairs={{6,4},{7,5},{14,12},{15,13},{22,20},{23,21},{30,28},{31,29}} | collective-permute-start | bytes 6291464 | tf_op jit(solution)/shard_map/ppermute | solution.py:439
  238.4 3.7 %collective-permute-start.28 = (f32[2048]{0:T(1024)S(1)}, f32[2048]{0:T(1024)S(1)}, u32[]{:S(2)}, u32[]{:S(2)}) collective-permute-start(f32[2048]{0:T(1024)S(1)} %broadcast_select_fusion.3), channel_id=1, source_target_pairs={{0,6},{6,0},{2,4},{4,2},{1,7},{7,1},{3,5},{5,3},{8,14},{14,8},{10,... | collective-permute-start | bytes 24584 | tf_op jit(solution)/shard_map/ppermute | solution.py:442
  241.4 10.7 %collective-permute-start.27 = (bf16[256,512]{1,0:T(8,128)(2,1)S(1)}, bf16[256,512]{1,0:T(8,128)(2,1)S(1)}, u32[]{:S(2)}, u32[]{:S(2)}) collective-permute-start(bf16[256,512]{1,0:T(8,128)(2,1)S(1)} %get-tuple-element.58), channel_id=1, source_target_pairs={{0,4},{4,0},{1,5},{5,1},{2,6},{6,2},{3,7},{7,3},{8,12},{12,8},{9,1... | collective-permute-start | bytes 786440 | tf_op jit(solution)/shard_map/ppermute | solution.py:425
  242.1 3.7 %collective-permute-start.29 = (f32[2048]{0:T(1024)S(1)}, f32[2048]{0:T(1024)S(1)}, u32[]{:S(2)}, u32[]{:S(2)}) collective-permute-start(f32[2048]{0:T(1024)S(1)} %fusion.18), channel_id=1, source_target_pairs={{0,8},{8,0},{16,24},{24,16},{1,9},{9,1},{17,25},{25,17},{2,10},{10... | collective-permute-start | bytes 24584 | tf_op jit(solution)/shard_map/ppermute | solution.py:445
  245.7 4.5 %collective-permute-start.30 = (f32[2048]{0:T(1024)S(1)}, f32[2048]{0:T(1024)S(1)}, u32[]{:S(2)}, u32[]{:S(2)}) collective-permute-start(f32[2048]{0:T(1024)S(1)} %add.56), channel_id=1, source_target_pairs={{0,16},{8,24},{16,0},{24,8},{1,17},{9,25},{17,1},{25,9},{2,18},{10... | collective-permute-start | bytes 24584 | tf_op jit(solution)/shard_map/ppermute | solution.py:445
  (19 other events, 211.4 us)
Sparse Core Ops, SparseCore 0:
  27.0 45.9 all-gather.2
  74.6 49.7 all-gather.4
  126.7 42.5 reduce-scatter.2
  171.6 43.1 reduce-scatter.4

commit v8 on v7

--- a/solution.py
+++ b/solution.py
@@ -302,8 +302,6 @@
     gains = [gain] + [lax.ppermute(gain_sent, "mp", turned(shards, t)) for t in range(1, shards)]
     key_count = jnp.where(straight, src_len, lax.ppermute(len_sent, "y", SWAP))
     there = lax.ppermute(after(packed, swapped[0], key_count, *gains), PLANE, [(0, 2), (2, 1)])
-    for k in range(1, CHUNKS):
-        swapped.append(lax.ppermute(after(chunk_of(1 - y, k), there), "y", SWAP))
     nears = [packed, here, there]
     fars = []
     for turn in range(1, shards):
@@ -314,6 +312,8 @@
                 across(there, turn, [(1, 1), (2, 2)]),
             ]
         )
+    for k in range(1, CHUNKS):
+        swapped.append(lax.ppermute(after(chunk_of(1 - y, k), there, fars[0][1]), "y", SWAP))
     blocks = [jnp.concatenate([chunk_of(y, k), swapped[k]], 0) for k in range(CHUNKS)]
     w_own, w_other = [], []
 
@@ -321,7 +321,7 @@
     is_grad = lax.broadcasted_iota(jnp.int32, (length, width), 1) % (2 * HEAD) >= HEAD
     masked = jnp.where(is_grad & (position >= tgt_len[0]), jnp.zeros((), BF16), packed)
     qg_near, qg_far = cut(masked, 1, y, half), cut(masked, 1, 1 - y, half)
-    qg_near, qg_far = lax.optimization_barrier((qg_near, qg_far, there))[:2]
+    qg_near, qg_far = lax.optimization_barrier((qg_near, qg_far, swapped[-1]))[:2]
     qgs = [
         qg_near,
         lax.ppermute(qg_near, PLANE, [(1, 0)]),
@@ -379,7 +379,10 @@
             if k > 0:
                 w_own[k] = after(w_own[k], grad)
         w_other.append(lax.ppermute(w_own[k], "phase", SWAP))
-        dec, gkv = attend(at, dot(enc_own, w_own[k]), enc_other, w_other[k], qgs, k)
+        part = dot(enc_own, w_own[k])
+        if k > 0:
+            part = after(part, decs[0][0], decs[0][2])
+        dec, gkv = attend(at, part, enc_other, w_other[k], qgs, k)
         gkvs.append(gkv)
         decs.append(
             (
@@ -388,17 +391,14 @@
                 lax.ppermute(dec, PLANE, [(2, 1), (1, 3)]),
             )
         )
-        parts = jnp.split(gkv, 2, axis=1)
+        gkv_sent = gkv
+        if tiled and k == CHUNKS - 1:
+            terms = [enc_grad(at, gkvs, w_own, w_other, groups, rows, s) for s in (1, 0)][::-1]
+            gkv_sent = after(gkv, *terms)
+        parts = jnp.split(gkv_sent, 2, axis=1)
         gkv_mate = jnp.concatenate([lax.ppermute(p, "phase", SWAP) for p in parts], 1)
         if tiled:
-            last = k == CHUNKS - 1
-            if last:
-                away = enc_grad(at, gkvs, w_own, w_other, groups, rows, 1)
-                gkv_mate = after(gkv_mate, away)
             grad = weight_grad(at, enc_own, enc_mate, gkv, gkv_mate, groups, pair_scale)
-            if last:
-                kept = [after(gkvs[0], grad)] + gkvs[1:]
-                terms = [enc_grad(at, kept, w_own, w_other, groups, rows, 0), away]
         else:
             grad = pair_scale * (dot(enc_own, gkv, TN) + dot(enc_mate, gkv_mate, TN))
             grad = grad.astype(BF16)
@@ -411,12 +411,11 @@
         full = full.astype(BF16).reshape(length, -1, rows)[:, back].reshape(length, D)
         terms = [cut(full, 1, (x + s) % shards, width) for s in range(shards)]
     far_terms = terms[0].astype(F32)
-    moved = []
     for turn in range(1, shards):
-        got = across(terms[turn], turn, [(1, 1), (2, 2)])
-        far_terms = far_terms + got.astype(F32)
-        moved.append(across(after(terms[turn], got), turn, [(0, 0), (3, 3)]))
-    moved.append(lax.ppermute(far_terms.astype(BF16), PLANE, [(2, 0), (1, 3)]))
+        far_terms = far_terms + across(terms[turn], turn, [(1, 1), (2, 2)]).astype(F32)
+    far_terms = after(far_terms.astype(BF16), decs[-1][2])
+    moved = [across(terms[turn], turn, [(0, 0), (3, 3)]) for turn in range(1, shards)]
+    moved.append(lax.ppermute(far_terms, PLANE, [(2, 0), (1, 3)]))
 
     dec_here = jnp.concatenate([jnp.where(y == 0, d[0], d[1]) for d in decs], 1)
     dec_there = jnp.concatenate([d[2] for d in decs], 1)
@@ -424,7 +423,7 @@
     kept = jnp.concatenate([w[:rows] for w in weight_sums], 1)
     got = [lax.ppermute(w[rows:], "y", SWAP) for w in weight_sums]
     if tiled:
-        moved[0], dec_grads, got[0] = lax.optimization_barrier((moved[0], dec_grads, got[0]))
+        moved[0], dec_grads = lax.optimization_barrier((moved[0], dec_grads))
         grad_normed, gain_term = collect(
             at, [terms[0]] + moved, packed, here, inv_rms, gain.astype(F32)[None], pair_scale
         )

time: 266 us -> 254 us (0.955)
  waiting for transfers between devices: 85.1 us -> 71.8 us
  local copies, waits for them, and re-layouts: 8.33 us -> 13 us
  other arithmetic: 21 us -> 17.5 us
    ppermute x2, waiting for transfers between devices: 25.3 us -> 0.01 us  [on_device(): got = [lax.ppermute(w[rows:], 'y', SWAP) for w in weight_sums]]
    ppermute x2, waiting for transfers between devices: 7.07 us -> 17.6 us  [the longest x1 13.2 us: on_device(): moved.append(lax.ppermute(far_terms, PLANE, [(2, 0), (1, 3)]))]
    all_gather x2, waiting for transfers between devices: 23.2 us -> 16.9 us  [on_device(): w_own.append(lax.all_gather(block, 'z', axis=0, tiled=True))]
    unnamed x30 -> x34, local copies, waits for them, and re-layouts: 2.21 us -> 7.54 us
    ppermute x1, starting transfers between devices: 0.34 us -> 5.28 us  [on_device(): enc_mate = lax.ppermute(enc_other, 'phase', SWAP)]
    ppermute x2, starting transfers between devices: 4.81 us -> 0.01 us  [on_device(): w_other.append(lax.ppermute(w_own[k], 'phase', SWAP))]
    ppermute x5, waiting for transfers between devices: 0.01 us -> 4.22 us  [across(): lax.ppermute(value, ('y', 'phase', 'mp'), [(a * shards + s, b * shards +...]
  transfers between devices with their start and end apart: 36 -> 36, of which waited for: 15 -> 15; matrix products, arithmetic and copies ran while one was open for 11% -> 10% of each run, Pallas kernels for 23% -> 24%
where the time goes in v8:
time: 254 us; the launch traced here: 252 us
  waiting for transfers between devices  71.8 us (28%)
  starting transfers between devices  67.1 us (26%)
  Pallas kernels  60 us (24%)
  other arithmetic  17.5 us (7%)
  between operations  16.1 us (6%)
  local copies, waits for them, and re-layouts  13 us (5%)
  matrix products  6.7 us (3%)
    pallas_call x2, Pallas kernels, attend(): pl.pallas_call(attend_kernel, grid_spec=pltpu.PrefetchScalarGridSpec(num_...  20.8 us
    ppermute x2, starting transfers between devices, on_device(): lax.ppermute(dec, PLANE, [(0, 1)])  18.8 us
    all_gather x2, waiting for transfers between devices, on_device(): w_own.append(lax.all_gather(block, 'z', axis=0, tiled=True))  16.9 us
    ppermute x1, waiting for transfers between devices, on_device(): lax.ppermute(after(packed, swapped[0], key_count, *gains), PLANE, [(0, 2)...  16.6 us
    pallas_call x2, Pallas kernels, enc_grad(): pl.pallas_call(enc_grad_kernel, grid_spec=pltpu.PrefetchScalarGridSpec(nu...  13.7 us
    ppermute x1, waiting for transfers between devices, on_device(): moved.append(lax.ppermute(far_terms, PLANE, [(2, 0), (1, 3)]))  13.2 us
    pallas_call x2, Pallas kernels, weight_grad(): pl.pallas_call(lambda *refs: weight_grad_kernel(scale, *refs), grid_spec=...  12.6 us
    ppermute x5, starting transfers between devices, across(): lax.ppermute(value, ('y', 'phase', 'mp'), [(a * shards + s, b * shards +...  10.5 us
  transfers between devices with their start and end apart: 36, of which 15 were waited for; matrix products, arithmetic and copies ran while one was open for 10% of the time, Pallas kernels for 24%

profile of v8, /device:TPU:0, one launch (start us, length us, event | category | flops | bytes accessed | tf_op | source)
XLA Modules:
  0.0 252.2 jit_solution(13879358467541049952)
XLA Ops:
  11.3 4.0 %collective-permute-start.2 = (bf16[256,512]{1,0:T(8,128)(2,1)S(1)}, bf16[256,512]{1,0:T(8,128)(2,1)S(1)}, u32[]{:S(2)}, u32[]{:S(2)}) collective-permute-start(bf16[256,512]{1,0:T(8,128)(2,1)S(1)} %get-tuple-element.51), channel_id=1, source_target_pairs={{0,4},{4,0},{1,5},{5,1},{2,6},{6,2},{3,7},{7,3},{8,12},{12,8},{9,1... | collective-permute-start | bytes 786440 | tf_op jit(solution)/shard_map/ppermute | solution.py:299
  18.4 3.0 %collective-permute-done.1 = s32[1]{0:T(128)} collective-permute-done((s32[1]{0:T(128)}, s32[1]{0:T(128)}, u32[]{:S(2)}, u32[]{:S(2)}) %collective-permute-start.1) | collective-permute-done | bytes 36 | tf_op jit(solution)/shard_map/ppermute | solution.py:303
  22.1 4.1 %collective-permute-start.4 = (bf16[512,2048]{1,0:T(8,128)(2,1)S(1)}, bf16[512,2048]{1,0:T(8,128)(2,1)}, u32[]{:S(2)}, u32[]{:S(2)}) collective-permute-start(bf16[512,2048]{1,0:T(8,128)(2,1)S(1)} %bitcast.17), channel_id=1, source_target_pairs={{0,4},{4,2},{1,5},{5,3},{8,12},{12,10},{9,13},{13,11},{16,20},{20,... | collective-permute-start | bytes 6291464 | tf_op jit(solution)/shard_map/ppermute | solution.py:304
  27.9 3.1 %collective-permute-start.5 = (bf16[512,2048]{1,0:T(8,128)(2,1)S(1)}, bf16[512,2048]{1,0:T(8,128)(2,1)}, u32[]{:S(2)}, u32[]{:S(2)}) collective-permute-start(bf16[512,2048]{1,0:T(8,128)(2,1)S(1)} %bitcast.18), channel_id=1, source_target_pairs={{0,1},{1,0},{8,9},{9,8},{16,17},{17,16},{24,25},{25,24}} | collective-permute-start | bytes 6291464 | tf_op jit(solution)/shard_map/ppermute | solution.py:287
  31.7 16.6 %collective-permute-done.4.refs_3_ = bf16[512,2048]{1,0:T(8,128)(2,1)} collective-permute-done((bf16[512,2048]{1,0:T(8,128)(2,1)S(1)}, bf16[512,2048]{1,0:T(8,128)(2,1)}, u32[]{:S(2)}, u32[]{:S(2)}) %collective-permute-start.4) | collective-permute-done | bytes 2097184 | tf_op jit(solution)/shard_map/ppermute | solution.py:304
  51.6 3.8 %collective-permute-start.8 = (bf16[256,512]{1,0:T(8,128)(2,1)}, bf16[256,512]{1,0:T(8,128)(2,1)S(1)}, u32[]{:S(2)}, u32[]{:S(2)}) collective-permute-start(bf16[256,512]{1,0:T(8,128)(2,1)} %get-tuple-element.28), channel_id=1, source_target_pairs={{0,4},{4,0},{1,5},{5,1},{2,6},{6,2},{3,7},{7,3},{8,12},{12,8},{9,1... | collective-permute-start | bytes 786440 | tf_op jit(solution)/shard_map/ppermute | solution.py:316
  57.2 4.4 %collective-permute-done.8 = bf16[256,512]{1,0:T(8,128)(2,1)S(1)} collective-permute-done((bf16[256,512]{1,0:T(8,128)(2,1)}, bf16[256,512]{1,0:T(8,128)(2,1)S(1)}, u32[]{:S(2)}, u32[]{:S(2)}) %collective-permute-start.8) | collective-permute-done | bytes 262176 | tf_op jit(solution)/shard_map/ppermute | solution.py:316
  65.5 7.7 %all-gather.3.cloned.1.call-done.own_0 = bf16[2048,512]{1,0:T(8,128)(2,1)} async-done(((bf16[512,512]{1,0:T(8,128)(2,1)}), bf16[2048,512]{1,0:T(8,128)(2,1)}) %all-gather.3.cloned.1.call-update) | async-done | bytes 2097168 | tf_op jit(solution)/shard_map/all_gather | solution.py:378
  75.0 6.9 %norm.1 = (bf16[512,2048]{1,0:T(8,128)(2,1)}, bf16[512,2048]{1,0:T(8,128)(2,1)}, f32[512,128]{1,0:T(8,128)S(1)}) custom-call(s32[6]{0:T(128)S(1)} %concatenate.59.refs_0_.at, bf16[512,2048]{1,0:T(8,128)(2,1)S(1)} %bitcast.19, bf16[512,2048]{1,0:T(8,128)(2,1)} %collective-permute-done.refs_2_.refs_5_, bf16[512,2048]{1,0:T(8,128)(2,1)} %collective-permute-done.4.refs_3_, ...), custom_call_target="tpu_custom_call" | custom-call | flops 16777216 | bytes 8388608 | tf_op jit(solution)/shard_map/norm/pallas_call | solution.py:73
  81.9 5.3 %collective-permute-start.12 = (bf16[512,2048]{1,0:T(8,128)(2,1)}, bf16[512,2048]{1,0:T(8,128)(2,1)S(1)}, u32[]{:S(2)}, u32[]{:S(2)}) collective-permute-start(bf16[512,2048]{1,0:T(8,128)(2,1)} %get-tuple-element.33.enc_other), channel_id=1, source_target_pairs={{0,2},{2,0},{1,3},{3,1},{4,6},{6,4},{5,7},{7,5},{8,10},{10,8},{9,1... | collective-permute-start | bytes 6291464 | tf_op jit(solution)/shard_map/ppermute | solution.py:364
  87.2 2.8 %fusion.12.part = f32[512,512]{1,0:T(8,128)S(1)} fusion(bf16[512,2048]{1,0:T(8,128)(2,1)} %get-tuple-element.32.refs_1_, bf16[2048,512]{1,0:T(8,128)(2,1)S(1)} %copy-done.16), kind=kOutput, calls=%fused_computation.35 | convolution fusion | flops 1073741824 | bytes 5242880 | tf_op jit(solution)/shard_map/dot_general | solution.py:24
  90.0 10.4 %attend.2 = (bf16[512,512]{1,0:T(8,128)(2,1)S(1)}, bf16[512,512]{1,0:T(8,128)(2,1)S(1)}) custom-call(s32[6]{0:T(128)S(1)} %concatenate.59.refs_0_.at, f32[512,512]{1,0:T(8,128)S(1)} %fusion.12.part, bf16[512,2048]{1,0:T(8,128)(2,1)} %get-tuple-element.33.enc_other, bf16[2048,512]{1,0:T(8,128)(2,1)} %collective-permute-done.11.w_other.other_0, ...), custom_call_target="tpu_custom_call" | custom-call | flops 4026531840 | bytes 8388608 | tf_op jit(solution)/shard_map/attend/pallas_call | solution.py:135
  103.9 6.3 %weight_grad.2 = bf16[2048,512]{1,0:T(8,128)(2,1)} custom-call(s32[6]{0:T(128)S(1)} %concatenate.59.refs_0_.at, bf16[512,2048]{1,0:T(8,128)(2,1)} %get-tuple-element.32.refs_1_, bf16[512,2048]{1,0:T(8,128)(2,1)} %copy-done.8, bf16[512,512]{1,0:T(8,128)(2,1)S(1)} %get-tuple-element.34.refs_3_.gkv_0, bf16[512,512]{1,0:T(8,128)(2,1)S(1)} %pad_maximum_fusion.2.refs_4_), custom_call_target="tpu_custom_call" | custom-call | flops 33554432 | tf_op jit(solution)/shard_map/weight_grad/pallas_call | solution.py:163
  110.2 9.2 %all-gather.5.cloned.1.call-done.own_1 = bf16[2048,512]{1,0:T(8,128)(2,1)} async-done(((bf16[512,512]{1,0:T(8,128)(2,1)}), bf16[2048,512]{1,0:T(8,128)(2,1)}) %all-gather.5.cloned.1.call-update) | async-done | bytes 2097168 | tf_op jit(solution)/shard_map/all_gather | solution.py:378
  120.2 5.0 %collective-permute-start.15 = (bf16[512,512]{1,0:T(8,128)(2,1)S(1)}, bf16[512,512]{1,0:T(8,128)(2,1)S(1)}, u32[]{:S(2)}, u32[]{:S(2)}) collective-permute-start(bf16[512,512]{1,0:T(8,128)(2,1)S(1)} %get-tuple-element.36), channel_id=1, source_target_pairs={{0,2},{1,3},{8,10},{9,11},{16,18},{17,19},{24,26},{25,27}} | collective-permute-start | bytes 1572872 | tf_op jit(solution)/shard_map/ppermute | solution.py:389
  125.2 3.9 %fusion.13.part = f32[512,512]{1,0:T(8,128)S(1)} fusion(bf16[512,2048]{1,0:T(8,128)(2,1)} %get-tuple-element.32.refs_1_, bf16[2048,512]{1,0:T(8,128)(2,1)} %all-gather.5.cloned.1.call-done.own_1), kind=kOutput, calls=%fused_computation.36 | convolution fusion | flops 1073741824 | bytes 5242880 | tf_op jit(solution)/shard_map/dot_general | solution.py:24
  130.7 10.4 %attend.3 = (bf16[512,512]{1,0:T(8,128)(2,1)S(1)}, bf16[512,512]{1,0:T(8,128)(2,1)S(1)}) custom-call(s32[6]{0:T(128)S(1)} %concatenate.59.refs_0_.at, f32[512,512]{1,0:T(8,128)S(1)} %fusion.13.part, bf16[512,2048]{1,0:T(8,128)(2,1)} %get-tuple-element.33.enc_other, bf16[2048,512]{1,0:T(8,128)(2,1)} %collective-permute-done.17.w_other.other_1, ...), custom_call_target="tpu_custom_call" | custom-call | flops 4026531840 | bytes 8388608 | tf_op jit(solution)/shard_map/attend/pallas_call | solution.py:135
  141.9 6.8 %enc_grad.3 = bf16[512,2048]{1,0:T(8,128)(2,1)} custom-call(s32[6]{0:T(128)S(1)} %concatenate.59.refs_0_.at, bf16[512,512]{1,0:T(8,128)(2,1)} %copy-done.4, bf16[512,512]{1,0:T(8,128)(2,1)} %copy-done.5, bf16[2048,512]{1,0:T(8,128)(2,1)} %all-gather.3.cloned.1.call-done.own_0, bf16[2048,512]{1,0:T(8,128)(2,1)} %all-gather.5.cloned.1.call-done.own_1, ...), custom_call_target="tpu_custom_call" | custom-call | flops 4294967296 | bytes 8388608 | tf_op jit(solution)/shard_map/enc_grad/pallas_call | solution.py:240
  150.9 6.9 %enc_grad.2.refs_1_ = bf16[512,2048]{1,0:T(8,128)(2,1)} custom-call(s32[6]{0:T(128)S(1)} %concatenate.59.refs_0_.at, bf16[512,512]{1,0:T(8,128)(2,1)} %copy-done.4, bf16[512,512]{1,0:T(8,128)(2,1)} %copy-done.5, bf16[2048,512]{1,0:T(8,128)(2,1)} %all-gather.3.cloned.1.call-done.own_0, bf16[2048,512]{1,0:T(8,128)(2,1)} %all-gather.5.cloned.1.call-done.own_1, ...), custom_call_target="tpu_custom_call" | custom-call | flops 4294967296 | bytes 8388608 | tf_op jit(solution)/shard_map/enc_grad/pallas_call | solution.py:240
  157.8 2.9 %collective-permute-start.24 = (bf16[512,256]{1,0:T(8,128)(2,1)S(1)}, bf16[512,256]{1,0:T(8,128)(2,1)S(1)}, u32[]{:S(2)}, u32[]{:S(2)}) collective-permute-start(bf16[512,256]{1,0:T(8,128)(2,1)S(1)} %get-tuple-element.57), channel_id=1, source_target_pairs={{0,2},{2,0},{1,3},{3,1},{4,6},{6,4},{5,7},{7,5},{8,10},{10,8},{9,1... | collective-permute-start | bytes 786440 | tf_op jit(solution)/shard_map/ppermute | solution.py:399
  162.3 6.3 %weight_grad.3 = bf16[2048,512]{1,0:T(8,128)(2,1)} custom-call(s32[6]{0:T(128)S(1)} %concatenate.59.refs_0_.at, bf16[512,2048]{1,0:T(8,128)(2,1)} %get-tuple-element.32.refs_1_, bf16[512,2048]{1,0:T(8,128)(2,1)} %copy-done.8, bf16[512,512]{1,0:T(8,128)(2,1)S(1)} %copy-done.6, bf16[512,512]{1,0:T(8,128)(2,1)S(1)} %pad_maximum_fusion.3.refs_4_), custom_call_target="tpu_custom_call" | custom-call | flops 33554432 | tf_op jit(solution)/shard_map/weight_grad/pallas_call | solution.py:163
  168.6 2.4 collective-permute-start.18
  171.8 4.5 %add_convert_fusion = bf16[512,2048]{1,0:T(8,128)(2,1)} fusion(bf16[512,2048]{1,0:T(8,128)(2,1)} %collective-permute-done.21, bf16[512,2048]{1,0:T(8,128)(2,1)} %enc_grad.2.refs_1_), kind=kLoop, calls=%fused_computation | loop fusion | flops 4194304 | bytes 6291456 | tf_op jit(solution)/shard_map/convert_element_type | solution.py:416
  178.4 13.7 %collective-permute-start.19 = (bf16[512,512]{1,0:T(8,128)(2,1)S(1)}, bf16[512,512]{1,0:T(8,128)(2,1)}, u32[]{:S(2)}, u32[]{:S(2)}) collective-permute-start(bf16[512,512]{1,0:T(8,128)(2,1)S(1)} %get-tuple-element.39), channel_id=1, source_target_pairs={{0,2},{1,3},{8,10},{9,11},{16,18},{17,19},{24,26},{25,27}} | collective-permute-start | bytes 1572872 | tf_op jit(solution)/shard_map/ppermute | solution.py:389
  196.2 4.2 %collective-permute-done.18.refs_2_ = bf16[512,2048]{1,0:T(8,128)(2,1)} collective-permute-done((bf16[512,2048]{1,0:T(8,128)(2,1)}, bf16[512,2048]{1,0:T(8,128)(2,1)}, u32[]{:S(2)}, u32[]{:S(2)}) %collective-permute-start.18) | collective-permute-done | bytes 2097184 | tf_op jit(solution)/shard_map/ppermute | solution.py:287
  200.4 13.2 %collective-permute-done.22.refs_3_ = bf16[512,2048]{1,0:T(8,128)(2,1)} collective-permute-done((bf16[512,2048]{1,0:T(8,128)(2,1)}, bf16[512,2048]{1,0:T(8,128)(2,1)}, u32[]{:S(2)}, u32[]{:S(2)}) %collective-permute-start.22) | collective-permute-done | bytes 2097184 | tf_op jit(solution)/shard_map/ppermute | solution.py:418
  213.6 6.0 %collect.1 = (bf16[512,2048]{1,0:T(8,128)(2,1)}, f32[4,1,2048]{2,1,0:T(1,128)S(1)}) custom-call(s32[6]{0:T(128)S(1)} %concatenate.59.refs_0_.at, bf16[512,2048]{1,0:T(8,128)(2,1)S(1)} %copy-done.1, bf16[512,2048]{1,0:T(8,128)(2,1)} %collective-permute-done.18.refs_2_, bf16[512,2048]{1,0:T(8,128)(2,1)} %collective-permute-done.22.refs_3_, ...), custom_call_target="tpu_custom_call" | custom-call | flops 8388608 | bytes 12582912 | tf_op jit(solution)/shard_map/collect/pallas_call | solution.py:197
  226.7 2.6 %collective-permute-done.28 = f32[2048]{0:T(1024)S(1)} collective-permute-done((f32[2048]{0:T(1024)S(1)}, f32[2048]{0:T(1024)S(1)}, u32[]{:S(2)}, u32[]{:S(2)}) %collective-permute-start.28) | collective-permute-done | bytes 8224 | tf_op jit(solution)/shard_map/ppermute | solution.py:441
  229.3 3.6 %collective-permute-done.29 = f32[2048]{0:T(1024)S(1)} collective-permute-done((f32[2048]{0:T(1024)S(1)}, f32[2048]{0:T(1024)S(1)}, u32[]{:S(2)}, u32[]{:S(2)}) %collective-permute-start.29) | collective-permute-done | bytes 8224 | tf_op jit(solution)/shard_map/ppermute | solution.py:444
  234.1 3.5 %collective-permute-done.30 = f32[2048]{0:T(1024)S(1)} collective-permute-done((f32[2048]{0:T(1024)S(1)}, f32[2048]{0:T(1024)S(1)}, u32[]{:S(2)}, u32[]{:S(2)}) %collective-permute-start.30) | collective-permute-done | bytes 8224 | tf_op jit(solution)/shard_map/ppermute | solution.py:444
  239.9 2.7 %fusion.2 = f32[256,2048]{1,0:T(8,128)} fusion(bf16[256,512]{1,0:T(8,128)(2,1)} %collective-permute-done.27, bf16[256,512]{1,0:T(8,128)(2,1)S(1)} %collective-permute-done.26, bf16[256,512]{1,0:T(8,128)(2,1)S(1)} %get-tuple-element.55, bf16[256,512]{1,0:T(8,128)(2,1)S(1)} %get-tuple-element.53, pred[]{:T(512)S(6)} %eq.19), kind=kLoop, calls=%fused_computation.7 | loop fusion | flops 9437184 | bytes 3145729 | tf_op jit(solution)/shard_map/convert_element_type | solution.py:449
  242.5 3.2 %select_bitcast_fusion = bf16[1,1,512,2048]{3,2,1,0:T(8,128)(2,1)} fusion(bf16[512,2048]{1,0:T(8,128)(2,1)S(1)} %copy-done.7, bf16[512,2048]{1,0:T(8,128)(2,1)} %get-tuple-element.43, bf16[512,2048]{1,0:T(8,128)(2,1)} %collective-permute-done.23, pred[]{:T(512)S(6)} %eq.19, pred[]{:T(512)S(6)} %eq.18), kind=kLoop, calls=%fused_computation.5 | loop fusion | flops 2097152 | bytes 8388610 | tf_op jit(solution)/shard_map/broadcast_in_dim | solution.py:450
  (119 shorter events, 46.6 us)
Async XLA Ops:
  7.2 66.0 %all-gather.3.cloned.1.call-start = ((), (), s32[]{:S(2)}) async-start(), calls=%async_computation.2 | async-start | bytes 2621440 | tf_op jit(solution)/shard_map/all_gather | solution.py:378
  7.2 8.2 %collective-permute-start = (bf16[512,2048]{1,0:T(8,128)(2,1)}, bf16[512,2048]{1,0:T(8,128)(2,1)}, u32[]{:S(2)}, u32[]{:S(2)}) collective-permute-start(bf16[512,2048]{1,0:T(8,128)(2,1)} %bitcast.16), channel_id=1, source_target_pairs={{4,6},{5,7},{12,14},{13,15},{20,22},{21,23},{28,30},{29,31}} | collective-permute-start | bytes 6291464 | tf_op jit(solution)/shard_map/ppermute | solution.py:300
  11.3 10.7 %collective-permute-start.2 = (bf16[256,512]{1,0:T(8,128)(2,1)S(1)}, bf16[256,512]{1,0:T(8,128)(2,1)S(1)}, u32[]{:S(2)}, u32[]{:S(2)}) collective-permute-start(bf16[256,512]{1,0:T(8,128)(2,1)S(1)} %get-tuple-element.51), channel_id=1, source_target_pairs={{0,4},{4,0},{1,5},{5,1},{2,6},{6,2},{3,7},{7,3},{8,12},{12,8},{9,1... | collective-permute-start | bytes 786440 | tf_op jit(solution)/shard_map/ppermute | solution.py:299
  15.4 6.6 %collective-permute-start.3 = (bf16[2048]{0:T(1024)(128)(2,1)S(1)}, bf16[2048]{0:T(1024)(128)(2,1)S(1)}, u32[]{:S(2)}, u32[]{:S(2)}) collective-permute-start(bf16[2048]{0:T(1024)(128)(2,1)S(1)} %copy-done.15), channel_id=1, source_target_pairs={{0,1},{1,0},{2,3},{3,2},{4,5},{5,4},{6,7},{7,6},{8,9},{9,8},{10,11... | collective-permute-start | bytes 12296 | tf_op jit(solution)/shard_map/ppermute | solution.py:302
  17.5 3.8 %collective-permute-start.1 = (s32[1]{0:T(128)}, s32[1]{0:T(128)}, u32[]{:S(2)}, u32[]{:S(2)}) collective-permute-start(s32[1]{0:T(128)} %param.8), channel_id=1, source_target_pairs={{0,4},{4,0},{1,5},{5,1},{2,6},{6,2},{3,7},{7,3},{8,12},{12,8},{9,1... | collective-permute-start | bytes 20 | tf_op jit(solution)/shard_map/ppermute | solution.py:303
  22.1 26.3 %collective-permute-start.4 = (bf16[512,2048]{1,0:T(8,128)(2,1)S(1)}, bf16[512,2048]{1,0:T(8,128)(2,1)}, u32[]{:S(2)}, u32[]{:S(2)}) collective-permute-start(bf16[512,2048]{1,0:T(8,128)(2,1)S(1)} %bitcast.17), channel_id=1, source_target_pairs={{0,4},{4,2},{1,5},{5,3},{8,12},{12,10},{9,13},{13,11},{16,20},{20,... | collective-permute-start | bytes 6291464 | tf_op jit(solution)/shard_map/ppermute | solution.py:304
  27.0 92.4 %all-gather.5.cloned.1.call-start = ((), (), s32[]{:S(2)}) async-start(), calls=%async_computation.3 | async-start | bytes 2621440 | tf_op jit(solution)/shard_map/all_gather | solution.py:378
  27.1 23.2 %collective-permute-start.6 = (bf16[512,2048]{1,0:T(8,128)(2,1)}, bf16[512,2048]{1,0:T(8,128)(2,1)S(1)}, u32[]{:S(2)}, u32[]{:S(2)}) collective-permute-start(bf16[512,2048]{1,0:T(8,128)(2,1)} %collective-permute-done.refs_2_.refs_5_), channel_id=1, source_target_pairs={{6,7},{7,6},{14,15},{15,14},{22,23},{23,22},{30,31},{31,30}} | collective-permute-start | bytes 6291464 | tf_op jit(solution)/shard_map/ppermute | solution.py:287
  27.9 45.5 %collective-permute-start.5 = (bf16[512,2048]{1,0:T(8,128)(2,1)S(1)}, bf16[512,2048]{1,0:T(8,128)(2,1)}, u32[]{:S(2)}, u32[]{:S(2)}) collective-permute-start(bf16[512,2048]{1,0:T(8,128)(2,1)S(1)} %bitcast.18), channel_id=1, source_target_pairs={{0,1},{1,0},{8,9},{9,8},{16,17},{17,16},{24,25},{25,24}} | collective-permute-start | bytes 6291464 | tf_op jit(solution)/shard_map/ppermute | solution.py:287
  48.3 25.0 %collective-permute-start.7 = (bf16[512,2048]{1,0:T(8,128)(2,1)}, bf16[512,2048]{1,0:T(8,128)(2,1)}, u32[]{:S(2)}, u32[]{:S(2)}) collective-permute-start(bf16[512,2048]{1,0:T(8,128)(2,1)} %collective-permute-done.4.refs_3_), channel_id=1, source_target_pairs={{2,3},{3,2},{4,5},{5,4},{10,11},{11,10},{12,13},{13,12},{18,19},{1... | collective-permute-start | bytes 6291464 | tf_op jit(solution)/shard_map/ppermute | solution.py:287
  51.6 10.0 %collective-permute-start.8 = (bf16[256,512]{1,0:T(8,128)(2,1)}, bf16[256,512]{1,0:T(8,128)(2,1)S(1)}, u32[]{:S(2)}, u32[]{:S(2)}) collective-permute-start(bf16[256,512]{1,0:T(8,128)(2,1)} %get-tuple-element.28), channel_id=1, source_target_pairs={{0,4},{4,0},{1,5},{5,1},{2,6},{6,2},{3,7},{7,3},{8,12},{12,8},{9,1... | collective-permute-start | bytes 786440 | tf_op jit(solution)/shard_map/ppermute | solution.py:316
  61.6 11.7 %collective-permute-start.10 = (bf16[512,1024]{1,0:T(8,128)(2,1)}, bf16[512,1024]{1,0:T(8,128)(2,1)}, u32[]{:S(2)}, u32[]{:S(2)}) collective-permute-start(bf16[512,1024]{1,0:T(8,128)(2,1)} %get-tuple-element.30), channel_id=1, source_target_pairs={{2,4},{6,2},{3,5},{7,3},{10,12},{14,10},{11,13},{15,11},{18,20},{2... | collective-permute-start | bytes 3145736 | tf_op jit(solution)/shard_map/ppermute | solution.py:328
  63.3 10.1 %collective-permute-start.9 = (bf16[512,1024]{1,0:T(8,128)(2,1)S(1)}, bf16[512,1024]{1,0:T(8,128)(2,1)}, u32[]{:S(2)}, u32[]{:S(2)}) collective-permute-start(bf16[512,1024]{1,0:T(8,128)(2,1)S(1)} %get-tuple-element.29.refs_0_), channel_id=1, source_target_pairs={{2,0},{3,1},{10,8},{11,9},{18,16},{19,17},{26,24},{27,25}} | collective-permute-start | bytes 3145736 | tf_op jit(solution)/shard_map/ppermute | solution.py:327
  65.4 156.2 %reduce-scatter.3.cloned.1.call-start = ((), (), s32[]{:S(2)}) async-start(), calls=%async_computation.4 | async-start | bytes 2621440 | tf_op jit(solution)/shard_map/reduce_scatter | solution.py:405
  73.2 16.8 %collective-permute-start.11 = (bf16[2048,512]{1,0:T(8,128)(2,1)}, bf16[2048,512]{1,0:T(8,128)(2,1)}, u32[]{:S(2)}, u32[]{:S(2)}) collective-permute-start(bf16[2048,512]{1,0:T(8,128)(2,1)} %all-gather.3.cloned.1.call-done.own_0), channel_id=1, source_target_pairs={{0,2},{2,0},{1,3},{3,1},{4,6},{6,4},{5,7},{7,5},{8,10},{10,8},{9,1... | collective-permute-start | bytes 6291464 | tf_op jit(solution)/shard_map/ppermute | solution.py:381
  81.9 20.6 %collective-permute-start.12 = (bf16[512,2048]{1,0:T(8,128)(2,1)}, bf16[512,2048]{1,0:T(8,128)(2,1)S(1)}, u32[]{:S(2)}, u32[]{:S(2)}) collective-permute-start(bf16[512,2048]{1,0:T(8,128)(2,1)} %get-tuple-element.33.enc_other), channel_id=1, source_target_pairs={{0,2},{2,0},{1,3},{3,1},{4,6},{6,4},{5,7},{7,5},{8,10},{10,8},{9,1... | collective-permute-start | bytes 6291464 | tf_op jit(solution)/shard_map/ppermute | solution.py:364
  119.4 11.3 %collective-permute-start.17 = (bf16[2048,512]{1,0:T(8,128)(2,1)}, bf16[2048,512]{1,0:T(8,128)(2,1)}, u32[]{:S(2)}, u32[]{:S(2)}) collective-permute-start(bf16[2048,512]{1,0:T(8,128)(2,1)} %all-gather.5.cloned.1.call-done.own_1), channel_id=1, source_target_pairs={{0,2},{2,0},{1,3},{3,1},{4,6},{6,4},{5,7},{7,5},{8,10},{10,8},{9,1... | collective-permute-start | bytes 6291464 | tf_op jit(solution)/shard_map/ppermute | solution.py:381
  119.4 104.4 %reduce-scatter.5.cloned.1.call-start = ((), (), s32[]{:S(2)}) async-start(), calls=%async_computation.5 | async-start | bytes 2621440 | tf_op jit(solution)/shard_map/reduce_scatter | solution.py:405
  119.5 9.6 %collective-permute-start.16 = (bf16[512,512]{1,0:T(8,128)(2,1)S(1)}, bf16[512,512]{1,0:T(8,128)(2,1)S(1)}, u32[]{:S(2)}, u32[]{:S(2)}) collective-permute-start(bf16[512,512]{1,0:T(8,128)(2,1)S(1)} %get-tuple-element.36), channel_id=1, source_target_pairs={{4,2},{2,6},{5,3},{3,7},{12,10},{10,14},{13,11},{11,15},{20,18},{1... | collective-permute-start | bytes 1572872 | tf_op jit(solution)/shard_map/ppermute | solution.py:391
  120.2 8.9 %collective-permute-start.15 = (bf16[512,512]{1,0:T(8,128)(2,1)S(1)}, bf16[512,512]{1,0:T(8,128)(2,1)S(1)}, u32[]{:S(2)}, u32[]{:S(2)}) collective-permute-start(bf16[512,512]{1,0:T(8,128)(2,1)S(1)} %get-tuple-element.36), channel_id=1, source_target_pairs={{0,2},{1,3},{8,10},{9,11},{16,18},{17,19},{24,26},{25,27}} | collective-permute-start | bytes 1572872 | tf_op jit(solution)/shard_map/ppermute | solution.py:389
  148.8 23.0 %collective-permute-start.21 = (bf16[512,2048]{1,0:T(8,128)(2,1)}, bf16[512,2048]{1,0:T(8,128)(2,1)}, u32[]{:S(2)}, u32[]{:S(2)}) collective-permute-start(bf16[512,2048]{1,0:T(8,128)(2,1)} %enc_grad.3), channel_id=1, source_target_pairs={{2,3},{3,2},{4,5},{5,4},{10,11},{11,10},{12,13},{13,12},{18,19},{1... | collective-permute-start | bytes 6291464 | tf_op jit(solution)/shard_map/ppermute | solution.py:287
  157.8 4.1 %collective-permute-start.24 = (bf16[512,256]{1,0:T(8,128)(2,1)S(1)}, bf16[512,256]{1,0:T(8,128)(2,1)S(1)}, u32[]{:S(2)}, u32[]{:S(2)}) collective-permute-start(bf16[512,256]{1,0:T(8,128)(2,1)S(1)} %get-tuple-element.57), channel_id=1, source_target_pairs={{0,2},{2,0},{1,3},{3,1},{4,6},{6,4},{5,7},{7,5},{8,10},{10,8},{9,1... | collective-permute-start | bytes 786440 | tf_op jit(solution)/shard_map/ppermute | solution.py:399
  168.6 31.8 %collective-permute-start.18 = (bf16[512,2048]{1,0:T(8,128)(2,1)}, bf16[512,2048]{1,0:T(8,128)(2,1)}, u32[]{:S(2)}, u32[]{:S(2)}) collective-permute-start(bf16[512,2048]{1,0:T(8,128)(2,1)} %enc_grad.3), channel_id=1, source_target_pairs={{0,1},{1,0},{6,7},{7,6},{8,9},{9,8},{14,15},{15,14},{16,17},{17,16... | collective-permute-start | bytes 6291464 | tf_op jit(solution)/shard_map/ppermute | solution.py:287
  171.1 5.2 %collective-permute-start.20 = (bf16[512,512]{1,0:T(8,128)(2,1)S(1)}, bf16[512,512]{1,0:T(8,128)(2,1)S(1)}, u32[]{:S(2)}, u32[]{:S(2)}) collective-permute-start(bf16[512,512]{1,0:T(8,128)(2,1)S(1)} %get-tuple-element.39), channel_id=1, source_target_pairs={{4,2},{2,6},{5,3},{3,7},{12,10},{10,14},{13,11},{11,15},{20,18},{1... | collective-permute-start | bytes 1572872 | tf_op jit(solution)/shard_map/ppermute | solution.py:391
  177.1 36.5 %collective-permute-start.22 = (bf16[512,2048]{1,0:T(8,128)(2,1)}, bf16[512,2048]{1,0:T(8,128)(2,1)}, u32[]{:S(2)}, u32[]{:S(2)}) collective-permute-start(bf16[512,2048]{1,0:T(8,128)(2,1)} %add_convert_fusion), channel_id=1, source_target_pairs={{4,0},{2,6},{5,1},{3,7},{12,8},{10,14},{13,9},{11,15},{20,16},{18,... | collective-permute-start | bytes 6291464 | tf_op jit(solution)/shard_map/ppermute | solution.py:418
  178.4 15.0 %collective-permute-start.19 = (bf16[512,512]{1,0:T(8,128)(2,1)S(1)}, bf16[512,512]{1,0:T(8,128)(2,1)}, u32[]{:S(2)}, u32[]{:S(2)}) collective-permute-start(bf16[512,512]{1,0:T(8,128)(2,1)S(1)} %get-tuple-element.39), channel_id=1, source_target_pairs={{0,2},{1,3},{8,10},{9,11},{16,18},{17,19},{24,26},{25,27}} | collective-permute-start | bytes 1572872 | tf_op jit(solution)/shard_map/ppermute | solution.py:389
  219.6 22.9 %collective-permute-start.23 = (bf16[512,2048]{1,0:T(8,128)(2,1)}, bf16[512,2048]{1,0:T(8,128)(2,1)}, u32[]{:S(2)}, u32[]{:S(2)}) collective-permute-start(bf16[512,2048]{1,0:T(8,128)(2,1)} %get-tuple-element.43), channel_id=1, source_target_pairs={{6,4},{7,5},{14,12},{15,13},{22,20},{23,21},{30,28},{31,29}} | collective-permute-start | bytes 6291464 | tf_op jit(solution)/shard_map/ppermute | solution.py:438
  222.7 17.2 %collective-permute-start.26 = (bf16[256,512]{1,0:T(8,128)(2,1)S(1)}, bf16[256,512]{1,0:T(8,128)(2,1)S(1)}, u32[]{:S(2)}, u32[]{:S(2)}) collective-permute-start(bf16[256,512]{1,0:T(8,128)(2,1)S(1)} %get-tuple-element.54), channel_id=1, source_target_pairs={{0,4},{4,0},{1,5},{5,1},{2,6},{6,2},{3,7},{7,3},{8,12},{12,8},{9,1... | collective-permute-start | bytes 786440 | tf_op jit(solution)/shard_map/ppermute | solution.py:424
  222.8 6.5 %collective-permute-start.28 = (f32[2048]{0:T(1024)S(1)}, f32[2048]{0:T(1024)S(1)}, u32[]{:S(2)}, u32[]{:S(2)}) collective-permute-start(f32[2048]{0:T(1024)S(1)} %broadcast_select_fusion.3), channel_id=1, source_target_pairs={{0,6},{6,0},{2,4},{4,2},{1,7},{7,1},{3,5},{5,3},{8,14},{14,8},{10,... | collective-permute-start | bytes 24584 | tf_op jit(solution)/shard_map/ppermute | solution.py:441
  224.9 15.0 %collective-permute-start.27 = (bf16[256,512]{1,0:T(8,128)(2,1)S(1)}, bf16[256,512]{1,0:T(8,128)(2,1)}, u32[]{:S(2)}, u32[]{:S(2)}) collective-permute-start(bf16[256,512]{1,0:T(8,128)(2,1)S(1)} %get-tuple-element.56), channel_id=1, source_target_pairs={{0,4},{4,0},{1,5},{5,1},{2,6},{6,2},{3,7},{7,3},{8,12},{12,8},{9,1... | collective-permute-start | bytes 786440 | tf_op jit(solution)/shard_map/ppermute | solution.py:424
  229.3 3.7 %collective-permute-start.29 = (f32[2048]{0:T(1024)S(1)}, f32[2048]{0:T(1024)S(1)}, u32[]{:S(2)}, u32[]{:S(2)}) collective-permute-start(f32[2048]{0:T(1024)S(1)} %fusion.18), channel_id=1, source_target_pairs={{0,8},{8,0},{16,24},{24,16},{1,9},{9,1},{17,25},{25,17},{2,10},{10... | collective-permute-start | bytes 24584 | tf_op jit(solution)/shard_map/ppermute | solution.py:444
  233.0 4.5 %collective-permute-start.30 = (f32[2048]{0:T(1024)S(1)}, f32[2048]{0:T(1024)S(1)}, u32[]{:S(2)}, u32[]{:S(2)}) collective-permute-start(f32[2048]{0:T(1024)S(1)} %add.56), channel_id=1, source_target_pairs={{0,16},{8,24},{16,0},{24,8},{1,17},{9,25},{17,1},{25,9},{2,18},{10... | collective-permute-start | bytes 24584 | tf_op jit(solution)/shard_map/ppermute | solution.py:444
  (21 other events, 128.0 us)
Sparse Core Ops, SparseCore 0:
  27.1 45.9 all-gather.2
  74.7 44.6 all-gather.4
  121.7 42.5 reduce-scatter.2
  168.8 40.9 reduce-scatter.4

commit v9 on v8

--- a/solution.py
+++ b/solution.py
@@ -9,6 +9,7 @@
 HEAD = 64
 EPS = 1e-06
 CHUNKS = 2
+PARTS = 2
 DIRECT = ()
 F32 = jnp.float32
 BF16 = jnp.bfloat16
@@ -176,10 +177,11 @@
 
 
 def collect_kernel(scale, at, *refs):
-    terms, (local, here, inv, gain, out, gain_term) = refs[:3], refs[3:]
-    total = terms[0][...].astype(F32)
-    for term in terms[1:]:
-        total = total + term[...].astype(F32)
+    terms, (local, here, inv, gain, out, gain_term) = refs[: 3 * PARTS], refs[3 * PARTS :]
+    late = pl.program_id(0) >= pl.num_programs(0) // PARTS
+    total = jnp.zeros(local.shape, F32)
+    for i in range(0, 3 * PARTS, PARTS):
+        total = total + jnp.where(late, terms[i + 1][...], terms[i][...]).astype(F32)
     out[...] = (total * gain[...]).astype(BF16)
     raw = jnp.where(at[0] == 0, local[...], here[...]).astype(F32)
     product = total * (raw * inv[:, :1])
@@ -189,17 +191,21 @@
 def collect(at, terms, local, here, inv_rms, gain, scale):
     length, width = local.shape
     step = 128
+    each = length // step // PARTS
     block = pl.BlockSpec((step, width), lambda i, s: (i, 0))
 
     def pick(want):
         return pl.BlockSpec((step, width), lambda i, s: (jnp.where(s[0] == want, i, 0), 0))
+
+    def piece(part):
+        return pl.BlockSpec((step, width), lambda i, s: (jnp.clip(i - part * each, 0, each - 1), 0))
 
     return pl.pallas_call(
         lambda *refs: collect_kernel(scale, *refs),
         grid_spec=pltpu.PrefetchScalarGridSpec(
             num_scalar_prefetch=1,
             grid=(length // step,),
-            in_specs=[block] * 3
+            in_specs=[piece(0), piece(1)] * 3
             + [pick(0), pick(1)]
             + [
                 pl.BlockSpec((step, 128), lambda i, s: (i, 0)),
@@ -212,18 +218,22 @@
             jax.ShapeDtypeStruct((length // step, 1, width), F32),
         ],
         cost_estimate=cost(8 * length * width, 12),
-        compiler_params=params(16),
+        compiler_params=params(20),
         name="collect",
-    )(at, *terms, local, here, inv_rms, gain)
-
-
-def enc_grad_kernel(at, gkv_0, gkv_1, own_0, own_1, other_0, other_1, out):
+    )(at, *[p for term in terms for p in term], local, here, inv_rms, gain)
+
+
+def enc_grad_kernel(at, gkv_0, gkv_1, own_0, own_1, other_0, other_1, *outs):
     rows = own_0.shape[0]
     own = dot(gkv_0[...], own_0[...], NT) + dot(gkv_1[...], own_1[...], NT)
     other = dot(gkv_0[...], other_0[...], NT) + dot(gkv_1[...], other_1[...], NT)
     first = at[3] == 0
-    out[:, :rows] = jnp.where(first, own, other).astype(BF16)
-    out[:, rows:] = jnp.where(first, other, own).astype(BF16)
+    left = jnp.where(first, own, other).astype(BF16)
+    right = jnp.where(first, other, own).astype(BF16)
+    for i, out in enumerate(outs):
+        part = slice(i * out.shape[0], (i + 1) * out.shape[0])
+        out[:, :rows] = left[part]
+        out[:, rows:] = right[part]
 
 
 def enc_grad(at, gkvs, owns, others, groups, rows, shard):
@@ -243,9 +253,9 @@
             num_scalar_prefetch=1,
             grid=(groups,),
             in_specs=[gkv, gkv, weight, weight, weight, weight],
-            out_specs=pl.BlockSpec((length, 2 * rows), lambda i, s: (0, i)),
-        ),
-        out_shape=pltpu.HBM((length, D // 2), BF16),
+            out_specs=[pl.BlockSpec((length // PARTS, 2 * rows), lambda i, s: (0, i))] * PARTS,
+        ),
+        out_shape=[pltpu.HBM((length // PARTS, D // 2), BF16)] * PARTS,
         compiler_params=params(12),
         cost_estimate=cost(4 * length * D * cols, 8),
         name="enc_grad",
@@ -394,7 +404,7 @@
         gkv_sent = gkv
         if tiled and k == CHUNKS - 1:
             terms = [enc_grad(at, gkvs, w_own, w_other, groups, rows, s) for s in (1, 0)][::-1]
-            gkv_sent = after(gkv, *terms)
+            gkv_sent = after(gkv, *terms[0], *terms[1])
         parts = jnp.split(gkv_sent, 2, axis=1)
         gkv_mate = jnp.concatenate([lax.ppermute(p, "phase", SWAP) for p in parts], 1)
         if tiled:
@@ -409,13 +419,17 @@
         full = dot(gkv_all, jnp.concatenate([jnp.concatenate(w, 0) for w in zip(w_own, w_other)], 1), NT)
         back = jnp.zeros_like(block_order).at[block_order].set(jnp.arange(block_order.shape[0]))
         full = full.astype(BF16).reshape(length, -1, rows)[:, back].reshape(length, D)
-        terms = [cut(full, 1, (x + s) % shards, width) for s in range(shards)]
-    far_terms = terms[0].astype(F32)
-    for turn in range(1, shards):
-        far_terms = far_terms + across(terms[turn], turn, [(1, 1), (2, 2)]).astype(F32)
-    far_terms = after(far_terms.astype(BF16), decs[-1][2])
-    moved = [across(terms[turn], turn, [(0, 0), (3, 3)]) for turn in range(1, shards)]
-    moved.append(lax.ppermute(far_terms, PLANE, [(2, 0), (1, 3)]))
+        terms = [jnp.split(cut(full, 1, (x + s) % shards, width), PARTS) for s in range(shards)]
+    far = []
+    for part in range(PARTS):
+        total = terms[0][part].astype(F32)
+        for turn in range(1, shards):
+            total = total + across(terms[turn][part], turn, [(1, 1), (2, 2)]).astype(F32)
+        far.append(after(total.astype(BF16), decs[-1][2]))
+    moved = [
+        [across(part, turn, [(0, 0), (3, 3)]) for part in terms[turn]] for turn in range(1, shards)
+    ]
+    moved.append([lax.ppermute(part, PLANE, [(2, 0), (1, 3)]) for part in far])
 
     dec_here = jnp.concatenate([jnp.where(y == 0, d[0], d[1]) for d in decs], 1)
     dec_there = jnp.concatenate([d[2] for d in decs], 1)
@@ -423,31 +437,30 @@
     kept = jnp.concatenate([w[:rows] for w in weight_sums], 1)
     got = [lax.ppermute(w[rows:], "y", SWAP) for w in weight_sums]
     if tiled:
-        moved[0], dec_grads = lax.optimization_barrier((moved[0], dec_grads))
+        moved[0][0], dec_grads, got[0] = lax.optimization_barrier((moved[0][0], dec_grads, got[0]))
         grad_normed, gain_term = collect(
             at, [terms[0]] + moved, packed, here, inv_rms, gain.astype(F32)[None], pair_scale
         )
         gain_term = jnp.sum(gain_term, axis=(0, 1))
     else:
-        grad_enc = terms[0].astype(F32)
-        for part in moved:
-            grad_enc = grad_enc + part.astype(F32)
+        grad_enc = sum(jnp.concatenate(t, 0).astype(F32) for t in [terms[0]] + moved)
         grad_normed = (grad_enc * gain.astype(F32)).astype(BF16)
-        normed = raw[0].astype(F32) * inv_rms
+        normed = chosen(enc_kind, *nears).astype(F32) * inv_rms
         gain_term = pair_scale * jnp.sum(grad_enc * normed, axis=0)
     enc_grads = jnp.where(y == 0, grad_normed, lax.ppermute(grad_normed, PLANE, [(3, 2)]))
+    sec_grads = jnp.where(core == 0, enc_grads, dec_grads)[None, None]
 
     gain_term = jnp.where(straight, gain_term, 0.0)
     gain_term = gain_term + lax.ppermute(gain_term, PLANE, [(0, 3), (3, 0), (1, 2), (2, 1)])
     turn = 1
     while turn < groups:
+        if 2 * turn == groups:
+            gain_term, sec_grads = lax.optimization_barrier((gain_term, sec_grads))
         gain_term = gain_term + lax.ppermute(gain_term, "z", [(i, i ^ turn) for i in range(groups)])
         turn *= 2
     d_gain = jnp.where(straight, gain_term, lax.ppermute(gain_term, "phase", SWAP))
-
     got = jnp.concatenate(got, 1)
     d_wkv = ordered(y == 0, kept, got, 1).astype(F32)
-    sec_grads = jnp.where(core == 0, enc_grads, dec_grads)[None, None]
     return (sec_grads, d_wkv, d_gain)
 
 

time: 254 us -> 252 us (level)
    ppermute x2, waiting for transfers between devices: 0.01 us -> 16.6 us  [on_device(): got = [lax.ppermute(w[rows:], 'y', SWAP) for w in weight_sums]]
    ppermute x1 -> x2, waiting for transfers between devices: 13.2 us -> 0.01 us  [on_device(): moved.append([lax.ppermute(part, PLANE, [(2, 0), (1, 3)]) for part in far])]
    ppermute x2, starting transfers between devices: 18.8 us -> 9.22 us  [on_device(): lax.ppermute(dec, PLANE, [(0, 1)])]
    ppermute x5 -> x7, starting transfers between devices: 10.5 us -> 15.1 us  [across(): lax.ppermute(value, ('y', 'phase', 'mp'), [(a * shards + s, b * shards +...]
    ppermute x5 -> x7, waiting for transfers between devices: 4.22 us -> 0.02 us  [across(): lax.ppermute(value, ('y', 'phase', 'mp'), [(a * shards + s, b * shards +...]
    ppermute x2, starting transfers between devices: 1.86 us -> 4.68 us  [on_device(): got = [lax.ppermute(w[rows:], 'y', SWAP) for w in weight_sums]]
    unnamed x34 -> x50, local copies, waits for them, and re-layouts: 7.54 us -> 8.79 us
    convert_element_type x1 -> x2, other arithmetic: 4.5 us -> 5.22 us  [on_device(): far.append(after(total.astype(BF16), decs[-1][2]))]
  transfers between devices with their start and end apart: 36 -> 39, of which waited for: 15 -> 12; matrix products, arithmetic and copies ran while one was open for 10% -> 12% of each run, Pallas kernels for 24% -> 24%
where the time goes in v9:
time: 252 us; the launch traced here: 251 us
  waiting for transfers between devices  69.5 us (28%)
  starting transfers between devices  64.6 us (26%)
  Pallas kernels  60.1 us (24%)
  other arithmetic  18.7 us (7%)
  between operations  16.2 us (6%)
  local copies, waits for them, and re-layouts  15 us (6%)
  matrix products  6.7 us (3%)
    pallas_call x2, Pallas kernels, attend(): pl.pallas_call(attend_kernel, grid_spec=pltpu.PrefetchScalarGridSpec(num_...  20.8 us
    all_gather x2, waiting for transfers between devices, on_device(): w_own.append(lax.all_gather(block, 'z', axis=0, tiled=True))  16.7 us
    ppermute x1, waiting for transfers between devices, on_device(): lax.ppermute(after(packed, swapped[0], key_count, *gains), PLANE, [(0, 2)...  16.7 us
    ppermute x2, waiting for transfers between devices, on_device(): got = [lax.ppermute(w[rows:], 'y', SWAP) for w in weight_sums]  16.6 us
    ppermute x7, starting transfers between devices, across(): lax.ppermute(value, ('y', 'phase', 'mp'), [(a * shards + s, b * shards +...  15.1 us
    pallas_call x2, Pallas kernels, enc_grad(): pl.pallas_call(enc_grad_kernel, grid_spec=pltpu.PrefetchScalarGridSpec(nu...  13.3 us
    pallas_call x2, Pallas kernels, weight_grad(): pl.pallas_call(lambda *refs: weight_grad_kernel(scale, *refs), grid_spec=...  12.5 us
    ppermute x2, starting transfers between devices, on_device(): lax.ppermute(dec, PLANE, [(0, 1)])  9.22 us
  transfers between devices with their start and end apart: 39, of which 12 were waited for; matrix products, arithmetic and copies ran while one was open for 12% of the time, Pallas kernels for 24%

profile of v9, /device:TPU:0, one launch (start us, length us, event | category | flops | bytes accessed | tf_op | source)
XLA Modules:
  0.0 250.8 jit_solution(16013503128107285715)
XLA Ops:
  11.3 4.0 %collective-permute-start.2 = (bf16[256,512]{1,0:T(8,128)(2,1)S(1)}, bf16[256,512]{1,0:T(8,128)(2,1)S(1)}, u32[]{:S(2)}, u32[]{:S(2)}) collective-permute-start(bf16[256,512]{1,0:T(8,128)(2,1)S(1)} %get-tuple-element.67), channel_id=1, source_target_pairs={{0,4},{4,0},{1,5},{5,1},{2,6},{6,2},{3,7},{7,3},{8,12},{12,8},{9,1... | collective-permute-start | bytes 786440 | tf_op jit(solution)/shard_map/ppermute | solution.py:309
  18.4 2.9 %collective-permute-done.1 = s32[1]{0:T(128)} collective-permute-done((s32[1]{0:T(128)}, s32[1]{0:T(128)}, u32[]{:S(2)}, u32[]{:S(2)}) %collective-permute-start.1) | collective-permute-done | bytes 36 | tf_op jit(solution)/shard_map/ppermute | solution.py:313
  22.0 4.1 %collective-permute-start.4 = (bf16[512,2048]{1,0:T(8,128)(2,1)S(1)}, bf16[512,2048]{1,0:T(8,128)(2,1)}, u32[]{:S(2)}, u32[]{:S(2)}) collective-permute-start(bf16[512,2048]{1,0:T(8,128)(2,1)S(1)} %bitcast.17), channel_id=1, source_target_pairs={{0,4},{4,2},{1,5},{5,3},{8,12},{12,10},{9,13},{13,11},{16,20},{20,... | collective-permute-start | bytes 6291464 | tf_op jit(solution)/shard_map/ppermute | solution.py:314
  27.8 3.1 %collective-permute-start.5 = (bf16[512,2048]{1,0:T(8,128)(2,1)S(1)}, bf16[512,2048]{1,0:T(8,128)(2,1)}, u32[]{:S(2)}, u32[]{:S(2)}) collective-permute-start(bf16[512,2048]{1,0:T(8,128)(2,1)S(1)} %bitcast.18), channel_id=1, source_target_pairs={{0,1},{1,0},{8,9},{9,8},{16,17},{17,16},{24,25},{25,24}} | collective-permute-start | bytes 6291464 | tf_op jit(solution)/shard_map/ppermute | solution.py:297
  31.6 16.7 %collective-permute-done.4.refs_3_ = bf16[512,2048]{1,0:T(8,128)(2,1)} collective-permute-done((bf16[512,2048]{1,0:T(8,128)(2,1)S(1)}, bf16[512,2048]{1,0:T(8,128)(2,1)}, u32[]{:S(2)}, u32[]{:S(2)}) %collective-permute-start.4) | collective-permute-done | bytes 2097184 | tf_op jit(solution)/shard_map/ppermute | solution.py:314
  51.6 3.7 %collective-permute-start.8 = (bf16[256,512]{1,0:T(8,128)(2,1)}, bf16[256,512]{1,0:T(8,128)(2,1)S(1)}, u32[]{:S(2)}, u32[]{:S(2)}) collective-permute-start(bf16[256,512]{1,0:T(8,128)(2,1)} %get-tuple-element.36), channel_id=1, source_target_pairs={{0,4},{4,0},{1,5},{5,1},{2,6},{6,2},{3,7},{7,3},{8,12},{12,8},{9,1... | collective-permute-start | bytes 786440 | tf_op jit(solution)/shard_map/ppermute | solution.py:326
  57.2 4.4 %collective-permute-done.8 = bf16[256,512]{1,0:T(8,128)(2,1)S(1)} collective-permute-done((bf16[256,512]{1,0:T(8,128)(2,1)}, bf16[256,512]{1,0:T(8,128)(2,1)S(1)}, u32[]{:S(2)}, u32[]{:S(2)}) %collective-permute-start.8) | collective-permute-done | bytes 262176 | tf_op jit(solution)/shard_map/ppermute | solution.py:326
  65.4 7.6 %all-gather.3.cloned.1.call-done.own_0 = bf16[2048,512]{1,0:T(8,128)(2,1)} async-done(((bf16[512,512]{1,0:T(8,128)(2,1)}), bf16[2048,512]{1,0:T(8,128)(2,1)}) %all-gather.3.cloned.1.call-update) | async-done | bytes 2097168 | tf_op jit(solution)/shard_map/all_gather | solution.py:388
  74.9 6.9 %norm.1 = (bf16[512,2048]{1,0:T(8,128)(2,1)}, bf16[512,2048]{1,0:T(8,128)(2,1)}, f32[512,128]{1,0:T(8,128)S(1)}) custom-call(s32[6]{0:T(128)S(1)} %concatenate.59.refs_0_.at, bf16[512,2048]{1,0:T(8,128)(2,1)S(1)} %bitcast.19, bf16[512,2048]{1,0:T(8,128)(2,1)} %collective-permute-done.refs_2_.refs_8_, bf16[512,2048]{1,0:T(8,128)(2,1)} %collective-permute-done.4.refs_3_, ...), custom_call_target="tpu_custom_call" | custom-call | flops 16777216 | bytes 8388608 | tf_op jit(solution)/shard_map/norm/pallas_call | solution.py:74
  81.8 5.3 %collective-permute-start.12 = (bf16[512,2048]{1,0:T(8,128)(2,1)}, bf16[512,2048]{1,0:T(8,128)(2,1)S(1)}, u32[]{:S(2)}, u32[]{:S(2)}) collective-permute-start(bf16[512,2048]{1,0:T(8,128)(2,1)} %get-tuple-element.41.enc_other), channel_id=1, source_target_pairs={{0,2},{2,0},{1,3},{3,1},{4,6},{6,4},{5,7},{7,5},{8,10},{10,8},{9,1... | collective-permute-start | bytes 6291464 | tf_op jit(solution)/shard_map/ppermute | solution.py:374
  87.1 2.8 %fusion.12.part = f32[512,512]{1,0:T(8,128)S(1)} fusion(bf16[512,2048]{1,0:T(8,128)(2,1)} %get-tuple-element.40.refs_1_, bf16[2048,512]{1,0:T(8,128)(2,1)S(1)} %copy-done.23), kind=kOutput, calls=%fused_computation.36 | convolution fusion | flops 1073741824 | bytes 5242880 | tf_op jit(solution)/shard_map/dot_general | solution.py:25
  89.9 10.4 %attend.2 = (bf16[512,512]{1,0:T(8,128)(2,1)S(1)}, bf16[512,512]{1,0:T(8,128)(2,1)S(1)}) custom-call(s32[6]{0:T(128)S(1)} %concatenate.59.refs_0_.at, f32[512,512]{1,0:T(8,128)S(1)} %fusion.12.part, bf16[512,2048]{1,0:T(8,128)(2,1)} %get-tuple-element.41.enc_other, bf16[2048,512]{1,0:T(8,128)(2,1)} %collective-permute-done.11.w_other.other_0, ...), custom_call_target="tpu_custom_call" | custom-call | flops 4026531840 | bytes 8388608 | tf_op jit(solution)/shard_map/attend/pallas_call | solution.py:136
  103.9 6.2 %weight_grad.2 = bf16[2048,512]{1,0:T(8,128)(2,1)} custom-call(s32[6]{0:T(128)S(1)} %concatenate.59.refs_0_.at, bf16[512,2048]{1,0:T(8,128)(2,1)} %get-tuple-element.40.refs_1_, bf16[512,2048]{1,0:T(8,128)(2,1)} %copy-done.13, bf16[512,512]{1,0:T(8,128)(2,1)S(1)} %get-tuple-element.42.refs_3_.gkv_0, bf16[512,512]{1,0:T(8,128)(2,1)S(1)} %pad_maximum_fusion.2.refs_4_), custom_call_target="tpu_custom_call" | custom-call | flops 33554432 | tf_op jit(solution)/shard_map/weight_grad/pallas_call | solution.py:164
  110.2 9.1 %all-gather.5.cloned.1.call-done.own_1 = bf16[2048,512]{1,0:T(8,128)(2,1)} async-done(((bf16[512,512]{1,0:T(8,128)(2,1)}), bf16[2048,512]{1,0:T(8,128)(2,1)}) %all-gather.5.cloned.1.call-update) | async-done | bytes 2097168 | tf_op jit(solution)/shard_map/all_gather | solution.py:388
  120.0 5.0 %collective-permute-start.15 = (bf16[512,512]{1,0:T(8,128)(2,1)S(1)}, bf16[512,512]{1,0:T(8,128)(2,1)S(1)}, u32[]{:S(2)}, u32[]{:S(2)}) collective-permute-start(bf16[512,512]{1,0:T(8,128)(2,1)S(1)} %get-tuple-element.44), channel_id=1, source_target_pairs={{0,2},{1,3},{8,10},{9,11},{16,18},{17,19},{24,26},{25,27}} | collective-permute-start | bytes 1572872 | tf_op jit(solution)/shard_map/ppermute | solution.py:399
  125.0 3.9 %fusion.13.part = f32[512,512]{1,0:T(8,128)S(1)} fusion(bf16[512,2048]{1,0:T(8,128)(2,1)} %get-tuple-element.40.refs_1_, bf16[2048,512]{1,0:T(8,128)(2,1)} %all-gather.5.cloned.1.call-done.own_1), kind=kOutput, calls=%fused_computation.37 | convolution fusion | flops 1073741824 | bytes 5242880 | tf_op jit(solution)/shard_map/dot_general | solution.py:25
  131.8 10.4 %attend.3 = (bf16[512,512]{1,0:T(8,128)(2,1)S(1)}, bf16[512,512]{1,0:T(8,128)(2,1)S(1)}) custom-call(s32[6]{0:T(128)S(1)} %concatenate.59.refs_0_.at, f32[512,512]{1,0:T(8,128)S(1)} %fusion.13.part, bf16[512,2048]{1,0:T(8,128)(2,1)} %get-tuple-element.41.enc_other, bf16[2048,512]{1,0:T(8,128)(2,1)} %copy-done.24, bf16[512,1024]{1,0:T(8,128)(2,1)} %copy-done.14, ...), custom_call_target="tpu_custom_call" | custom-call | flops 4026531840 | bytes 8388608 | tf_op jit(solution)/shard_map/attend/pallas_call | solution.py:136
  143.1 6.7 %enc_grad.3 = (bf16[256,2048]{1,0:T(8,128)(2,1)}, bf16[256,2048]{1,0:T(8,128)(2,1)}) custom-call(s32[6]{0:T(128)S(1)} %concatenate.59.refs_0_.at, bf16[512,512]{1,0:T(8,128)(2,1)} %copy-done.6, bf16[512,512]{1,0:T(8,128)(2,1)} %copy-done.7, bf16[2048,512]{1,0:T(8,128)(2,1)} %all-gather.3.cloned.1.call-done.own_0, ...), custom_call_target="tpu_custom_call" | custom-call | flops 4294967296 | bytes 8388608 | tf_op jit(solution)/shard_map/enc_grad/pallas_call | solution.py:250
  151.6 6.6 %enc_grad.2 = (bf16[256,2048]{1,0:T(8,128)(2,1)}, bf16[256,2048]{1,0:T(8,128)(2,1)}) custom-call(s32[6]{0:T(128)S(1)} %concatenate.59.refs_0_.at, bf16[512,512]{1,0:T(8,128)(2,1)} %copy-done.6, bf16[512,512]{1,0:T(8,128)(2,1)} %copy-done.7, bf16[2048,512]{1,0:T(8,128)(2,1)} %all-gather.3.cloned.1.call-done.own_0, ...), custom_call_target="tpu_custom_call" | custom-call | flops 4294967296 | bytes 8388608 | tf_op jit(solution)/shard_map/enc_grad/pallas_call | solution.py:250
  158.2 3.2 %collective-permute-start.30 = (bf16[512,256]{1,0:T(8,128)(2,1)S(1)}, bf16[512,256]{1,0:T(8,128)(2,1)S(1)}, u32[]{:S(2)}, u32[]{:S(2)}) collective-permute-start(bf16[512,256]{1,0:T(8,128)(2,1)S(1)} %get-tuple-element.73), channel_id=1, source_target_pairs={{0,2},{2,0},{1,3},{3,1},{4,6},{6,4},{5,7},{7,5},{8,10},{10,8},{9,1... | collective-permute-start | bytes 786440 | tf_op jit(solution)/shard_map/ppermute | solution.py:409
  163.3 6.3 %weight_grad.3 = bf16[2048,512]{1,0:T(8,128)(2,1)} custom-call(s32[6]{0:T(128)S(1)} %concatenate.59.refs_0_.at, bf16[512,2048]{1,0:T(8,128)(2,1)} %get-tuple-element.40.refs_1_, bf16[512,2048]{1,0:T(8,128)(2,1)} %copy-done.13, bf16[512,512]{1,0:T(8,128)(2,1)S(1)} %copy-done.8, bf16[512,512]{1,0:T(8,128)(2,1)S(1)} %pad_maximum_fusion.3.refs_4_), custom_call_target="tpu_custom_call" | custom-call | flops 33554432 | tf_op jit(solution)/shard_map/weight_grad/pallas_call | solution.py:164
  170.4 4.2 %collective-permute-start.19 = (bf16[512,512]{1,0:T(8,128)(2,1)}, bf16[512,512]{1,0:T(8,128)(2,1)S(1)}, u32[]{:S(2)}, u32[]{:S(2)}) collective-permute-start(bf16[512,512]{1,0:T(8,128)(2,1)} %copy-done.11), channel_id=1, source_target_pairs={{0,2},{1,3},{8,10},{9,11},{16,18},{17,19},{24,26},{25,27}} | collective-permute-start | bytes 1572872 | tf_op jit(solution)/shard_map/ppermute | solution.py:399
  174.6 3.3 %collective-permute-start.18 = (bf16[256,2048]{1,0:T(8,128)(2,1)}, bf16[256,2048]{1,0:T(8,128)(2,1)}, u32[]{:S(2)}, u32[]{:S(2)}) collective-permute-start(bf16[256,2048]{1,0:T(8,128)(2,1)} %get-tuple-element.49), channel_id=1, source_target_pairs={{0,1},{1,0},{6,7},{7,6},{8,9},{9,8},{14,15},{15,14},{16,17},{17,16... | collective-permute-start | bytes 3145736 | tf_op jit(solution)/shard_map/ppermute | solution.py:297
  180.5 2.6 %add_convert_fusion.1 = bf16[256,2048]{1,0:T(8,128)(2,1)} fusion(bf16[256,2048]{1,0:T(8,128)(2,1)} %collective-permute-done.23, bf16[256,2048]{1,0:T(8,128)(2,1)S(1)} %copy-done.1), kind=kLoop, calls=%fused_computation.6 | loop fusion | flops 2097152 | bytes 3145728 | tf_op jit(solution)/shard_map/convert_element_type | solution.py:428
  184.6 2.6 %add_convert_fusion = bf16[256,2048]{1,0:T(8,128)(2,1)} fusion(bf16[256,2048]{1,0:T(8,128)(2,1)} %collective-permute-done.25, bf16[256,2048]{1,0:T(8,128)(2,1)S(1)} %copy-done.2), kind=kLoop, calls=%fused_computation.5 | loop fusion | flops 2097152 | bytes 3145728 | tf_op jit(solution)/shard_map/convert_element_type | solution.py:428
  192.1 4.6 %collective-permute-start.21 = (bf16[256,512]{1,0:T(8,128)(2,1)S(1)}, bf16[256,512]{1,0:T(8,128)(2,1)S(1)}, u32[]{:S(2)}, u32[]{:S(2)}) collective-permute-start(bf16[256,512]{1,0:T(8,128)(2,1)S(1)} %get-tuple-element.70), channel_id=1, source_target_pairs={{0,4},{4,0},{1,5},{5,1},{2,6},{6,2},{3,7},{7,3},{8,12},{12,8},{9,1... | collective-permute-start | bytes 786440 | tf_op jit(solution)/shard_map/ppermute | solution.py:438
  196.6 3.8 %maximum_select_fusion = bf16[512,2048]{1,0:T(8,128)(2,1)} fusion(bf16[512,512]{1,0:T(8,128)(2,1)} %copy-done.17, bf16[512,512]{1,0:T(8,128)(2,1)} %copy-done.16, bf16[512,512]{1,0:T(8,128)(2,1)} %broadcast_select_fusion, bf16[512,512]{1,0:T(8,128)(2,1)} %broadcast_select_fusion.1, pred[]{:T(512)S(6)} %eq.20), kind=kLoop, calls=%fused_computation.3 | loop fusion | flops 17825792 | bytes 4194305 | tf_op jit(solution)/shard_map/jit(_where)/select_n | solution.py:270
  200.4 16.6 %collective-permute-done.21 = bf16[256,512]{1,0:T(8,128)(2,1)S(1)} collective-permute-done((bf16[256,512]{1,0:T(8,128)(2,1)S(1)}, bf16[256,512]{1,0:T(8,128)(2,1)S(1)}, u32[]{:S(2)}, u32[]{:S(2)}) %collective-permute-start.21) | collective-permute-done | bytes 262176 | tf_op jit(solution)/shard_map/ppermute | solution.py:438
  217.8 6.5 %collect.1 = (bf16[512,2048]{1,0:T(8,128)(2,1)}, f32[4,1,2048]{2,1,0:T(1,128)S(1)}) custom-call(s32[6]{0:T(128)S(1)} %concatenate.59.refs_0_.at, bf16[256,2048]{1,0:T(8,128)(2,1)S(1)} %copy-done.1, bf16[256,2048]{1,0:T(8,128)(2,1)S(1)} %copy-done.3, bf16[256,2048]{1,0:T(8,128)(2,1)} %collective-permute-done.18.refs_3_, ...), custom_call_target="tpu_custom_call" | custom-call | flops 8388608 | bytes 12582912 | tf_op jit(solution)/shard_map/collect/pallas_call | solution.py:203
  228.2 3.6 %collective-permute-done.28 = f32[2048]{0:T(1024)S(1)} collective-permute-done((f32[2048]{0:T(1024)S(1)}, f32[2048]{0:T(1024)S(1)}, u32[]{:S(2)}, u32[]{:S(2)}) %collective-permute-start.28) | collective-permute-done | bytes 8224 | tf_op jit(solution)/shard_map/ppermute | solution.py:459
  233.1 3.2 %select_bitcast_fusion = bf16[1,1,512,2048]{3,2,1,0:T(8,128)(2,1)} fusion(bf16[512,2048]{1,0:T(8,128)(2,1)} %maximum_select_fusion, bf16[512,2048]{1,0:T(8,128)(2,1)} %get-tuple-element.57, bf16[512,2048]{1,0:T(8,128)(2,1)S(1)} %collective-permute-done.29, pred[]{:T(512)S(6)} %eq.21, pred[]{:T(512)S(6)} %eq.20), kind=kLoop, calls=%fused_computation.4 | loop fusion | flops 2097152 | bytes 8388610 | tf_op jit(solution)/shard_map/broadcast_in_dim | solution.py:451
  237.2 3.6 %collective-permute-done.33 = f32[2048]{0:T(1024)S(1)} collective-permute-done((f32[2048]{0:T(1024)S(1)}, f32[2048]{0:T(1024)S(1)}, u32[]{:S(2)}, u32[]{:S(2)}) %collective-permute-start.33) | collective-permute-done | bytes 8224 | tf_op jit(solution)/shard_map/ppermute | solution.py:459
  (142 shorter events, 50.3 us)
Async XLA Ops:
  7.2 65.9 %all-gather.3.cloned.1.call-start = ((), (), s32[]{:S(2)}) async-start(), calls=%async_computation.2 | async-start | bytes 2621440 | tf_op jit(solution)/shard_map/all_gather | solution.py:388
  7.2 8.1 %collective-permute-start = (bf16[512,2048]{1,0:T(8,128)(2,1)}, bf16[512,2048]{1,0:T(8,128)(2,1)}, u32[]{:S(2)}, u32[]{:S(2)}) collective-permute-start(bf16[512,2048]{1,0:T(8,128)(2,1)} %bitcast.16), channel_id=1, source_target_pairs={{4,6},{5,7},{12,14},{13,15},{20,22},{21,23},{28,30},{29,31}} | collective-permute-start | bytes 6291464 | tf_op jit(solution)/shard_map/ppermute | solution.py:310
  11.3 10.6 %collective-permute-start.2 = (bf16[256,512]{1,0:T(8,128)(2,1)S(1)}, bf16[256,512]{1,0:T(8,128)(2,1)S(1)}, u32[]{:S(2)}, u32[]{:S(2)}) collective-permute-start(bf16[256,512]{1,0:T(8,128)(2,1)S(1)} %get-tuple-element.67), channel_id=1, source_target_pairs={{0,4},{4,0},{1,5},{5,1},{2,6},{6,2},{3,7},{7,3},{8,12},{12,8},{9,1... | collective-permute-start | bytes 786440 | tf_op jit(solution)/shard_map/ppermute | solution.py:309
  15.4 6.6 %collective-permute-start.3 = (bf16[2048]{0:T(1024)(128)(2,1)S(1)}, bf16[2048]{0:T(1024)(128)(2,1)S(1)}, u32[]{:S(2)}, u32[]{:S(2)}) collective-permute-start(bf16[2048]{0:T(1024)(128)(2,1)S(1)} %copy-done.22), channel_id=1, source_target_pairs={{0,1},{1,0},{2,3},{3,2},{4,5},{5,4},{6,7},{7,6},{8,9},{9,8},{10,11... | collective-permute-start | bytes 12296 | tf_op jit(solution)/shard_map/ppermute | solution.py:312
  22.0 26.3 %collective-permute-start.4 = (bf16[512,2048]{1,0:T(8,128)(2,1)S(1)}, bf16[512,2048]{1,0:T(8,128)(2,1)}, u32[]{:S(2)}, u32[]{:S(2)}) collective-permute-start(bf16[512,2048]{1,0:T(8,128)(2,1)S(1)} %bitcast.17), channel_id=1, source_target_pairs={{0,4},{4,2},{1,5},{5,3},{8,12},{12,10},{9,13},{13,11},{16,20},{20,... | collective-permute-start | bytes 6291464 | tf_op jit(solution)/shard_map/ppermute | solution.py:314
  27.0 92.3 %all-gather.5.cloned.1.call-start = ((), (), s32[]{:S(2)}) async-start(), calls=%async_computation.3 | async-start | bytes 2621440 | tf_op jit(solution)/shard_map/all_gather | solution.py:388
  27.0 23.2 %collective-permute-start.6 = (bf16[512,2048]{1,0:T(8,128)(2,1)}, bf16[512,2048]{1,0:T(8,128)(2,1)S(1)}, u32[]{:S(2)}, u32[]{:S(2)}) collective-permute-start(bf16[512,2048]{1,0:T(8,128)(2,1)} %collective-permute-done.refs_2_.refs_8_), channel_id=1, source_target_pairs={{6,7},{7,6},{14,15},{15,14},{22,23},{23,22},{30,31},{31,30}} | collective-permute-start | bytes 6291464 | tf_op jit(solution)/shard_map/ppermute | solution.py:297
  27.8 45.4 %collective-permute-start.5 = (bf16[512,2048]{1,0:T(8,128)(2,1)S(1)}, bf16[512,2048]{1,0:T(8,128)(2,1)}, u32[]{:S(2)}, u32[]{:S(2)}) collective-permute-start(bf16[512,2048]{1,0:T(8,128)(2,1)S(1)} %bitcast.18), channel_id=1, source_target_pairs={{0,1},{1,0},{8,9},{9,8},{16,17},{17,16},{24,25},{25,24}} | collective-permute-start | bytes 6291464 | tf_op jit(solution)/shard_map/ppermute | solution.py:297
  48.3 25.0 %collective-permute-start.7 = (bf16[512,2048]{1,0:T(8,128)(2,1)}, bf16[512,2048]{1,0:T(8,128)(2,1)}, u32[]{:S(2)}, u32[]{:S(2)}) collective-permute-start(bf16[512,2048]{1,0:T(8,128)(2,1)} %collective-permute-done.4.refs_3_), channel_id=1, source_target_pairs={{2,3},{3,2},{4,5},{5,4},{10,11},{11,10},{12,13},{13,12},{18,19},{1... | collective-permute-start | bytes 6291464 | tf_op jit(solution)/shard_map/ppermute | solution.py:297
  51.6 10.0 %collective-permute-start.8 = (bf16[256,512]{1,0:T(8,128)(2,1)}, bf16[256,512]{1,0:T(8,128)(2,1)S(1)}, u32[]{:S(2)}, u32[]{:S(2)}) collective-permute-start(bf16[256,512]{1,0:T(8,128)(2,1)} %get-tuple-element.36), channel_id=1, source_target_pairs={{0,4},{4,0},{1,5},{5,1},{2,6},{6,2},{3,7},{7,3},{8,12},{12,8},{9,1... | collective-permute-start | bytes 786440 | tf_op jit(solution)/shard_map/ppermute | solution.py:326
  61.5 11.7 %collective-permute-start.10 = (bf16[512,1024]{1,0:T(8,128)(2,1)}, bf16[512,1024]{1,0:T(8,128)(2,1)}, u32[]{:S(2)}, u32[]{:S(2)}) collective-permute-start(bf16[512,1024]{1,0:T(8,128)(2,1)} %get-tuple-element.38), channel_id=1, source_target_pairs={{2,4},{6,2},{3,5},{7,3},{10,12},{14,10},{11,13},{15,11},{18,20},{2... | collective-permute-start | bytes 3145736 | tf_op jit(solution)/shard_map/ppermute | solution.py:338
  63.2 10.0 %collective-permute-start.9 = (bf16[512,1024]{1,0:T(8,128)(2,1)S(1)}, bf16[512,1024]{1,0:T(8,128)(2,1)}, u32[]{:S(2)}, u32[]{:S(2)}) collective-permute-start(bf16[512,1024]{1,0:T(8,128)(2,1)S(1)} %get-tuple-element.37.refs_0_), channel_id=1, source_target_pairs={{2,0},{3,1},{10,8},{11,9},{18,16},{19,17},{26,24},{27,25}} | collective-permute-start | bytes 3145736 | tf_op jit(solution)/shard_map/ppermute | solution.py:337
  65.3 124.9 %reduce-scatter.3.cloned.1.call-start = ((), (), s32[]{:S(2)}) async-start(), calls=%async_computation.4 | async-start | bytes 2621440 | tf_op jit(solution)/shard_map/reduce_scatter | solution.py:415
  73.0 16.9 %collective-permute-start.11 = (bf16[2048,512]{1,0:T(8,128)(2,1)}, bf16[2048,512]{1,0:T(8,128)(2,1)}, u32[]{:S(2)}, u32[]{:S(2)}) collective-permute-start(bf16[2048,512]{1,0:T(8,128)(2,1)} %all-gather.3.cloned.1.call-done.own_0), channel_id=1, source_target_pairs={{0,2},{2,0},{1,3},{3,1},{4,6},{6,4},{5,7},{7,5},{8,10},{10,8},{9,1... | collective-permute-start | bytes 6291464 | tf_op jit(solution)/shard_map/ppermute | solution.py:391
  81.8 20.7 %collective-permute-start.12 = (bf16[512,2048]{1,0:T(8,128)(2,1)}, bf16[512,2048]{1,0:T(8,128)(2,1)S(1)}, u32[]{:S(2)}, u32[]{:S(2)}) collective-permute-start(bf16[512,2048]{1,0:T(8,128)(2,1)} %get-tuple-element.41.enc_other), channel_id=1, source_target_pairs={{0,2},{2,0},{1,3},{3,1},{4,6},{6,4},{5,7},{7,5},{8,10},{10,8},{9,1... | collective-permute-start | bytes 6291464 | tf_op jit(solution)/shard_map/ppermute | solution.py:374
  110.2 121.7 %reduce-scatter.5.cloned.1.call-start = ((), (), s32[]{:S(2)}) async-start(), calls=%async_computation.5 | async-start | bytes 2621440 | tf_op jit(solution)/shard_map/reduce_scatter | solution.py:415
  119.3 11.2 %collective-permute-start.17 = (bf16[2048,512]{1,0:T(8,128)(2,1)}, bf16[2048,512]{1,0:T(8,128)(2,1)S(1)}, u32[]{:S(2)}, u32[]{:S(2)}) collective-permute-start(bf16[2048,512]{1,0:T(8,128)(2,1)} %all-gather.5.cloned.1.call-done.own_1), channel_id=1, source_target_pairs={{0,2},{2,0},{1,3},{3,1},{4,6},{6,4},{5,7},{7,5},{8,10},{10,8},{9,1... | collective-permute-start | bytes 6291464 | tf_op jit(solution)/shard_map/ppermute | solution.py:391
  119.3 9.6 %collective-permute-start.16 = (bf16[512,512]{1,0:T(8,128)(2,1)S(1)}, bf16[512,512]{1,0:T(8,128)(2,1)S(1)}, u32[]{:S(2)}, u32[]{:S(2)}) collective-permute-start(bf16[512,512]{1,0:T(8,128)(2,1)S(1)} %get-tuple-element.44), channel_id=1, source_target_pairs={{4,2},{2,6},{5,3},{3,7},{12,10},{10,14},{13,11},{11,15},{20,18},{1... | collective-permute-start | bytes 1572872 | tf_op jit(solution)/shard_map/ppermute | solution.py:401
  120.0 8.9 %collective-permute-start.15 = (bf16[512,512]{1,0:T(8,128)(2,1)S(1)}, bf16[512,512]{1,0:T(8,128)(2,1)S(1)}, u32[]{:S(2)}, u32[]{:S(2)}) collective-permute-start(bf16[512,512]{1,0:T(8,128)(2,1)S(1)} %get-tuple-element.44), channel_id=1, source_target_pairs={{0,2},{1,3},{8,10},{9,11},{16,18},{17,19},{24,26},{25,27}} | collective-permute-start | bytes 1572872 | tf_op jit(solution)/shard_map/ppermute | solution.py:399
  149.8 28.2 %collective-permute-start.23 = (bf16[256,2048]{1,0:T(8,128)(2,1)}, bf16[256,2048]{1,0:T(8,128)(2,1)}, u32[]{:S(2)}, u32[]{:S(2)}) collective-permute-start(bf16[256,2048]{1,0:T(8,128)(2,1)} %get-tuple-element.49), channel_id=1, source_target_pairs={{2,3},{3,2},{4,5},{5,4},{10,11},{11,10},{12,13},{13,12},{18,19},{1... | collective-permute-start | bytes 3145736 | tf_op jit(solution)/shard_map/ppermute | solution.py:297
  158.2 5.0 %collective-permute-start.30 = (bf16[512,256]{1,0:T(8,128)(2,1)S(1)}, bf16[512,256]{1,0:T(8,128)(2,1)S(1)}, u32[]{:S(2)}, u32[]{:S(2)}) collective-permute-start(bf16[512,256]{1,0:T(8,128)(2,1)S(1)} %get-tuple-element.73), channel_id=1, source_target_pairs={{0,2},{2,0},{1,3},{3,1},{4,6},{6,4},{5,7},{7,5},{8,10},{10,8},{9,1... | collective-permute-start | bytes 786440 | tf_op jit(solution)/shard_map/ppermute | solution.py:409
  161.6 23.0 %collective-permute-start.25 = (bf16[256,2048]{1,0:T(8,128)(2,1)}, bf16[256,2048]{1,0:T(8,128)(2,1)}, u32[]{:S(2)}, u32[]{:S(2)}) collective-permute-start(bf16[256,2048]{1,0:T(8,128)(2,1)} %get-tuple-element.52), channel_id=1, source_target_pairs={{2,3},{3,2},{4,5},{5,4},{10,11},{11,10},{12,13},{13,12},{18,19},{1... | collective-permute-start | bytes 3145736 | tf_op jit(solution)/shard_map/ppermute | solution.py:297
  169.6 13.5 %collective-permute-start.20 = (bf16[512,512]{1,0:T(8,128)(2,1)}, bf16[512,512]{1,0:T(8,128)(2,1)S(1)}, u32[]{:S(2)}, u32[]{:S(2)}) collective-permute-start(bf16[512,512]{1,0:T(8,128)(2,1)} %copy-done.11), channel_id=1, source_target_pairs={{4,2},{2,6},{5,3},{3,7},{12,10},{10,14},{13,11},{11,15},{20,18},{1... | collective-permute-start | bytes 1572872 | tf_op jit(solution)/shard_map/ppermute | solution.py:401
  170.4 19.0 %collective-permute-start.19 = (bf16[512,512]{1,0:T(8,128)(2,1)}, bf16[512,512]{1,0:T(8,128)(2,1)S(1)}, u32[]{:S(2)}, u32[]{:S(2)}) collective-permute-start(bf16[512,512]{1,0:T(8,128)(2,1)} %copy-done.11), channel_id=1, source_target_pairs={{0,2},{1,3},{8,10},{9,11},{16,18},{17,19},{24,26},{25,27}} | collective-permute-start | bytes 1572872 | tf_op jit(solution)/shard_map/ppermute | solution.py:399
  174.6 25.8 %collective-permute-start.18 = (bf16[256,2048]{1,0:T(8,128)(2,1)}, bf16[256,2048]{1,0:T(8,128)(2,1)}, u32[]{:S(2)}, u32[]{:S(2)}) collective-permute-start(bf16[256,2048]{1,0:T(8,128)(2,1)} %get-tuple-element.49), channel_id=1, source_target_pairs={{0,1},{1,0},{6,7},{7,6},{8,9},{9,8},{14,15},{15,14},{16,17},{17,16... | collective-permute-start | bytes 3145736 | tf_op jit(solution)/shard_map/ppermute | solution.py:297
  178.0 39.1 %collective-permute-start.22 = (bf16[256,2048]{1,0:T(8,128)(2,1)}, bf16[256,2048]{1,0:T(8,128)(2,1)}, u32[]{:S(2)}, u32[]{:S(2)}) collective-permute-start(bf16[256,2048]{1,0:T(8,128)(2,1)} %get-tuple-element.52), channel_id=1, source_target_pairs={{0,1},{1,0},{6,7},{7,6},{8,9},{9,8},{14,15},{15,14},{16,17},{17,16... | collective-permute-start | bytes 3145736 | tf_op jit(solution)/shard_map/ppermute | solution.py:297
  183.1 33.9 %collective-permute-start.24 = (bf16[256,2048]{1,0:T(8,128)(2,1)}, bf16[256,2048]{1,0:T(8,128)(2,1)}, u32[]{:S(2)}, u32[]{:S(2)}) collective-permute-start(bf16[256,2048]{1,0:T(8,128)(2,1)} %add_convert_fusion.1), channel_id=1, source_target_pairs={{4,0},{2,6},{5,1},{3,7},{12,8},{10,14},{13,9},{11,15},{20,16},{18,... | collective-permute-start | bytes 3145736 | tf_op jit(solution)/shard_map/ppermute | solution.py:432
  187.2 29.8 %collective-permute-start.26 = (bf16[256,2048]{1,0:T(8,128)(2,1)}, bf16[256,2048]{1,0:T(8,128)(2,1)}, u32[]{:S(2)}, u32[]{:S(2)}) collective-permute-start(bf16[256,2048]{1,0:T(8,128)(2,1)} %add_convert_fusion), channel_id=1, source_target_pairs={{4,0},{2,6},{5,1},{3,7},{12,8},{10,14},{13,9},{11,15},{20,16},{18,... | collective-permute-start | bytes 3145736 | tf_op jit(solution)/shard_map/ppermute | solution.py:432
  192.1 25.0 %collective-permute-start.21 = (bf16[256,512]{1,0:T(8,128)(2,1)S(1)}, bf16[256,512]{1,0:T(8,128)(2,1)S(1)}, u32[]{:S(2)}, u32[]{:S(2)}) collective-permute-start(bf16[256,512]{1,0:T(8,128)(2,1)S(1)} %get-tuple-element.70), channel_id=1, source_target_pairs={{0,4},{4,0},{1,5},{5,1},{2,6},{6,2},{3,7},{7,3},{8,12},{12,8},{9,1... | collective-permute-start | bytes 786440 | tf_op jit(solution)/shard_map/ppermute | solution.py:438
  224.2 8.8 %collective-permute-start.29 = (bf16[512,2048]{1,0:T(8,128)(2,1)}, bf16[512,2048]{1,0:T(8,128)(2,1)S(1)}, u32[]{:S(2)}, u32[]{:S(2)}) collective-permute-start(bf16[512,2048]{1,0:T(8,128)(2,1)} %get-tuple-element.57), channel_id=1, source_target_pairs={{6,4},{7,5},{14,12},{15,13},{22,20},{23,21},{30,28},{31,29}} | collective-permute-start | bytes 6291464 | tf_op jit(solution)/shard_map/ppermute | solution.py:450
  233.0 9.7 %collective-permute-start.32 = (bf16[256,512]{1,0:T(8,128)(2,1)S(1)}, bf16[256,512]{1,0:T(8,128)(2,1)S(1)}, u32[]{:S(2)}, u32[]{:S(2)}) collective-permute-start(bf16[256,512]{1,0:T(8,128)(2,1)S(1)} %get-tuple-element.72), channel_id=1, source_target_pairs={{0,4},{4,0},{1,5},{5,1},{2,6},{6,2},{3,7},{7,3},{8,12},{12,8},{9,1... | collective-permute-start | bytes 786440 | tf_op jit(solution)/shard_map/ppermute | solution.py:438
  236.3 4.5 %collective-permute-start.33 = (f32[2048]{0:T(1024)S(1)}, f32[2048]{0:T(1024)S(1)}, u32[]{:S(2)}, u32[]{:S(2)}) collective-permute-start(f32[2048]{0:T(1024)S(1)} %add.60), channel_id=1, source_target_pairs={{0,16},{8,24},{16,0},{24,8},{1,17},{9,25},{17,1},{25,9},{2,18},{10... | collective-permute-start | bytes 24584 | tf_op jit(solution)/shard_map/ppermute | solution.py:459
  (32 other events, 216.0 us)
Sparse Core Ops, SparseCore 0:
  27.1 45.9 all-gather.2
  74.6 44.6 all-gather.4
  121.6 42.4 reduce-scatter.2
  169.7 42.3 reduce-scatter.4

commit v10 on v9

--- a/solution.py
+++ b/solution.py
@@ -308,23 +308,25 @@
 
     swapped = [lax.ppermute(chunk_of(1 - y, 0), "y", SWAP)]
     here = lax.ppermute(packed, PLANE, [(2, 3)])
-    gain_sent, len_sent = lax.optimization_barrier((gain, src_len, here))[:2]
-    gains = [gain] + [lax.ppermute(gain_sent, "mp", turned(shards, t)) for t in range(1, shards)]
-    key_count = jnp.where(straight, src_len, lax.ppermute(len_sent, "y", SWAP))
-    there = lax.ppermute(after(packed, swapped[0], key_count, *gains), PLANE, [(0, 2), (2, 1)])
+    gains = [gain] + [
+        lax.ppermute(after(gain, here), "mp", turned(shards, t)) for t in range(1, shards)
+    ]
+    blocks = [jnp.concatenate([chunk_of(y, 0), swapped[0]], 0)]
+    there = lax.ppermute(after(packed, blocks[0]), PLANE, [(0, 2), (2, 1)])
+    key_count = jnp.where(straight, src_len, lax.ppermute(after(src_len, there), "y", SWAP))
     nears = [packed, here, there]
     fars = []
     for turn in range(1, shards):
         fars.append(
             [
-                across(packed, turn, [(0, 0)]),
+                across(after(packed, *gains), turn, [(0, 0)]),
                 across(here, turn, [(3, 3)]),
                 across(there, turn, [(1, 1), (2, 2)]),
             ]
         )
     for k in range(1, CHUNKS):
         swapped.append(lax.ppermute(after(chunk_of(1 - y, k), there, fars[0][1]), "y", SWAP))
-    blocks = [jnp.concatenate([chunk_of(y, k), swapped[k]], 0) for k in range(CHUNKS)]
+    blocks += [jnp.concatenate([chunk_of(y, k), swapped[k]], 0) for k in range(1, CHUNKS)]
     w_own, w_other = [], []
 
     position = lax.broadcasted_iota(jnp.int32, (length, width), 0)
@@ -389,10 +391,7 @@
             if k > 0:
                 w_own[k] = after(w_own[k], grad)
         w_other.append(lax.ppermute(w_own[k], "phase", SWAP))
-        part = dot(enc_own, w_own[k])
-        if k > 0:
-            part = after(part, decs[0][0], decs[0][2])
-        dec, gkv = attend(at, part, enc_other, w_other[k], qgs, k)
+        dec, gkv = attend(at, dot(enc_own, w_own[k]), enc_other, w_other[k], qgs, k)
         gkvs.append(gkv)
         decs.append(
             (
@@ -401,14 +400,19 @@
                 lax.ppermute(dec, PLANE, [(2, 1), (1, 3)]),
             )
         )
-        gkv_sent = gkv
-        if tiled and k == CHUNKS - 1:
-            terms = [enc_grad(at, gkvs, w_own, w_other, groups, rows, s) for s in (1, 0)][::-1]
-            gkv_sent = after(gkv, *terms[0], *terms[1])
-        parts = jnp.split(gkv_sent, 2, axis=1)
+        last = k == CHUNKS - 1
+        parts = jnp.split(gkv, 2, axis=1)
         gkv_mate = jnp.concatenate([lax.ppermute(p, "phase", SWAP) for p in parts], 1)
         if tiled:
+            if last:
+                away = enc_grad(at, gkvs, w_own, w_other, groups, rows, 1)
+                gkv_mate = after(gkv_mate, *away)
+            else:
+                gkv_mate = after(gkv_mate, decs[k][0], decs[k][2])
             grad = weight_grad(at, enc_own, enc_mate, gkv, gkv_mate, groups, pair_scale)
+            if last:
+                kept = [after(gkvs[0], grad)] + gkvs[1:]
+                terms = [enc_grad(at, kept, w_own, w_other, groups, rows, 0), away]
         else:
             grad = pair_scale * (dot(enc_own, gkv, TN) + dot(enc_mate, gkv_mate, TN))
             grad = grad.astype(BF16)
@@ -420,24 +424,28 @@
         back = jnp.zeros_like(block_order).at[block_order].set(jnp.arange(block_order.shape[0]))
         full = full.astype(BF16).reshape(length, -1, rows)[:, back].reshape(length, D)
         terms = [jnp.split(cut(full, 1, (x + s) % shards, width), PARTS) for s in range(shards)]
-    far = []
+    kept = jnp.concatenate([w[:rows] for w in weight_sums], 1)
+    got = [lax.ppermute(w[rows:], "y", SWAP) for w in weight_sums]
+    far, first_far = [], None
     for part in range(PARTS):
         total = terms[0][part].astype(F32)
         for turn in range(1, shards):
-            total = total + across(terms[turn][part], turn, [(1, 1), (2, 2)]).astype(F32)
-        far.append(after(total.astype(BF16), decs[-1][2]))
+            term = across(terms[turn][part], turn, [(1, 1), (2, 2)])
+            first_far = term if first_far is None else first_far
+            total = total + term.astype(F32)
+        done = decs[-1][2] if part == 0 else got[0]
+        far.append(after(total.astype(BF16), done))
     moved = [
-        [across(part, turn, [(0, 0), (3, 3)]) for part in terms[turn]] for turn in range(1, shards)
+        [across(after(part, first_far), turn, [(0, 0), (3, 3)]) for part in terms[turn]]
+        for turn in range(1, shards)
     ]
     moved.append([lax.ppermute(part, PLANE, [(2, 0), (1, 3)]) for part in far])
 
     dec_here = jnp.concatenate([jnp.where(y == 0, d[0], d[1]) for d in decs], 1)
     dec_there = jnp.concatenate([d[2] for d in decs], 1)
     dec_grads = ordered(y == 0, dec_here, dec_there, 1)
-    kept = jnp.concatenate([w[:rows] for w in weight_sums], 1)
-    got = [lax.ppermute(w[rows:], "y", SWAP) for w in weight_sums]
     if tiled:
-        moved[0][0], dec_grads, got[0] = lax.optimization_barrier((moved[0][0], dec_grads, got[0]))
+        moved[0][0], dec_grads = lax.optimization_barrier((moved[0][0], dec_grads))
         grad_normed, gain_term = collect(
             at, [terms[0]] + moved, packed, here, inv_rms, gain.astype(F32)[None], pair_scale
         )

time: 252 us -> 248 us (0.984)
  waiting for transfers between devices: 69.5 us -> 59.5 us
  starting transfers between devices: 64.6 us -> 69.5 us
    all_gather x2, waiting for transfers between devices: 16.7 us -> 3.27 us  [on_device(): w_own.append(lax.all_gather(block, 'z', axis=0, tiled=True))]
    ppermute x2, waiting for transfers between devices: 0.01 us -> 10.5 us  [on_device(): moved.append([lax.ppermute(part, PLANE, [(2, 0), (1, 3)]) for part in far])]
    ppermute x2, starting transfers between devices: 0.01 us -> 8.95 us  [on_device(): w_other.append(lax.ppermute(w_own[k], 'phase', SWAP))]
    ppermute x2, waiting for transfers between devices: 16.6 us -> 9.98 us  [on_device(): got = [lax.ppermute(w[rows:], 'y', SWAP) for w in weight_sums]]
    ppermute x1, waiting for transfers between devices: 0.01 us -> 4.62 us  [on_device(): swapped = [lax.ppermute(chunk_of(1 - y, 0), 'y', SWAP)]]
    ppermute x2, starting transfers between devices: 4.68 us -> 1.09 us  [on_device(): got = [lax.ppermute(w[rows:], 'y', SWAP) for w in weight_sums]]
    ppermute x2, starting transfers between devices: 0.92 us -> 3.89 us  [on_device(): lax.ppermute(gain_term, 'z', [(i, i ^ turn) for i in range(groups)])]
    ppermute x2, waiting for transfers between devices: 7.28 us -> 4.31 us  [on_device(): lax.ppermute(gain_term, 'z', [(i, i ^ turn) for i in range(groups)])]
  transfers between devices with their start and end apart: 39 -> 39, of which waited for: 12 -> 15; matrix products, arithmetic and copies ran while one was open for 12% -> 12% of each run, Pallas kernels for 24% -> 25%
where the time goes in v10:
time: 248 us; the launch traced here: 246 us
  starting transfers between devices  69.5 us (28%)
  Pallas kernels  61 us (25%)
  waiting for transfers between devices  59.5 us (24%)
  other arithmetic  18.7 us (8%)
  between operations  16.2 us (7%)
  local copies, waits for them, and re-layouts  15.3 us (6%)
  matrix products  6.3 us (3%)
    pallas_call x2, Pallas kernels, attend(): pl.pallas_call(attend_kernel, grid_spec=pltpu.PrefetchScalarGridSpec(num_...  21.4 us
    ppermute x7, starting transfers between devices, across(): lax.ppermute(value, ('y', 'phase', 'mp'), [(a * shards + s, b * shards +...  14.3 us
    ppermute x1, waiting for transfers between devices, on_device(): there = lax.ppermute(after(packed, blocks[0]), PLANE, [(0, 2), (2, 1)])  14.2 us
    pallas_call x2, Pallas kernels, enc_grad(): pl.pallas_call(enc_grad_kernel, grid_spec=pltpu.PrefetchScalarGridSpec(nu...  13.4 us
    pallas_call x2, Pallas kernels, weight_grad(): pl.pallas_call(lambda *refs: weight_grad_kernel(scale, *refs), grid_spec=...  12.6 us
    ppermute x2, waiting for transfers between devices, on_device(): moved.append([lax.ppermute(part, PLANE, [(2, 0), (1, 3)]) for part in far])  10.5 us
    ppermute x2, waiting for transfers between devices, on_device(): got = [lax.ppermute(w[rows:], 'y', SWAP) for w in weight_sums]  9.98 us
    unnamed x42, local copies, waits for them, and re-layouts  9.13 us
  transfers between devices with their start and end apart: 39, of which 15 were waited for; matrix products, arithmetic and copies ran while one was open for 12% of the time, Pallas kernels for 25%

profile of v10, /device:TPU:0, one launch (start us, length us, event | category | flops | bytes accessed | tf_op | source)
XLA Modules:
  0.0 246.5 jit_solution(13763316736229680613)
XLA Ops:
  11.3 4.0 %collective-permute-start = (bf16[256,512]{1,0:T(8,128)(2,1)S(1)}, bf16[256,512]{1,0:T(8,128)(2,1)S(1)}, u32[]{:S(2)}, u32[]{:S(2)}) collective-permute-start(bf16[256,512]{1,0:T(8,128)(2,1)S(1)} %get-tuple-element.72), channel_id=1, source_target_pairs={{0,4},{4,0},{1,5},{5,1},{2,6},{6,2},{3,7},{7,3},{8,12},{12,8},{9,1... | collective-permute-start | bytes 786440 | tf_op jit(solution)/shard_map/ppermute | solution.py:309
  15.4 4.6 %collective-permute-done = bf16[256,512]{1,0:T(8,128)(2,1)S(1)} collective-permute-done((bf16[256,512]{1,0:T(8,128)(2,1)S(1)}, bf16[256,512]{1,0:T(8,128)(2,1)S(1)}, u32[]{:S(2)}, u32[]{:S(2)}) %collective-permute-start) | collective-permute-done | bytes 262176 | tf_op jit(solution)/shard_map/ppermute | solution.py:309
  20.9 5.1 %collective-permute-start.1 = (bf16[512,2048]{1,0:T(8,128)(2,1)S(1)}, bf16[512,2048]{1,0:T(8,128)(2,1)}, u32[]{:S(2)}, u32[]{:S(2)}) collective-permute-start(bf16[512,2048]{1,0:T(8,128)(2,1)S(1)} %bitcast.17), channel_id=1, source_target_pairs={{0,4},{4,2},{1,5},{5,3},{8,12},{12,10},{9,13},{13,11},{16,20},{20,... | collective-permute-start | bytes 6291464 | tf_op jit(solution)/shard_map/ppermute | solution.py:315
  30.5 3.4 %collective-permute-start.5 = (bf16[512,2048]{1,0:T(8,128)(2,1)S(1)}, bf16[512,2048]{1,0:T(8,128)(2,1)}, u32[]{:S(2)}, u32[]{:S(2)}) collective-permute-start(bf16[512,2048]{1,0:T(8,128)(2,1)S(1)} %bitcast.18), channel_id=1, source_target_pairs={{0,1},{1,0},{8,9},{9,8},{16,17},{17,16},{24,25},{25,24}} | collective-permute-start | bytes 6291464 | tf_op jit(solution)/shard_map/ppermute | solution.py:297
  33.9 14.2 %collective-permute-done.1.refs_3_ = bf16[512,2048]{1,0:T(8,128)(2,1)} collective-permute-done((bf16[512,2048]{1,0:T(8,128)(2,1)S(1)}, bf16[512,2048]{1,0:T(8,128)(2,1)}, u32[]{:S(2)}, u32[]{:S(2)}) %collective-permute-start.1) | collective-permute-done | bytes 2097184 | tf_op jit(solution)/shard_map/ppermute | solution.py:315
  51.4 4.0 %collective-permute-start.8 = (bf16[256,512]{1,0:T(8,128)(2,1)}, bf16[256,512]{1,0:T(8,128)(2,1)S(1)}, u32[]{:S(2)}, u32[]{:S(2)}) collective-permute-start(bf16[256,512]{1,0:T(8,128)(2,1)} %get-tuple-element.40), channel_id=1, source_target_pairs={{0,4},{4,0},{1,5},{5,1},{2,6},{6,2},{3,7},{7,3},{8,12},{12,8},{9,1... | collective-permute-start | bytes 786440 | tf_op jit(solution)/shard_map/ppermute | solution.py:328
  57.2 4.4 %collective-permute-done.8 = bf16[256,512]{1,0:T(8,128)(2,1)S(1)} collective-permute-done((bf16[256,512]{1,0:T(8,128)(2,1)}, bf16[256,512]{1,0:T(8,128)(2,1)S(1)}, u32[]{:S(2)}, u32[]{:S(2)}) %collective-permute-start.8) | collective-permute-done | bytes 262176 | tf_op jit(solution)/shard_map/ppermute | solution.py:328
  69.2 3.1 %all-gather.3.cloned.1.call-done.own_0 = bf16[2048,512]{1,0:T(8,128)(2,1)} async-done(((bf16[512,512]{1,0:T(8,128)(2,1)}), bf16[2048,512]{1,0:T(8,128)(2,1)}) %all-gather.3.cloned.1.call-update) | async-done | bytes 2097168 | tf_op jit(solution)/shard_map/all_gather | solution.py:390
  72.3 4.7 %collective-permute-start.11 = (bf16[2048,512]{1,0:T(8,128)(2,1)}, bf16[2048,512]{1,0:T(8,128)(2,1)}, u32[]{:S(2)}, u32[]{:S(2)}) collective-permute-start(bf16[2048,512]{1,0:T(8,128)(2,1)} %all-gather.3.cloned.1.call-done.own_0), channel_id=1, source_target_pairs={{0,2},{2,0},{1,3},{3,1},{4,6},{6,4},{5,7},{7,5},{8,10},{10,8},{9,1... | collective-permute-start | bytes 6291464 | tf_op jit(solution)/shard_map/ppermute | solution.py:393
  80.2 7.1 %norm.1 = (bf16[512,2048]{1,0:T(8,128)(2,1)}, bf16[512,2048]{1,0:T(8,128)(2,1)}, f32[512,128]{1,0:T(8,128)S(1)}) custom-call(s32[6]{0:T(128)S(1)} %concatenate.60.refs_0_.at, bf16[512,2048]{1,0:T(8,128)(2,1)S(1)} %bitcast.19, bf16[512,2048]{1,0:T(8,128)(2,1)} %collective-permute-done.3.refs_2_.refs_8_, bf16[512,2048]{1,0:T(8,128)(2,1)} %collective-permute-done.1.refs_3_, ...), custom_call_target="tpu_custom_call" | custom-call | flops 16777216 | bytes 8388608 | tf_op jit(solution)/shard_map/norm/pallas_call | solution.py:74
  87.3 2.4 collective-permute-start.12
  89.7 2.8 %fusion.12.part = f32[512,512]{1,0:T(8,128)S(1)} fusion(bf16[512,2048]{1,0:T(8,128)(2,1)} %get-tuple-element.44.refs_1_, bf16[2048,512]{1,0:T(8,128)(2,1)S(1)} %copy-done.19), kind=kOutput, calls=%fused_computation.36 | convolution fusion | flops 1073741824 | bytes 5242880 | tf_op jit(solution)/shard_map/dot_general | solution.py:25
  92.5 10.4 %attend.2 = (bf16[512,512]{1,0:T(8,128)(2,1)S(1)}, bf16[512,512]{1,0:T(8,128)(2,1)S(1)}) custom-call(s32[6]{0:T(128)S(1)} %concatenate.60.refs_0_.at, f32[512,512]{1,0:T(8,128)S(1)} %fusion.12.part, bf16[512,2048]{1,0:T(8,128)(2,1)} %get-tuple-element.45.enc_other, bf16[2048,512]{1,0:T(8,128)(2,1)} %collective-permute-done.11.w_other.other_0, ...), custom_call_target="tpu_custom_call" | custom-call | flops 4026531840 | bytes 8388608 | tf_op jit(solution)/shard_map/attend/pallas_call | solution.py:136
  103.7 3.6 %collective-permute-start.15 = (bf16[512,512]{1,0:T(8,128)(2,1)S(1)}, bf16[512,512]{1,0:T(8,128)(2,1)S(1)}, u32[]{:S(2)}, u32[]{:S(2)}) collective-permute-start(bf16[512,512]{1,0:T(8,128)(2,1)S(1)} %get-tuple-element.47), channel_id=1, source_target_pairs={{0,2},{1,3},{8,10},{9,11},{16,18},{17,19},{24,26},{25,27}} | collective-permute-start | bytes 1572872 | tf_op jit(solution)/shard_map/ppermute | solution.py:398
  111.9 6.3 %weight_grad.2 = bf16[2048,512]{1,0:T(8,128)(2,1)} custom-call(s32[6]{0:T(128)S(1)} %concatenate.60.refs_0_.at, bf16[512,2048]{1,0:T(8,128)(2,1)} %get-tuple-element.44.refs_1_, bf16[512,2048]{1,0:T(8,128)(2,1)} %copy-done.9, bf16[512,512]{1,0:T(8,128)(2,1)S(1)} %get-tuple-element.54.refs_3_.gkv_0, bf16[512,512]{1,0:T(8,128)(2,1)S(1)} %pad_maximum_fusion.2.refs_4_), custom_call_target="tpu_custom_call" | custom-call | flops 33554432 | tf_op jit(solution)/shard_map/weight_grad/pallas_call | solution.py:164
  118.6 4.2 %collective-permute-start.17 = (bf16[2048,512]{1,0:T(8,128)(2,1)}, bf16[2048,512]{1,0:T(8,128)(2,1)S(1)}, u32[]{:S(2)}, u32[]{:S(2)}) collective-permute-start(bf16[2048,512]{1,0:T(8,128)(2,1)} %all-gather.5.cloned.1.call-done.own_1), channel_id=1, source_target_pairs={{0,2},{2,0},{1,3},{3,1},{4,6},{6,4},{5,7},{7,5},{8,10},{10,8},{9,1... | collective-permute-start | bytes 6291464 | tf_op jit(solution)/shard_map/ppermute | solution.py:393
  122.8 3.5 %fusion.13.part = f32[512,512]{1,0:T(8,128)S(1)} fusion(bf16[512,2048]{1,0:T(8,128)(2,1)} %get-tuple-element.44.refs_1_, bf16[2048,512]{1,0:T(8,128)(2,1)} %all-gather.5.cloned.1.call-done.own_1), kind=kOutput, calls=%fused_computation.37 | convolution fusion | flops 1073741824 | bytes 5242880 | tf_op jit(solution)/shard_map/dot_general | solution.py:25
  128.1 11.0 %attend.3 = (bf16[512,512]{1,0:T(8,128)(2,1)}, bf16[512,512]{1,0:T(8,128)(2,1)S(1)}) custom-call(s32[6]{0:T(128)S(1)} %concatenate.60.refs_0_.at, f32[512,512]{1,0:T(8,128)S(1)} %fusion.13.part, bf16[512,2048]{1,0:T(8,128)(2,1)} %get-tuple-element.45.enc_other, bf16[2048,512]{1,0:T(8,128)(2,1)} %copy-done.20, bf16[512,1024]{1,0:T(8,128)(2,1)} %copy-done.10, ...), custom_call_target="tpu_custom_call" | custom-call | flops 4026531840 | bytes 8388608 | tf_op jit(solution)/shard_map/attend/pallas_call | solution.py:136
  140.0 6.8 %enc_grad.2 = (bf16[256,2048]{1,0:T(8,128)(2,1)}, bf16[256,2048]{1,0:T(8,128)(2,1)}) custom-call(s32[6]{0:T(128)S(1)} %concatenate.60.refs_0_.at, bf16[512,512]{1,0:T(8,128)(2,1)} %copy-done.5, bf16[512,512]{1,0:T(8,128)(2,1)} %copy-done.6, bf16[2048,512]{1,0:T(8,128)(2,1)} %all-gather.3.cloned.1.call-done.own_0, ...), custom_call_target="tpu_custom_call" | custom-call | flops 4294967296 | bytes 8388608 | tf_op jit(solution)/shard_map/enc_grad/pallas_call | solution.py:250
  147.6 2.8 %collective-permute-start.18 = (bf16[512,256]{1,0:T(8,128)(2,1)S(1)}, bf16[512,256]{1,0:T(8,128)(2,1)S(1)}, u32[]{:S(2)}, u32[]{:S(2)}) collective-permute-start(bf16[512,256]{1,0:T(8,128)(2,1)S(1)} %get-tuple-element.79), channel_id=1, source_target_pairs={{0,2},{2,0},{1,3},{3,1},{4,6},{6,4},{5,7},{7,5},{8,10},{10,8},{9,1... | collective-permute-start | bytes 786440 | tf_op jit(solution)/shard_map/ppermute | solution.py:405
  151.9 3.8 %collective-permute-start.22 = (bf16[512,512]{1,0:T(8,128)(2,1)}, bf16[512,512]{1,0:T(8,128)(2,1)}, u32[]{:S(2)}, u32[]{:S(2)}) collective-permute-start(bf16[512,512]{1,0:T(8,128)(2,1)} %get-tuple-element.58), channel_id=1, source_target_pairs={{0,2},{1,3},{8,10},{9,11},{16,18},{17,19},{24,26},{25,27}} | collective-permute-start | bytes 1572872 | tf_op jit(solution)/shard_map/ppermute | solution.py:398
  157.4 6.3 %weight_grad.3 = bf16[2048,512]{1,0:T(8,128)(2,1)} custom-call(s32[6]{0:T(128)S(1)} %concatenate.60.refs_0_.at, bf16[512,2048]{1,0:T(8,128)(2,1)} %get-tuple-element.44.refs_1_, bf16[512,2048]{1,0:T(8,128)(2,1)} %copy-done.9, bf16[512,512]{1,0:T(8,128)(2,1)S(1)} %copy-done.7, bf16[512,512]{1,0:T(8,128)(2,1)S(1)} %pad_maximum_fusion.3.refs_4_), custom_call_target="tpu_custom_call" | custom-call | flops 33554432 | tf_op jit(solution)/shard_map/weight_grad/pallas_call | solution.py:164
  163.8 6.6 %enc_grad.3 = (bf16[256,2048]{1,0:T(8,128)(2,1)}, bf16[256,2048]{1,0:T(8,128)(2,1)}) custom-call(s32[6]{0:T(128)S(1)} %concatenate.60.refs_0_.at, bf16[512,512]{1,0:T(8,128)(2,1)} %copy-done.5, bf16[512,512]{1,0:T(8,128)(2,1)} %copy-done.6, bf16[2048,512]{1,0:T(8,128)(2,1)} %all-gather.3.cloned.1.call-done.own_0, ...), custom_call_target="tpu_custom_call" | custom-call | flops 4294967296 | bytes 8388608 | tf_op jit(solution)/shard_map/enc_grad/pallas_call | solution.py:250
  171.4 3.0 %add_convert_fusion.1 = bf16[256,2048]{1,0:T(8,128)(2,1)} fusion(bf16[256,2048]{1,0:T(8,128)(2,1)} %copy-done.11, bf16[256,2048]{1,0:T(8,128)(2,1)} %get-tuple-element.55.refs_1_), kind=kLoop, calls=%fused_computation.6 | loop fusion | flops 2097152 | bytes 3145728 | tf_op jit(solution)/shard_map/convert_element_type | solution.py:437
  175.7 2.5 %collective-permute-start.21 = (bf16[256,2048]{1,0:T(8,128)(2,1)}, bf16[256,2048]{1,0:T(8,128)(2,1)}, u32[]{:S(2)}, u32[]{:S(2)}) collective-permute-start(bf16[256,2048]{1,0:T(8,128)(2,1)} %get-tuple-element.57), channel_id=1, source_target_pairs={{0,1},{1,0},{6,7},{7,6},{8,9},{9,8},{14,15},{15,14},{16,17},{17,16... | collective-permute-start | bytes 3145736 | tf_op jit(solution)/shard_map/ppermute | solution.py:297
  178.2 3.3 %collective-permute-start.24 = (bf16[256,2048]{1,0:T(8,128)(2,1)}, bf16[256,2048]{1,0:T(8,128)(2,1)}, u32[]{:S(2)}, u32[]{:S(2)}) collective-permute-start(bf16[256,2048]{1,0:T(8,128)(2,1)} %get-tuple-element.60), channel_id=1, source_target_pairs={{0,1},{1,0},{6,7},{7,6},{8,9},{9,8},{14,15},{15,14},{16,17},{17,16... | collective-permute-start | bytes 3145736 | tf_op jit(solution)/shard_map/ppermute | solution.py:297
  184.3 2.6 %add_convert_fusion = bf16[256,2048]{1,0:T(8,128)(2,1)} fusion(bf16[256,2048]{1,0:T(8,128)(2,1)} %collective-permute-done.26, bf16[256,2048]{1,0:T(8,128)(2,1)S(1)} %copy-done.2), kind=kLoop, calls=%fused_computation.5 | loop fusion | flops 2097152 | bytes 3145728 | tf_op jit(solution)/shard_map/convert_element_type | solution.py:437
  186.9 10.0 %collective-permute-done.27 = bf16[256,512]{1,0:T(8,128)(2,1)S(1)} collective-permute-done((bf16[256,512]{1,0:T(8,128)(2,1)S(1)}, bf16[256,512]{1,0:T(8,128)(2,1)S(1)}, u32[]{:S(2)}, u32[]{:S(2)}) %collective-permute-start.27) | collective-permute-done | bytes 262176 | tf_op jit(solution)/shard_map/ppermute | solution.py:428
  201.2 2.9 %maximum_select_fusion = bf16[512,2048]{1,0:T(8,128)(2,1)} fusion(bf16[512,512]{1,0:T(8,128)(2,1)} %collective-permute-done.23, bf16[512,512]{1,0:T(8,128)(2,1)S(1)} %copy-done.14, bf16[512,512]{1,0:T(8,128)(2,1)S(1)} %broadcast_select_fusion, bf16[512,512]{1,0:T(8,128)(2,1)S(1)} %broadcast_select_fusion.1, pred[]{:T(512)S(6)} %eq.20), kind=kLoop, calls=%fused_computation.3 | loop fusion | flops 17825792 | bytes 4194305 | tf_op jit(solution)/shard_map/jit(_where)/select_n | solution.py:270
  204.1 10.5 %collective-permute-done.28.refs_6_ = bf16[256,2048]{1,0:T(8,128)(2,1)} collective-permute-done((bf16[256,2048]{1,0:T(8,128)(2,1)}, bf16[256,2048]{1,0:T(8,128)(2,1)}, u32[]{:S(2)}, u32[]{:S(2)}) %collective-permute-start.28) | collective-permute-done | bytes 1048608 | tf_op jit(solution)/shard_map/ppermute | solution.py:442
  214.6 6.5 %collect.1 = (bf16[512,2048]{1,0:T(8,128)(2,1)}, f32[4,1,2048]{2,1,0:T(1,128)S(1)}) custom-call(s32[6]{0:T(128)S(1)} %concatenate.60.refs_0_.at, bf16[256,2048]{1,0:T(8,128)(2,1)S(1)} %copy-done.1, bf16[256,2048]{1,0:T(8,128)(2,1)S(1)} %copy-done.2, bf16[256,2048]{1,0:T(8,128)(2,1)} %collective-permute-done.21.refs_3_, ...), custom_call_target="tpu_custom_call" | custom-call | flops 8388608 | bytes 12582912 | tf_op jit(solution)/shard_map/collect/pallas_call | solution.py:203
  229.9 3.2 %select_bitcast_fusion = bf16[1,1,512,2048]{3,2,1,0:T(8,128)(2,1)} fusion(bf16[512,2048]{1,0:T(8,128)(2,1)} %maximum_select_fusion, bf16[512,2048]{1,0:T(8,128)(2,1)} %get-tuple-element.65, bf16[512,2048]{1,0:T(8,128)(2,1)S(1)} %collective-permute-done.31, pred[]{:T(512)S(6)} %eq.21, pred[]{:T(512)S(6)} %eq.20), kind=kLoop, calls=%fused_computation.4 | loop fusion | flops 2097152 | bytes 8388610 | tf_op jit(solution)/shard_map/broadcast_in_dim | solution.py:459
  (134 shorter events, 60.6 us)
Async XLA Ops:
  7.2 65.1 %all-gather.3.cloned.1.call-start = ((), (), s32[]{:S(2)}) async-start(), calls=%async_computation.2 | async-start | bytes 2621440 | tf_op jit(solution)/shard_map/all_gather | solution.py:390
  7.2 18.8 %collective-permute-start.3 = (bf16[512,2048]{1,0:T(8,128)(2,1)}, bf16[512,2048]{1,0:T(8,128)(2,1)}, u32[]{:S(2)}, u32[]{:S(2)}) collective-permute-start(bf16[512,2048]{1,0:T(8,128)(2,1)} %bitcast.16), channel_id=1, source_target_pairs={{4,6},{5,7},{12,14},{13,15},{20,22},{21,23},{28,30},{29,31}} | collective-permute-start | bytes 6291464 | tf_op jit(solution)/shard_map/ppermute | solution.py:310
  11.3 8.7 %collective-permute-start = (bf16[256,512]{1,0:T(8,128)(2,1)S(1)}, bf16[256,512]{1,0:T(8,128)(2,1)S(1)}, u32[]{:S(2)}, u32[]{:S(2)}) collective-permute-start(bf16[256,512]{1,0:T(8,128)(2,1)S(1)} %get-tuple-element.72), channel_id=1, source_target_pairs={{0,4},{4,0},{1,5},{5,1},{2,6},{6,2},{3,7},{7,3},{8,12},{12,8},{9,1... | collective-permute-start | bytes 786440 | tf_op jit(solution)/shard_map/ppermute | solution.py:309
  20.9 27.2 %collective-permute-start.1 = (bf16[512,2048]{1,0:T(8,128)(2,1)S(1)}, bf16[512,2048]{1,0:T(8,128)(2,1)}, u32[]{:S(2)}, u32[]{:S(2)}) collective-permute-start(bf16[512,2048]{1,0:T(8,128)(2,1)S(1)} %bitcast.17), channel_id=1, source_target_pairs={{0,4},{4,2},{1,5},{5,3},{8,12},{12,10},{9,13},{13,11},{16,20},{20,... | collective-permute-start | bytes 6291464 | tf_op jit(solution)/shard_map/ppermute | solution.py:315
  25.9 92.6 %all-gather.5.cloned.1.call-start = ((), (), s32[]{:S(2)}) async-start(), calls=%async_computation.3 | async-start | bytes 2621440 | tf_op jit(solution)/shard_map/all_gather | solution.py:390
  26.0 24.0 %collective-permute-start.6 = (bf16[512,2048]{1,0:T(8,128)(2,1)}, bf16[512,2048]{1,0:T(8,128)(2,1)S(1)}, u32[]{:S(2)}, u32[]{:S(2)}) collective-permute-start(bf16[512,2048]{1,0:T(8,128)(2,1)} %collective-permute-done.3.refs_2_.refs_8_), channel_id=1, source_target_pairs={{6,7},{7,6},{14,15},{15,14},{22,23},{23,22},{30,31},{31,30}} | collective-permute-start | bytes 6291464 | tf_op jit(solution)/shard_map/ppermute | solution.py:297
  30.5 48.0 %collective-permute-start.5 = (bf16[512,2048]{1,0:T(8,128)(2,1)S(1)}, bf16[512,2048]{1,0:T(8,128)(2,1)}, u32[]{:S(2)}, u32[]{:S(2)}) collective-permute-start(bf16[512,2048]{1,0:T(8,128)(2,1)S(1)} %bitcast.18), channel_id=1, source_target_pairs={{0,1},{1,0},{8,9},{9,8},{16,17},{17,16},{24,25},{25,24}} | collective-permute-start | bytes 6291464 | tf_op jit(solution)/shard_map/ppermute | solution.py:297
  48.1 30.5 %collective-permute-start.7 = (bf16[512,2048]{1,0:T(8,128)(2,1)}, bf16[512,2048]{1,0:T(8,128)(2,1)}, u32[]{:S(2)}, u32[]{:S(2)}) collective-permute-start(bf16[512,2048]{1,0:T(8,128)(2,1)} %collective-permute-done.1.refs_3_), channel_id=1, source_target_pairs={{2,3},{3,2},{4,5},{5,4},{10,11},{11,10},{12,13},{13,12},{18,19},{1... | collective-permute-start | bytes 6291464 | tf_op jit(solution)/shard_map/ppermute | solution.py:297
  51.4 10.3 %collective-permute-start.8 = (bf16[256,512]{1,0:T(8,128)(2,1)}, bf16[256,512]{1,0:T(8,128)(2,1)S(1)}, u32[]{:S(2)}, u32[]{:S(2)}) collective-permute-start(bf16[256,512]{1,0:T(8,128)(2,1)} %get-tuple-element.40), channel_id=1, source_target_pairs={{0,4},{4,0},{1,5},{5,1},{2,6},{6,2},{3,7},{7,3},{8,12},{12,8},{9,1... | collective-permute-start | bytes 786440 | tf_op jit(solution)/shard_map/ppermute | solution.py:328
  61.6 16.9 %collective-permute-start.10 = (bf16[512,1024]{1,0:T(8,128)(2,1)}, bf16[512,1024]{1,0:T(8,128)(2,1)}, u32[]{:S(2)}, u32[]{:S(2)}) collective-permute-start(bf16[512,1024]{1,0:T(8,128)(2,1)} %get-tuple-element.42), channel_id=1, source_target_pairs={{2,4},{6,2},{3,5},{7,3},{10,12},{14,10},{11,13},{15,11},{18,20},{2... | collective-permute-start | bytes 3145736 | tf_op jit(solution)/shard_map/ppermute | solution.py:340
  63.3 15.2 %collective-permute-start.9 = (bf16[512,1024]{1,0:T(8,128)(2,1)S(1)}, bf16[512,1024]{1,0:T(8,128)(2,1)}, u32[]{:S(2)}, u32[]{:S(2)}) collective-permute-start(bf16[512,1024]{1,0:T(8,128)(2,1)S(1)} %get-tuple-element.41.refs_0_), channel_id=1, source_target_pairs={{2,0},{3,1},{10,8},{11,9},{18,16},{19,17},{26,24},{27,25}} | collective-permute-start | bytes 3145736 | tf_op jit(solution)/shard_map/ppermute | solution.py:339
  65.4 116.1 %reduce-scatter.3.cloned.1.call-start = ((), (), s32[]{:S(2)}) async-start(), calls=%async_computation.4 | async-start | bytes 2621440 | tf_op jit(solution)/shard_map/reduce_scatter | solution.py:419
  72.3 20.2 %collective-permute-start.11 = (bf16[2048,512]{1,0:T(8,128)(2,1)}, bf16[2048,512]{1,0:T(8,128)(2,1)}, u32[]{:S(2)}, u32[]{:S(2)}) collective-permute-start(bf16[2048,512]{1,0:T(8,128)(2,1)} %all-gather.3.cloned.1.call-done.own_0), channel_id=1, source_target_pairs={{0,2},{2,0},{1,3},{3,1},{4,6},{6,4},{5,7},{7,5},{8,10},{10,8},{9,1... | collective-permute-start | bytes 6291464 | tf_op jit(solution)/shard_map/ppermute | solution.py:393
  87.3 22.3 %collective-permute-start.12 = (bf16[512,2048]{1,0:T(8,128)(2,1)}, bf16[512,2048]{1,0:T(8,128)(2,1)S(1)}, u32[]{:S(2)}, u32[]{:S(2)}) collective-permute-start(bf16[512,2048]{1,0:T(8,128)(2,1)} %get-tuple-element.45.enc_other), channel_id=1, source_target_pairs={{0,2},{2,0},{1,3},{3,1},{4,6},{6,4},{5,7},{7,5},{8,10},{10,8},{9,1... | collective-permute-start | bytes 6291464 | tf_op jit(solution)/shard_map/ppermute | solution.py:376
  103.0 6.6 %collective-permute-start.16 = (bf16[512,512]{1,0:T(8,128)(2,1)S(1)}, bf16[512,512]{1,0:T(8,128)(2,1)S(1)}, u32[]{:S(2)}, u32[]{:S(2)}) collective-permute-start(bf16[512,512]{1,0:T(8,128)(2,1)S(1)} %get-tuple-element.47), channel_id=1, source_target_pairs={{4,2},{2,6},{5,3},{3,7},{12,10},{10,14},{13,11},{11,15},{20,18},{1... | collective-permute-start | bytes 1572872 | tf_op jit(solution)/shard_map/ppermute | solution.py:400
  103.7 5.9 %collective-permute-start.15 = (bf16[512,512]{1,0:T(8,128)(2,1)S(1)}, bf16[512,512]{1,0:T(8,128)(2,1)S(1)}, u32[]{:S(2)}, u32[]{:S(2)}) collective-permute-start(bf16[512,512]{1,0:T(8,128)(2,1)S(1)} %get-tuple-element.47), channel_id=1, source_target_pairs={{0,2},{1,3},{8,10},{9,11},{16,18},{17,19},{24,26},{25,27}} | collective-permute-start | bytes 1572872 | tf_op jit(solution)/shard_map/ppermute | solution.py:398
  118.2 110.5 %reduce-scatter.5.cloned.1.call-start = ((), (), s32[]{:S(2)}) async-start(), calls=%async_computation.5 | async-start | bytes 2621440 | tf_op jit(solution)/shard_map/reduce_scatter | solution.py:419
  118.6 8.2 %collective-permute-start.17 = (bf16[2048,512]{1,0:T(8,128)(2,1)}, bf16[2048,512]{1,0:T(8,128)(2,1)S(1)}, u32[]{:S(2)}, u32[]{:S(2)}) collective-permute-start(bf16[2048,512]{1,0:T(8,128)(2,1)} %all-gather.5.cloned.1.call-done.own_1), channel_id=1, source_target_pairs={{0,2},{2,0},{1,3},{3,1},{4,6},{6,4},{5,7},{7,5},{8,10},{10,8},{9,1... | collective-permute-start | bytes 6291464 | tf_op jit(solution)/shard_map/ppermute | solution.py:393
  146.8 23.6 %collective-permute-start.20 = (bf16[256,2048]{1,0:T(8,128)(2,1)}, bf16[256,2048]{1,0:T(8,128)(2,1)S(1)}, u32[]{:S(2)}, u32[]{:S(2)}) collective-permute-start(bf16[256,2048]{1,0:T(8,128)(2,1)} %get-tuple-element.57), channel_id=1, source_target_pairs={{2,3},{3,2},{4,5},{5,4},{10,11},{11,10},{12,13},{13,12},{18,19},{1... | collective-permute-start | bytes 3145736 | tf_op jit(solution)/shard_map/ppermute | solution.py:297
  147.6 8.1 %collective-permute-start.18 = (bf16[512,256]{1,0:T(8,128)(2,1)S(1)}, bf16[512,256]{1,0:T(8,128)(2,1)S(1)}, u32[]{:S(2)}, u32[]{:S(2)}) collective-permute-start(bf16[512,256]{1,0:T(8,128)(2,1)S(1)} %get-tuple-element.79), channel_id=1, source_target_pairs={{0,2},{2,0},{1,3},{3,1},{4,6},{6,4},{5,7},{7,5},{8,10},{10,8},{9,1... | collective-permute-start | bytes 786440 | tf_op jit(solution)/shard_map/ppermute | solution.py:405
  150.4 7.0 %collective-permute-start.19 = (bf16[512,256]{1,0:T(8,128)(2,1)S(1)}, bf16[512,256]{1,0:T(8,128)(2,1)S(1)}, u32[]{:S(2)}, u32[]{:S(2)}) collective-permute-start(bf16[512,256]{1,0:T(8,128)(2,1)S(1)} %get-tuple-element.80), channel_id=1, source_target_pairs={{0,2},{2,0},{1,3},{3,1},{4,6},{6,4},{5,7},{7,5},{8,10},{10,8},{9,1... | collective-permute-start | bytes 786440 | tf_op jit(solution)/shard_map/ppermute | solution.py:405
  150.4 23.9 %collective-permute-start.23 = (bf16[512,512]{1,0:T(8,128)(2,1)}, bf16[512,512]{1,0:T(8,128)(2,1)}, u32[]{:S(2)}, u32[]{:S(2)}) collective-permute-start(bf16[512,512]{1,0:T(8,128)(2,1)} %get-tuple-element.58), channel_id=1, source_target_pairs={{4,2},{2,6},{5,3},{3,7},{12,10},{10,14},{13,11},{11,15},{20,18},{1... | collective-permute-start | bytes 1572872 | tf_op jit(solution)/shard_map/ppermute | solution.py:400
  151.9 48.2 %collective-permute-start.22 = (bf16[512,512]{1,0:T(8,128)(2,1)}, bf16[512,512]{1,0:T(8,128)(2,1)}, u32[]{:S(2)}, u32[]{:S(2)}) collective-permute-start(bf16[512,512]{1,0:T(8,128)(2,1)} %get-tuple-element.58), channel_id=1, source_target_pairs={{0,2},{1,3},{8,10},{9,11},{16,18},{17,19},{24,26},{25,27}} | collective-permute-start | bytes 1572872 | tf_op jit(solution)/shard_map/ppermute | solution.py:398
  155.8 27.6 %collective-permute-start.26 = (bf16[256,2048]{1,0:T(8,128)(2,1)}, bf16[256,2048]{1,0:T(8,128)(2,1)}, u32[]{:S(2)}, u32[]{:S(2)}) collective-permute-start(bf16[256,2048]{1,0:T(8,128)(2,1)} %get-tuple-element.60), channel_id=1, source_target_pairs={{2,3},{3,2},{4,5},{5,4},{10,11},{11,10},{12,13},{13,12},{18,19},{1... | collective-permute-start | bytes 3145736 | tf_op jit(solution)/shard_map/ppermute | solution.py:297
  174.4 29.7 %collective-permute-start.25 = (bf16[256,2048]{1,0:T(8,128)(2,1)}, bf16[256,2048]{1,0:T(8,128)(2,1)}, u32[]{:S(2)}, u32[]{:S(2)}) collective-permute-start(bf16[256,2048]{1,0:T(8,128)(2,1)} %add_convert_fusion.1), channel_id=1, source_target_pairs={{4,0},{2,6},{5,1},{3,7},{12,8},{10,14},{13,9},{11,15},{20,16},{18,... | collective-permute-start | bytes 3145736 | tf_op jit(solution)/shard_map/ppermute | solution.py:442
  175.7 28.4 %collective-permute-start.21 = (bf16[256,2048]{1,0:T(8,128)(2,1)}, bf16[256,2048]{1,0:T(8,128)(2,1)}, u32[]{:S(2)}, u32[]{:S(2)}) collective-permute-start(bf16[256,2048]{1,0:T(8,128)(2,1)} %get-tuple-element.57), channel_id=1, source_target_pairs={{0,1},{1,0},{6,7},{7,6},{8,9},{9,8},{14,15},{15,14},{16,17},{17,16... | collective-permute-start | bytes 3145736 | tf_op jit(solution)/shard_map/ppermute | solution.py:297
  178.2 25.9 %collective-permute-start.24 = (bf16[256,2048]{1,0:T(8,128)(2,1)}, bf16[256,2048]{1,0:T(8,128)(2,1)}, u32[]{:S(2)}, u32[]{:S(2)}) collective-permute-start(bf16[256,2048]{1,0:T(8,128)(2,1)} %get-tuple-element.60), channel_id=1, source_target_pairs={{0,1},{1,0},{6,7},{7,6},{8,9},{9,8},{14,15},{15,14},{16,17},{17,16... | collective-permute-start | bytes 3145736 | tf_op jit(solution)/shard_map/ppermute | solution.py:297
  183.3 13.6 %collective-permute-start.27 = (bf16[256,512]{1,0:T(8,128)(2,1)S(1)}, bf16[256,512]{1,0:T(8,128)(2,1)S(1)}, u32[]{:S(2)}, u32[]{:S(2)}) collective-permute-start(bf16[256,512]{1,0:T(8,128)(2,1)S(1)} %get-tuple-element.76), channel_id=1, source_target_pairs={{0,4},{4,0},{1,5},{5,1},{2,6},{6,2},{3,7},{7,3},{8,12},{12,8},{9,1... | collective-permute-start | bytes 786440 | tf_op jit(solution)/shard_map/ppermute | solution.py:428
  197.6 17.0 %collective-permute-start.28 = (bf16[256,2048]{1,0:T(8,128)(2,1)}, bf16[256,2048]{1,0:T(8,128)(2,1)}, u32[]{:S(2)}, u32[]{:S(2)}) collective-permute-start(bf16[256,2048]{1,0:T(8,128)(2,1)} %add_convert_fusion), channel_id=1, source_target_pairs={{4,0},{2,6},{5,1},{3,7},{12,8},{10,14},{13,9},{11,15},{20,16},{18,... | collective-permute-start | bytes 3145736 | tf_op jit(solution)/shard_map/ppermute | solution.py:442
  221.1 8.8 %collective-permute-start.31 = (bf16[512,2048]{1,0:T(8,128)(2,1)}, bf16[512,2048]{1,0:T(8,128)(2,1)S(1)}, u32[]{:S(2)}, u32[]{:S(2)}) collective-permute-start(bf16[512,2048]{1,0:T(8,128)(2,1)} %get-tuple-element.65), channel_id=1, source_target_pairs={{6,4},{7,5},{14,12},{15,13},{22,20},{23,21},{30,28},{31,29}} | collective-permute-start | bytes 6291464 | tf_op jit(solution)/shard_map/ppermute | solution.py:458
  229.8 7.9 %collective-permute-start.32 = (bf16[256,512]{1,0:T(8,128)(2,1)S(1)}, bf16[256,512]{1,0:T(8,128)(2,1)S(1)}, u32[]{:S(2)}, u32[]{:S(2)}) collective-permute-start(bf16[256,512]{1,0:T(8,128)(2,1)S(1)} %get-tuple-element.78), channel_id=1, source_target_pairs={{0,4},{4,0},{1,5},{5,1},{2,6},{6,2},{3,7},{7,3},{8,12},{12,8},{9,1... | collective-permute-start | bytes 786440 | tf_op jit(solution)/shard_map/ppermute | solution.py:428
  233.1 4.5 %collective-permute-start.33 = (f32[2048]{0:T(1024)S(1)}, f32[2048]{0:T(1024)S(1)}, u32[]{:S(2)}, u32[]{:S(2)}) collective-permute-start(f32[2048]{0:T(1024)S(1)} %add.60), channel_id=1, source_target_pairs={{0,16},{8,24},{16,0},{24,8},{1,17},{9,25},{17,1},{25,9},{2,18},{10... | collective-permute-start | bytes 24584 | tf_op jit(solution)/shard_map/ppermute | solution.py:467
  (28 other events, 176.0 us)
Sparse Core Ops, SparseCore 0:
  26.1 46.2 all-gather.2
  73.9 44.6 all-gather.4
  120.9 45.5 reduce-scatter.2
  168.7 43.1 reduce-scatter.4

commit v11 on v10

--- a/solution.py
+++ b/solution.py
@@ -111,7 +111,7 @@
 
 
 def attend_kernel(at, part, enc_other, w_other, *refs):
-    qgs, (dec, gkv) = refs[:3], refs[3:]
+    qgs, (dec, gkv) = refs[:3], refs[-2:]
     kv = (part[...] + dot(enc_other[...], w_other[...])).astype(BF16)
     keys = lax.broadcasted_iota(jnp.int32, (1, kv.shape[0]), 1)
     bias = jnp.where(keys < at[4], 0.0, -1e30).astype(F32)
@@ -121,11 +121,12 @@
         dec[:, lanes], gkv[:, lanes] = attend_head(bias, qg, kv[:, lanes])
 
 
-def attend(at, part, enc_other, w_other, qgs, chunk):
+def attend(at, part, enc_other, w_other, qgs, chunk, dec_before):
     length = part.shape[0]
     half, cols = w_other.shape
     step = min(256, cols)
     first = chunk * (cols // step)
+    before = [] if dec_before is None else [dec_before]
     enc = pl.BlockSpec((length, half), lambda i, s: (0, 0))
     weight = pl.BlockSpec((half, step), lambda i, s: (0, i))
     out = pl.BlockSpec((length, step), lambda i, s: (0, i))
@@ -138,16 +139,17 @@
         grid_spec=pltpu.PrefetchScalarGridSpec(
             num_scalar_prefetch=1,
             grid=(cols // step,),
-            in_specs=[out, enc, weight, pick(0), pick(1), pick(2)],
-            out_specs=[out, out],
-        ),
-        out_shape=[jax.ShapeDtypeStruct((length, cols), BF16)] * 2,
+            in_specs=[out, enc, weight, pick(0), pick(1), pick(2)] + [pl.BlockSpec(memory_space=pl.ANY)] * len(before),
+            out_specs=[pl.BlockSpec((length, step), lambda i, s: (0, first + i)), out],
+        ),
+        out_shape=[pltpu.HBM(qgs[0].shape, BF16), jax.ShapeDtypeStruct((length, cols), BF16)],
+        input_output_aliases={7: 0} if before else {},
         compiler_params=params(26),
         cost_estimate=cost(
             length * cols * (4 * half + 14 * length), 8, length * length * cols // (2 * HEAD)
         ),
         name="attend",
-    )(at, part, *in_hbm(enc_other, w_other, *qgs))
+    )(at, part, *in_hbm(enc_other, w_other, *qgs), *before)
 
 
 def weight_grad_kernel(scale, at, enc_a, enc_b, gkv_a, gkv_b, out):
@@ -333,7 +335,7 @@
     is_grad = lax.broadcasted_iota(jnp.int32, (length, width), 1) % (2 * HEAD) >= HEAD
     masked = jnp.where(is_grad & (position >= tgt_len[0]), jnp.zeros((), BF16), packed)
     qg_near, qg_far = cut(masked, 1, y, half), cut(masked, 1, 1 - y, half)
-    qg_near, qg_far = lax.optimization_barrier((qg_near, qg_far, swapped[-1]))[:2]
+    qg_near, qg_far = lax.optimization_barrier((qg_near, qg_far, swapped[-1], key_count))[:2]
     qgs = [
         qg_near,
         lax.ppermute(qg_near, PLANE, [(1, 0)]),
@@ -375,7 +377,7 @@
         enc_own, enc_other = encoded[:, 0], encoded[:, 1]
     enc_mate = lax.ppermute(enc_other, "phase", SWAP)
 
-    decs, gkvs, weight_sums = [], [], []
+    dec, gkvs, weight_sums = None, [], []
     for k in range(CHUNKS):
         if k in DIRECT:
             pieces = [blocks[k]] + slots(after(blocks[k], w_own[0]))
@@ -391,24 +393,14 @@
             if k > 0:
                 w_own[k] = after(w_own[k], grad)
         w_other.append(lax.ppermute(w_own[k], "phase", SWAP))
-        dec, gkv = attend(at, dot(enc_own, w_own[k]), enc_other, w_other[k], qgs, k)
+        dec, gkv = attend(at, dot(enc_own, w_own[k]), enc_other, w_other[k], qgs, k, dec)
         gkvs.append(gkv)
-        decs.append(
-            (
-                lax.ppermute(dec, PLANE, [(0, 1)]),
-                dec,
-                lax.ppermute(dec, PLANE, [(2, 1), (1, 3)]),
-            )
-        )
         last = k == CHUNKS - 1
-        parts = jnp.split(gkv, 2, axis=1)
-        gkv_mate = jnp.concatenate([lax.ppermute(p, "phase", SWAP) for p in parts], 1)
+        gkv_mate = lax.ppermute(gkv, "phase", SWAP)
         if tiled:
             if last:
                 away = enc_grad(at, gkvs, w_own, w_other, groups, rows, 1)
                 gkv_mate = after(gkv_mate, *away)
-            else:
-                gkv_mate = after(gkv_mate, decs[k][0], decs[k][2])
             grad = weight_grad(at, enc_own, enc_mate, gkv, gkv_mate, groups, pair_scale)
             if last:
                 kept = [after(gkvs[0], grad)] + gkvs[1:]
@@ -426,6 +418,10 @@
         terms = [jnp.split(cut(full, 1, (x + s) % shards, width), PARTS) for s in range(shards)]
     kept = jnp.concatenate([w[:rows] for w in weight_sums], 1)
     got = [lax.ppermute(w[rows:], "y", SWAP) for w in weight_sums]
+    dec_here = jnp.where(y == 0, lax.ppermute(dec, PLANE, [(0, 1)]), dec)
+    dec_there = lax.ppermute(dec, PLANE, [(2, 1), (1, 3)])
+    dec_grads = ordered(y == 0, dec_here, dec_there, 1)
+
     far, first_far = [], None
     for part in range(PARTS):
         total = terms[0][part].astype(F32)
@@ -433,17 +429,13 @@
             term = across(terms[turn][part], turn, [(1, 1), (2, 2)])
             first_far = term if first_far is None else first_far
             total = total + term.astype(F32)
-        done = decs[-1][2] if part == 0 else got[0]
-        far.append(after(total.astype(BF16), done))
+        far.append(after(total.astype(BF16), dec_there, got[0]))
     moved = [
         [across(after(part, first_far), turn, [(0, 0), (3, 3)]) for part in terms[turn]]
         for turn in range(1, shards)
     ]
     moved.append([lax.ppermute(part, PLANE, [(2, 0), (1, 3)]) for part in far])
 
-    dec_here = jnp.concatenate([jnp.where(y == 0, d[0], d[1]) for d in decs], 1)
-    dec_there = jnp.concatenate([d[2] for d in decs], 1)
-    dec_grads = ordered(y == 0, dec_here, dec_there, 1)
     if tiled:
         moved[0][0], dec_grads = lax.optimization_barrier((moved[0][0], dec_grads))
         grad_normed, gain_term = collect(

time: 248 us -> 247 us (level)
  starting transfers between devices: 69.5 us -> 57.4 us
  waiting for transfers between devices: 59.5 us -> 68.4 us
    ppermute x2, starting transfers between devices: 8.95 us -> 0.01 us  [on_device(): w_other.append(lax.ppermute(w_own[k], 'phase', SWAP))]
    ppermute x2, waiting for transfers between devices: 10.5 us -> 17.7 us  [on_device(): moved.append([lax.ppermute(part, PLANE, [(2, 0), (1, 3)]) for part in far])]
    ppermute x1, starting transfers between devices: 2.37 us -> 8.63 us  [on_device(): enc_mate = lax.ppermute(enc_other, 'phase', SWAP)]
    ppermute x2, waiting for transfers between devices: 9.98 us -> 3.76 us  [on_device(): got = [lax.ppermute(w[rows:], 'y', SWAP) for w in weight_sums]]
    ppermute x1, waiting for transfers between devices: 4.39 us -> 0.01 us  [on_device(): lax.ppermute(after(chunk_of(1 - y, k), there, fars[0][1]), 'y', SWAP)]
    all_gather x2, waiting for transfers between devices: 3.27 us -> 7.57 us  [on_device(): w_own.append(lax.all_gather(block, 'z', axis=0, tiled=True))]
    ppermute x8 -> x4, starting transfers between devices: 13 us -> 9.15 us  [the longest x1 5 us: on_device(): dec_here = jnp.where(y == 0, lax.ppermute(dec, PLANE, [(0, 1)]), dec)]
    ppermute x2, waiting for transfers between devices: 4.31 us -> 7.48 us  [on_device(): lax.ppermute(gain_term, 'z', [(i, i ^ turn) for i in range(groups)])]
  transfers between devices with their start and end apart: 39 -> 35, of which waited for: 15 -> 15; matrix products, arithmetic and copies ran while one was open for 12% -> 14% of each run, Pallas kernels for 25% -> 25%
where the time goes in v11:
time: 247 us; the launch traced here: 246 us
  waiting for transfers between devices  68.4 us (28%)
  Pallas kernels  61.9 us (25%)
  starting transfers between devices  57.4 us (23%)
  other arithmetic  20.9 us (8%)
  between operations  16 us (6%)
  local copies, waits for them, and re-layouts  14.8 us (6%)
  matrix products  6.3 us (3%)
    pallas_call x2, Pallas kernels, attend(): pl.pallas_call(attend_kernel, grid_spec=pltpu.PrefetchScalarGridSpec(num_...  22.4 us
    ppermute x2, waiting for transfers between devices, on_device(): moved.append([lax.ppermute(part, PLANE, [(2, 0), (1, 3)]) for part in far])  17.7 us
    ppermute x7, starting transfers between devices, across(): lax.ppermute(value, ('y', 'phase', 'mp'), [(a * shards + s, b * shards +...  14.4 us
    ppermute x1, waiting for transfers between devices, on_device(): there = lax.ppermute(after(packed, blocks[0]), PLANE, [(0, 2), (2, 1)])  14.2 us
    pallas_call x2, Pallas kernels, enc_grad(): pl.pallas_call(enc_grad_kernel, grid_spec=pltpu.PrefetchScalarGridSpec(nu...  13.6 us
    pallas_call x2, Pallas kernels, weight_grad(): pl.pallas_call(lambda *refs: weight_grad_kernel(scale, *refs), grid_spec=...  12.6 us
    ppermute x1, starting transfers between devices, on_device(): enc_mate = lax.ppermute(enc_other, 'phase', SWAP)  8.63 us
    all_gather x2, waiting for transfers between devices, on_device(): w_own.append(lax.all_gather(block, 'z', axis=0, tiled=True))  7.57 us
  transfers between devices with their start and end apart: 35, of which 15 were waited for; matrix products, arithmetic and copies ran while one was open for 14% of the time, Pallas kernels for 25%

profile of v11, /device:TPU:0, one launch (start us, length us, event | category | flops | bytes accessed | tf_op | source)
XLA Modules:
  0.0 245.7 jit_solution(3452600061153994149)
XLA Ops:
  11.4 4.0 %collective-permute-start = (bf16[256,512]{1,0:T(8,128)(2,1)S(1)}, bf16[256,512]{1,0:T(8,128)(2,1)S(1)}, u32[]{:S(2)}, u32[]{:S(2)}) collective-permute-start(bf16[256,512]{1,0:T(8,128)(2,1)S(1)} %get-tuple-element.70), channel_id=1, source_target_pairs={{0,4},{4,0},{1,5},{5,1},{2,6},{6,2},{3,7},{7,3},{8,12},{12,8},{9,1... | collective-permute-start | bytes 786440 | tf_op jit(solution)/shard_map/ppermute | solution.py:311
  15.4 4.6 %collective-permute-done = bf16[256,512]{1,0:T(8,128)(2,1)S(1)} collective-permute-done((bf16[256,512]{1,0:T(8,128)(2,1)S(1)}, bf16[256,512]{1,0:T(8,128)(2,1)S(1)}, u32[]{:S(2)}, u32[]{:S(2)}) %collective-permute-start) | collective-permute-done | bytes 262176 | tf_op jit(solution)/shard_map/ppermute | solution.py:311
  20.9 5.0 %collective-permute-start.1 = (bf16[512,2048]{1,0:T(8,128)(2,1)S(1)}, bf16[512,2048]{1,0:T(8,128)(2,1)}, u32[]{:S(2)}, u32[]{:S(2)}) collective-permute-start(bf16[512,2048]{1,0:T(8,128)(2,1)S(1)} %bitcast.17), channel_id=1, source_target_pairs={{0,4},{4,2},{1,5},{5,3},{8,12},{12,10},{9,13},{13,11},{16,20},{20,... | collective-permute-start | bytes 6291464 | tf_op jit(solution)/shard_map/ppermute | solution.py:317
  30.5 3.4 %collective-permute-start.5 = (bf16[512,2048]{1,0:T(8,128)(2,1)S(1)}, bf16[512,2048]{1,0:T(8,128)(2,1)}, u32[]{:S(2)}, u32[]{:S(2)}) collective-permute-start(bf16[512,2048]{1,0:T(8,128)(2,1)S(1)} %bitcast.18), channel_id=1, source_target_pairs={{0,1},{1,0},{8,9},{9,8},{16,17},{17,16},{24,25},{25,24}} | collective-permute-start | bytes 6291464 | tf_op jit(solution)/shard_map/ppermute | solution.py:299
  33.8 14.2 %collective-permute-done.1.refs_3_ = bf16[512,2048]{1,0:T(8,128)(2,1)} collective-permute-done((bf16[512,2048]{1,0:T(8,128)(2,1)S(1)}, bf16[512,2048]{1,0:T(8,128)(2,1)}, u32[]{:S(2)}, u32[]{:S(2)}) %collective-permute-start.1) | collective-permute-done | bytes 2097184 | tf_op jit(solution)/shard_map/ppermute | solution.py:317
  51.3 4.0 %collective-permute-start.8 = (bf16[256,512]{1,0:T(8,128)(2,1)}, bf16[256,512]{1,0:T(8,128)(2,1)}, u32[]{:S(2)}, u32[]{:S(2)}) collective-permute-start(bf16[256,512]{1,0:T(8,128)(2,1)} %get-tuple-element.39), channel_id=1, source_target_pairs={{0,4},{4,0},{1,5},{5,1},{2,6},{6,2},{3,7},{7,3},{8,12},{12,8},{9,1... | collective-permute-start | bytes 786440 | tf_op jit(solution)/shard_map/ppermute | solution.py:330
  58.0 2.7 %constant_dynamic-slice_fusion.2 = (bf16[512,1024]{1,0:T(8,128)(2,1)}, bf16[512,1024]{1,0:T(8,128)(2,1)S(1)}) fusion(bf16[512,2048]{1,0:T(8,128)(2,1)} %fusion.1, s32[]{:T(128)S(6)} %select_n.107, s32[]{:T(128)S(6)} %select_n.106), kind=kLoop, calls=%fused_computation.25 | loop fusion | bytes 4194312 | tf_op jit(solution)/shard_map/dynamic_slice | solution.py:268
  60.8 3.8 %collective-permute-done.2 = s32[1]{0:T(128)} collective-permute-done((s32[1]{0:T(128)}, s32[1]{0:T(128)}, u32[]{:S(2)}, u32[]{:S(2)}) %collective-permute-start.2) | collective-permute-done | bytes 36 | tf_op jit(solution)/shard_map/ppermute | solution.py:318
  74.1 6.9 %norm.1 = (bf16[512,2048]{1,0:T(8,128)(2,1)}, bf16[512,2048]{1,0:T(8,128)(2,1)}, f32[512,128]{1,0:T(8,128)S(1)}) custom-call(s32[6]{0:T(128)S(1)} %concatenate.50.refs_0_.at, bf16[512,2048]{1,0:T(8,128)(2,1)S(1)} %bitcast.19, bf16[512,2048]{1,0:T(8,128)(2,1)} %collective-permute-done.3.refs_2_.refs_8_, bf16[512,2048]{1,0:T(8,128)(2,1)} %collective-permute-done.1.refs_3_, ...), custom_call_target="tpu_custom_call" | custom-call | flops 16777216 | bytes 8388608 | tf_op jit(solution)/shard_map/norm/pallas_call | solution.py:74
  81.0 8.6 %collective-permute-start.12 = (bf16[512,2048]{1,0:T(8,128)(2,1)}, bf16[512,2048]{1,0:T(8,128)(2,1)S(1)}, u32[]{:S(2)}, u32[]{:S(2)}) collective-permute-start(bf16[512,2048]{1,0:T(8,128)(2,1)} %get-tuple-element.44.enc_other), channel_id=1, source_target_pairs={{0,2},{2,0},{1,3},{3,1},{4,6},{6,4},{5,7},{7,5},{8,10},{10,8},{9,1... | collective-permute-start | bytes 6291464 | tf_op jit(solution)/shard_map/ppermute | solution.py:378
  89.6 2.8 %fusion.10.part = f32[512,512]{1,0:T(8,128)S(1)} fusion(bf16[512,2048]{1,0:T(8,128)(2,1)} %get-tuple-element.43.refs_1_, bf16[2048,512]{1,0:T(8,128)(2,1)S(1)} %copy-done.15), kind=kOutput, calls=%fused_computation.31 | convolution fusion | flops 1073741824 | bytes 5242880 | tf_op jit(solution)/shard_map/dot_general | solution.py:25
  92.5 11.0 %attend.2 = (bf16[512,1024]{1,0:T(8,128)(2,1)}, bf16[512,512]{1,0:T(8,128)(2,1)S(1)}) custom-call(s32[6]{0:T(128)S(1)} %concatenate.50.refs_0_.at, f32[512,512]{1,0:T(8,128)S(1)} %fusion.10.part, bf16[512,2048]{1,0:T(8,128)(2,1)} %get-tuple-element.44.enc_other, bf16[2048,512]{1,0:T(8,128)(2,1)} %collective-permute-done.11.w_other.other_0, ...), custom_call_target="tpu_custom_call" | custom-call | flops 4026531840 | bytes 8388608 | tf_op jit(solution)/shard_map/attend/pallas_call | solution.py:137
  106.8 6.3 %weight_grad.2 = bf16[2048,512]{1,0:T(8,128)(2,1)} custom-call(s32[6]{0:T(128)S(1)} %concatenate.50.refs_0_.at, bf16[512,2048]{1,0:T(8,128)(2,1)} %get-tuple-element.43.refs_1_, bf16[512,2048]{1,0:T(8,128)(2,1)} %copy-done.8, bf16[512,512]{1,0:T(8,128)(2,1)S(1)} %get-tuple-element.52.refs_3_.gkv_0, bf16[512,512]{1,0:T(8,128)(2,1)S(1)} %collective-permute-done.13.refs_4_), custom_call_target="tpu_custom_call" | custom-call | flops 33554432 | tf_op jit(solution)/shard_map/weight_grad/pallas_call | solution.py:166
  113.4 5.2 %all-gather.5.cloned.1.call-done.own_1 = bf16[2048,512]{1,0:T(8,128)(2,1)} async-done(((bf16[512,512]{1,0:T(8,128)(2,1)}), bf16[2048,512]{1,0:T(8,128)(2,1)}) %all-gather.5.cloned.1.call-update) | async-done | bytes 2097168 | tf_op jit(solution)/shard_map/all_gather | solution.py:392
  118.6 3.5 %fusion.11.part = f32[512,512]{1,0:T(8,128)S(1)} fusion(bf16[512,2048]{1,0:T(8,128)(2,1)} %get-tuple-element.43.refs_1_, bf16[2048,512]{1,0:T(8,128)(2,1)} %all-gather.5.cloned.1.call-done.own_1), kind=kOutput, calls=%fused_computation.32 | convolution fusion | flops 1073741824 | bytes 5242880 | tf_op jit(solution)/shard_map/dot_general | solution.py:25
  124.2 11.3 %attend.3 = (bf16[512,1024]{1,0:T(8,128)(2,1)}, bf16[512,512]{1,0:T(8,128)(2,1)S(1)}) custom-call(s32[6]{0:T(128)S(1)} %concatenate.50.refs_0_.at, f32[512,512]{1,0:T(8,128)S(1)} %fusion.11.part, bf16[512,2048]{1,0:T(8,128)(2,1)} %get-tuple-element.44.enc_other, bf16[2048,512]{1,0:T(8,128)(2,1)} %copy-done.16, ...), custom_call_target="tpu_custom_call", output_to_operand_aliasing={{0}: (7, {})} | custom-call | flops 4026531840 | bytes 8388608 | tf_op jit(solution)/shard_map/attend/pallas_call | solution.py:137
  136.4 7.0 %enc_grad.2 = (bf16[256,2048]{1,0:T(8,128)(2,1)}, bf16[256,2048]{1,0:T(8,128)(2,1)}) custom-call(s32[6]{0:T(128)S(1)} %concatenate.50.refs_0_.at, bf16[512,512]{1,0:T(8,128)(2,1)} %copy-done.5, bf16[512,512]{1,0:T(8,128)(2,1)} %copy-done.6, bf16[2048,512]{1,0:T(8,128)(2,1)} %all-gather.3.cloned.1.call-done.own_0, ...), custom_call_target="tpu_custom_call" | custom-call | flops 4294967296 | bytes 8388608 | tf_op jit(solution)/shard_map/enc_grad/pallas_call | solution.py:252
  148.2 5.0 %collective-permute-start.18 = (bf16[512,1024]{1,0:T(8,128)(2,1)}, bf16[512,1024]{1,0:T(8,128)(2,1)}, u32[]{:S(2)}, u32[]{:S(2)}) collective-permute-start(bf16[512,1024]{1,0:T(8,128)(2,1)} %get-tuple-element.56), channel_id=1, source_target_pairs={{0,2},{1,3},{8,10},{9,11},{16,18},{17,19},{24,26},{25,27}} | collective-permute-start | bytes 3145736 | tf_op jit(solution)/shard_map/ppermute | solution.py:421
  154.9 6.3 %weight_grad.3 = bf16[2048,512]{1,0:T(8,128)(2,1)} custom-call(s32[6]{0:T(128)S(1)} %concatenate.50.refs_0_.at, bf16[512,2048]{1,0:T(8,128)(2,1)} %get-tuple-element.43.refs_1_, bf16[512,2048]{1,0:T(8,128)(2,1)} %copy-done.8, bf16[512,512]{1,0:T(8,128)(2,1)S(1)} %copy-done.7, bf16[512,512]{1,0:T(8,128)(2,1)S(1)} %collective-permute-done.15.refs_4_), custom_call_target="tpu_custom_call" | custom-call | flops 33554432 | tf_op jit(solution)/shard_map/weight_grad/pallas_call | solution.py:166
  161.2 6.6 %enc_grad.3 = (bf16[256,2048]{1,0:T(8,128)(2,1)}, bf16[256,2048]{1,0:T(8,128)(2,1)}) custom-call(s32[6]{0:T(128)S(1)} %concatenate.50.refs_0_.at, bf16[512,512]{1,0:T(8,128)(2,1)} %copy-done.5, bf16[512,512]{1,0:T(8,128)(2,1)} %copy-done.6, bf16[2048,512]{1,0:T(8,128)(2,1)} %all-gather.3.cloned.1.call-done.own_0, ...), custom_call_target="tpu_custom_call" | custom-call | flops 4294967296 | bytes 8388608 | tf_op jit(solution)/shard_map/enc_grad/pallas_call | solution.py:252
  167.8 2.7 %collective-permute-start.17 = (bf16[256,2048]{1,0:T(8,128)(2,1)}, bf16[256,2048]{1,0:T(8,128)(2,1)}, u32[]{:S(2)}, u32[]{:S(2)}) collective-permute-start(bf16[256,2048]{1,0:T(8,128)(2,1)} %get-tuple-element.55), channel_id=1, source_target_pairs={{0,1},{1,0},{6,7},{7,6},{8,9},{9,8},{14,15},{15,14},{16,17},{17,16... | collective-permute-start | bytes 3145736 | tf_op jit(solution)/shard_map/ppermute | solution.py:299
  170.5 3.1 %collective-permute-start.20 = (bf16[256,2048]{1,0:T(8,128)(2,1)}, bf16[256,2048]{1,0:T(8,128)(2,1)}, u32[]{:S(2)}, u32[]{:S(2)}) collective-permute-start(bf16[256,2048]{1,0:T(8,128)(2,1)} %get-tuple-element.58), channel_id=1, source_target_pairs={{0,1},{1,0},{6,7},{7,6},{8,9},{9,8},{14,15},{15,14},{16,17},{17,16... | collective-permute-start | bytes 3145736 | tf_op jit(solution)/shard_map/ppermute | solution.py:299
  173.7 3.0 %add_convert_fusion.1 = bf16[256,2048]{1,0:T(8,128)(2,1)} fusion(bf16[256,2048]{1,0:T(8,128)(2,1)} %copy-done.10, bf16[256,2048]{1,0:T(8,128)(2,1)} %get-tuple-element.53.refs_1_), kind=kLoop, calls=%fused_computation.6 | loop fusion | flops 2097152 | bytes 3145728 | tf_op jit(solution)/shard_map/convert_element_type | solution.py:432
  181.1 3.8 %collective-permute-done.21 = bf16[256,512]{1,0:T(8,128)(2,1)S(1)} collective-permute-done((bf16[256,512]{1,0:T(8,128)(2,1)S(1)}, bf16[256,512]{1,0:T(8,128)(2,1)S(1)}, u32[]{:S(2)}, u32[]{:S(2)}) %collective-permute-start.21) | collective-permute-done | bytes 262176 | tf_op jit(solution)/shard_map/ppermute | solution.py:420
  189.6 3.7 %maximum_select_fusion = bf16[512,2048]{1,0:T(8,128)(2,1)} fusion(bf16[512,1024]{1,0:T(8,128)(2,1)} %collective-permute-done.19, bf16[512,1024]{1,0:T(8,128)(2,1)S(1)} %broadcast_select_fusion, pred[]{:T(512)S(6)} %eq.19), kind=kLoop, calls=%fused_computation.3 | loop fusion | flops 9437184 | bytes 4194305 | tf_op jit(solution)/shard_map/jit(_where)/select_n | solution.py:272
  193.3 2.8 %collective-permute-done.20.refs_4_ = bf16[256,2048]{1,0:T(8,128)(2,1)} collective-permute-done((bf16[256,2048]{1,0:T(8,128)(2,1)}, bf16[256,2048]{1,0:T(8,128)(2,1)}, u32[]{:S(2)}, u32[]{:S(2)}) %collective-permute-start.20) | collective-permute-done | bytes 1048608 | tf_op jit(solution)/shard_map/ppermute | solution.py:299
  196.1 6.5 %collective-permute-done.22.refs_5_ = bf16[256,2048]{1,0:T(8,128)(2,1)} collective-permute-done((bf16[256,2048]{1,0:T(8,128)(2,1)}, bf16[256,2048]{1,0:T(8,128)(2,1)}, u32[]{:S(2)}, u32[]{:S(2)}) %collective-permute-start.22) | collective-permute-done | bytes 1048608 | tf_op jit(solution)/shard_map/ppermute | solution.py:437
  202.6 11.2 %collective-permute-done.24.refs_6_ = bf16[256,2048]{1,0:T(8,128)(2,1)} collective-permute-done((bf16[256,2048]{1,0:T(8,128)(2,1)}, bf16[256,2048]{1,0:T(8,128)(2,1)}, u32[]{:S(2)}, u32[]{:S(2)}) %collective-permute-start.24) | collective-permute-done | bytes 1048608 | tf_op jit(solution)/shard_map/ppermute | solution.py:437
  213.8 6.5 %collect.1 = (bf16[512,2048]{1,0:T(8,128)(2,1)}, f32[4,1,2048]{2,1,0:T(1,128)S(1)}) custom-call(s32[6]{0:T(128)S(1)} %concatenate.50.refs_0_.at, bf16[256,2048]{1,0:T(8,128)(2,1)S(1)} %copy-done.1, bf16[256,2048]{1,0:T(8,128)(2,1)S(1)} %copy-done.2, bf16[256,2048]{1,0:T(8,128)(2,1)} %collective-permute-done.17.refs_3_, ...), custom_call_target="tpu_custom_call" | custom-call | flops 8388608 | bytes 12582912 | tf_op jit(solution)/shard_map/collect/pallas_call | solution.py:205
  224.3 3.6 %collective-permute-done.26 = f32[2048]{0:T(1024)S(1)} collective-permute-done((f32[2048]{0:T(1024)S(1)}, f32[2048]{0:T(1024)S(1)}, u32[]{:S(2)}, u32[]{:S(2)}) %collective-permute-start.26) | collective-permute-done | bytes 8224 | tf_op jit(solution)/shard_map/ppermute | solution.py:459
  229.1 3.2 %select_bitcast_fusion = bf16[1,1,512,2048]{3,2,1,0:T(8,128)(2,1)} fusion(bf16[512,2048]{1,0:T(8,128)(2,1)} %maximum_select_fusion, bf16[512,2048]{1,0:T(8,128)(2,1)} %get-tuple-element.63, bf16[512,2048]{1,0:T(8,128)(2,1)S(1)} %collective-permute-done.27, pred[]{:T(512)S(6)} %eq.20, pred[]{:T(512)S(6)} %eq.19), kind=kLoop, calls=%fused_computation.4 | loop fusion | flops 2097152 | bytes 8388610 | tf_op jit(solution)/shard_map/broadcast_in_dim | solution.py:451
  233.0 3.8 %collective-permute-done.29 = f32[2048]{0:T(1024)S(1)} collective-permute-done((f32[2048]{0:T(1024)S(1)}, f32[2048]{0:T(1024)S(1)}, u32[]{:S(2)}, u32[]{:S(2)}) %collective-permute-start.29) | collective-permute-done | bytes 8224 | tf_op jit(solution)/shard_map/ppermute | solution.py:459
  (113 shorter events, 53.3 us)
Async XLA Ops:
  7.2 65.1 %all-gather.3.cloned.1.call-start = ((), (), s32[]{:S(2)}) async-start(), calls=%async_computation.2 | async-start | bytes 2621440 | tf_op jit(solution)/shard_map/all_gather | solution.py:392
  7.2 18.7 %collective-permute-start.3 = (bf16[512,2048]{1,0:T(8,128)(2,1)}, bf16[512,2048]{1,0:T(8,128)(2,1)}, u32[]{:S(2)}, u32[]{:S(2)}) collective-permute-start(bf16[512,2048]{1,0:T(8,128)(2,1)} %bitcast.16), channel_id=1, source_target_pairs={{4,6},{5,7},{12,14},{13,15},{20,22},{21,23},{28,30},{29,31}} | collective-permute-start | bytes 6291464 | tf_op jit(solution)/shard_map/ppermute | solution.py:312
  11.4 8.7 %collective-permute-start = (bf16[256,512]{1,0:T(8,128)(2,1)S(1)}, bf16[256,512]{1,0:T(8,128)(2,1)S(1)}, u32[]{:S(2)}, u32[]{:S(2)}) collective-permute-start(bf16[256,512]{1,0:T(8,128)(2,1)S(1)} %get-tuple-element.70), channel_id=1, source_target_pairs={{0,4},{4,0},{1,5},{5,1},{2,6},{6,2},{3,7},{7,3},{8,12},{12,8},{9,1... | collective-permute-start | bytes 786440 | tf_op jit(solution)/shard_map/ppermute | solution.py:311
  20.9 27.2 %collective-permute-start.1 = (bf16[512,2048]{1,0:T(8,128)(2,1)S(1)}, bf16[512,2048]{1,0:T(8,128)(2,1)}, u32[]{:S(2)}, u32[]{:S(2)}) collective-permute-start(bf16[512,2048]{1,0:T(8,128)(2,1)S(1)} %bitcast.17), channel_id=1, source_target_pairs={{0,4},{4,2},{1,5},{5,3},{8,12},{12,10},{9,13},{13,11},{16,20},{20,... | collective-permute-start | bytes 6291464 | tf_op jit(solution)/shard_map/ppermute | solution.py:317
  25.9 92.6 %all-gather.5.cloned.1.call-start = ((), (), s32[]{:S(2)}) async-start(), calls=%async_computation.3 | async-start | bytes 2621440 | tf_op jit(solution)/shard_map/all_gather | solution.py:392
  26.0 24.1 %collective-permute-start.6 = (bf16[512,2048]{1,0:T(8,128)(2,1)}, bf16[512,2048]{1,0:T(8,128)(2,1)S(1)}, u32[]{:S(2)}, u32[]{:S(2)}) collective-permute-start(bf16[512,2048]{1,0:T(8,128)(2,1)} %collective-permute-done.3.refs_2_.refs_8_), channel_id=1, source_target_pairs={{6,7},{7,6},{14,15},{15,14},{22,23},{23,22},{30,31},{31,30}} | collective-permute-start | bytes 6291464 | tf_op jit(solution)/shard_map/ppermute | solution.py:299
  26.8 3.7 %collective-permute-start.4 = (bf16[2048]{0:T(1024)(128)(2,1)S(1)}, bf16[2048]{0:T(1024)(128)(2,1)S(1)}, u32[]{:S(2)}, u32[]{:S(2)}) collective-permute-start(bf16[2048]{0:T(1024)(128)(2,1)S(1)} %copy-done.14), channel_id=1, source_target_pairs={{0,1},{1,0},{2,3},{3,2},{4,5},{5,4},{6,7},{7,6},{8,9},{9,8},{10,11... | collective-permute-start | bytes 12296 | tf_op jit(solution)/shard_map/ppermute | solution.py:314
  30.5 42.0 %collective-permute-start.5 = (bf16[512,2048]{1,0:T(8,128)(2,1)S(1)}, bf16[512,2048]{1,0:T(8,128)(2,1)}, u32[]{:S(2)}, u32[]{:S(2)}) collective-permute-start(bf16[512,2048]{1,0:T(8,128)(2,1)S(1)} %bitcast.18), channel_id=1, source_target_pairs={{0,1},{1,0},{8,9},{9,8},{16,17},{17,16},{24,25},{25,24}} | collective-permute-start | bytes 6291464 | tf_op jit(solution)/shard_map/ppermute | solution.py:299
  48.1 24.4 %collective-permute-start.7 = (bf16[512,2048]{1,0:T(8,128)(2,1)}, bf16[512,2048]{1,0:T(8,128)(2,1)}, u32[]{:S(2)}, u32[]{:S(2)}) collective-permute-start(bf16[512,2048]{1,0:T(8,128)(2,1)} %collective-permute-done.1.refs_3_), channel_id=1, source_target_pairs={{2,3},{3,2},{4,5},{5,4},{10,11},{11,10},{12,13},{13,12},{18,19},{1... | collective-permute-start | bytes 6291464 | tf_op jit(solution)/shard_map/ppermute | solution.py:299
  51.3 13.8 %collective-permute-start.8 = (bf16[256,512]{1,0:T(8,128)(2,1)}, bf16[256,512]{1,0:T(8,128)(2,1)}, u32[]{:S(2)}, u32[]{:S(2)}) collective-permute-start(bf16[256,512]{1,0:T(8,128)(2,1)} %get-tuple-element.39), channel_id=1, source_target_pairs={{0,4},{4,0},{1,5},{5,1},{2,6},{6,2},{3,7},{7,3},{8,12},{12,8},{9,1... | collective-permute-start | bytes 786440 | tf_op jit(solution)/shard_map/ppermute | solution.py:330
  60.8 3.8 %collective-permute-start.2 = (s32[1]{0:T(128)}, s32[1]{0:T(128)}, u32[]{:S(2)}, u32[]{:S(2)}) collective-permute-start(s32[1]{0:T(128)} %param.8), channel_id=1, source_target_pairs={{0,4},{4,0},{1,5},{5,1},{2,6},{6,2},{3,7},{7,3},{8,12},{12,8},{9,1... | collective-permute-start | bytes 20 | tf_op jit(solution)/shard_map/ppermute | solution.py:318
  65.1 7.4 %collective-permute-start.10 = (bf16[512,1024]{1,0:T(8,128)(2,1)}, bf16[512,1024]{1,0:T(8,128)(2,1)}, u32[]{:S(2)}, u32[]{:S(2)}) collective-permute-start(bf16[512,1024]{1,0:T(8,128)(2,1)} %get-tuple-element.41), channel_id=1, source_target_pairs={{2,4},{6,2},{3,5},{7,3},{10,12},{14,10},{11,13},{15,11},{18,20},{2... | collective-permute-start | bytes 3145736 | tf_op jit(solution)/shard_map/ppermute | solution.py:342
  66.8 5.7 %collective-permute-start.9 = (bf16[512,1024]{1,0:T(8,128)(2,1)S(1)}, bf16[512,1024]{1,0:T(8,128)(2,1)}, u32[]{:S(2)}, u32[]{:S(2)}) collective-permute-start(bf16[512,1024]{1,0:T(8,128)(2,1)S(1)} %get-tuple-element.40.refs_0_), channel_id=1, source_target_pairs={{2,0},{3,1},{10,8},{11,9},{18,16},{19,17},{26,24},{27,25}} | collective-permute-start | bytes 3145736 | tf_op jit(solution)/shard_map/ppermute | solution.py:341
  69.9 106.8 %reduce-scatter.3.cloned.1.call-start = ((), (), s32[]{:S(2)}) async-start(), calls=%async_computation.4 | async-start | bytes 2621440 | tf_op jit(solution)/shard_map/reduce_scatter | solution.py:411
  72.3 20.2 %collective-permute-start.11 = (bf16[2048,512]{1,0:T(8,128)(2,1)}, bf16[2048,512]{1,0:T(8,128)(2,1)}, u32[]{:S(2)}, u32[]{:S(2)}) collective-permute-start(bf16[2048,512]{1,0:T(8,128)(2,1)} %all-gather.3.cloned.1.call-done.own_0), channel_id=1, source_target_pairs={{0,2},{2,0},{1,3},{3,1},{4,6},{6,4},{5,7},{7,5},{8,10},{10,8},{9,1... | collective-permute-start | bytes 6291464 | tf_op jit(solution)/shard_map/ppermute | solution.py:395
  81.0 24.4 %collective-permute-start.12 = (bf16[512,2048]{1,0:T(8,128)(2,1)}, bf16[512,2048]{1,0:T(8,128)(2,1)S(1)}, u32[]{:S(2)}, u32[]{:S(2)}) collective-permute-start(bf16[512,2048]{1,0:T(8,128)(2,1)} %get-tuple-element.44.enc_other), channel_id=1, source_target_pairs={{0,2},{2,0},{1,3},{3,1},{4,6},{6,4},{5,7},{7,5},{8,10},{10,8},{9,1... | collective-permute-start | bytes 6291464 | tf_op jit(solution)/shard_map/ppermute | solution.py:378
  113.1 114.8 %reduce-scatter.5.cloned.1.call-start = ((), (), s32[]{:S(2)}) async-start(), calls=%async_computation.5 | async-start | bytes 2621440 | tf_op jit(solution)/shard_map/reduce_scatter | solution.py:411
  118.5 4.4 %collective-permute-start.14 = (bf16[2048,512]{1,0:T(8,128)(2,1)}, bf16[2048,512]{1,0:T(8,128)(2,1)S(1)}, u32[]{:S(2)}, u32[]{:S(2)}) collective-permute-start(bf16[2048,512]{1,0:T(8,128)(2,1)} %all-gather.5.cloned.1.call-done.own_1), channel_id=1, source_target_pairs={{0,2},{2,0},{1,3},{3,1},{4,6},{6,4},{5,7},{7,5},{8,10},{10,8},{9,1... | collective-permute-start | bytes 6291464 | tf_op jit(solution)/shard_map/ppermute | solution.py:395
  143.4 24.4 %collective-permute-start.16 = (bf16[256,2048]{1,0:T(8,128)(2,1)}, bf16[256,2048]{1,0:T(8,128)(2,1)S(1)}, u32[]{:S(2)}, u32[]{:S(2)}) collective-permute-start(bf16[256,2048]{1,0:T(8,128)(2,1)} %get-tuple-element.55), channel_id=1, source_target_pairs={{2,3},{3,2},{4,5},{5,4},{10,11},{11,10},{12,13},{13,12},{18,19},{1... | collective-permute-start | bytes 3145736 | tf_op jit(solution)/shard_map/ppermute | solution.py:299
  144.1 10.8 %collective-permute-start.15 = (bf16[512,512]{1,0:T(8,128)(2,1)S(1)}, bf16[512,512]{1,0:T(8,128)(2,1)S(1)}, u32[]{:S(2)}, u32[]{:S(2)}) collective-permute-start(bf16[512,512]{1,0:T(8,128)(2,1)S(1)} %copy-done.7), channel_id=1, source_target_pairs={{0,2},{2,0},{1,3},{3,1},{4,6},{6,4},{5,7},{7,5},{8,10},{10,8},{9,1... | collective-permute-start | bytes 1572872 | tf_op jit(solution)/shard_map/ppermute | solution.py:399
  146.6 34.5 %collective-permute-start.19 = (bf16[512,1024]{1,0:T(8,128)(2,1)}, bf16[512,1024]{1,0:T(8,128)(2,1)}, u32[]{:S(2)}, u32[]{:S(2)}) collective-permute-start(bf16[512,1024]{1,0:T(8,128)(2,1)} %get-tuple-element.56), channel_id=1, source_target_pairs={{4,2},{2,6},{5,3},{3,7},{12,10},{10,14},{13,11},{11,15},{20,18},{1... | collective-permute-start | bytes 3145736 | tf_op jit(solution)/shard_map/ppermute | solution.py:422
  148.2 40.0 %collective-permute-start.18 = (bf16[512,1024]{1,0:T(8,128)(2,1)}, bf16[512,1024]{1,0:T(8,128)(2,1)}, u32[]{:S(2)}, u32[]{:S(2)}) collective-permute-start(bf16[512,1024]{1,0:T(8,128)(2,1)} %get-tuple-element.56), channel_id=1, source_target_pairs={{0,2},{1,3},{8,10},{9,11},{16,18},{17,19},{24,26},{25,27}} | collective-permute-start | bytes 3145736 | tf_op jit(solution)/shard_map/ppermute | solution.py:421
  153.2 25.3 %collective-permute-start.23 = (bf16[256,2048]{1,0:T(8,128)(2,1)}, bf16[256,2048]{1,0:T(8,128)(2,1)}, u32[]{:S(2)}, u32[]{:S(2)}) collective-permute-start(bf16[256,2048]{1,0:T(8,128)(2,1)} %get-tuple-element.58), channel_id=1, source_target_pairs={{2,3},{3,2},{4,5},{5,4},{10,11},{11,10},{12,13},{13,12},{18,19},{1... | collective-permute-start | bytes 3145736 | tf_op jit(solution)/shard_map/ppermute | solution.py:299
  167.8 25.5 %collective-permute-start.17 = (bf16[256,2048]{1,0:T(8,128)(2,1)}, bf16[256,2048]{1,0:T(8,128)(2,1)}, u32[]{:S(2)}, u32[]{:S(2)}) collective-permute-start(bf16[256,2048]{1,0:T(8,128)(2,1)} %get-tuple-element.55), channel_id=1, source_target_pairs={{0,1},{1,0},{6,7},{7,6},{8,9},{9,8},{14,15},{15,14},{16,17},{17,16... | collective-permute-start | bytes 3145736 | tf_op jit(solution)/shard_map/ppermute | solution.py:299
  170.5 25.5 %collective-permute-start.20 = (bf16[256,2048]{1,0:T(8,128)(2,1)}, bf16[256,2048]{1,0:T(8,128)(2,1)}, u32[]{:S(2)}, u32[]{:S(2)}) collective-permute-start(bf16[256,2048]{1,0:T(8,128)(2,1)} %get-tuple-element.58), channel_id=1, source_target_pairs={{0,1},{1,0},{6,7},{7,6},{8,9},{9,8},{14,15},{15,14},{16,17},{17,16... | collective-permute-start | bytes 3145736 | tf_op jit(solution)/shard_map/ppermute | solution.py:299
  178.5 6.4 %collective-permute-start.21 = (bf16[256,512]{1,0:T(8,128)(2,1)S(1)}, bf16[256,512]{1,0:T(8,128)(2,1)S(1)}, u32[]{:S(2)}, u32[]{:S(2)}) collective-permute-start(bf16[256,512]{1,0:T(8,128)(2,1)S(1)} %get-tuple-element.74), channel_id=1, source_target_pairs={{0,4},{4,0},{1,5},{5,1},{2,6},{6,2},{3,7},{7,3},{8,12},{12,8},{9,1... | collective-permute-start | bytes 786440 | tf_op jit(solution)/shard_map/ppermute | solution.py:420
  185.6 17.0 %collective-permute-start.22 = (bf16[256,2048]{1,0:T(8,128)(2,1)}, bf16[256,2048]{1,0:T(8,128)(2,1)}, u32[]{:S(2)}, u32[]{:S(2)}) collective-permute-start(bf16[256,2048]{1,0:T(8,128)(2,1)} %add_convert_fusion.1), channel_id=1, source_target_pairs={{4,0},{2,6},{5,1},{3,7},{12,8},{10,14},{13,9},{11,15},{20,16},{18,... | collective-permute-start | bytes 3145736 | tf_op jit(solution)/shard_map/ppermute | solution.py:437
  186.8 26.9 %collective-permute-start.24 = (bf16[256,2048]{1,0:T(8,128)(2,1)}, bf16[256,2048]{1,0:T(8,128)(2,1)}, u32[]{:S(2)}, u32[]{:S(2)}) collective-permute-start(bf16[256,2048]{1,0:T(8,128)(2,1)} %add_convert_fusion), channel_id=1, source_target_pairs={{4,0},{2,6},{5,1},{3,7},{12,8},{10,14},{13,9},{11,15},{20,16},{18,... | collective-permute-start | bytes 3145736 | tf_op jit(solution)/shard_map/ppermute | solution.py:437
  220.3 8.8 %collective-permute-start.27 = (bf16[512,2048]{1,0:T(8,128)(2,1)}, bf16[512,2048]{1,0:T(8,128)(2,1)S(1)}, u32[]{:S(2)}, u32[]{:S(2)}) collective-permute-start(bf16[512,2048]{1,0:T(8,128)(2,1)} %get-tuple-element.63), channel_id=1, source_target_pairs={{6,4},{7,5},{14,12},{15,13},{22,20},{23,21},{30,28},{31,29}} | collective-permute-start | bytes 6291464 | tf_op jit(solution)/shard_map/ppermute | solution.py:450
  224.3 3.7 %collective-permute-start.26 = (f32[2048]{0:T(1024)S(1)}, f32[2048]{0:T(1024)S(1)}, u32[]{:S(2)}, u32[]{:S(2)}) collective-permute-start(f32[2048]{0:T(1024)S(1)} %fusion.16), channel_id=1, source_target_pairs={{0,8},{8,0},{16,24},{24,16},{1,9},{9,1},{17,25},{25,17},{2,10},{10... | collective-permute-start | bytes 24584 | tf_op jit(solution)/shard_map/ppermute | solution.py:459
  229.0 7.9 %collective-permute-start.28 = (bf16[256,512]{1,0:T(8,128)(2,1)S(1)}, bf16[256,512]{1,0:T(8,128)(2,1)S(1)}, u32[]{:S(2)}, u32[]{:S(2)}) collective-permute-start(bf16[256,512]{1,0:T(8,128)(2,1)S(1)} %get-tuple-element.76), channel_id=1, source_target_pairs={{0,4},{4,0},{1,5},{5,1},{2,6},{6,2},{3,7},{7,3},{8,12},{12,8},{9,1... | collective-permute-start | bytes 786440 | tf_op jit(solution)/shard_map/ppermute | solution.py:420
  232.3 4.5 %collective-permute-start.29 = (f32[2048]{0:T(1024)S(1)}, f32[2048]{0:T(1024)S(1)}, u32[]{:S(2)}, u32[]{:S(2)}) collective-permute-start(f32[2048]{0:T(1024)S(1)} %add.60), channel_id=1, source_target_pairs={{0,16},{8,24},{16,0},{24,8},{1,17},{9,25},{17,1},{25,9},{2,18},{10... | collective-permute-start | bytes 24584 | tf_op jit(solution)/shard_map/ppermute | solution.py:459
  (20 other events, 150.9 us)
Sparse Core Ops, SparseCore 0:
  26.0 46.2 all-gather.2
  73.9 44.6 all-gather.4
  120.8 42.5 reduce-scatter.2
  165.7 43.1 reduce-scatter.4

commit v12 on v11

--- a/solution.py
+++ b/solution.py
@@ -178,39 +178,32 @@
     )(at, *in_hbm(enc_a, enc_b), gkv_a, gkv_b)
 
 
-def collect_kernel(scale, at, *refs):
-    terms, (local, here, inv, gain, out, gain_term) = refs[: 3 * PARTS], refs[3 * PARTS :]
-    late = pl.program_id(0) >= pl.num_programs(0) // PARTS
-    total = jnp.zeros(local.shape, F32)
-    for i in range(0, 3 * PARTS, PARTS):
-        total = total + jnp.where(late, terms[i + 1][...], terms[i][...]).astype(F32)
+def collect_kernel(scale, at, own, near, far, local, here, inv, gain, out, gain_term):
+    total = own[...].astype(F32) + near[...].astype(F32) + far[...].astype(F32)
     out[...] = (total * gain[...]).astype(BF16)
     raw = jnp.where(at[0] == 0, local[...], here[...]).astype(F32)
     product = total * (raw * inv[:, :1])
     gain_term[0] = scale * jnp.sum(product, axis=0, keepdims=True)
 
 
-def collect(at, terms, local, here, inv_rms, gain, scale):
-    length, width = local.shape
+def collect(at, terms, part, local, here, inv_rms, gain, scale):
+    length, width = terms[0].shape
     step = 128
-    each = length // step // PARTS
+    first = part * (length // step)
     block = pl.BlockSpec((step, width), lambda i, s: (i, 0))
 
     def pick(want):
-        return pl.BlockSpec((step, width), lambda i, s: (jnp.where(s[0] == want, i, 0), 0))
-
-    def piece(part):
-        return pl.BlockSpec((step, width), lambda i, s: (jnp.clip(i - part * each, 0, each - 1), 0))
+        return pl.BlockSpec((step, width), lambda i, s: (jnp.where(s[0] == want, first + i, 0), 0))
 
     return pl.pallas_call(
         lambda *refs: collect_kernel(scale, *refs),
         grid_spec=pltpu.PrefetchScalarGridSpec(
             num_scalar_prefetch=1,
             grid=(length // step,),
-            in_specs=[piece(0), piece(1)] * 3
+            in_specs=[block] * 3
             + [pick(0), pick(1)]
             + [
-                pl.BlockSpec((step, 128), lambda i, s: (i, 0)),
+                pl.BlockSpec((step, 128), lambda i, s: (first + i, 0)),
                 pl.BlockSpec((1, width), lambda i, s: (0, 0)),
             ],
             out_specs=[block, pl.BlockSpec((1, 1, width), lambda i, s: (i, 0, 0))],
@@ -219,10 +212,45 @@
             jax.ShapeDtypeStruct((length, width), BF16),
             jax.ShapeDtypeStruct((length // step, 1, width), F32),
         ],
-        cost_estimate=cost(8 * length * width, 12),
-        compiler_params=params(20),
+        cost_estimate=cost(8 * length * width, 6),
+        compiler_params=params(16),
         name="collect",
-    )(at, *[p for term in terms for p in term], local, here, inv_rms, gain)
+    )(at, *terms, local, here, inv_rms, gain)
+
+
+def assemble_kernel(at, *refs):
+    sums, moved, (dec, out) = refs[:PARTS], refs[PARTS:-2], refs[-2:]
+    late = pl.program_id(0) >= pl.num_programs(0) // PARTS
+    enc = [jnp.where(late, r[1][...], r[0][...]) for r in (sums, moved)]
+    out[...] = jnp.where(at[3] == 1, dec[...], jnp.where(at[2] == 1, enc[1], enc[0]))
+
+
+def assemble(at, sums, moved, dec):
+    length, width = dec.shape
+    step = 128
+    each = length // step // PARTS
+
+    def piece(part, row):
+        def block(i, s):
+            wanted = (s[3] == 0) & (s[2] == row)
+            return (jnp.where(wanted, jnp.clip(i - part * each, 0, each - 1), 0), 0)
+
+        return pl.BlockSpec((step, width), block)
+
+    return pl.pallas_call(
+        assemble_kernel,
+        grid_spec=pltpu.PrefetchScalarGridSpec(
+            num_scalar_prefetch=1,
+            grid=(length // step,),
+            in_specs=[piece(p, row) for row in range(2) for p in range(PARTS)]
+            + [pl.BlockSpec((step, width), lambda i, s: (jnp.where(s[3] == 1, i, 0), 0))],
+            out_specs=pl.BlockSpec((step, width), lambda i, s: (i, 0)),
+        ),
+        out_shape=jax.ShapeDtypeStruct((length, width), BF16),
+        cost_estimate=cost(length * width, 4),
+        compiler_params=params(14),
+        name="assemble",
+    )(at, *sums, *moved, dec)
 
 
 def enc_grad_kernel(at, gkv_0, gkv_1, own_0, own_1, other_0, other_1, *outs):
@@ -429,7 +457,7 @@
             term = across(terms[turn][part], turn, [(1, 1), (2, 2)])
             first_far = term if first_far is None else first_far
             total = total + term.astype(F32)
-        far.append(after(total.astype(BF16), dec_there, got[0]))
+        far.append(after(total.astype(BF16), dec_there))
     moved = [
         [across(after(part, first_far), turn, [(0, 0), (3, 3)]) for part in terms[turn]]
         for turn in range(1, shards)
@@ -437,18 +465,29 @@
     moved.append([lax.ppermute(part, PLANE, [(2, 0), (1, 3)]) for part in far])
 
     if tiled:
-        moved[0][0], dec_grads = lax.optimization_barrier((moved[0][0], dec_grads))
-        grad_normed, gain_term = collect(
-            at, [terms[0]] + moved, packed, here, inv_rms, gain.astype(F32)[None], pair_scale
-        )
-        gain_term = jnp.sum(gain_term, axis=(0, 1))
+        grad_normed, gain_term = [], 0.0
+        for part in range(PARTS):
+            pieces = [t[part] for t in [terms[0]] + moved]
+            if part > 0:
+                pieces[1], grad_normed[-1], dec_grads, got[0] = lax.optimization_barrier(
+                    (pieces[1], grad_normed[-1], dec_grads, got[0])
+                )
+            summed, term = collect(
+                at, pieces, part, packed, here, inv_rms, gain.astype(F32)[None], pair_scale
+            )
+            grad_normed.append(summed)
+            gain_term = gain_term + jnp.sum(term, axis=(0, 1))
     else:
         grad_enc = sum(jnp.concatenate(t, 0).astype(F32) for t in [terms[0]] + moved)
-        grad_normed = (grad_enc * gain.astype(F32)).astype(BF16)
+        grad_normed = jnp.split((grad_enc * gain.astype(F32)).astype(BF16), PARTS)
         normed = chosen(enc_kind, *nears).astype(F32) * inv_rms
         gain_term = pair_scale * jnp.sum(grad_enc * normed, axis=0)
-    enc_grads = jnp.where(y == 0, grad_normed, lax.ppermute(grad_normed, PLANE, [(3, 2)]))
-    sec_grads = jnp.where(core == 0, enc_grads, dec_grads)[None, None]
+    sent = [lax.ppermute(g, PLANE, [(3, 2)]) for g in grad_normed]
+    if tiled:
+        sec_grads = assemble(at, grad_normed, sent, dec_grads)[None, None]
+    else:
+        enc_grads = jnp.where(y == 0, jnp.concatenate(grad_normed, 0), jnp.concatenate(sent, 0))
+        sec_grads = jnp.where(core == 0, enc_grads, dec_grads)[None, None]
 
     gain_term = jnp.where(straight, gain_term, 0.0)
     gain_term = gain_term + lax.ppermute(gain_term, PLANE, [(0, 3), (3, 0), (1, 2), (2, 1)])

time: 247 us -> 247 us (level)
  waiting for transfers between devices: 68.4 us -> 53.7 us
  starting transfers between devices: 57.4 us -> 67.5 us
  Pallas kernels: 61.9 us -> 67.9 us
  other arithmetic: 20.9 us -> 18.1 us
    ppermute x2, waiting for transfers between devices: 17.7 us -> 0.01 us  [on_device(): moved.append([lax.ppermute(part, PLANE, [(2, 0), (1, 3)]) for part in far])]
    ppermute x2, starting transfers between devices: 0.11 us -> 9.13 us  [on_device(): got = [lax.ppermute(w[rows:], 'y', SWAP) for w in weight_sums]]
    pallas_call x0 -> x1, Pallas kernels: none -> 4.83 us  [assemble(): pl.pallas_call(assemble_kernel, grid_spec=pltpu.PrefetchScalarGridSpec(nu...]
    ppermute x1, waiting for transfers between devices: 2.17 us -> 6.2 us  [on_device(): lax.ppermute(gain_term, PLANE, [(0, 3), (3, 0), (1, 2), (2, 1)])]
    broadcast_in_dim x1 -> x0, other arithmetic: 3.22 us -> none  [on_device(): sec_grads = jnp.where(core == 0, enc_grads, dec_grads)[None, None]]
    ppermute x7, waiting for transfers between devices: 2.78 us -> 0.02 us  [across(): lax.ppermute(value, ('y', 'phase', 'mp'), [(a * shards + s, b * shards +...]
    pallas_call x1 -> x2, Pallas kernels: 6.46 us -> 7.93 us  [collect(): pl.pallas_call(lambda *refs: collect_kernel(scale, *refs), grid_spec=pltp...]
  transfers between devices with their start and end apart: 35 -> 36, of which waited for: 15 -> 13; matrix products, arithmetic and copies ran while one was open for 14% -> 12% of each run, Pallas kernels for 25% -> 28%
where the time goes in v12:
time: 247 us; the launch traced here: 246 us
  Pallas kernels  67.9 us (27%)
  starting transfers between devices  67.5 us (27%)
  waiting for transfers between devices  53.7 us (22%)
  other arithmetic  18.1 us (7%)
  local copies, waits for them, and re-layouts  16.5 us (7%)
  between operations  16 us (6%)
  matrix products  6.3 us (3%)
    pallas_call x2, Pallas kernels, attend(): pl.pallas_call(attend_kernel, grid_spec=pltpu.PrefetchScalarGridSpec(num_...  22.3 us
    ppermute x7, starting transfers between devices, across(): lax.ppermute(value, ('y', 'phase', 'mp'), [(a * shards + s, b * shards +...  15.3 us
    ppermute x1, waiting for transfers between devices, on_device(): there = lax.ppermute(after(packed, blocks[0]), PLANE, [(0, 2), (2, 1)])  14.2 us
    pallas_call x2, Pallas kernels, enc_grad(): pl.pallas_call(enc_grad_kernel, grid_spec=pltpu.PrefetchScalarGridSpec(nu...  13.3 us
    pallas_call x2, Pallas kernels, weight_grad(): pl.pallas_call(lambda *refs: weight_grad_kernel(scale, *refs), grid_spec=...  12.6 us
    ppermute x2, starting transfers between devices, on_device(): got = [lax.ppermute(w[rows:], 'y', SWAP) for w in weight_sums]  9.13 us
    unnamed x34, local copies, waits for them, and re-layouts  8.86 us
    ppermute x1, starting transfers between devices, on_device(): enc_mate = lax.ppermute(enc_other, 'phase', SWAP)  8.63 us
  transfers between devices with their start and end apart: 36, of which 13 were waited for; matrix products, arithmetic and copies ran while one was open for 12% of the time, Pallas kernels for 28%

profile of v12, /device:TPU:0, one launch (start us, length us, event | category | flops | bytes accessed | tf_op | source)
XLA Modules:
  0.0 246.0 jit_solution(5817412581944041824)
XLA Ops:
  11.4 4.0 %collective-permute-start = (bf16[256,512]{1,0:T(8,128)(2,1)S(1)}, bf16[256,512]{1,0:T(8,128)(2,1)S(1)}, u32[]{:S(2)}, u32[]{:S(2)}) collective-permute-start(bf16[256,512]{1,0:T(8,128)(2,1)S(1)} %get-tuple-element.78), channel_id=1, source_target_pairs={{0,4},{4,0},{1,5},{5,1},{2,6},{6,2},{3,7},{7,3},{8,12},{12,8},{9,1... | collective-permute-start | bytes 786440 | tf_op jit(solution)/shard_map/ppermute | solution.py:339
  15.4 4.6 %collective-permute-done = bf16[256,512]{1,0:T(8,128)(2,1)S(1)} collective-permute-done((bf16[256,512]{1,0:T(8,128)(2,1)S(1)}, bf16[256,512]{1,0:T(8,128)(2,1)S(1)}, u32[]{:S(2)}, u32[]{:S(2)}) %collective-permute-start) | collective-permute-done | bytes 262176 | tf_op jit(solution)/shard_map/ppermute | solution.py:339
  20.9 5.0 %collective-permute-start.1 = (bf16[512,2048]{1,0:T(8,128)(2,1)S(1)}, bf16[512,2048]{1,0:T(8,128)(2,1)}, u32[]{:S(2)}, u32[]{:S(2)}) collective-permute-start(bf16[512,2048]{1,0:T(8,128)(2,1)S(1)} %bitcast.16), channel_id=1, source_target_pairs={{0,4},{4,2},{1,5},{5,3},{8,12},{12,10},{9,13},{13,11},{16,20},{20,... | collective-permute-start | bytes 6291464 | tf_op jit(solution)/shard_map/ppermute | solution.py:345
  30.5 3.4 %collective-permute-start.5 = (bf16[512,2048]{1,0:T(8,128)(2,1)S(1)}, bf16[512,2048]{1,0:T(8,128)(2,1)}, u32[]{:S(2)}, u32[]{:S(2)}) collective-permute-start(bf16[512,2048]{1,0:T(8,128)(2,1)S(1)} %bitcast.17), channel_id=1, source_target_pairs={{0,1},{1,0},{8,9},{9,8},{16,17},{17,16},{24,25},{25,24}} | collective-permute-start | bytes 6291464 | tf_op jit(solution)/shard_map/ppermute | solution.py:327
  33.9 14.2 %collective-permute-done.1.refs_3_ = bf16[512,2048]{1,0:T(8,128)(2,1)} collective-permute-done((bf16[512,2048]{1,0:T(8,128)(2,1)S(1)}, bf16[512,2048]{1,0:T(8,128)(2,1)}, u32[]{:S(2)}, u32[]{:S(2)}) %collective-permute-start.1) | collective-permute-done | bytes 2097184 | tf_op jit(solution)/shard_map/ppermute | solution.py:345
  51.3 4.1 %collective-permute-start.8 = (bf16[256,512]{1,0:T(8,128)(2,1)}, bf16[256,512]{1,0:T(8,128)(2,1)}, u32[]{:S(2)}, u32[]{:S(2)}) collective-permute-start(bf16[256,512]{1,0:T(8,128)(2,1)} %get-tuple-element.43), channel_id=1, source_target_pairs={{0,4},{4,0},{1,5},{5,1},{2,6},{6,2},{3,7},{7,3},{8,12},{12,8},{9,1... | collective-permute-start | bytes 786440 | tf_op jit(solution)/shard_map/ppermute | solution.py:358
  58.0 2.7 %constant_dynamic-slice_fusion.2 = (bf16[512,1024]{1,0:T(8,128)(2,1)}, bf16[512,1024]{1,0:T(8,128)(2,1)S(1)}) fusion(bf16[512,2048]{1,0:T(8,128)(2,1)} %fusion.1, s32[]{:T(128)S(6)} %select_n.97, s32[]{:T(128)S(6)} %select_n.96), kind=kLoop, calls=%fused_computation.24 | loop fusion | bytes 4194312 | tf_op jit(solution)/shard_map/dynamic_slice | solution.py:296
  60.8 3.8 %collective-permute-done.2 = s32[1]{0:T(128)} collective-permute-done((s32[1]{0:T(128)}, s32[1]{0:T(128)}, u32[]{:S(2)}, u32[]{:S(2)}) %collective-permute-start.2) | collective-permute-done | bytes 36 | tf_op jit(solution)/shard_map/ppermute | solution.py:346
  74.1 6.9 %norm.1 = (bf16[512,2048]{1,0:T(8,128)(2,1)}, bf16[512,2048]{1,0:T(8,128)(2,1)}, f32[512,128]{1,0:T(8,128)S(1)}) custom-call(s32[6]{0:T(128)S(1)} %concatenate.50.refs_0_.at, bf16[512,2048]{1,0:T(8,128)(2,1)S(1)} %bitcast.18, bf16[512,2048]{1,0:T(8,128)(2,1)} %collective-permute-done.3.refs_2_.refs_5_, bf16[512,2048]{1,0:T(8,128)(2,1)} %collective-permute-done.1.refs_3_, ...), custom_call_target="tpu_custom_call" | custom-call | flops 16777216 | bytes 8388608 | tf_op jit(solution)/shard_map/norm/pallas_call | solution.py:74
  81.0 8.6 %collective-permute-start.12 = (bf16[512,2048]{1,0:T(8,128)(2,1)}, bf16[512,2048]{1,0:T(8,128)(2,1)S(1)}, u32[]{:S(2)}, u32[]{:S(2)}) collective-permute-start(bf16[512,2048]{1,0:T(8,128)(2,1)} %get-tuple-element.48.enc_other), channel_id=1, source_target_pairs={{0,2},{2,0},{1,3},{3,1},{4,6},{6,4},{5,7},{7,5},{8,10},{10,8},{9,1... | collective-permute-start | bytes 6291464 | tf_op jit(solution)/shard_map/ppermute | solution.py:406
  89.6 2.8 %fusion.10.part = f32[512,512]{1,0:T(8,128)S(1)} fusion(bf16[512,2048]{1,0:T(8,128)(2,1)} %get-tuple-element.47.refs_1_, bf16[2048,512]{1,0:T(8,128)(2,1)S(1)} %copy-done.15), kind=kOutput, calls=%fused_computation.30 | convolution fusion | flops 1073741824 | bytes 5242880 | tf_op jit(solution)/shard_map/dot_general | solution.py:25
  92.5 11.0 %attend.2 = (bf16[512,1024]{1,0:T(8,128)(2,1)}, bf16[512,512]{1,0:T(8,128)(2,1)S(1)}) custom-call(s32[6]{0:T(128)S(1)} %concatenate.50.refs_0_.at, f32[512,512]{1,0:T(8,128)S(1)} %fusion.10.part, bf16[512,2048]{1,0:T(8,128)(2,1)} %get-tuple-element.48.enc_other, bf16[2048,512]{1,0:T(8,128)(2,1)} %collective-permute-done.11.w_other.other_0, ...), custom_call_target="tpu_custom_call" | custom-call | flops 4026531840 | bytes 8388608 | tf_op jit(solution)/shard_map/attend/pallas_call | solution.py:137
  106.7 6.3 %weight_grad.2 = bf16[2048,512]{1,0:T(8,128)(2,1)} custom-call(s32[6]{0:T(128)S(1)} %concatenate.50.refs_0_.at, bf16[512,2048]{1,0:T(8,128)(2,1)} %get-tuple-element.47.refs_1_, bf16[512,2048]{1,0:T(8,128)(2,1)} %copy-done.9, bf16[512,512]{1,0:T(8,128)(2,1)S(1)} %get-tuple-element.56.refs_3_.gkv_0, bf16[512,512]{1,0:T(8,128)(2,1)S(1)} %collective-permute-done.13.refs_4_), custom_call_target="tpu_custom_call" | custom-call | flops 33554432 | tf_op jit(solution)/shard_map/weight_grad/pallas_call | solution.py:166
  113.3 5.2 %all-gather.5.cloned.1.call-done.own_1 = bf16[2048,512]{1,0:T(8,128)(2,1)} async-done(((bf16[512,512]{1,0:T(8,128)(2,1)}), bf16[2048,512]{1,0:T(8,128)(2,1)}) %all-gather.5.cloned.1.call-update) | async-done | bytes 2097168 | tf_op jit(solution)/shard_map/all_gather | solution.py:420
  118.6 3.5 %fusion.11.part = f32[512,512]{1,0:T(8,128)S(1)} fusion(bf16[512,2048]{1,0:T(8,128)(2,1)} %get-tuple-element.47.refs_1_, bf16[2048,512]{1,0:T(8,128)(2,1)} %all-gather.5.cloned.1.call-done.own_1), kind=kOutput, calls=%fused_computation.31 | convolution fusion | flops 1073741824 | bytes 5242880 | tf_op jit(solution)/shard_map/dot_general | solution.py:25
  124.3 11.3 %attend.3 = (bf16[512,1024]{1,0:T(8,128)(2,1)}, bf16[512,512]{1,0:T(8,128)(2,1)S(1)}) custom-call(s32[6]{0:T(128)S(1)} %concatenate.50.refs_0_.at, f32[512,512]{1,0:T(8,128)S(1)} %fusion.11.part, bf16[512,2048]{1,0:T(8,128)(2,1)} %get-tuple-element.48.enc_other, bf16[2048,512]{1,0:T(8,128)(2,1)} %copy-done.16, ...), custom_call_target="tpu_custom_call", output_to_operand_aliasing={{0}: (7, {})} | custom-call | flops 4026531840 | bytes 8388608 | tf_op jit(solution)/shard_map/attend/pallas_call | solution.py:137
  136.4 6.7 %enc_grad.2 = (bf16[256,2048]{1,0:T(8,128)(2,1)}, bf16[256,2048]{1,0:T(8,128)(2,1)}) custom-call(s32[6]{0:T(128)S(1)} %concatenate.50.refs_0_.at, bf16[512,512]{1,0:T(8,128)(2,1)} %copy-done.6, bf16[512,512]{1,0:T(8,128)(2,1)} %copy-done.7, bf16[2048,512]{1,0:T(8,128)(2,1)} %all-gather.3.cloned.1.call-done.own_0, ...), custom_call_target="tpu_custom_call" | custom-call | flops 4294967296 | bytes 8388608 | tf_op jit(solution)/shard_map/enc_grad/pallas_call | solution.py:280
  144.2 6.3 %weight_grad.3 = bf16[2048,512]{1,0:T(8,128)(2,1)} custom-call(s32[6]{0:T(128)S(1)} %concatenate.50.refs_0_.at, bf16[512,2048]{1,0:T(8,128)(2,1)} %get-tuple-element.47.refs_1_, bf16[512,2048]{1,0:T(8,128)(2,1)} %copy-done.9, bf16[512,512]{1,0:T(8,128)(2,1)S(1)} %copy-done.8, bf16[512,512]{1,0:T(8,128)(2,1)S(1)} %collective-permute-done.15.refs_4_), custom_call_target="tpu_custom_call" | custom-call | flops 33554432 | tf_op jit(solution)/shard_map/weight_grad/pallas_call | solution.py:166
  155.4 5.1 %collective-permute-start.21 = (bf16[512,1024]{1,0:T(8,128)(2,1)}, bf16[512,1024]{1,0:T(8,128)(2,1)S(1)}, u32[]{:S(2)}, u32[]{:S(2)}) collective-permute-start(bf16[512,1024]{1,0:T(8,128)(2,1)} %get-tuple-element.59), channel_id=1, source_target_pairs={{0,2},{1,3},{8,10},{9,11},{16,18},{17,19},{24,26},{25,27}} | collective-permute-start | bytes 3145736 | tf_op jit(solution)/shard_map/ppermute | solution.py:449
  160.5 6.6 %enc_grad.3 = (bf16[256,2048]{1,0:T(8,128)(2,1)}, bf16[256,2048]{1,0:T(8,128)(2,1)}) custom-call(s32[6]{0:T(128)S(1)} %concatenate.50.refs_0_.at, bf16[512,512]{1,0:T(8,128)(2,1)} %copy-done.6, bf16[512,512]{1,0:T(8,128)(2,1)} %copy-done.7, bf16[2048,512]{1,0:T(8,128)(2,1)} %all-gather.3.cloned.1.call-done.own_0, ...), custom_call_target="tpu_custom_call" | custom-call | flops 4294967296 | bytes 8388608 | tf_op jit(solution)/shard_map/enc_grad/pallas_call | solution.py:280
  167.1 3.0 %add_convert_fusion.1 = bf16[256,2048]{1,0:T(8,128)(2,1)} fusion(bf16[256,2048]{1,0:T(8,128)(2,1)} %collective-permute-done.16, bf16[256,2048]{1,0:T(8,128)(2,1)} %get-tuple-element.57.refs_1_), kind=kLoop, calls=%fused_computation.5 | loop fusion | flops 2097152 | bytes 3145728 | tf_op jit(solution)/shard_map/convert_element_type | solution.py:460
  171.4 2.8 %collective-permute-start.17 = (bf16[256,2048]{1,0:T(8,128)(2,1)}, bf16[256,2048]{1,0:T(8,128)(2,1)}, u32[]{:S(2)}, u32[]{:S(2)}) collective-permute-start(bf16[256,2048]{1,0:T(8,128)(2,1)} %get-tuple-element.58), channel_id=1, source_target_pairs={{0,1},{1,0},{6,7},{7,6},{8,9},{9,8},{14,15},{15,14},{16,17},{17,16... | collective-permute-start | bytes 3145736 | tf_op jit(solution)/shard_map/ppermute | solution.py:327
  174.2 3.1 %collective-permute-start.20 = (bf16[256,2048]{1,0:T(8,128)(2,1)}, bf16[256,2048]{1,0:T(8,128)(2,1)}, u32[]{:S(2)}, u32[]{:S(2)}) collective-permute-start(bf16[256,2048]{1,0:T(8,128)(2,1)} %get-tuple-element.64), channel_id=1, source_target_pairs={{0,1},{1,0},{6,7},{7,6},{8,9},{9,8},{14,15},{15,14},{16,17},{17,16... | collective-permute-start | bytes 3145736 | tf_op jit(solution)/shard_map/ppermute | solution.py:327
  184.1 9.1 %collective-permute-start.22 = (bf16[256,512]{1,0:T(8,128)(2,1)S(1)}, bf16[256,512]{1,0:T(8,128)(2,1)S(1)}, u32[]{:S(2)}, u32[]{:S(2)}) collective-permute-start(bf16[256,512]{1,0:T(8,128)(2,1)S(1)} %get-tuple-element.82), channel_id=1, source_target_pairs={{0,4},{4,0},{1,5},{5,1},{2,6},{6,2},{3,7},{7,3},{8,12},{12,8},{9,1... | collective-permute-start | bytes 786440 | tf_op jit(solution)/shard_map/ppermute | solution.py:448
  193.2 4.4 %maximum_select_fusion.refs_4_ = bf16[512,2048]{1,0:T(8,128)(2,1)} fusion(bf16[512,1024]{1,0:T(8,128)(2,1)} %collective-permute-done.18, bf16[512,1024]{1,0:T(8,128)(2,1)} %broadcast_select_fusion, pred[]{:T(512)S(6)} %eq.15), kind=kLoop, calls=%fused_computation.3 | loop fusion | flops 9437184 | bytes 4194305 | tf_op jit(solution)/shard_map/jit(_where)/select_n | solution.py:300
  197.6 4.0 %collect.2 = (bf16[256,2048]{1,0:T(8,128)(2,1)}, f32[2,1,2048]{2,1,0:T(1,128)S(1)}) custom-call(s32[6]{0:T(128)S(1)} %concatenate.50.refs_0_.at, bf16[256,2048]{1,0:T(8,128)(2,1)S(1)} %copy-done.3, bf16[256,2048]{1,0:T(8,128)(2,1)} %collective-permute-done.17.refs_2_, bf16[256,2048]{1,0:T(8,128)(2,1)} %collective-permute-done.19.refs_3_, ...), custom_call_target="tpu_custom_call" | custom-call | flops 4194304 | bytes 6291456 | tf_op jit(solution)/shard_map/collect/pallas_call | solution.py:198
  201.6 4.4 %collective-permute-done.22 = bf16[256,512]{1,0:T(8,128)(2,1)S(1)} collective-permute-done((bf16[256,512]{1,0:T(8,128)(2,1)S(1)}, bf16[256,512]{1,0:T(8,128)(2,1)S(1)}, u32[]{:S(2)}, u32[]{:S(2)}) %collective-permute-start.22) | collective-permute-done | bytes 262176 | tf_op jit(solution)/shard_map/ppermute | solution.py:448
  207.6 4.0 %collect.3 = (bf16[256,2048]{1,0:T(8,128)(2,1)}, f32[2,1,2048]{2,1,0:T(1,128)S(1)}) custom-call(s32[6]{0:T(128)S(1)} %concatenate.50.refs_0_.at, bf16[256,2048]{1,0:T(8,128)(2,1)S(1)} %copy-done.2, bf16[256,2048]{1,0:T(8,128)(2,1)} %collective-permute-done.20.refs_2_, bf16[256,2048]{1,0:T(8,128)(2,1)} %collective-permute-done.24.refs_3_, ...), custom_call_target="tpu_custom_call" | custom-call | flops 4194304 | bytes 6291456 | tf_op jit(solution)/shard_map/collect/pallas_call | solution.py:198
  215.2 6.2 %collective-permute-done.25 = f32[2048]{0:T(1024)S(1)} collective-permute-done((f32[2048]{0:T(1024)S(1)}, f32[2048]{0:T(1024)S(1)}, u32[]{:S(2)}, u32[]{:S(2)}) %collective-permute-start.25) | collective-permute-done | bytes 8224 | tf_op jit(solution)/shard_map/ppermute | solution.py:493
  221.4 3.6 %collective-permute-done.26 = f32[2048]{0:T(1024)S(1)} collective-permute-done((f32[2048]{0:T(1024)S(1)}, f32[2048]{0:T(1024)S(1)}, u32[]{:S(2)}, u32[]{:S(2)}) %collective-permute-start.26) | collective-permute-done | bytes 8224 | tf_op jit(solution)/shard_map/ppermute | solution.py:498
  226.6 4.8 %assemble.1 = bf16[512,2048]{1,0:T(8,128)(2,1)} custom-call(s32[6]{0:T(128)S(1)} %concatenate.50.refs_0_.at, bf16[256,2048]{1,0:T(8,128)(2,1)} %get-tuple-element.69.refs_0_, bf16[256,2048]{1,0:T(8,128)(2,1)} %get-tuple-element.70.refs_1_, bf16[256,2048]{1,0:T(8,128)(2,1)} %collective-permute-done.27.refs_2_, ...), custom_call_target="tpu_custom_call" | custom-call | flops 1048576 | bytes 4194304 | tf_op jit(solution)/shard_map/assemble/pallas_call | solution.py:240
  232.2 3.9 %collective-permute-done.30 = f32[2048]{0:T(1024)S(1)} collective-permute-done((f32[2048]{0:T(1024)S(1)}, f32[2048]{0:T(1024)S(1)}, u32[]{:S(2)}, u32[]{:S(2)}) %collective-permute-start.30) | collective-permute-done | bytes 8224 | tf_op jit(solution)/shard_map/ppermute | solution.py:498
  (117 shorter events, 54.6 us)
Async XLA Ops:
  7.2 65.1 %all-gather.3.cloned.1.call-start = ((), (), s32[]{:S(2)}) async-start(), calls=%async_computation.2 | async-start | bytes 2621440 | tf_op jit(solution)/shard_map/all_gather | solution.py:420
  7.2 18.7 %collective-permute-start.3 = (bf16[512,2048]{1,0:T(8,128)(2,1)}, bf16[512,2048]{1,0:T(8,128)(2,1)}, u32[]{:S(2)}, u32[]{:S(2)}) collective-permute-start(bf16[512,2048]{1,0:T(8,128)(2,1)} %bitcast.15), channel_id=1, source_target_pairs={{4,6},{5,7},{12,14},{13,15},{20,22},{21,23},{28,30},{29,31}} | collective-permute-start | bytes 6291464 | tf_op jit(solution)/shard_map/ppermute | solution.py:340
  11.4 8.7 %collective-permute-start = (bf16[256,512]{1,0:T(8,128)(2,1)S(1)}, bf16[256,512]{1,0:T(8,128)(2,1)S(1)}, u32[]{:S(2)}, u32[]{:S(2)}) collective-permute-start(bf16[256,512]{1,0:T(8,128)(2,1)S(1)} %get-tuple-element.78), channel_id=1, source_target_pairs={{0,4},{4,0},{1,5},{5,1},{2,6},{6,2},{3,7},{7,3},{8,12},{12,8},{9,1... | collective-permute-start | bytes 786440 | tf_op jit(solution)/shard_map/ppermute | solution.py:339
  20.9 27.2 %collective-permute-start.1 = (bf16[512,2048]{1,0:T(8,128)(2,1)S(1)}, bf16[512,2048]{1,0:T(8,128)(2,1)}, u32[]{:S(2)}, u32[]{:S(2)}) collective-permute-start(bf16[512,2048]{1,0:T(8,128)(2,1)S(1)} %bitcast.16), channel_id=1, source_target_pairs={{0,4},{4,2},{1,5},{5,3},{8,12},{12,10},{9,13},{13,11},{16,20},{20,... | collective-permute-start | bytes 6291464 | tf_op jit(solution)/shard_map/ppermute | solution.py:345
  25.9 92.6 %all-gather.5.cloned.1.call-start = ((), (), s32[]{:S(2)}) async-start(), calls=%async_computation.3 | async-start | bytes 2621440 | tf_op jit(solution)/shard_map/all_gather | solution.py:420
  26.0 24.0 %collective-permute-start.6 = (bf16[512,2048]{1,0:T(8,128)(2,1)}, bf16[512,2048]{1,0:T(8,128)(2,1)S(1)}, u32[]{:S(2)}, u32[]{:S(2)}) collective-permute-start(bf16[512,2048]{1,0:T(8,128)(2,1)} %collective-permute-done.3.refs_2_.refs_5_), channel_id=1, source_target_pairs={{6,7},{7,6},{14,15},{15,14},{22,23},{23,22},{30,31},{31,30}} | collective-permute-start | bytes 6291464 | tf_op jit(solution)/shard_map/ppermute | solution.py:327
  30.5 42.0 %collective-permute-start.5 = (bf16[512,2048]{1,0:T(8,128)(2,1)S(1)}, bf16[512,2048]{1,0:T(8,128)(2,1)}, u32[]{:S(2)}, u32[]{:S(2)}) collective-permute-start(bf16[512,2048]{1,0:T(8,128)(2,1)S(1)} %bitcast.17), channel_id=1, source_target_pairs={{0,1},{1,0},{8,9},{9,8},{16,17},{17,16},{24,25},{25,24}} | collective-permute-start | bytes 6291464 | tf_op jit(solution)/shard_map/ppermute | solution.py:327
  48.0 24.5 %collective-permute-start.7 = (bf16[512,2048]{1,0:T(8,128)(2,1)}, bf16[512,2048]{1,0:T(8,128)(2,1)}, u32[]{:S(2)}, u32[]{:S(2)}) collective-permute-start(bf16[512,2048]{1,0:T(8,128)(2,1)} %collective-permute-done.1.refs_3_), channel_id=1, source_target_pairs={{2,3},{3,2},{4,5},{5,4},{10,11},{11,10},{12,13},{13,12},{18,19},{1... | collective-permute-start | bytes 6291464 | tf_op jit(solution)/shard_map/ppermute | solution.py:327
  51.3 13.8 %collective-permute-start.8 = (bf16[256,512]{1,0:T(8,128)(2,1)}, bf16[256,512]{1,0:T(8,128)(2,1)}, u32[]{:S(2)}, u32[]{:S(2)}) collective-permute-start(bf16[256,512]{1,0:T(8,128)(2,1)} %get-tuple-element.43), channel_id=1, source_target_pairs={{0,4},{4,0},{1,5},{5,1},{2,6},{6,2},{3,7},{7,3},{8,12},{12,8},{9,1... | collective-permute-start | bytes 786440 | tf_op jit(solution)/shard_map/ppermute | solution.py:358
  60.8 3.8 %collective-permute-start.2 = (s32[1]{0:T(128)}, s32[1]{0:T(128)}, u32[]{:S(2)}, u32[]{:S(2)}) collective-permute-start(s32[1]{0:T(128)} %param.8), channel_id=1, source_target_pairs={{0,4},{4,0},{1,5},{5,1},{2,6},{6,2},{3,7},{7,3},{8,12},{12,8},{9,1... | collective-permute-start | bytes 20 | tf_op jit(solution)/shard_map/ppermute | solution.py:346
  65.2 7.3 %collective-permute-start.10 = (bf16[512,1024]{1,0:T(8,128)(2,1)}, bf16[512,1024]{1,0:T(8,128)(2,1)}, u32[]{:S(2)}, u32[]{:S(2)}) collective-permute-start(bf16[512,1024]{1,0:T(8,128)(2,1)} %get-tuple-element.45), channel_id=1, source_target_pairs={{2,4},{6,2},{3,5},{7,3},{10,12},{14,10},{11,13},{15,11},{18,20},{2... | collective-permute-start | bytes 3145736 | tf_op jit(solution)/shard_map/ppermute | solution.py:370
  66.9 5.6 %collective-permute-start.9 = (bf16[512,1024]{1,0:T(8,128)(2,1)S(1)}, bf16[512,1024]{1,0:T(8,128)(2,1)}, u32[]{:S(2)}, u32[]{:S(2)}) collective-permute-start(bf16[512,1024]{1,0:T(8,128)(2,1)S(1)} %get-tuple-element.44.refs_0_), channel_id=1, source_target_pairs={{2,0},{3,1},{10,8},{11,9},{18,16},{19,17},{26,24},{27,25}} | collective-permute-start | bytes 3145736 | tf_op jit(solution)/shard_map/ppermute | solution.py:369
  70.0 112.4 %reduce-scatter.3.cloned.1.call-start = ((), (), s32[]{:S(2)}) async-start(), calls=%async_computation.4 | async-start | bytes 2621440 | tf_op jit(solution)/shard_map/reduce_scatter | solution.py:439
  72.3 20.2 %collective-permute-start.11 = (bf16[2048,512]{1,0:T(8,128)(2,1)}, bf16[2048,512]{1,0:T(8,128)(2,1)}, u32[]{:S(2)}, u32[]{:S(2)}) collective-permute-start(bf16[2048,512]{1,0:T(8,128)(2,1)} %all-gather.3.cloned.1.call-done.own_0), channel_id=1, source_target_pairs={{0,2},{2,0},{1,3},{3,1},{4,6},{6,4},{5,7},{7,5},{8,10},{10,8},{9,1... | collective-permute-start | bytes 6291464 | tf_op jit(solution)/shard_map/ppermute | solution.py:423
  81.0 24.4 %collective-permute-start.12 = (bf16[512,2048]{1,0:T(8,128)(2,1)}, bf16[512,2048]{1,0:T(8,128)(2,1)S(1)}, u32[]{:S(2)}, u32[]{:S(2)}) collective-permute-start(bf16[512,2048]{1,0:T(8,128)(2,1)} %get-tuple-element.48.enc_other), channel_id=1, source_target_pairs={{0,2},{2,0},{1,3},{3,1},{4,6},{6,4},{5,7},{7,5},{8,10},{10,8},{9,1... | collective-permute-start | bytes 6291464 | tf_op jit(solution)/shard_map/ppermute | solution.py:406
  113.1 99.3 %reduce-scatter.5.cloned.1.call-start = ((), (), s32[]{:S(2)}) async-start(), calls=%async_computation.5 | async-start | bytes 2621440 | tf_op jit(solution)/shard_map/reduce_scatter | solution.py:439
  118.6 4.4 %collective-permute-start.14 = (bf16[2048,512]{1,0:T(8,128)(2,1)}, bf16[2048,512]{1,0:T(8,128)(2,1)S(1)}, u32[]{:S(2)}, u32[]{:S(2)}) collective-permute-start(bf16[2048,512]{1,0:T(8,128)(2,1)} %all-gather.5.cloned.1.call-done.own_1), channel_id=1, source_target_pairs={{0,2},{2,0},{1,3},{3,1},{4,6},{6,4},{5,7},{7,5},{8,10},{10,8},{9,1... | collective-permute-start | bytes 6291464 | tf_op jit(solution)/shard_map/ppermute | solution.py:423
  135.6 7.5 %collective-permute-start.15 = (bf16[512,512]{1,0:T(8,128)(2,1)S(1)}, bf16[512,512]{1,0:T(8,128)(2,1)S(1)}, u32[]{:S(2)}, u32[]{:S(2)}) collective-permute-start(bf16[512,512]{1,0:T(8,128)(2,1)S(1)} %get-tuple-element.52.gkv_1.refs_3_), channel_id=1, source_target_pairs={{0,2},{2,0},{1,3},{3,1},{4,6},{6,4},{5,7},{7,5},{8,10},{10,8},{9,1... | collective-permute-start | bytes 1572872 | tf_op jit(solution)/shard_map/ppermute | solution.py:427
  150.5 16.7 %collective-permute-start.16 = (bf16[256,2048]{1,0:T(8,128)(2,1)}, bf16[256,2048]{1,0:T(8,128)(2,1)}, u32[]{:S(2)}, u32[]{:S(2)}) collective-permute-start(bf16[256,2048]{1,0:T(8,128)(2,1)} %get-tuple-element.58), channel_id=1, source_target_pairs={{2,3},{3,2},{4,5},{5,4},{10,11},{11,10},{12,13},{13,12},{18,19},{1... | collective-permute-start | bytes 3145736 | tf_op jit(solution)/shard_map/ppermute | solution.py:327
  152.1 18.0 %collective-permute-start.18 = (bf16[512,1024]{1,0:T(8,128)(2,1)}, bf16[512,1024]{1,0:T(8,128)(2,1)}, u32[]{:S(2)}, u32[]{:S(2)}) collective-permute-start(bf16[512,1024]{1,0:T(8,128)(2,1)} %get-tuple-element.59), channel_id=1, source_target_pairs={{4,2},{2,6},{5,3},{3,7},{12,10},{10,14},{13,11},{11,15},{20,18},{1... | collective-permute-start | bytes 3145736 | tf_op jit(solution)/shard_map/ppermute | solution.py:450
  153.8 23.5 %collective-permute-start.23 = (bf16[256,2048]{1,0:T(8,128)(2,1)}, bf16[256,2048]{1,0:T(8,128)(2,1)}, u32[]{:S(2)}, u32[]{:S(2)}) collective-permute-start(bf16[256,2048]{1,0:T(8,128)(2,1)} %get-tuple-element.64), channel_id=1, source_target_pairs={{2,3},{3,2},{4,5},{5,4},{10,11},{11,10},{12,13},{13,12},{18,19},{1... | collective-permute-start | bytes 3145736 | tf_op jit(solution)/shard_map/ppermute | solution.py:327
  155.4 25.8 %collective-permute-start.21 = (bf16[512,1024]{1,0:T(8,128)(2,1)}, bf16[512,1024]{1,0:T(8,128)(2,1)S(1)}, u32[]{:S(2)}, u32[]{:S(2)}) collective-permute-start(bf16[512,1024]{1,0:T(8,128)(2,1)} %get-tuple-element.59), channel_id=1, source_target_pairs={{0,2},{1,3},{8,10},{9,11},{16,18},{17,19},{24,26},{25,27}} | collective-permute-start | bytes 3145736 | tf_op jit(solution)/shard_map/ppermute | solution.py:449
  170.1 27.5 %collective-permute-start.19 = (bf16[256,2048]{1,0:T(8,128)(2,1)}, bf16[256,2048]{1,0:T(8,128)(2,1)}, u32[]{:S(2)}, u32[]{:S(2)}) collective-permute-start(bf16[256,2048]{1,0:T(8,128)(2,1)} %add_convert_fusion.1), channel_id=1, source_target_pairs={{4,0},{2,6},{5,1},{3,7},{12,8},{10,14},{13,9},{11,15},{20,16},{18,... | collective-permute-start | bytes 3145736 | tf_op jit(solution)/shard_map/ppermute | solution.py:465
  171.4 26.2 %collective-permute-start.17 = (bf16[256,2048]{1,0:T(8,128)(2,1)}, bf16[256,2048]{1,0:T(8,128)(2,1)}, u32[]{:S(2)}, u32[]{:S(2)}) collective-permute-start(bf16[256,2048]{1,0:T(8,128)(2,1)} %get-tuple-element.58), channel_id=1, source_target_pairs={{0,1},{1,0},{6,7},{7,6},{8,9},{9,8},{14,15},{15,14},{16,17},{17,16... | collective-permute-start | bytes 3145736 | tf_op jit(solution)/shard_map/ppermute | solution.py:327
  174.2 27.4 %collective-permute-start.20 = (bf16[256,2048]{1,0:T(8,128)(2,1)}, bf16[256,2048]{1,0:T(8,128)(2,1)}, u32[]{:S(2)}, u32[]{:S(2)}) collective-permute-start(bf16[256,2048]{1,0:T(8,128)(2,1)} %get-tuple-element.64), channel_id=1, source_target_pairs={{0,1},{1,0},{6,7},{7,6},{8,9},{9,8},{14,15},{15,14},{16,17},{17,16... | collective-permute-start | bytes 3145736 | tf_op jit(solution)/shard_map/ppermute | solution.py:327
  179.9 27.7 %collective-permute-start.24 = (bf16[256,2048]{1,0:T(8,128)(2,1)}, bf16[256,2048]{1,0:T(8,128)(2,1)}, u32[]{:S(2)}, u32[]{:S(2)}) collective-permute-start(bf16[256,2048]{1,0:T(8,128)(2,1)} %add_convert_fusion), channel_id=1, source_target_pairs={{4,0},{2,6},{5,1},{3,7},{12,8},{10,14},{13,9},{11,15},{20,16},{18,... | collective-permute-start | bytes 3145736 | tf_op jit(solution)/shard_map/ppermute | solution.py:465
  184.1 21.8 %collective-permute-start.22 = (bf16[256,512]{1,0:T(8,128)(2,1)S(1)}, bf16[256,512]{1,0:T(8,128)(2,1)S(1)}, u32[]{:S(2)}, u32[]{:S(2)}) collective-permute-start(bf16[256,512]{1,0:T(8,128)(2,1)S(1)} %get-tuple-element.82), channel_id=1, source_target_pairs={{0,4},{4,0},{1,5},{5,1},{2,6},{6,2},{3,7},{7,3},{8,12},{12,8},{9,1... | collective-permute-start | bytes 786440 | tf_op jit(solution)/shard_map/ppermute | solution.py:448
  205.9 19.1 %collective-permute-start.27 = (bf16[256,2048]{1,0:T(8,128)(2,1)}, bf16[256,2048]{1,0:T(8,128)(2,1)}, u32[]{:S(2)}, u32[]{:S(2)}) collective-permute-start(bf16[256,2048]{1,0:T(8,128)(2,1)} %get-tuple-element.69.refs_0_), channel_id=1, source_target_pairs={{6,4},{7,5},{14,12},{15,13},{22,20},{23,21},{30,28},{31,29}} | collective-permute-start | bytes 3145736 | tf_op jit(solution)/shard_map/ppermute | solution.py:485
  211.6 13.5 %collective-permute-start.28 = (bf16[256,2048]{1,0:T(8,128)(2,1)}, bf16[256,2048]{1,0:T(8,128)(2,1)S(1)}, u32[]{:S(2)}, u32[]{:S(2)}) collective-permute-start(bf16[256,2048]{1,0:T(8,128)(2,1)} %get-tuple-element.70.refs_1_), channel_id=1, source_target_pairs={{6,4},{7,5},{14,12},{15,13},{22,20},{23,21},{30,28},{31,29}} | collective-permute-start | bytes 3145736 | tf_op jit(solution)/shard_map/ppermute | solution.py:485
  213.5 24.3 %collective-permute-start.29 = (bf16[256,512]{1,0:T(8,128)(2,1)S(1)}, bf16[256,512]{1,0:T(8,128)(2,1)S(1)}, u32[]{:S(2)}, u32[]{:S(2)}) collective-permute-start(bf16[256,512]{1,0:T(8,128)(2,1)S(1)} %get-tuple-element.84), channel_id=1, source_target_pairs={{0,4},{4,0},{1,5},{5,1},{2,6},{6,2},{3,7},{7,3},{8,12},{12,8},{9,1... | collective-permute-start | bytes 786440 | tf_op jit(solution)/shard_map/ppermute | solution.py:448
  213.6 7.8 %collective-permute-start.25 = (f32[2048]{0:T(1024)S(1)}, f32[2048]{0:T(1024)S(1)}, u32[]{:S(2)}, u32[]{:S(2)}) collective-permute-start(f32[2048]{0:T(1024)S(1)} %add_select_fusion), channel_id=1, source_target_pairs={{0,6},{6,0},{2,4},{4,2},{1,7},{7,1},{3,5},{5,3},{8,14},{14,8},{10,... | collective-permute-start | bytes 24584 | tf_op jit(solution)/shard_map/ppermute | solution.py:493
  231.5 4.5 %collective-permute-start.30 = (f32[2048]{0:T(1024)S(1)}, f32[2048]{0:T(1024)S(1)}, u32[]{:S(2)}, u32[]{:S(2)}) collective-permute-start(f32[2048]{0:T(1024)S(1)} %add.64), channel_id=1, source_target_pairs={{0,16},{8,24},{16,0},{24,8},{1,17},{9,25},{17,1},{25,9},{2,18},{10... | collective-permute-start | bytes 24584 | tf_op jit(solution)/shard_map/ppermute | solution.py:498
  (21 other events, 149.7 us)
Sparse Core Ops, SparseCore 0:
  26.0 46.2 all-gather.2
  73.9 44.6 all-gather.4
  120.9 42.5 reduce-scatter.2
  166.3 43.1 reduce-scatter.4

commit v13 on v12

--- a/solution.py
+++ b/solution.py
@@ -250,7 +250,7 @@
         cost_estimate=cost(length * width, 4),
         compiler_params=params(14),
         name="assemble",
-    )(at, *sums, *moved, dec)
+    )(at, *sums, *moved, *in_hbm(dec))
 
 
 def enc_grad_kernel(at, gkv_0, gkv_1, own_0, own_1, other_0, other_1, *outs):
@@ -457,7 +457,8 @@
             term = across(terms[turn][part], turn, [(1, 1), (2, 2)])
             first_far = term if first_far is None else first_far
             total = total + term.astype(F32)
-        far.append(after(total.astype(BF16), dec_there))
+        done = dec_there if part == 0 else got[0]
+        far.append(after(total.astype(BF16), done))
     moved = [
         [across(after(part, first_far), turn, [(0, 0), (3, 3)]) for part in terms[turn]]
         for turn in range(1, shards)
@@ -469,8 +470,8 @@
         for part in range(PARTS):
             pieces = [t[part] for t in [terms[0]] + moved]
             if part > 0:
-                pieces[1], grad_normed[-1], dec_grads, got[0] = lax.optimization_barrier(
-                    (pieces[1], grad_normed[-1], dec_grads, got[0])
+                pieces[1], grad_normed[-1], dec_grads = lax.optimization_barrier(
+                    (pieces[1], grad_normed[-1], dec_grads)
                 )
             summed, term = collect(
                 at, pieces, part, packed, here, inv_rms, gain.astype(F32)[None], pair_scale

time: 247 us -> 247 us (level)
  waiting for transfers between devices: 53.7 us -> 59.3 us
  starting transfers between devices: 67.5 us -> 63.1 us
    ppermute x2, waiting for transfers between devices: 0.01 us -> 4.96 us  [on_device(): moved.append([lax.ppermute(part, PLANE, [(2, 0), (1, 3)]) for part in far])]
    ppermute x2, starting transfers between devices: 9.13 us -> 5.83 us  [on_device(): got = [lax.ppermute(w[rows:], 'y', SWAP) for w in weight_sums]]
    unnamed x34 -> x32, local copies, waits for them, and re-layouts: 8.86 us -> 8.01 us
  transfers between devices with their start and end apart: 36 -> 36, of which waited for: 13 -> 14; matrix products, arithmetic and copies ran while one was open for 12% -> 12% of each run, Pallas kernels for 28% -> 28%
where the time goes in v13:
time: 247 us; the launch traced here: 246 us
  Pallas kernels  68 us (28%)
  starting transfers between devices  63.1 us (26%)
  waiting for transfers between devices  59.3 us (24%)
  other arithmetic  17.4 us (7%)
  between operations  16 us (6%)
  local copies, waits for them, and re-layouts  15.6 us (6%)
  matrix products  6.3 us (3%)
    pallas_call x2, Pallas kernels, attend(): pl.pallas_call(attend_kernel, grid_spec=pltpu.PrefetchScalarGridSpec(num_...  22.3 us
    ppermute x7, starting transfers between devices, across(): lax.ppermute(value, ('y', 'phase', 'mp'), [(a * shards + s, b * shards +...  14.3 us
    ppermute x1, waiting for transfers between devices, on_device(): there = lax.ppermute(after(packed, blocks[0]), PLANE, [(0, 2), (2, 1)])  14.3 us
    pallas_call x2, Pallas kernels, enc_grad(): pl.pallas_call(enc_grad_kernel, grid_spec=pltpu.PrefetchScalarGridSpec(nu...  13.3 us
    pallas_call x2, Pallas kernels, weight_grad(): pl.pallas_call(lambda *refs: weight_grad_kernel(scale, *refs), grid_spec=...  12.5 us
    ppermute x1, starting transfers between devices, on_device(): enc_mate = lax.ppermute(enc_other, 'phase', SWAP)  8.63 us
    unnamed x32, local copies, waits for them, and re-layouts  8.01 us
    pallas_call x2, Pallas kernels, collect(): pl.pallas_call(lambda *refs: collect_kernel(scale, *refs), grid_spec=pltp...  7.97 us
  transfers between devices with their start and end apart: 36, of which 14 were waited for; matrix products, arithmetic and copies ran while one was open for 12% of the time, Pallas kernels for 28%

profile of v13, /device:TPU:0, one launch (start us, length us, event | category | flops | bytes accessed | tf_op | source)
XLA Modules:
  0.0 245.7 jit_solution(2521257429238569133)
XLA Ops:
  11.3 4.0 %collective-permute-start = (bf16[256,512]{1,0:T(8,128)(2,1)S(1)}, bf16[256,512]{1,0:T(8,128)(2,1)S(1)}, u32[]{:S(2)}, u32[]{:S(2)}) collective-permute-start(bf16[256,512]{1,0:T(8,128)(2,1)S(1)} %get-tuple-element.76), channel_id=1, source_target_pairs={{0,4},{4,0},{1,5},{5,1},{2,6},{6,2},{3,7},{7,3},{8,12},{12,8},{9,1... | collective-permute-start | bytes 786440 | tf_op jit(solution)/shard_map/ppermute | solution.py:339
  15.4 4.6 %collective-permute-done = bf16[256,512]{1,0:T(8,128)(2,1)S(1)} collective-permute-done((bf16[256,512]{1,0:T(8,128)(2,1)S(1)}, bf16[256,512]{1,0:T(8,128)(2,1)S(1)}, u32[]{:S(2)}, u32[]{:S(2)}) %collective-permute-start) | collective-permute-done | bytes 262176 | tf_op jit(solution)/shard_map/ppermute | solution.py:339
  20.9 5.0 %collective-permute-start.1 = (bf16[512,2048]{1,0:T(8,128)(2,1)S(1)}, bf16[512,2048]{1,0:T(8,128)(2,1)}, u32[]{:S(2)}, u32[]{:S(2)}) collective-permute-start(bf16[512,2048]{1,0:T(8,128)(2,1)S(1)} %bitcast.16), channel_id=1, source_target_pairs={{0,4},{4,2},{1,5},{5,3},{8,12},{12,10},{9,13},{13,11},{16,20},{20,... | collective-permute-start | bytes 6291464 | tf_op jit(solution)/shard_map/ppermute | solution.py:345
  30.4 3.4 %collective-permute-start.5 = (bf16[512,2048]{1,0:T(8,128)(2,1)S(1)}, bf16[512,2048]{1,0:T(8,128)(2,1)}, u32[]{:S(2)}, u32[]{:S(2)}) collective-permute-start(bf16[512,2048]{1,0:T(8,128)(2,1)S(1)} %bitcast.17), channel_id=1, source_target_pairs={{0,1},{1,0},{8,9},{9,8},{16,17},{17,16},{24,25},{25,24}} | collective-permute-start | bytes 6291464 | tf_op jit(solution)/shard_map/ppermute | solution.py:327
  33.8 14.3 %collective-permute-done.1.refs_3_ = bf16[512,2048]{1,0:T(8,128)(2,1)} collective-permute-done((bf16[512,2048]{1,0:T(8,128)(2,1)S(1)}, bf16[512,2048]{1,0:T(8,128)(2,1)}, u32[]{:S(2)}, u32[]{:S(2)}) %collective-permute-start.1) | collective-permute-done | bytes 2097184 | tf_op jit(solution)/shard_map/ppermute | solution.py:345
  51.3 4.1 %collective-permute-start.8 = (bf16[256,512]{1,0:T(8,128)(2,1)}, bf16[256,512]{1,0:T(8,128)(2,1)}, u32[]{:S(2)}, u32[]{:S(2)}) collective-permute-start(bf16[256,512]{1,0:T(8,128)(2,1)} %get-tuple-element.42), channel_id=1, source_target_pairs={{0,4},{4,0},{1,5},{5,1},{2,6},{6,2},{3,7},{7,3},{8,12},{12,8},{9,1... | collective-permute-start | bytes 786440 | tf_op jit(solution)/shard_map/ppermute | solution.py:358
  58.0 2.7 %constant_dynamic-slice_fusion.2 = (bf16[512,1024]{1,0:T(8,128)(2,1)}, bf16[512,1024]{1,0:T(8,128)(2,1)S(1)}) fusion(bf16[512,2048]{1,0:T(8,128)(2,1)} %fusion.1, s32[]{:T(128)S(6)} %select_n.97, s32[]{:T(128)S(6)} %select_n.96), kind=kLoop, calls=%fused_computation.24 | loop fusion | bytes 4194312 | tf_op jit(solution)/shard_map/dynamic_slice | solution.py:296
  60.8 3.6 %collective-permute-done.2 = s32[1]{0:T(128)} collective-permute-done((s32[1]{0:T(128)}, s32[1]{0:T(128)}, u32[]{:S(2)}, u32[]{:S(2)}) %collective-permute-start.2) | collective-permute-done | bytes 36 | tf_op jit(solution)/shard_map/ppermute | solution.py:346
  74.0 6.9 %norm.1 = (bf16[512,2048]{1,0:T(8,128)(2,1)}, bf16[512,2048]{1,0:T(8,128)(2,1)}, f32[512,128]{1,0:T(8,128)S(1)}) custom-call(s32[6]{0:T(128)S(1)} %concatenate.50.refs_0_.at, bf16[512,2048]{1,0:T(8,128)(2,1)S(1)} %bitcast.18, bf16[512,2048]{1,0:T(8,128)(2,1)} %collective-permute-done.3.refs_2_.refs_5_, bf16[512,2048]{1,0:T(8,128)(2,1)} %collective-permute-done.1.refs_3_, ...), custom_call_target="tpu_custom_call" | custom-call | flops 16777216 | bytes 8388608 | tf_op jit(solution)/shard_map/norm/pallas_call | solution.py:74
  81.0 8.6 %collective-permute-start.12 = (bf16[512,2048]{1,0:T(8,128)(2,1)}, bf16[512,2048]{1,0:T(8,128)(2,1)S(1)}, u32[]{:S(2)}, u32[]{:S(2)}) collective-permute-start(bf16[512,2048]{1,0:T(8,128)(2,1)} %get-tuple-element.47.enc_other), channel_id=1, source_target_pairs={{0,2},{2,0},{1,3},{3,1},{4,6},{6,4},{5,7},{7,5},{8,10},{10,8},{9,1... | collective-permute-start | bytes 6291464 | tf_op jit(solution)/shard_map/ppermute | solution.py:406
  89.6 2.8 %fusion.10.part = f32[512,512]{1,0:T(8,128)S(1)} fusion(bf16[512,2048]{1,0:T(8,128)(2,1)} %get-tuple-element.46.refs_1_, bf16[2048,512]{1,0:T(8,128)(2,1)S(1)} %copy-done.14), kind=kOutput, calls=%fused_computation.30 | convolution fusion | flops 1073741824 | bytes 5242880 | tf_op jit(solution)/shard_map/dot_general | solution.py:25
  92.4 11.0 %attend.2 = (bf16[512,1024]{1,0:T(8,128)(2,1)}, bf16[512,512]{1,0:T(8,128)(2,1)S(1)}) custom-call(s32[6]{0:T(128)S(1)} %concatenate.50.refs_0_.at, f32[512,512]{1,0:T(8,128)S(1)} %fusion.10.part, bf16[512,2048]{1,0:T(8,128)(2,1)} %get-tuple-element.47.enc_other, bf16[2048,512]{1,0:T(8,128)(2,1)} %collective-permute-done.11.w_other.other_0, ...), custom_call_target="tpu_custom_call" | custom-call | flops 4026531840 | bytes 8388608 | tf_op jit(solution)/shard_map/attend/pallas_call | solution.py:137
  106.7 6.3 %weight_grad.2 = bf16[2048,512]{1,0:T(8,128)(2,1)} custom-call(s32[6]{0:T(128)S(1)} %concatenate.50.refs_0_.at, bf16[512,2048]{1,0:T(8,128)(2,1)} %get-tuple-element.46.refs_1_, bf16[512,2048]{1,0:T(8,128)(2,1)} %copy-done.8, bf16[512,512]{1,0:T(8,128)(2,1)S(1)} %get-tuple-element.55.refs_3_.gkv_0, bf16[512,512]{1,0:T(8,128)(2,1)S(1)} %collective-permute-done.13.refs_4_), custom_call_target="tpu_custom_call" | custom-call | flops 33554432 | tf_op jit(solution)/shard_map/weight_grad/pallas_call | solution.py:166
  113.2 5.3 %all-gather.5.cloned.1.call-done.own_1 = bf16[2048,512]{1,0:T(8,128)(2,1)} async-done(((bf16[512,512]{1,0:T(8,128)(2,1)}), bf16[2048,512]{1,0:T(8,128)(2,1)}) %all-gather.5.cloned.1.call-update) | async-done | bytes 2097168 | tf_op jit(solution)/shard_map/all_gather | solution.py:420
  118.5 3.5 %fusion.11.part = f32[512,512]{1,0:T(8,128)S(1)} fusion(bf16[512,2048]{1,0:T(8,128)(2,1)} %get-tuple-element.46.refs_1_, bf16[2048,512]{1,0:T(8,128)(2,1)} %all-gather.5.cloned.1.call-done.own_1), kind=kOutput, calls=%fused_computation.31 | convolution fusion | flops 1073741824 | bytes 5242880 | tf_op jit(solution)/shard_map/dot_general | solution.py:25
  124.3 11.3 %attend.3 = (bf16[512,1024]{1,0:T(8,128)(2,1)}, bf16[512,512]{1,0:T(8,128)(2,1)S(1)}) custom-call(s32[6]{0:T(128)S(1)} %concatenate.50.refs_0_.at, f32[512,512]{1,0:T(8,128)S(1)} %fusion.11.part, bf16[512,2048]{1,0:T(8,128)(2,1)} %get-tuple-element.47.enc_other, bf16[2048,512]{1,0:T(8,128)(2,1)} %copy-done.15, ...), custom_call_target="tpu_custom_call", output_to_operand_aliasing={{0}: (7, {})} | custom-call | flops 4026531840 | bytes 8388608 | tf_op jit(solution)/shard_map/attend/pallas_call | solution.py:137
  136.4 6.7 %enc_grad.2 = (bf16[256,2048]{1,0:T(8,128)(2,1)}, bf16[256,2048]{1,0:T(8,128)(2,1)}) custom-call(s32[6]{0:T(128)S(1)} %concatenate.50.refs_0_.at, bf16[512,512]{1,0:T(8,128)(2,1)} %copy-done.5, bf16[512,512]{1,0:T(8,128)(2,1)} %copy-done.6, bf16[2048,512]{1,0:T(8,128)(2,1)} %all-gather.3.cloned.1.call-done.own_0, ...), custom_call_target="tpu_custom_call" | custom-call | flops 4294967296 | bytes 8388608 | tf_op jit(solution)/shard_map/enc_grad/pallas_call | solution.py:280
  144.1 6.3 %weight_grad.3 = bf16[2048,512]{1,0:T(8,128)(2,1)} custom-call(s32[6]{0:T(128)S(1)} %concatenate.50.refs_0_.at, bf16[512,2048]{1,0:T(8,128)(2,1)} %get-tuple-element.46.refs_1_, bf16[512,2048]{1,0:T(8,128)(2,1)} %copy-done.8, bf16[512,512]{1,0:T(8,128)(2,1)S(1)} %copy-done.7, bf16[512,512]{1,0:T(8,128)(2,1)S(1)} %collective-permute-done.15.refs_4_), custom_call_target="tpu_custom_call" | custom-call | flops 33554432 | tf_op jit(solution)/shard_map/weight_grad/pallas_call | solution.py:166
  152.8 5.8 %collective-permute-start.21 = (bf16[512,1024]{1,0:T(8,128)(2,1)}, bf16[512,1024]{1,0:T(8,128)(2,1)}, u32[]{:S(2)}, u32[]{:S(2)}) collective-permute-start(bf16[512,1024]{1,0:T(8,128)(2,1)} %get-tuple-element.58), channel_id=1, source_target_pairs={{0,2},{1,3},{8,10},{9,11},{16,18},{17,19},{24,26},{25,27}} | collective-permute-start | bytes 3145736 | tf_op jit(solution)/shard_map/ppermute | solution.py:449
  160.2 6.6 %enc_grad.3 = (bf16[256,2048]{1,0:T(8,128)(2,1)}, bf16[256,2048]{1,0:T(8,128)(2,1)}) custom-call(s32[6]{0:T(128)S(1)} %concatenate.50.refs_0_.at, bf16[512,512]{1,0:T(8,128)(2,1)} %copy-done.5, bf16[512,512]{1,0:T(8,128)(2,1)} %copy-done.6, bf16[2048,512]{1,0:T(8,128)(2,1)} %all-gather.3.cloned.1.call-done.own_0, ...), custom_call_target="tpu_custom_call" | custom-call | flops 4294967296 | bytes 8388608 | tf_op jit(solution)/shard_map/enc_grad/pallas_call | solution.py:280
  166.9 2.7 %add_convert_fusion.1 = bf16[256,2048]{1,0:T(8,128)(2,1)} fusion(bf16[256,2048]{1,0:T(8,128)(2,1)S(1)} %collective-permute-done.16, bf16[256,2048]{1,0:T(8,128)(2,1)} %get-tuple-element.56.refs_1_), kind=kLoop, calls=%fused_computation.5 | loop fusion | flops 2097152 | bytes 3145728 | tf_op jit(solution)/shard_map/convert_element_type | solution.py:461
  173.3 3.4 %collective-permute-start.20 = (bf16[256,2048]{1,0:T(8,128)(2,1)}, bf16[256,2048]{1,0:T(8,128)(2,1)}, u32[]{:S(2)}, u32[]{:S(2)}) collective-permute-start(bf16[256,2048]{1,0:T(8,128)(2,1)} %get-tuple-element.63), channel_id=1, source_target_pairs={{0,1},{1,0},{6,7},{7,6},{8,9},{9,8},{14,15},{15,14},{16,17},{17,16... | collective-permute-start | bytes 3145736 | tf_op jit(solution)/shard_map/ppermute | solution.py:327
  178.5 5.6 %collective-permute-start.23 = (bf16[256,512]{1,0:T(8,128)(2,1)S(1)}, bf16[256,512]{1,0:T(8,128)(2,1)S(1)}, u32[]{:S(2)}, u32[]{:S(2)}) collective-permute-start(bf16[256,512]{1,0:T(8,128)(2,1)S(1)} %get-tuple-element.80), channel_id=1, source_target_pairs={{0,4},{4,0},{1,5},{5,1},{2,6},{6,2},{3,7},{7,3},{8,12},{12,8},{9,1... | collective-permute-start | bytes 786440 | tf_op jit(solution)/shard_map/ppermute | solution.py:448
  186.8 5.3 %collective-permute-done.23 = bf16[256,512]{1,0:T(8,128)(2,1)S(1)} collective-permute-done((bf16[256,512]{1,0:T(8,128)(2,1)S(1)}, bf16[256,512]{1,0:T(8,128)(2,1)S(1)}, u32[]{:S(2)}, u32[]{:S(2)}) %collective-permute-start.23) | collective-permute-done | bytes 262176 | tf_op jit(solution)/shard_map/ppermute | solution.py:448
  195.5 3.7 %maximum_select_fusion.refs_4_ = bf16[512,2048]{1,0:T(8,128)(2,1)} fusion(bf16[512,1024]{1,0:T(8,128)(2,1)} %collective-permute-done.18, bf16[512,1024]{1,0:T(8,128)(2,1)S(1)} %broadcast_select_fusion, pred[]{:T(512)S(6)} %eq.15), kind=kLoop, calls=%fused_computation.3 | loop fusion | flops 9437184 | bytes 4194305 | tf_op jit(solution)/shard_map/jit(_where)/select_n | solution.py:300
  199.2 4.0 %collect.2 = (bf16[256,2048]{1,0:T(8,128)(2,1)}, f32[2,1,2048]{2,1,0:T(1,128)S(1)}) custom-call(s32[6]{0:T(128)S(1)} %concatenate.50.refs_0_.at, bf16[256,2048]{1,0:T(8,128)(2,1)S(1)} %copy-done.2, bf16[256,2048]{1,0:T(8,128)(2,1)} %collective-permute-done.17.refs_2_, bf16[256,2048]{1,0:T(8,128)(2,1)} %collective-permute-done.19.refs_3_, ...), custom_call_target="tpu_custom_call" | custom-call | flops 4194304 | bytes 6291456 | tf_op jit(solution)/shard_map/collect/pallas_call | solution.py:198
  204.8 5.0 %collective-permute-done.24.refs_3_ = bf16[256,2048]{1,0:T(8,128)(2,1)} collective-permute-done((bf16[256,2048]{1,0:T(8,128)(2,1)}, bf16[256,2048]{1,0:T(8,128)(2,1)}, u32[]{:S(2)}, u32[]{:S(2)}) %collective-permute-start.24) | collective-permute-done | bytes 1048608 | tf_op jit(solution)/shard_map/ppermute | solution.py:466
  209.8 4.0 %collect.3 = (bf16[256,2048]{1,0:T(8,128)(2,1)}, f32[2,1,2048]{2,1,0:T(1,128)S(1)}) custom-call(s32[6]{0:T(128)S(1)} %concatenate.50.refs_0_.at, bf16[256,2048]{1,0:T(8,128)(2,1)S(1)} %copy-done.1, bf16[256,2048]{1,0:T(8,128)(2,1)} %collective-permute-done.20.refs_2_, bf16[256,2048]{1,0:T(8,128)(2,1)} %collective-permute-done.24.refs_3_, ...), custom_call_target="tpu_custom_call" | custom-call | flops 4194304 | bytes 6291456 | tf_op jit(solution)/shard_map/collect/pallas_call | solution.py:198
  216.8 5.8 %collective-permute-done.25 = f32[2048]{0:T(1024)S(1)} collective-permute-done((f32[2048]{0:T(1024)S(1)}, f32[2048]{0:T(1024)S(1)}, u32[]{:S(2)}, u32[]{:S(2)}) %collective-permute-start.25) | collective-permute-done | bytes 8224 | tf_op jit(solution)/shard_map/ppermute | solution.py:494
  222.5 3.6 %collective-permute-done.26 = f32[2048]{0:T(1024)S(1)} collective-permute-done((f32[2048]{0:T(1024)S(1)}, f32[2048]{0:T(1024)S(1)}, u32[]{:S(2)}, u32[]{:S(2)}) %collective-permute-start.26) | collective-permute-done | bytes 8224 | tf_op jit(solution)/shard_map/ppermute | solution.py:499
  226.2 5.0 %assemble.1 = bf16[512,2048]{1,0:T(8,128)(2,1)} custom-call(s32[6]{0:T(128)S(1)} %concatenate.50.refs_0_.at, bf16[256,2048]{1,0:T(8,128)(2,1)} %get-tuple-element.68.refs_0_, bf16[256,2048]{1,0:T(8,128)(2,1)} %get-tuple-element.69.refs_1_, bf16[256,2048]{1,0:T(8,128)(2,1)} %collective-permute-done.27.refs_2_, ...), custom_call_target="tpu_custom_call" | custom-call | flops 1048576 | bytes 4194304 | tf_op jit(solution)/shard_map/assemble/pallas_call | solution.py:240
  231.9 3.9 %collective-permute-done.30 = f32[2048]{0:T(1024)S(1)} collective-permute-done((f32[2048]{0:T(1024)S(1)}, f32[2048]{0:T(1024)S(1)}, u32[]{:S(2)}, u32[]{:S(2)}) %collective-permute-start.30) | collective-permute-done | bytes 8224 | tf_op jit(solution)/shard_map/ppermute | solution.py:499
  (115 shorter events, 55.0 us)
Async XLA Ops:
  7.2 65.1 %all-gather.3.cloned.1.call-start = ((), (), s32[]{:S(2)}) async-start(), calls=%async_computation.2 | async-start | bytes 2621440 | tf_op jit(solution)/shard_map/all_gather | solution.py:420
  7.2 18.7 %collective-permute-start.3 = (bf16[512,2048]{1,0:T(8,128)(2,1)}, bf16[512,2048]{1,0:T(8,128)(2,1)}, u32[]{:S(2)}, u32[]{:S(2)}) collective-permute-start(bf16[512,2048]{1,0:T(8,128)(2,1)} %bitcast.15), channel_id=1, source_target_pairs={{4,6},{5,7},{12,14},{13,15},{20,22},{21,23},{28,30},{29,31}} | collective-permute-start | bytes 6291464 | tf_op jit(solution)/shard_map/ppermute | solution.py:340
  11.3 8.7 %collective-permute-start = (bf16[256,512]{1,0:T(8,128)(2,1)S(1)}, bf16[256,512]{1,0:T(8,128)(2,1)S(1)}, u32[]{:S(2)}, u32[]{:S(2)}) collective-permute-start(bf16[256,512]{1,0:T(8,128)(2,1)S(1)} %get-tuple-element.76), channel_id=1, source_target_pairs={{0,4},{4,0},{1,5},{5,1},{2,6},{6,2},{3,7},{7,3},{8,12},{12,8},{9,1... | collective-permute-start | bytes 786440 | tf_op jit(solution)/shard_map/ppermute | solution.py:339
  20.9 27.2 %collective-permute-start.1 = (bf16[512,2048]{1,0:T(8,128)(2,1)S(1)}, bf16[512,2048]{1,0:T(8,128)(2,1)}, u32[]{:S(2)}, u32[]{:S(2)}) collective-permute-start(bf16[512,2048]{1,0:T(8,128)(2,1)S(1)} %bitcast.16), channel_id=1, source_target_pairs={{0,4},{4,2},{1,5},{5,3},{8,12},{12,10},{9,13},{13,11},{16,20},{20,... | collective-permute-start | bytes 6291464 | tf_op jit(solution)/shard_map/ppermute | solution.py:345
  25.9 92.6 %all-gather.5.cloned.1.call-start = ((), (), s32[]{:S(2)}) async-start(), calls=%async_computation.3 | async-start | bytes 2621440 | tf_op jit(solution)/shard_map/all_gather | solution.py:420
  25.9 24.1 %collective-permute-start.6 = (bf16[512,2048]{1,0:T(8,128)(2,1)}, bf16[512,2048]{1,0:T(8,128)(2,1)S(1)}, u32[]{:S(2)}, u32[]{:S(2)}) collective-permute-start(bf16[512,2048]{1,0:T(8,128)(2,1)} %collective-permute-done.3.refs_2_.refs_5_), channel_id=1, source_target_pairs={{6,7},{7,6},{14,15},{15,14},{22,23},{23,22},{30,31},{31,30}} | collective-permute-start | bytes 6291464 | tf_op jit(solution)/shard_map/ppermute | solution.py:327
  26.7 3.7 %collective-permute-start.4 = (bf16[2048]{0:T(1024)(128)(2,1)S(1)}, bf16[2048]{0:T(1024)(128)(2,1)S(1)}, u32[]{:S(2)}, u32[]{:S(2)}) collective-permute-start(bf16[2048]{0:T(1024)(128)(2,1)S(1)} %copy-done.13), channel_id=1, source_target_pairs={{0,1},{1,0},{2,3},{3,2},{4,5},{5,4},{6,7},{7,6},{8,9},{9,8},{10,11... | collective-permute-start | bytes 12296 | tf_op jit(solution)/shard_map/ppermute | solution.py:342
  30.4 42.0 %collective-permute-start.5 = (bf16[512,2048]{1,0:T(8,128)(2,1)S(1)}, bf16[512,2048]{1,0:T(8,128)(2,1)}, u32[]{:S(2)}, u32[]{:S(2)}) collective-permute-start(bf16[512,2048]{1,0:T(8,128)(2,1)S(1)} %bitcast.17), channel_id=1, source_target_pairs={{0,1},{1,0},{8,9},{9,8},{16,17},{17,16},{24,25},{25,24}} | collective-permute-start | bytes 6291464 | tf_op jit(solution)/shard_map/ppermute | solution.py:327
  48.0 24.4 %collective-permute-start.7 = (bf16[512,2048]{1,0:T(8,128)(2,1)}, bf16[512,2048]{1,0:T(8,128)(2,1)}, u32[]{:S(2)}, u32[]{:S(2)}) collective-permute-start(bf16[512,2048]{1,0:T(8,128)(2,1)} %collective-permute-done.1.refs_3_), channel_id=1, source_target_pairs={{2,3},{3,2},{4,5},{5,4},{10,11},{11,10},{12,13},{13,12},{18,19},{1... | collective-permute-start | bytes 6291464 | tf_op jit(solution)/shard_map/ppermute | solution.py:327
  51.3 13.7 %collective-permute-start.8 = (bf16[256,512]{1,0:T(8,128)(2,1)}, bf16[256,512]{1,0:T(8,128)(2,1)}, u32[]{:S(2)}, u32[]{:S(2)}) collective-permute-start(bf16[256,512]{1,0:T(8,128)(2,1)} %get-tuple-element.42), channel_id=1, source_target_pairs={{0,4},{4,0},{1,5},{5,1},{2,6},{6,2},{3,7},{7,3},{8,12},{12,8},{9,1... | collective-permute-start | bytes 786440 | tf_op jit(solution)/shard_map/ppermute | solution.py:358
  65.0 7.4 %collective-permute-start.10 = (bf16[512,1024]{1,0:T(8,128)(2,1)}, bf16[512,1024]{1,0:T(8,128)(2,1)}, u32[]{:S(2)}, u32[]{:S(2)}) collective-permute-start(bf16[512,1024]{1,0:T(8,128)(2,1)} %get-tuple-element.44), channel_id=1, source_target_pairs={{2,4},{6,2},{3,5},{7,3},{10,12},{14,10},{11,13},{15,11},{18,20},{2... | collective-permute-start | bytes 3145736 | tf_op jit(solution)/shard_map/ppermute | solution.py:370
  66.7 5.7 %collective-permute-start.9 = (bf16[512,1024]{1,0:T(8,128)(2,1)S(1)}, bf16[512,1024]{1,0:T(8,128)(2,1)}, u32[]{:S(2)}, u32[]{:S(2)}) collective-permute-start(bf16[512,1024]{1,0:T(8,128)(2,1)S(1)} %get-tuple-element.43.refs_0_), channel_id=1, source_target_pairs={{2,0},{3,1},{10,8},{11,9},{18,16},{19,17},{26,24},{27,25}} | collective-permute-start | bytes 3145736 | tf_op jit(solution)/shard_map/ppermute | solution.py:369
  69.8 106.9 %reduce-scatter.3.cloned.1.call-start = ((), (), s32[]{:S(2)}) async-start(), calls=%async_computation.4 | async-start | bytes 2621440 | tf_op jit(solution)/shard_map/reduce_scatter | solution.py:439
  72.2 20.2 %collective-permute-start.11 = (bf16[2048,512]{1,0:T(8,128)(2,1)}, bf16[2048,512]{1,0:T(8,128)(2,1)}, u32[]{:S(2)}, u32[]{:S(2)}) collective-permute-start(bf16[2048,512]{1,0:T(8,128)(2,1)} %all-gather.3.cloned.1.call-done.own_0), channel_id=1, source_target_pairs={{0,2},{2,0},{1,3},{3,1},{4,6},{6,4},{5,7},{7,5},{8,10},{10,8},{9,1... | collective-permute-start | bytes 6291464 | tf_op jit(solution)/shard_map/ppermute | solution.py:423
  81.0 24.4 %collective-permute-start.12 = (bf16[512,2048]{1,0:T(8,128)(2,1)}, bf16[512,2048]{1,0:T(8,128)(2,1)S(1)}, u32[]{:S(2)}, u32[]{:S(2)}) collective-permute-start(bf16[512,2048]{1,0:T(8,128)(2,1)} %get-tuple-element.47.enc_other), channel_id=1, source_target_pairs={{0,2},{2,0},{1,3},{3,1},{4,6},{6,4},{5,7},{7,5},{8,10},{10,8},{9,1... | collective-permute-start | bytes 6291464 | tf_op jit(solution)/shard_map/ppermute | solution.py:406
  113.0 101.6 %reduce-scatter.5.cloned.1.call-start = ((), (), s32[]{:S(2)}) async-start(), calls=%async_computation.5 | async-start | bytes 2621440 | tf_op jit(solution)/shard_map/reduce_scatter | solution.py:439
  118.5 4.4 %collective-permute-start.14 = (bf16[2048,512]{1,0:T(8,128)(2,1)}, bf16[2048,512]{1,0:T(8,128)(2,1)S(1)}, u32[]{:S(2)}, u32[]{:S(2)}) collective-permute-start(bf16[2048,512]{1,0:T(8,128)(2,1)} %all-gather.5.cloned.1.call-done.own_1), channel_id=1, source_target_pairs={{0,2},{2,0},{1,3},{3,1},{4,6},{6,4},{5,7},{7,5},{8,10},{10,8},{9,1... | collective-permute-start | bytes 6291464 | tf_op jit(solution)/shard_map/ppermute | solution.py:423
  135.5 7.5 %collective-permute-start.15 = (bf16[512,512]{1,0:T(8,128)(2,1)S(1)}, bf16[512,512]{1,0:T(8,128)(2,1)S(1)}, u32[]{:S(2)}, u32[]{:S(2)}) collective-permute-start(bf16[512,512]{1,0:T(8,128)(2,1)S(1)} %get-tuple-element.51.gkv_1.refs_3_), channel_id=1, source_target_pairs={{0,2},{2,0},{1,3},{3,1},{4,6},{6,4},{5,7},{7,5},{8,10},{10,8},{9,1... | collective-permute-start | bytes 1572872 | tf_op jit(solution)/shard_map/ppermute | solution.py:427
  150.4 16.4 %collective-permute-start.16 = (bf16[256,2048]{1,0:T(8,128)(2,1)}, bf16[256,2048]{1,0:T(8,128)(2,1)S(1)}, u32[]{:S(2)}, u32[]{:S(2)}) collective-permute-start(bf16[256,2048]{1,0:T(8,128)(2,1)} %get-tuple-element.57), channel_id=1, source_target_pairs={{2,3},{3,2},{4,5},{5,4},{10,11},{11,10},{12,13},{13,12},{18,19},{1... | collective-permute-start | bytes 3145736 | tf_op jit(solution)/shard_map/ppermute | solution.py:327
  151.1 18.4 %collective-permute-start.18 = (bf16[512,1024]{1,0:T(8,128)(2,1)}, bf16[512,1024]{1,0:T(8,128)(2,1)}, u32[]{:S(2)}, u32[]{:S(2)}) collective-permute-start(bf16[512,1024]{1,0:T(8,128)(2,1)} %get-tuple-element.58), channel_id=1, source_target_pairs={{4,2},{2,6},{5,3},{3,7},{12,10},{10,14},{13,11},{11,15},{20,18},{1... | collective-permute-start | bytes 3145736 | tf_op jit(solution)/shard_map/ppermute | solution.py:450
  152.8 41.3 %collective-permute-start.21 = (bf16[512,1024]{1,0:T(8,128)(2,1)}, bf16[512,1024]{1,0:T(8,128)(2,1)}, u32[]{:S(2)}, u32[]{:S(2)}) collective-permute-start(bf16[512,1024]{1,0:T(8,128)(2,1)} %get-tuple-element.58), channel_id=1, source_target_pairs={{0,2},{1,3},{8,10},{9,11},{16,18},{17,19},{24,26},{25,27}} | collective-permute-start | bytes 3145736 | tf_op jit(solution)/shard_map/ppermute | solution.py:449
  158.6 19.9 %collective-permute-start.22 = (bf16[256,2048]{1,0:T(8,128)(2,1)}, bf16[256,2048]{1,0:T(8,128)(2,1)}, u32[]{:S(2)}, u32[]{:S(2)}) collective-permute-start(bf16[256,2048]{1,0:T(8,128)(2,1)} %get-tuple-element.63), channel_id=1, source_target_pairs={{2,3},{3,2},{4,5},{5,4},{10,11},{11,10},{12,13},{13,12},{18,19},{1... | collective-permute-start | bytes 3145736 | tf_op jit(solution)/shard_map/ppermute | solution.py:327
  169.6 29.6 %collective-permute-start.19 = (bf16[256,2048]{1,0:T(8,128)(2,1)}, bf16[256,2048]{1,0:T(8,128)(2,1)}, u32[]{:S(2)}, u32[]{:S(2)}) collective-permute-start(bf16[256,2048]{1,0:T(8,128)(2,1)} %add_convert_fusion.1), channel_id=1, source_target_pairs={{4,0},{2,6},{5,1},{3,7},{12,8},{10,14},{13,9},{11,15},{20,16},{18,... | collective-permute-start | bytes 3145736 | tf_op jit(solution)/shard_map/ppermute | solution.py:466
  170.9 28.4 %collective-permute-start.17 = (bf16[256,2048]{1,0:T(8,128)(2,1)}, bf16[256,2048]{1,0:T(8,128)(2,1)}, u32[]{:S(2)}, u32[]{:S(2)}) collective-permute-start(bf16[256,2048]{1,0:T(8,128)(2,1)} %get-tuple-element.57), channel_id=1, source_target_pairs={{0,1},{1,0},{6,7},{7,6},{8,9},{9,8},{14,15},{15,14},{16,17},{17,16... | collective-permute-start | bytes 3145736 | tf_op jit(solution)/shard_map/ppermute | solution.py:327
  173.3 29.9 %collective-permute-start.20 = (bf16[256,2048]{1,0:T(8,128)(2,1)}, bf16[256,2048]{1,0:T(8,128)(2,1)}, u32[]{:S(2)}, u32[]{:S(2)}) collective-permute-start(bf16[256,2048]{1,0:T(8,128)(2,1)} %get-tuple-element.63), channel_id=1, source_target_pairs={{0,1},{1,0},{6,7},{7,6},{8,9},{9,8},{14,15},{15,14},{16,17},{17,16... | collective-permute-start | bytes 3145736 | tf_op jit(solution)/shard_map/ppermute | solution.py:327
  178.5 13.6 %collective-permute-start.23 = (bf16[256,512]{1,0:T(8,128)(2,1)S(1)}, bf16[256,512]{1,0:T(8,128)(2,1)S(1)}, u32[]{:S(2)}, u32[]{:S(2)}) collective-permute-start(bf16[256,512]{1,0:T(8,128)(2,1)S(1)} %get-tuple-element.80), channel_id=1, source_target_pairs={{0,4},{4,0},{1,5},{5,1},{2,6},{6,2},{3,7},{7,3},{8,12},{12,8},{9,1... | collective-permute-start | bytes 786440 | tf_op jit(solution)/shard_map/ppermute | solution.py:448
  192.8 17.0 %collective-permute-start.24 = (bf16[256,2048]{1,0:T(8,128)(2,1)}, bf16[256,2048]{1,0:T(8,128)(2,1)}, u32[]{:S(2)}, u32[]{:S(2)}) collective-permute-start(bf16[256,2048]{1,0:T(8,128)(2,1)} %add_convert_fusion), channel_id=1, source_target_pairs={{4,0},{2,6},{5,1},{3,7},{12,8},{10,14},{13,9},{11,15},{20,16},{18,... | collective-permute-start | bytes 3145736 | tf_op jit(solution)/shard_map/ppermute | solution.py:466
  203.2 23.0 %collective-permute-start.27 = (bf16[256,2048]{1,0:T(8,128)(2,1)}, bf16[256,2048]{1,0:T(8,128)(2,1)}, u32[]{:S(2)}, u32[]{:S(2)}) collective-permute-start(bf16[256,2048]{1,0:T(8,128)(2,1)} %get-tuple-element.68.refs_0_), channel_id=1, source_target_pairs={{6,4},{7,5},{14,12},{15,13},{22,20},{23,21},{30,28},{31,29}} | collective-permute-start | bytes 3145736 | tf_op jit(solution)/shard_map/ppermute | solution.py:486
  213.8 12.4 %collective-permute-start.28 = (bf16[256,2048]{1,0:T(8,128)(2,1)}, bf16[256,2048]{1,0:T(8,128)(2,1)S(1)}, u32[]{:S(2)}, u32[]{:S(2)}) collective-permute-start(bf16[256,2048]{1,0:T(8,128)(2,1)} %get-tuple-element.69.refs_1_), channel_id=1, source_target_pairs={{6,4},{7,5},{14,12},{15,13},{22,20},{23,21},{30,28},{31,29}} | collective-permute-start | bytes 3145736 | tf_op jit(solution)/shard_map/ppermute | solution.py:486
  215.7 21.9 %collective-permute-start.29 = (bf16[256,512]{1,0:T(8,128)(2,1)S(1)}, bf16[256,512]{1,0:T(8,128)(2,1)S(1)}, u32[]{:S(2)}, u32[]{:S(2)}) collective-permute-start(bf16[256,512]{1,0:T(8,128)(2,1)S(1)} %get-tuple-element.82), channel_id=1, source_target_pairs={{0,4},{4,0},{1,5},{5,1},{2,6},{6,2},{3,7},{7,3},{8,12},{12,8},{9,1... | collective-permute-start | bytes 786440 | tf_op jit(solution)/shard_map/ppermute | solution.py:448
  215.9 6.7 %collective-permute-start.25 = (f32[2048]{0:T(1024)S(1)}, f32[2048]{0:T(1024)S(1)}, u32[]{:S(2)}, u32[]{:S(2)}) collective-permute-start(f32[2048]{0:T(1024)S(1)} %add_select_fusion), channel_id=1, source_target_pairs={{0,6},{6,0},{2,4},{4,2},{1,7},{7,1},{3,5},{5,3},{8,14},{14,8},{10,... | collective-permute-start | bytes 24584 | tf_op jit(solution)/shard_map/ppermute | solution.py:494
  231.2 4.5 %collective-permute-start.30 = (f32[2048]{0:T(1024)S(1)}, f32[2048]{0:T(1024)S(1)}, u32[]{:S(2)}, u32[]{:S(2)}) collective-permute-start(f32[2048]{0:T(1024)S(1)} %add.64), channel_id=1, source_target_pairs={{0,16},{8,24},{16,0},{24,8},{1,17},{9,25},{17,1},{25,9},{2,18},{10... | collective-permute-start | bytes 24584 | tf_op jit(solution)/shard_map/ppermute | solution.py:499
  (20 other events, 140.8 us)
Sparse Core Ops, SparseCore 0:
  26.0 46.2 all-gather.2
  73.8 44.6 all-gather.4
  120.8 42.5 reduce-scatter.2
  166.2 43.1 reduce-scatter.4

commit v14 on v13

--- a/solution.py
+++ b/solution.py
@@ -445,7 +445,7 @@
         full = full.astype(BF16).reshape(length, -1, rows)[:, back].reshape(length, D)
         terms = [jnp.split(cut(full, 1, (x + s) % shards, width), PARTS) for s in range(shards)]
     kept = jnp.concatenate([w[:rows] for w in weight_sums], 1)
-    got = [lax.ppermute(w[rows:], "y", SWAP) for w in weight_sums]
+    got = lax.ppermute(jnp.concatenate([w[rows:] for w in weight_sums], 1), "y", SWAP)
     dec_here = jnp.where(y == 0, lax.ppermute(dec, PLANE, [(0, 1)]), dec)
     dec_there = lax.ppermute(dec, PLANE, [(2, 1), (1, 3)])
     dec_grads = ordered(y == 0, dec_here, dec_there, 1)
@@ -457,8 +457,7 @@
             term = across(terms[turn][part], turn, [(1, 1), (2, 2)])
             first_far = term if first_far is None else first_far
             total = total + term.astype(F32)
-        done = dec_there if part == 0 else got[0]
-        far.append(after(total.astype(BF16), done))
+        far.append(after(total.astype(BF16), dec_there))
     moved = [
         [across(after(part, first_far), turn, [(0, 0), (3, 3)]) for part in terms[turn]]
         for turn in range(1, shards)
@@ -484,22 +483,20 @@
         normed = chosen(enc_kind, *nears).astype(F32) * inv_rms
         gain_term = pair_scale * jnp.sum(grad_enc * normed, axis=0)
     sent = [lax.ppermute(g, PLANE, [(3, 2)]) for g in grad_normed]
+    gain_term = jnp.where(straight, gain_term, 0.0)
+    gain_term = gain_term + lax.ppermute(gain_term, PLANE, [(0, 3), (3, 0), (1, 2), (2, 1)])
+    turn = 1
+    while turn < groups:
+        gain_term = gain_term + lax.ppermute(gain_term, "z", [(i, i ^ turn) for i in range(groups)])
+        turn *= 2
     if tiled:
+        sent[0] = after(sent[0], gain_term)
         sec_grads = assemble(at, grad_normed, sent, dec_grads)[None, None]
     else:
         enc_grads = jnp.where(y == 0, jnp.concatenate(grad_normed, 0), jnp.concatenate(sent, 0))
         sec_grads = jnp.where(core == 0, enc_grads, dec_grads)[None, None]
 
-    gain_term = jnp.where(straight, gain_term, 0.0)
-    gain_term = gain_term + lax.ppermute(gain_term, PLANE, [(0, 3), (3, 0), (1, 2), (2, 1)])
-    turn = 1
-    while turn < groups:
-        if 2 * turn == groups:
-            gain_term, sec_grads = lax.optimization_barrier((gain_term, sec_grads))
-        gain_term = gain_term + lax.ppermute(gain_term, "z", [(i, i ^ turn) for i in range(groups)])
-        turn *= 2
     d_gain = jnp.where(straight, gain_term, lax.ppermute(gain_term, "phase", SWAP))
-    got = jnp.concatenate(got, 1)
     d_wkv = ordered(y == 0, kept, got, 1).astype(F32)
     return (sec_grads, d_wkv, d_gain)
 

time: 247 us -> 252 us (1.020)
  waiting for transfers between devices: 59.3 us -> 70.1 us
  starting transfers between devices: 63.1 us -> 59.3 us
    ppermute x7, waiting for transfers between devices: 0.02 us -> 13.3 us  [across(): lax.ppermute(value, ('y', 'phase', 'mp'), [(a * shards + s, b * shards +...]
    ppermute x1, waiting for transfers between devices: 5.77 us -> 11.7 us  [on_device(): lax.ppermute(gain_term, PLANE, [(0, 3), (3, 0), (1, 2), (2, 1)])]
    ppermute x2 -> x1, starting transfers between devices: 5.83 us -> 0.01 us  [on_device(): lax.ppermute(jnp.concatenate([w[rows:] for w in weight_sums], 1), 'y', SWAP)]
    ppermute x2 -> x1, waiting for transfers between devices: 5.28 us -> 0.01 us  [on_device(): lax.ppermute(jnp.concatenate([w[rows:] for w in weight_sums], 1), 'y', SWAP)]
    ppermute x2, waiting for transfers between devices: 4.96 us -> 2.06 us  [on_device(): moved.append([lax.ppermute(part, PLANE, [(2, 0), (1, 3)]) for part in far])]
    unnamed x32 -> x26, local copies, waits for them, and re-layouts: 8.01 us -> 7.2 us
  transfers between devices with their start and end apart: 36 -> 35, of which waited for: 14 -> 14; matrix products, arithmetic and copies ran while one was open for 12% -> 11% of each run, Pallas kernels for 28% -> 27%
where the time goes in v14:
time: 252 us; the launch traced here: 251 us
  waiting for transfers between devices  70.1 us (28%)
  Pallas kernels  67.9 us (27%)
  starting transfers between devices  59.3 us (24%)
  other arithmetic  17.1 us (7%)
  between operations  16.1 us (6%)
  local copies, waits for them, and re-layouts  14.2 us (6%)
  matrix products  6.31 us (3%)
    pallas_call x2, Pallas kernels, attend(): pl.pallas_call(attend_kernel, grid_spec=pltpu.PrefetchScalarGridSpec(num_...  22.4 us
    ppermute x1, waiting for transfers between devices, on_device(): there = lax.ppermute(after(packed, blocks[0]), PLANE, [(0, 2), (2, 1)])  14.2 us
    ppermute x7, starting transfers between devices, across(): lax.ppermute(value, ('y', 'phase', 'mp'), [(a * shards + s, b * shards +...  13.4 us
    pallas_call x2, Pallas kernels, enc_grad(): pl.pallas_call(enc_grad_kernel, grid_spec=pltpu.PrefetchScalarGridSpec(nu...  13.3 us
    ppermute x7, waiting for transfers between devices, across(): lax.ppermute(value, ('y', 'phase', 'mp'), [(a * shards + s, b * shards +...  13.3 us
    pallas_call x2, Pallas kernels, weight_grad(): pl.pallas_call(lambda *refs: weight_grad_kernel(scale, *refs), grid_spec=...  12.5 us
    ppermute x1, waiting for transfers between devices, on_device(): lax.ppermute(gain_term, PLANE, [(0, 3), (3, 0), (1, 2), (2, 1)])  11.7 us
    ppermute x1, starting transfers between devices, on_device(): enc_mate = lax.ppermute(enc_other, 'phase', SWAP)  8.63 us
  transfers between devices with their start and end apart: 35, of which 14 were waited for; matrix products, arithmetic and copies ran while one was open for 11% of the time, Pallas kernels for 27%

profile of v14, /device:TPU:0, one launch (start us, length us, event | category | flops | bytes accessed | tf_op | source)
XLA Modules:
  0.0 251.0 jit_solution(4177995242933333893)
XLA Ops:
  11.3 4.0 %collective-permute-start = (bf16[256,512]{1,0:T(8,128)(2,1)S(1)}, bf16[256,512]{1,0:T(8,128)(2,1)S(1)}, u32[]{:S(2)}, u32[]{:S(2)}) collective-permute-start(bf16[256,512]{1,0:T(8,128)(2,1)S(1)} %get-tuple-element.74), channel_id=1, source_target_pairs={{0,4},{4,0},{1,5},{5,1},{2,6},{6,2},{3,7},{7,3},{8,12},{12,8},{9,1... | collective-permute-start | bytes 786440 | tf_op jit(solution)/shard_map/ppermute | solution.py:339
  15.4 4.6 %collective-permute-done = bf16[256,512]{1,0:T(8,128)(2,1)S(1)} collective-permute-done((bf16[256,512]{1,0:T(8,128)(2,1)S(1)}, bf16[256,512]{1,0:T(8,128)(2,1)S(1)}, u32[]{:S(2)}, u32[]{:S(2)}) %collective-permute-start) | collective-permute-done | bytes 262176 | tf_op jit(solution)/shard_map/ppermute | solution.py:339
  20.8 5.0 %collective-permute-start.1 = (bf16[512,2048]{1,0:T(8,128)(2,1)S(1)}, bf16[512,2048]{1,0:T(8,128)(2,1)}, u32[]{:S(2)}, u32[]{:S(2)}) collective-permute-start(bf16[512,2048]{1,0:T(8,128)(2,1)S(1)} %bitcast.16), channel_id=1, source_target_pairs={{0,4},{4,2},{1,5},{5,3},{8,12},{12,10},{9,13},{13,11},{16,20},{20,... | collective-permute-start | bytes 6291464 | tf_op jit(solution)/shard_map/ppermute | solution.py:345
  30.4 3.4 %collective-permute-start.5 = (bf16[512,2048]{1,0:T(8,128)(2,1)S(1)}, bf16[512,2048]{1,0:T(8,128)(2,1)}, u32[]{:S(2)}, u32[]{:S(2)}) collective-permute-start(bf16[512,2048]{1,0:T(8,128)(2,1)S(1)} %bitcast.17), channel_id=1, source_target_pairs={{0,1},{1,0},{8,9},{9,8},{16,17},{17,16},{24,25},{25,24}} | collective-permute-start | bytes 6291464 | tf_op jit(solution)/shard_map/ppermute | solution.py:327
  33.8 14.2 %collective-permute-done.1.refs_3_ = bf16[512,2048]{1,0:T(8,128)(2,1)} collective-permute-done((bf16[512,2048]{1,0:T(8,128)(2,1)S(1)}, bf16[512,2048]{1,0:T(8,128)(2,1)}, u32[]{:S(2)}, u32[]{:S(2)}) %collective-permute-start.1) | collective-permute-done | bytes 2097184 | tf_op jit(solution)/shard_map/ppermute | solution.py:345
  51.3 4.0 %collective-permute-start.8 = (bf16[256,512]{1,0:T(8,128)(2,1)}, bf16[256,512]{1,0:T(8,128)(2,1)}, u32[]{:S(2)}, u32[]{:S(2)}) collective-permute-start(bf16[256,512]{1,0:T(8,128)(2,1)} %get-tuple-element.41), channel_id=1, source_target_pairs={{0,4},{4,0},{1,5},{5,1},{2,6},{6,2},{3,7},{7,3},{8,12},{12,8},{9,1... | collective-permute-start | bytes 786440 | tf_op jit(solution)/shard_map/ppermute | solution.py:358
  58.0 2.8 %constant_dynamic-slice_fusion.2 = (bf16[512,1024]{1,0:T(8,128)(2,1)}, bf16[512,1024]{1,0:T(8,128)(2,1)S(1)}) fusion(bf16[512,2048]{1,0:T(8,128)(2,1)} %fusion.1, s32[]{:T(128)S(6)} %select_n.96, s32[]{:T(128)S(6)} %select_n.95), kind=kLoop, calls=%fused_computation.25 | loop fusion | bytes 4194312 | tf_op jit(solution)/shard_map/dynamic_slice | solution.py:296
  60.8 3.6 %collective-permute-done.2 = s32[1]{0:T(128)} collective-permute-done((s32[1]{0:T(128)}, s32[1]{0:T(128)}, u32[]{:S(2)}, u32[]{:S(2)}) %collective-permute-start.2) | collective-permute-done | bytes 36 | tf_op jit(solution)/shard_map/ppermute | solution.py:346
  74.1 6.9 %norm.1 = (bf16[512,2048]{1,0:T(8,128)(2,1)}, bf16[512,2048]{1,0:T(8,128)(2,1)}, f32[512,128]{1,0:T(8,128)S(1)}) custom-call(s32[6]{0:T(128)S(1)} %concatenate.52.refs_0_.at, bf16[512,2048]{1,0:T(8,128)(2,1)S(1)} %bitcast.18, bf16[512,2048]{1,0:T(8,128)(2,1)} %collective-permute-done.3.refs_2_.refs_5_, bf16[512,2048]{1,0:T(8,128)(2,1)} %collective-permute-done.1.refs_3_, ...), custom_call_target="tpu_custom_call" | custom-call | flops 16777216 | bytes 8388608 | tf_op jit(solution)/shard_map/norm/pallas_call | solution.py:74
  81.0 8.6 %collective-permute-start.12 = (bf16[512,2048]{1,0:T(8,128)(2,1)}, bf16[512,2048]{1,0:T(8,128)(2,1)S(1)}, u32[]{:S(2)}, u32[]{:S(2)}) collective-permute-start(bf16[512,2048]{1,0:T(8,128)(2,1)} %get-tuple-element.46.enc_other), channel_id=1, source_target_pairs={{0,2},{2,0},{1,3},{3,1},{4,6},{6,4},{5,7},{7,5},{8,10},{10,8},{9,1... | collective-permute-start | bytes 6291464 | tf_op jit(solution)/shard_map/ppermute | solution.py:406
  89.6 2.8 %fusion.10.part = f32[512,512]{1,0:T(8,128)S(1)} fusion(bf16[512,2048]{1,0:T(8,128)(2,1)} %get-tuple-element.45.refs_1_, bf16[2048,512]{1,0:T(8,128)(2,1)S(1)} %copy-done.11), kind=kOutput, calls=%fused_computation.31 | convolution fusion | flops 1073741824 | bytes 5242880 | tf_op jit(solution)/shard_map/dot_general | solution.py:25
  92.5 11.1 %attend.2 = (bf16[512,1024]{1,0:T(8,128)(2,1)}, bf16[512,512]{1,0:T(8,128)(2,1)S(1)}) custom-call(s32[6]{0:T(128)S(1)} %concatenate.52.refs_0_.at, f32[512,512]{1,0:T(8,128)S(1)} %fusion.10.part, bf16[512,2048]{1,0:T(8,128)(2,1)} %get-tuple-element.46.enc_other, bf16[2048,512]{1,0:T(8,128)(2,1)} %collective-permute-done.11.w_other.other_0, ...), custom_call_target="tpu_custom_call" | custom-call | flops 4026531840 | bytes 8388608 | tf_op jit(solution)/shard_map/attend/pallas_call | solution.py:137
  106.7 6.3 %weight_grad.2 = bf16[2048,512]{1,0:T(8,128)(2,1)} custom-call(s32[6]{0:T(128)S(1)} %concatenate.52.refs_0_.at, bf16[512,2048]{1,0:T(8,128)(2,1)} %get-tuple-element.45.refs_1_, bf16[512,2048]{1,0:T(8,128)(2,1)} %copy-done.8, bf16[512,512]{1,0:T(8,128)(2,1)S(1)} %get-tuple-element.55.refs_3_.gkv_0, bf16[512,512]{1,0:T(8,128)(2,1)S(1)} %collective-permute-done.13.refs_4_), custom_call_target="tpu_custom_call" | custom-call | flops 33554432 | tf_op jit(solution)/shard_map/weight_grad/pallas_call | solution.py:166
  113.3 5.2 %all-gather.5.cloned.1.call-done.own_1 = bf16[2048,512]{1,0:T(8,128)(2,1)} async-done(((bf16[512,512]{1,0:T(8,128)(2,1)}), bf16[2048,512]{1,0:T(8,128)(2,1)}) %all-gather.5.cloned.1.call-update) | async-done | bytes 2097168 | tf_op jit(solution)/shard_map/all_gather | solution.py:420
  118.5 3.5 %fusion.11.part = f32[512,512]{1,0:T(8,128)S(1)} fusion(bf16[512,2048]{1,0:T(8,128)(2,1)} %get-tuple-element.45.refs_1_, bf16[2048,512]{1,0:T(8,128)(2,1)} %all-gather.5.cloned.1.call-done.own_1), kind=kOutput, calls=%fused_computation.32 | convolution fusion | flops 1073741824 | bytes 5242880 | tf_op jit(solution)/shard_map/dot_general | solution.py:25
  124.2 11.3 %attend.3 = (bf16[512,1024]{1,0:T(8,128)(2,1)}, bf16[512,512]{1,0:T(8,128)(2,1)S(1)}) custom-call(s32[6]{0:T(128)S(1)} %concatenate.52.refs_0_.at, f32[512,512]{1,0:T(8,128)S(1)} %fusion.11.part, bf16[512,2048]{1,0:T(8,128)(2,1)} %get-tuple-element.46.enc_other, bf16[2048,512]{1,0:T(8,128)(2,1)} %copy-done.12, ...), custom_call_target="tpu_custom_call", output_to_operand_aliasing={{0}: (7, {})} | custom-call | flops 4026531840 | bytes 8388608 | tf_op jit(solution)/shard_map/attend/pallas_call | solution.py:137
  136.3 6.7 %enc_grad.2 = (bf16[256,2048]{1,0:T(8,128)(2,1)}, bf16[256,2048]{1,0:T(8,128)(2,1)}) custom-call(s32[6]{0:T(128)S(1)} %concatenate.52.refs_0_.at, bf16[512,512]{1,0:T(8,128)(2,1)} %copy-done.5, bf16[512,512]{1,0:T(8,128)(2,1)} %copy-done.6, bf16[2048,512]{1,0:T(8,128)(2,1)} %all-gather.3.cloned.1.call-done.own_0, ...), custom_call_target="tpu_custom_call" | custom-call | flops 4294967296 | bytes 8388608 | tf_op jit(solution)/shard_map/enc_grad/pallas_call | solution.py:280
  144.1 6.3 %weight_grad.3 = bf16[2048,512]{1,0:T(8,128)(2,1)} custom-call(s32[6]{0:T(128)S(1)} %concatenate.52.refs_0_.at, bf16[512,2048]{1,0:T(8,128)(2,1)} %get-tuple-element.45.refs_1_, bf16[512,2048]{1,0:T(8,128)(2,1)} %copy-done.8, bf16[512,512]{1,0:T(8,128)(2,1)S(1)} %copy-done.7, bf16[512,512]{1,0:T(8,128)(2,1)S(1)} %collective-permute-done.17.refs_4_), custom_call_target="tpu_custom_call" | custom-call | flops 33554432 | tf_op jit(solution)/shard_map/weight_grad/pallas_call | solution.py:166
  153.5 7.2 %collective-permute-start.21 = (bf16[512,1024]{1,0:T(8,128)(2,1)}, bf16[512,1024]{1,0:T(8,128)(2,1)}, u32[]{:S(2)}, u32[]{:S(2)}) collective-permute-start(bf16[512,1024]{1,0:T(8,128)(2,1)} %get-tuple-element.58), channel_id=1, source_target_pairs={{0,2},{1,3},{8,10},{9,11},{16,18},{17,19},{24,26},{25,27}} | collective-permute-start | bytes 3145736 | tf_op jit(solution)/shard_map/ppermute | solution.py:449
  160.7 6.6 %enc_grad.3 = (bf16[256,2048]{1,0:T(8,128)(2,1)}, bf16[256,2048]{1,0:T(8,128)(2,1)}) custom-call(s32[6]{0:T(128)S(1)} %concatenate.52.refs_0_.at, bf16[512,512]{1,0:T(8,128)(2,1)} %copy-done.5, bf16[512,512]{1,0:T(8,128)(2,1)} %copy-done.6, bf16[2048,512]{1,0:T(8,128)(2,1)} %all-gather.3.cloned.1.call-done.own_0, ...), custom_call_target="tpu_custom_call" | custom-call | flops 4294967296 | bytes 8388608 | tf_op jit(solution)/shard_map/enc_grad/pallas_call | solution.py:280
  167.3 2.8 %add_convert_fusion.1 = bf16[256,2048]{1,0:T(8,128)(2,1)} fusion(bf16[256,2048]{1,0:T(8,128)(2,1)S(1)} %collective-permute-done.15, bf16[256,2048]{1,0:T(8,128)(2,1)} %get-tuple-element.56.refs_1_), kind=kLoop, calls=%fused_computation.5 | loop fusion | flops 2097152 | bytes 3145728 | tf_op jit(solution)/shard_map/convert_element_type | solution.py:460
  171.3 3.4 %collective-permute-start.16 = (bf16[256,2048]{1,0:T(8,128)(2,1)}, bf16[256,2048]{1,0:T(8,128)(2,1)}, u32[]{:S(2)}, u32[]{:S(2)}) collective-permute-start(bf16[256,2048]{1,0:T(8,128)(2,1)} %get-tuple-element.53), channel_id=1, source_target_pairs={{0,1},{1,0},{6,7},{7,6},{8,9},{9,8},{14,15},{15,14},{16,17},{17,16... | collective-permute-start | bytes 3145736 | tf_op jit(solution)/shard_map/ppermute | solution.py:327
  174.8 2.4 collective-permute-start.18
  181.2 3.7 %maximum_select_fusion.refs_4_ = bf16[512,2048]{1,0:T(8,128)(2,1)} fusion(bf16[512,1024]{1,0:T(8,128)(2,1)} %collective-permute-done.19, bf16[512,1024]{1,0:T(8,128)(2,1)S(1)} %broadcast_select_fusion, pred[]{:T(512)S(6)} %eq.15), kind=kLoop, calls=%fused_computation.3 | loop fusion | flops 9437184 | bytes 4194305 | tf_op jit(solution)/shard_map/jit(_where)/select_n | solution.py:300
  187.0 13.2 %collective-permute-done.18.refs_2_ = bf16[256,2048]{1,0:T(8,128)(2,1)} collective-permute-done((bf16[256,2048]{1,0:T(8,128)(2,1)}, bf16[256,2048]{1,0:T(8,128)(2,1)}, u32[]{:S(2)}, u32[]{:S(2)}) %collective-permute-start.18) | collective-permute-done | bytes 1048608 | tf_op jit(solution)/shard_map/ppermute | solution.py:327
  200.3 4.0 %collect.2 = (bf16[256,2048]{1,0:T(8,128)(2,1)}, f32[2,1,2048]{2,1,0:T(1,128)S(1)}) custom-call(s32[6]{0:T(128)S(1)} %concatenate.52.refs_0_.at, bf16[256,2048]{1,0:T(8,128)(2,1)S(1)} %copy-done.2, bf16[256,2048]{1,0:T(8,128)(2,1)} %collective-permute-done.18.refs_2_, bf16[256,2048]{1,0:T(8,128)(2,1)} %collective-permute-done.20.refs_3_, ...), custom_call_target="tpu_custom_call" | custom-call | flops 4194304 | bytes 6291456 | tf_op jit(solution)/shard_map/collect/pallas_call | solution.py:198
  204.3 4.0 %collect.3 = (bf16[256,2048]{1,0:T(8,128)(2,1)}, f32[2,1,2048]{2,1,0:T(1,128)S(1)}) custom-call(s32[6]{0:T(128)S(1)} %concatenate.52.refs_0_.at, bf16[256,2048]{1,0:T(8,128)(2,1)S(1)} %copy-done.1, bf16[256,2048]{1,0:T(8,128)(2,1)} %collective-permute-done.16.refs_2_, bf16[256,2048]{1,0:T(8,128)(2,1)} %collective-permute-done.23.refs_3_, ...), custom_call_target="tpu_custom_call" | custom-call | flops 4194304 | bytes 6291456 | tf_op jit(solution)/shard_map/collect/pallas_call | solution.py:198
  212.9 3.4 %collective-permute-start.25 = (f32[2048]{0:T(1024)S(1)}, f32[2048]{0:T(1024)S(1)}, u32[]{:S(2)}, u32[]{:S(2)}) collective-permute-start(f32[2048]{0:T(1024)S(1)} %add_select_fusion), channel_id=1, source_target_pairs={{0,6},{6,0},{2,4},{4,2},{1,7},{7,1},{3,5},{5,3},{8,14},{14,8},{10,... | collective-permute-start | bytes 24584 | tf_op jit(solution)/shard_map/ppermute | solution.py:487
  216.3 11.7 %collective-permute-done.25 = f32[2048]{0:T(1024)S(1)} collective-permute-done((f32[2048]{0:T(1024)S(1)}, f32[2048]{0:T(1024)S(1)}, u32[]{:S(2)}, u32[]{:S(2)}) %collective-permute-start.25) | collective-permute-done | bytes 8224 | tf_op jit(solution)/shard_map/ppermute | solution.py:487
  228.0 3.6 %collective-permute-done.26 = f32[2048]{0:T(1024)S(1)} collective-permute-done((f32[2048]{0:T(1024)S(1)}, f32[2048]{0:T(1024)S(1)}, u32[]{:S(2)}, u32[]{:S(2)}) %collective-permute-start.26) | collective-permute-done | bytes 8224 | tf_op jit(solution)/shard_map/ppermute | solution.py:490
  232.3 3.9 %collective-permute-done.27 = f32[2048]{0:T(1024)S(1)} collective-permute-done((f32[2048]{0:T(1024)S(1)}, f32[2048]{0:T(1024)S(1)}, u32[]{:S(2)}, u32[]{:S(2)}) %collective-permute-start.27) | collective-permute-done | bytes 8224 | tf_op jit(solution)/shard_map/ppermute | solution.py:490
  238.0 4.9 %assemble.1 = bf16[512,2048]{1,0:T(8,128)(2,1)} custom-call(s32[6]{0:T(128)S(1)} %concatenate.52.refs_0_.at, bf16[256,2048]{1,0:T(8,128)(2,1)} %get-tuple-element.62.refs_0_, bf16[256,2048]{1,0:T(8,128)(2,1)} %get-tuple-element.66.refs_1_, bf16[256,2048]{1,0:T(8,128)(2,1)S(1)} %collective-permute-done.24.refs_2_, ...), custom_call_target="tpu_custom_call" | custom-call | flops 1048576 | bytes 4194304 | tf_op jit(solution)/shard_map/assemble/pallas_call | solution.py:240
  (108 shorter events, 49.7 us)
Async XLA Ops:
  7.2 65.1 %all-gather.3.cloned.1.call-start = ((), (), s32[]{:S(2)}) async-start(), calls=%async_computation.2 | async-start | bytes 2621440 | tf_op jit(solution)/shard_map/all_gather | solution.py:420
  7.2 18.7 %collective-permute-start.3 = (bf16[512,2048]{1,0:T(8,128)(2,1)}, bf16[512,2048]{1,0:T(8,128)(2,1)}, u32[]{:S(2)}, u32[]{:S(2)}) collective-permute-start(bf16[512,2048]{1,0:T(8,128)(2,1)} %bitcast.15), channel_id=1, source_target_pairs={{4,6},{5,7},{12,14},{13,15},{20,22},{21,23},{28,30},{29,31}} | collective-permute-start | bytes 6291464 | tf_op jit(solution)/shard_map/ppermute | solution.py:340
  11.3 8.7 %collective-permute-start = (bf16[256,512]{1,0:T(8,128)(2,1)S(1)}, bf16[256,512]{1,0:T(8,128)(2,1)S(1)}, u32[]{:S(2)}, u32[]{:S(2)}) collective-permute-start(bf16[256,512]{1,0:T(8,128)(2,1)S(1)} %get-tuple-element.74), channel_id=1, source_target_pairs={{0,4},{4,0},{1,5},{5,1},{2,6},{6,2},{3,7},{7,3},{8,12},{12,8},{9,1... | collective-permute-start | bytes 786440 | tf_op jit(solution)/shard_map/ppermute | solution.py:339
  20.8 27.2 %collective-permute-start.1 = (bf16[512,2048]{1,0:T(8,128)(2,1)S(1)}, bf16[512,2048]{1,0:T(8,128)(2,1)}, u32[]{:S(2)}, u32[]{:S(2)}) collective-permute-start(bf16[512,2048]{1,0:T(8,128)(2,1)S(1)} %bitcast.16), channel_id=1, source_target_pairs={{0,4},{4,2},{1,5},{5,3},{8,12},{12,10},{9,13},{13,11},{16,20},{20,... | collective-permute-start | bytes 6291464 | tf_op jit(solution)/shard_map/ppermute | solution.py:345
  25.9 92.6 %all-gather.5.cloned.1.call-start = ((), (), s32[]{:S(2)}) async-start(), calls=%async_computation.3 | async-start | bytes 2621440 | tf_op jit(solution)/shard_map/all_gather | solution.py:420
  25.9 24.1 %collective-permute-start.6 = (bf16[512,2048]{1,0:T(8,128)(2,1)}, bf16[512,2048]{1,0:T(8,128)(2,1)S(1)}, u32[]{:S(2)}, u32[]{:S(2)}) collective-permute-start(bf16[512,2048]{1,0:T(8,128)(2,1)} %collective-permute-done.3.refs_2_.refs_5_), channel_id=1, source_target_pairs={{6,7},{7,6},{14,15},{15,14},{22,23},{23,22},{30,31},{31,30}} | collective-permute-start | bytes 6291464 | tf_op jit(solution)/shard_map/ppermute | solution.py:327
  26.7 3.7 %collective-permute-start.4 = (bf16[2048]{0:T(1024)(128)(2,1)S(1)}, bf16[2048]{0:T(1024)(128)(2,1)S(1)}, u32[]{:S(2)}, u32[]{:S(2)}) collective-permute-start(bf16[2048]{0:T(1024)(128)(2,1)S(1)} %copy-done.10), channel_id=1, source_target_pairs={{0,1},{1,0},{2,3},{3,2},{4,5},{5,4},{6,7},{7,6},{8,9},{9,8},{10,11... | collective-permute-start | bytes 12296 | tf_op jit(solution)/shard_map/ppermute | solution.py:342
  30.4 42.0 %collective-permute-start.5 = (bf16[512,2048]{1,0:T(8,128)(2,1)S(1)}, bf16[512,2048]{1,0:T(8,128)(2,1)}, u32[]{:S(2)}, u32[]{:S(2)}) collective-permute-start(bf16[512,2048]{1,0:T(8,128)(2,1)S(1)} %bitcast.17), channel_id=1, source_target_pairs={{0,1},{1,0},{8,9},{9,8},{16,17},{17,16},{24,25},{25,24}} | collective-permute-start | bytes 6291464 | tf_op jit(solution)/shard_map/ppermute | solution.py:327
  48.0 24.4 %collective-permute-start.7 = (bf16[512,2048]{1,0:T(8,128)(2,1)}, bf16[512,2048]{1,0:T(8,128)(2,1)}, u32[]{:S(2)}, u32[]{:S(2)}) collective-permute-start(bf16[512,2048]{1,0:T(8,128)(2,1)} %collective-permute-done.1.refs_3_), channel_id=1, source_target_pairs={{2,3},{3,2},{4,5},{5,4},{10,11},{11,10},{12,13},{13,12},{18,19},{1... | collective-permute-start | bytes 6291464 | tf_op jit(solution)/shard_map/ppermute | solution.py:327
  51.3 13.8 %collective-permute-start.8 = (bf16[256,512]{1,0:T(8,128)(2,1)}, bf16[256,512]{1,0:T(8,128)(2,1)}, u32[]{:S(2)}, u32[]{:S(2)}) collective-permute-start(bf16[256,512]{1,0:T(8,128)(2,1)} %get-tuple-element.41), channel_id=1, source_target_pairs={{0,4},{4,0},{1,5},{5,1},{2,6},{6,2},{3,7},{7,3},{8,12},{12,8},{9,1... | collective-permute-start | bytes 786440 | tf_op jit(solution)/shard_map/ppermute | solution.py:358
  65.1 7.3 %collective-permute-start.10 = (bf16[512,1024]{1,0:T(8,128)(2,1)}, bf16[512,1024]{1,0:T(8,128)(2,1)}, u32[]{:S(2)}, u32[]{:S(2)}) collective-permute-start(bf16[512,1024]{1,0:T(8,128)(2,1)} %get-tuple-element.43), channel_id=1, source_target_pairs={{2,4},{6,2},{3,5},{7,3},{10,12},{14,10},{11,13},{15,11},{18,20},{2... | collective-permute-start | bytes 3145736 | tf_op jit(solution)/shard_map/ppermute | solution.py:370
  66.8 5.6 %collective-permute-start.9 = (bf16[512,1024]{1,0:T(8,128)(2,1)S(1)}, bf16[512,1024]{1,0:T(8,128)(2,1)}, u32[]{:S(2)}, u32[]{:S(2)}) collective-permute-start(bf16[512,1024]{1,0:T(8,128)(2,1)S(1)} %get-tuple-element.42.refs_0_), channel_id=1, source_target_pairs={{2,0},{3,1},{10,8},{11,9},{18,16},{19,17},{26,24},{27,25}} | collective-permute-start | bytes 3145736 | tf_op jit(solution)/shard_map/ppermute | solution.py:369
  69.9 139.9 %reduce-scatter.3.cloned.1.call-start = ((), (), s32[]{:S(2)}) async-start(), calls=%async_computation.4 | async-start | bytes 2621440 | tf_op jit(solution)/shard_map/reduce_scatter | solution.py:439
  72.3 20.2 %collective-permute-start.11 = (bf16[2048,512]{1,0:T(8,128)(2,1)}, bf16[2048,512]{1,0:T(8,128)(2,1)}, u32[]{:S(2)}, u32[]{:S(2)}) collective-permute-start(bf16[2048,512]{1,0:T(8,128)(2,1)} %all-gather.3.cloned.1.call-done.own_0), channel_id=1, source_target_pairs={{0,2},{2,0},{1,3},{3,1},{4,6},{6,4},{5,7},{7,5},{8,10},{10,8},{9,1... | collective-permute-start | bytes 6291464 | tf_op jit(solution)/shard_map/ppermute | solution.py:423
  81.0 24.5 %collective-permute-start.12 = (bf16[512,2048]{1,0:T(8,128)(2,1)}, bf16[512,2048]{1,0:T(8,128)(2,1)S(1)}, u32[]{:S(2)}, u32[]{:S(2)}) collective-permute-start(bf16[512,2048]{1,0:T(8,128)(2,1)} %get-tuple-element.46.enc_other), channel_id=1, source_target_pairs={{0,2},{2,0},{1,3},{3,1},{4,6},{6,4},{5,7},{7,5},{8,10},{10,8},{9,1... | collective-permute-start | bytes 6291464 | tf_op jit(solution)/shard_map/ppermute | solution.py:406
  113.0 97.8 %reduce-scatter.5.cloned.1.call-start = ((), (), s32[]{:S(2)}) async-start(), calls=%async_computation.5 | async-start | bytes 2621440 | tf_op jit(solution)/shard_map/reduce_scatter | solution.py:439
  118.5 4.4 %collective-permute-start.14 = (bf16[2048,512]{1,0:T(8,128)(2,1)}, bf16[2048,512]{1,0:T(8,128)(2,1)S(1)}, u32[]{:S(2)}, u32[]{:S(2)}) collective-permute-start(bf16[2048,512]{1,0:T(8,128)(2,1)} %all-gather.5.cloned.1.call-done.own_1), channel_id=1, source_target_pairs={{0,2},{2,0},{1,3},{3,1},{4,6},{6,4},{5,7},{7,5},{8,10},{10,8},{9,1... | collective-permute-start | bytes 6291464 | tf_op jit(solution)/shard_map/ppermute | solution.py:423
  135.5 7.5 %collective-permute-start.17 = (bf16[512,512]{1,0:T(8,128)(2,1)S(1)}, bf16[512,512]{1,0:T(8,128)(2,1)S(1)}, u32[]{:S(2)}, u32[]{:S(2)}) collective-permute-start(bf16[512,512]{1,0:T(8,128)(2,1)S(1)} %get-tuple-element.50.gkv_1.refs_3_), channel_id=1, source_target_pairs={{0,2},{2,0},{1,3},{3,1},{4,6},{6,4},{5,7},{7,5},{8,10},{10,8},{9,1... | collective-permute-start | bytes 1572872 | tf_op jit(solution)/shard_map/ppermute | solution.py:427
  150.3 16.9 %collective-permute-start.15 = (bf16[256,2048]{1,0:T(8,128)(2,1)}, bf16[256,2048]{1,0:T(8,128)(2,1)S(1)}, u32[]{:S(2)}, u32[]{:S(2)}) collective-permute-start(bf16[256,2048]{1,0:T(8,128)(2,1)} %get-tuple-element.57), channel_id=1, source_target_pairs={{2,3},{3,2},{4,5},{5,4},{10,11},{11,10},{12,13},{13,12},{18,19},{1... | collective-permute-start | bytes 3145736 | tf_op jit(solution)/shard_map/ppermute | solution.py:327
  151.1 19.0 %collective-permute-start.19 = (bf16[512,1024]{1,0:T(8,128)(2,1)}, bf16[512,1024]{1,0:T(8,128)(2,1)}, u32[]{:S(2)}, u32[]{:S(2)}) collective-permute-start(bf16[512,1024]{1,0:T(8,128)(2,1)} %get-tuple-element.58), channel_id=1, source_target_pairs={{4,2},{2,6},{5,3},{3,7},{12,10},{10,14},{13,11},{11,15},{20,18},{1... | collective-permute-start | bytes 3145736 | tf_op jit(solution)/shard_map/ppermute | solution.py:450
  152.7 24.4 %collective-permute-start.22 = (bf16[256,2048]{1,0:T(8,128)(2,1)}, bf16[256,2048]{1,0:T(8,128)(2,1)S(1)}, u32[]{:S(2)}, u32[]{:S(2)}) collective-permute-start(bf16[256,2048]{1,0:T(8,128)(2,1)} %get-tuple-element.53), channel_id=1, source_target_pairs={{2,3},{3,2},{4,5},{5,4},{10,11},{11,10},{12,13},{13,12},{18,19},{1... | collective-permute-start | bytes 3145736 | tf_op jit(solution)/shard_map/ppermute | solution.py:327
  153.5 26.4 %collective-permute-start.21 = (bf16[512,1024]{1,0:T(8,128)(2,1)}, bf16[512,1024]{1,0:T(8,128)(2,1)}, u32[]{:S(2)}, u32[]{:S(2)}) collective-permute-start(bf16[512,1024]{1,0:T(8,128)(2,1)} %get-tuple-element.58), channel_id=1, source_target_pairs={{0,2},{1,3},{8,10},{9,11},{16,18},{17,19},{24,26},{25,27}} | collective-permute-start | bytes 3145736 | tf_op jit(solution)/shard_map/ppermute | solution.py:449
  170.0 17.0 %collective-permute-start.20 = (bf16[256,2048]{1,0:T(8,128)(2,1)}, bf16[256,2048]{1,0:T(8,128)(2,1)}, u32[]{:S(2)}, u32[]{:S(2)}) collective-permute-start(bf16[256,2048]{1,0:T(8,128)(2,1)} %add_convert_fusion.1), channel_id=1, source_target_pairs={{4,0},{2,6},{5,1},{3,7},{12,8},{10,14},{13,9},{11,15},{20,16},{18,... | collective-permute-start | bytes 3145736 | tf_op jit(solution)/shard_map/ppermute | solution.py:465
  171.3 33.0 %collective-permute-start.16 = (bf16[256,2048]{1,0:T(8,128)(2,1)}, bf16[256,2048]{1,0:T(8,128)(2,1)}, u32[]{:S(2)}, u32[]{:S(2)}) collective-permute-start(bf16[256,2048]{1,0:T(8,128)(2,1)} %get-tuple-element.53), channel_id=1, source_target_pairs={{0,1},{1,0},{6,7},{7,6},{8,9},{9,8},{14,15},{15,14},{16,17},{17,16... | collective-permute-start | bytes 3145736 | tf_op jit(solution)/shard_map/ppermute | solution.py:327
  174.8 25.5 %collective-permute-start.18 = (bf16[256,2048]{1,0:T(8,128)(2,1)}, bf16[256,2048]{1,0:T(8,128)(2,1)}, u32[]{:S(2)}, u32[]{:S(2)}) collective-permute-start(bf16[256,2048]{1,0:T(8,128)(2,1)} %get-tuple-element.57), channel_id=1, source_target_pairs={{0,1},{1,0},{6,7},{7,6},{8,9},{9,8},{14,15},{15,14},{16,17},{17,16... | collective-permute-start | bytes 3145736 | tf_op jit(solution)/shard_map/ppermute | solution.py:327
  178.6 25.7 %collective-permute-start.23 = (bf16[256,2048]{1,0:T(8,128)(2,1)}, bf16[256,2048]{1,0:T(8,128)(2,1)}, u32[]{:S(2)}, u32[]{:S(2)}) collective-permute-start(bf16[256,2048]{1,0:T(8,128)(2,1)} %add_convert_fusion), channel_id=1, source_target_pairs={{4,0},{2,6},{5,1},{3,7},{12,8},{10,14},{13,9},{11,15},{20,16},{18,... | collective-permute-start | bytes 3145736 | tf_op jit(solution)/shard_map/ppermute | solution.py:465
  208.3 29.7 %collective-permute-start.28 = (bf16[256,2048]{1,0:T(8,128)(2,1)}, bf16[256,2048]{1,0:T(8,128)(2,1)S(1)}, u32[]{:S(2)}, u32[]{:S(2)}) collective-permute-start(bf16[256,2048]{1,0:T(8,128)(2,1)} %get-tuple-element.66.refs_1_), channel_id=1, source_target_pairs={{6,4},{7,5},{14,12},{15,13},{22,20},{23,21},{30,28},{31,29}} | collective-permute-start | bytes 3145736 | tf_op jit(solution)/shard_map/ppermute | solution.py:485
  209.0 29.0 %collective-permute-start.24 = (bf16[256,2048]{1,0:T(8,128)(2,1)}, bf16[256,2048]{1,0:T(8,128)(2,1)S(1)}, u32[]{:S(2)}, u32[]{:S(2)}) collective-permute-start(bf16[256,2048]{1,0:T(8,128)(2,1)} %get-tuple-element.62.refs_0_), channel_id=1, source_target_pairs={{6,4},{7,5},{14,12},{15,13},{22,20},{23,21},{30,28},{31,29}} | collective-permute-start | bytes 3145736 | tf_op jit(solution)/shard_map/ppermute | solution.py:485
  212.8 30.1 %collective-permute-start.29 = (bf16[256,1024]{1,0:T(8,128)(2,1)}, bf16[256,1024]{1,0:T(8,128)(2,1)S(1)}, u32[]{:S(2)}, u32[]{:S(2)}) collective-permute-start(bf16[256,1024]{1,0:T(8,128)(2,1)} %pad_maximum_fusion.2), channel_id=1, source_target_pairs={{0,4},{4,0},{1,5},{5,1},{2,6},{6,2},{3,7},{7,3},{8,12},{12,8},{9,1... | collective-permute-start | bytes 1572872 | tf_op jit(solution)/shard_map/ppermute | solution.py:448
  212.9 15.1 %collective-permute-start.25 = (f32[2048]{0:T(1024)S(1)}, f32[2048]{0:T(1024)S(1)}, u32[]{:S(2)}, u32[]{:S(2)}) collective-permute-start(f32[2048]{0:T(1024)S(1)} %add_select_fusion), channel_id=1, source_target_pairs={{0,6},{6,0},{2,4},{4,2},{1,7},{7,1},{3,5},{5,3},{8,14},{14,8},{10,... | collective-permute-start | bytes 24584 | tf_op jit(solution)/shard_map/ppermute | solution.py:487
  228.0 3.7 %collective-permute-start.26 = (f32[2048]{0:T(1024)S(1)}, f32[2048]{0:T(1024)S(1)}, u32[]{:S(2)}, u32[]{:S(2)}) collective-permute-start(f32[2048]{0:T(1024)S(1)} %add.63), channel_id=1, source_target_pairs={{0,8},{8,0},{16,24},{24,16},{1,9},{9,1},{17,25},{25,17},{2,10},{10... | collective-permute-start | bytes 24584 | tf_op jit(solution)/shard_map/ppermute | solution.py:490
  231.6 4.5 %collective-permute-start.27 = (f32[2048]{0:T(1024)S(1)}, f32[2048]{0:T(1024)S(1)}, u32[]{:S(2)}, u32[]{:S(2)}) collective-permute-start(f32[2048]{0:T(1024)S(1)} %add.64), channel_id=1, source_target_pairs={{0,16},{8,24},{16,0},{24,8},{1,17},{9,25},{17,1},{25,9},{2,18},{10... | collective-permute-start | bytes 24584 | tf_op jit(solution)/shard_map/ppermute | solution.py:490
  (16 other events, 121.6 us)
Sparse Core Ops, SparseCore 0:
  26.0 46.2 all-gather.2
  73.8 44.6 all-gather.4
  120.8 42.5 reduce-scatter.2
  166.2 43.1 reduce-scatter.4

commit v15 on v13

--- a/solution.py
+++ b/solution.py
@@ -227,7 +227,7 @@
 
 def assemble(at, sums, moved, dec):
     length, width = dec.shape
-    step = 128
+    step = 256
     each = length // step // PARTS
 
     def piece(part, row):
@@ -248,7 +248,7 @@
         ),
         out_shape=jax.ShapeDtypeStruct((length, width), BF16),
         cost_estimate=cost(length * width, 4),
-        compiler_params=params(14),
+        compiler_params=params(24),
         name="assemble",
     )(at, *sums, *moved, *in_hbm(dec))
 

time: 247 us -> 246 us (level)
  transfers between devices with their start and end apart: 36 -> 36, of which waited for: 14 -> 14; matrix products, arithmetic and copies ran while one was open for 12% -> 12% of each run, Pallas kernels for 28% -> 27%
where the time goes in v15:
time: 246 us; the launch traced here: 245 us
  Pallas kernels  67.3 us (27%)
  starting transfers between devices  63.1 us (26%)
  waiting for transfers between devices  59.3 us (24%)
  other arithmetic  17.4 us (7%)
  between operations  16 us (7%)
  local copies, waits for them, and re-layouts  15.6 us (6%)
  matrix products  6.3 us (3%)
    pallas_call x2, Pallas kernels, attend(): pl.pallas_call(attend_kernel, grid_spec=pltpu.PrefetchScalarGridSpec(num_...  22.3 us
    ppermute x7, starting transfers between devices, across(): lax.ppermute(value, ('y', 'phase', 'mp'), [(a * shards + s, b * shards +...  14.3 us
    ppermute x1, waiting for transfers between devices, on_device(): there = lax.ppermute(after(packed, blocks[0]), PLANE, [(0, 2), (2, 1)])  14.3 us
    pallas_call x2, Pallas kernels, enc_grad(): pl.pallas_call(enc_grad_kernel, grid_spec=pltpu.PrefetchScalarGridSpec(nu...  13.3 us
    pallas_call x2, Pallas kernels, weight_grad(): pl.pallas_call(lambda *refs: weight_grad_kernel(scale, *refs), grid_spec=...  12.5 us
    ppermute x1, starting transfers between devices, on_device(): enc_mate = lax.ppermute(enc_other, 'phase', SWAP)  8.63 us
    unnamed x32, local copies, waits for them, and re-layouts  8.01 us
    pallas_call x2, Pallas kernels, collect(): pl.pallas_call(lambda *refs: collect_kernel(scale, *refs), grid_spec=pltp...  7.97 us
  transfers between devices with their start and end apart: 36, of which 14 were waited for; matrix products, arithmetic and copies ran while one was open for 12% of the time, Pallas kernels for 27%

profile of v15, /device:TPU:0, one launch (start us, length us, event | category | flops | bytes accessed | tf_op | source)
XLA Modules:
  0.0 245.0 jit_solution(2974567449795512409)
XLA Ops:
  11.3 4.0 %collective-permute-start = (bf16[256,512]{1,0:T(8,128)(2,1)S(1)}, bf16[256,512]{1,0:T(8,128)(2,1)S(1)}, u32[]{:S(2)}, u32[]{:S(2)}) collective-permute-start(bf16[256,512]{1,0:T(8,128)(2,1)S(1)} %get-tuple-element.76), channel_id=1, source_target_pairs={{0,4},{4,0},{1,5},{5,1},{2,6},{6,2},{3,7},{7,3},{8,12},{12,8},{9,1... | collective-permute-start | bytes 786440 | tf_op jit(solution)/shard_map/ppermute | solution.py:339
  15.4 4.6 %collective-permute-done = bf16[256,512]{1,0:T(8,128)(2,1)S(1)} collective-permute-done((bf16[256,512]{1,0:T(8,128)(2,1)S(1)}, bf16[256,512]{1,0:T(8,128)(2,1)S(1)}, u32[]{:S(2)}, u32[]{:S(2)}) %collective-permute-start) | collective-permute-done | bytes 262176 | tf_op jit(solution)/shard_map/ppermute | solution.py:339
  20.9 5.0 %collective-permute-start.1 = (bf16[512,2048]{1,0:T(8,128)(2,1)S(1)}, bf16[512,2048]{1,0:T(8,128)(2,1)}, u32[]{:S(2)}, u32[]{:S(2)}) collective-permute-start(bf16[512,2048]{1,0:T(8,128)(2,1)S(1)} %bitcast.16), channel_id=1, source_target_pairs={{0,4},{4,2},{1,5},{5,3},{8,12},{12,10},{9,13},{13,11},{16,20},{20,... | collective-permute-start | bytes 6291464 | tf_op jit(solution)/shard_map/ppermute | solution.py:345
  30.4 3.4 %collective-permute-start.5 = (bf16[512,2048]{1,0:T(8,128)(2,1)S(1)}, bf16[512,2048]{1,0:T(8,128)(2,1)}, u32[]{:S(2)}, u32[]{:S(2)}) collective-permute-start(bf16[512,2048]{1,0:T(8,128)(2,1)S(1)} %bitcast.17), channel_id=1, source_target_pairs={{0,1},{1,0},{8,9},{9,8},{16,17},{17,16},{24,25},{25,24}} | collective-permute-start | bytes 6291464 | tf_op jit(solution)/shard_map/ppermute | solution.py:327
  33.8 14.3 %collective-permute-done.1.refs_3_ = bf16[512,2048]{1,0:T(8,128)(2,1)} collective-permute-done((bf16[512,2048]{1,0:T(8,128)(2,1)S(1)}, bf16[512,2048]{1,0:T(8,128)(2,1)}, u32[]{:S(2)}, u32[]{:S(2)}) %collective-permute-start.1) | collective-permute-done | bytes 2097184 | tf_op jit(solution)/shard_map/ppermute | solution.py:345
  51.3 4.1 %collective-permute-start.8 = (bf16[256,512]{1,0:T(8,128)(2,1)}, bf16[256,512]{1,0:T(8,128)(2,1)}, u32[]{:S(2)}, u32[]{:S(2)}) collective-permute-start(bf16[256,512]{1,0:T(8,128)(2,1)} %get-tuple-element.42), channel_id=1, source_target_pairs={{0,4},{4,0},{1,5},{5,1},{2,6},{6,2},{3,7},{7,3},{8,12},{12,8},{9,1... | collective-permute-start | bytes 786440 | tf_op jit(solution)/shard_map/ppermute | solution.py:358
  58.0 2.7 %constant_dynamic-slice_fusion.2 = (bf16[512,1024]{1,0:T(8,128)(2,1)}, bf16[512,1024]{1,0:T(8,128)(2,1)S(1)}) fusion(bf16[512,2048]{1,0:T(8,128)(2,1)} %fusion.1, s32[]{:T(128)S(6)} %select_n.97, s32[]{:T(128)S(6)} %select_n.96), kind=kLoop, calls=%fused_computation.24 | loop fusion | bytes 4194312 | tf_op jit(solution)/shard_map/dynamic_slice | solution.py:296
  60.8 3.6 %collective-permute-done.2 = s32[1]{0:T(128)} collective-permute-done((s32[1]{0:T(128)}, s32[1]{0:T(128)}, u32[]{:S(2)}, u32[]{:S(2)}) %collective-permute-start.2) | collective-permute-done | bytes 36 | tf_op jit(solution)/shard_map/ppermute | solution.py:346
  74.0 6.9 %norm.1 = (bf16[512,2048]{1,0:T(8,128)(2,1)}, bf16[512,2048]{1,0:T(8,128)(2,1)}, f32[512,128]{1,0:T(8,128)S(1)}) custom-call(s32[6]{0:T(128)S(1)} %concatenate.50.refs_0_.at, bf16[512,2048]{1,0:T(8,128)(2,1)S(1)} %bitcast.18, bf16[512,2048]{1,0:T(8,128)(2,1)} %collective-permute-done.3.refs_2_.refs_5_, bf16[512,2048]{1,0:T(8,128)(2,1)} %collective-permute-done.1.refs_3_, ...), custom_call_target="tpu_custom_call" | custom-call | flops 16777216 | bytes 8388608 | tf_op jit(solution)/shard_map/norm/pallas_call | solution.py:74
  81.0 8.6 %collective-permute-start.12 = (bf16[512,2048]{1,0:T(8,128)(2,1)}, bf16[512,2048]{1,0:T(8,128)(2,1)S(1)}, u32[]{:S(2)}, u32[]{:S(2)}) collective-permute-start(bf16[512,2048]{1,0:T(8,128)(2,1)} %get-tuple-element.47.enc_other), channel_id=1, source_target_pairs={{0,2},{2,0},{1,3},{3,1},{4,6},{6,4},{5,7},{7,5},{8,10},{10,8},{9,1... | collective-permute-start | bytes 6291464 | tf_op jit(solution)/shard_map/ppermute | solution.py:406
  89.6 2.8 %fusion.10.part = f32[512,512]{1,0:T(8,128)S(1)} fusion(bf16[512,2048]{1,0:T(8,128)(2,1)} %get-tuple-element.46.refs_1_, bf16[2048,512]{1,0:T(8,128)(2,1)S(1)} %copy-done.14), kind=kOutput, calls=%fused_computation.30 | convolution fusion | flops 1073741824 | bytes 5242880 | tf_op jit(solution)/shard_map/dot_general | solution.py:25
  92.4 11.0 %attend.2 = (bf16[512,1024]{1,0:T(8,128)(2,1)}, bf16[512,512]{1,0:T(8,128)(2,1)S(1)}) custom-call(s32[6]{0:T(128)S(1)} %concatenate.50.refs_0_.at, f32[512,512]{1,0:T(8,128)S(1)} %fusion.10.part, bf16[512,2048]{1,0:T(8,128)(2,1)} %get-tuple-element.47.enc_other, bf16[2048,512]{1,0:T(8,128)(2,1)} %collective-permute-done.11.w_other.other_0, ...), custom_call_target="tpu_custom_call" | custom-call | flops 4026531840 | bytes 8388608 | tf_op jit(solution)/shard_map/attend/pallas_call | solution.py:137
  106.7 6.3 %weight_grad.2 = bf16[2048,512]{1,0:T(8,128)(2,1)} custom-call(s32[6]{0:T(128)S(1)} %concatenate.50.refs_0_.at, bf16[512,2048]{1,0:T(8,128)(2,1)} %get-tuple-element.46.refs_1_, bf16[512,2048]{1,0:T(8,128)(2,1)} %copy-done.8, bf16[512,512]{1,0:T(8,128)(2,1)S(1)} %get-tuple-element.55.refs_3_.gkv_0, bf16[512,512]{1,0:T(8,128)(2,1)S(1)} %collective-permute-done.13.refs_4_), custom_call_target="tpu_custom_call" | custom-call | flops 33554432 | tf_op jit(solution)/shard_map/weight_grad/pallas_call | solution.py:166
  113.2 5.3 %all-gather.5.cloned.1.call-done.own_1 = bf16[2048,512]{1,0:T(8,128)(2,1)} async-done(((bf16[512,512]{1,0:T(8,128)(2,1)}), bf16[2048,512]{1,0:T(8,128)(2,1)}) %all-gather.5.cloned.1.call-update) | async-done | bytes 2097168 | tf_op jit(solution)/shard_map/all_gather | solution.py:420
  118.5 3.5 %fusion.11.part = f32[512,512]{1,0:T(8,128)S(1)} fusion(bf16[512,2048]{1,0:T(8,128)(2,1)} %get-tuple-element.46.refs_1_, bf16[2048,512]{1,0:T(8,128)(2,1)} %all-gather.5.cloned.1.call-done.own_1), kind=kOutput, calls=%fused_computation.31 | convolution fusion | flops 1073741824 | bytes 5242880 | tf_op jit(solution)/shard_map/dot_general | solution.py:25
  124.3 11.3 %attend.3 = (bf16[512,1024]{1,0:T(8,128)(2,1)}, bf16[512,512]{1,0:T(8,128)(2,1)S(1)}) custom-call(s32[6]{0:T(128)S(1)} %concatenate.50.refs_0_.at, f32[512,512]{1,0:T(8,128)S(1)} %fusion.11.part, bf16[512,2048]{1,0:T(8,128)(2,1)} %get-tuple-element.47.enc_other, bf16[2048,512]{1,0:T(8,128)(2,1)} %copy-done.15, ...), custom_call_target="tpu_custom_call", output_to_operand_aliasing={{0}: (7, {})} | custom-call | flops 4026531840 | bytes 8388608 | tf_op jit(solution)/shard_map/attend/pallas_call | solution.py:137
  136.4 6.7 %enc_grad.2 = (bf16[256,2048]{1,0:T(8,128)(2,1)}, bf16[256,2048]{1,0:T(8,128)(2,1)}) custom-call(s32[6]{0:T(128)S(1)} %concatenate.50.refs_0_.at, bf16[512,512]{1,0:T(8,128)(2,1)} %copy-done.5, bf16[512,512]{1,0:T(8,128)(2,1)} %copy-done.6, bf16[2048,512]{1,0:T(8,128)(2,1)} %all-gather.3.cloned.1.call-done.own_0, ...), custom_call_target="tpu_custom_call" | custom-call | flops 4294967296 | bytes 8388608 | tf_op jit(solution)/shard_map/enc_grad/pallas_call | solution.py:280
  144.1 6.3 %weight_grad.3 = bf16[2048,512]{1,0:T(8,128)(2,1)} custom-call(s32[6]{0:T(128)S(1)} %concatenate.50.refs_0_.at, bf16[512,2048]{1,0:T(8,128)(2,1)} %get-tuple-element.46.refs_1_, bf16[512,2048]{1,0:T(8,128)(2,1)} %copy-done.8, bf16[512,512]{1,0:T(8,128)(2,1)S(1)} %copy-done.7, bf16[512,512]{1,0:T(8,128)(2,1)S(1)} %collective-permute-done.15.refs_4_), custom_call_target="tpu_custom_call" | custom-call | flops 33554432 | tf_op jit(solution)/shard_map/weight_grad/pallas_call | solution.py:166
  152.8 5.8 %collective-permute-start.21 = (bf16[512,1024]{1,0:T(8,128)(2,1)}, bf16[512,1024]{1,0:T(8,128)(2,1)}, u32[]{:S(2)}, u32[]{:S(2)}) collective-permute-start(bf16[512,1024]{1,0:T(8,128)(2,1)} %get-tuple-element.58), channel_id=1, source_target_pairs={{0,2},{1,3},{8,10},{9,11},{16,18},{17,19},{24,26},{25,27}} | collective-permute-start | bytes 3145736 | tf_op jit(solution)/shard_map/ppermute | solution.py:449
  160.2 6.6 %enc_grad.3 = (bf16[256,2048]{1,0:T(8,128)(2,1)}, bf16[256,2048]{1,0:T(8,128)(2,1)}) custom-call(s32[6]{0:T(128)S(1)} %concatenate.50.refs_0_.at, bf16[512,512]{1,0:T(8,128)(2,1)} %copy-done.5, bf16[512,512]{1,0:T(8,128)(2,1)} %copy-done.6, bf16[2048,512]{1,0:T(8,128)(2,1)} %all-gather.3.cloned.1.call-done.own_0, ...), custom_call_target="tpu_custom_call" | custom-call | flops 4294967296 | bytes 8388608 | tf_op jit(solution)/shard_map/enc_grad/pallas_call | solution.py:280
  166.9 2.7 %add_convert_fusion.1 = bf16[256,2048]{1,0:T(8,128)(2,1)} fusion(bf16[256,2048]{1,0:T(8,128)(2,1)S(1)} %collective-permute-done.16, bf16[256,2048]{1,0:T(8,128)(2,1)} %get-tuple-element.56.refs_1_), kind=kLoop, calls=%fused_computation.5 | loop fusion | flops 2097152 | bytes 3145728 | tf_op jit(solution)/shard_map/convert_element_type | solution.py:461
  173.3 3.4 %collective-permute-start.20 = (bf16[256,2048]{1,0:T(8,128)(2,1)}, bf16[256,2048]{1,0:T(8,128)(2,1)}, u32[]{:S(2)}, u32[]{:S(2)}) collective-permute-start(bf16[256,2048]{1,0:T(8,128)(2,1)} %get-tuple-element.63), channel_id=1, source_target_pairs={{0,1},{1,0},{6,7},{7,6},{8,9},{9,8},{14,15},{15,14},{16,17},{17,16... | collective-permute-start | bytes 3145736 | tf_op jit(solution)/shard_map/ppermute | solution.py:327
  178.5 5.6 %collective-permute-start.23 = (bf16[256,512]{1,0:T(8,128)(2,1)S(1)}, bf16[256,512]{1,0:T(8,128)(2,1)S(1)}, u32[]{:S(2)}, u32[]{:S(2)}) collective-permute-start(bf16[256,512]{1,0:T(8,128)(2,1)S(1)} %get-tuple-element.80), channel_id=1, source_target_pairs={{0,4},{4,0},{1,5},{5,1},{2,6},{6,2},{3,7},{7,3},{8,12},{12,8},{9,1... | collective-permute-start | bytes 786440 | tf_op jit(solution)/shard_map/ppermute | solution.py:448
  186.8 5.3 %collective-permute-done.23 = bf16[256,512]{1,0:T(8,128)(2,1)S(1)} collective-permute-done((bf16[256,512]{1,0:T(8,128)(2,1)S(1)}, bf16[256,512]{1,0:T(8,128)(2,1)S(1)}, u32[]{:S(2)}, u32[]{:S(2)}) %collective-permute-start.23) | collective-permute-done | bytes 262176 | tf_op jit(solution)/shard_map/ppermute | solution.py:448
  195.5 3.7 %maximum_select_fusion.refs_4_ = bf16[512,2048]{1,0:T(8,128)(2,1)} fusion(bf16[512,1024]{1,0:T(8,128)(2,1)} %collective-permute-done.18, bf16[512,1024]{1,0:T(8,128)(2,1)S(1)} %broadcast_select_fusion, pred[]{:T(512)S(6)} %eq.15), kind=kLoop, calls=%fused_computation.3 | loop fusion | flops 9437184 | bytes 4194305 | tf_op jit(solution)/shard_map/jit(_where)/select_n | solution.py:300
  199.2 4.0 %collect.2 = (bf16[256,2048]{1,0:T(8,128)(2,1)}, f32[2,1,2048]{2,1,0:T(1,128)S(1)}) custom-call(s32[6]{0:T(128)S(1)} %concatenate.50.refs_0_.at, bf16[256,2048]{1,0:T(8,128)(2,1)S(1)} %copy-done.2, bf16[256,2048]{1,0:T(8,128)(2,1)} %collective-permute-done.17.refs_2_, bf16[256,2048]{1,0:T(8,128)(2,1)} %collective-permute-done.19.refs_3_, ...), custom_call_target="tpu_custom_call" | custom-call | flops 4194304 | bytes 6291456 | tf_op jit(solution)/shard_map/collect/pallas_call | solution.py:198
  204.8 5.0 %collective-permute-done.24.refs_3_ = bf16[256,2048]{1,0:T(8,128)(2,1)} collective-permute-done((bf16[256,2048]{1,0:T(8,128)(2,1)}, bf16[256,2048]{1,0:T(8,128)(2,1)}, u32[]{:S(2)}, u32[]{:S(2)}) %collective-permute-start.24) | collective-permute-done | bytes 1048608 | tf_op jit(solution)/shard_map/ppermute | solution.py:466
  209.8 4.0 %collect.3 = (bf16[256,2048]{1,0:T(8,128)(2,1)}, f32[2,1,2048]{2,1,0:T(1,128)S(1)}) custom-call(s32[6]{0:T(128)S(1)} %concatenate.50.refs_0_.at, bf16[256,2048]{1,0:T(8,128)(2,1)S(1)} %copy-done.1, bf16[256,2048]{1,0:T(8,128)(2,1)} %collective-permute-done.20.refs_2_, bf16[256,2048]{1,0:T(8,128)(2,1)} %collective-permute-done.24.refs_3_, ...), custom_call_target="tpu_custom_call" | custom-call | flops 4194304 | bytes 6291456 | tf_op jit(solution)/shard_map/collect/pallas_call | solution.py:198
  216.8 5.8 %collective-permute-done.25 = f32[2048]{0:T(1024)S(1)} collective-permute-done((f32[2048]{0:T(1024)S(1)}, f32[2048]{0:T(1024)S(1)}, u32[]{:S(2)}, u32[]{:S(2)}) %collective-permute-start.25) | collective-permute-done | bytes 8224 | tf_op jit(solution)/shard_map/ppermute | solution.py:494
  222.5 3.6 %collective-permute-done.26 = f32[2048]{0:T(1024)S(1)} collective-permute-done((f32[2048]{0:T(1024)S(1)}, f32[2048]{0:T(1024)S(1)}, u32[]{:S(2)}, u32[]{:S(2)}) %collective-permute-start.26) | collective-permute-done | bytes 8224 | tf_op jit(solution)/shard_map/ppermute | solution.py:499
  226.2 4.3 %assemble.1 = bf16[512,2048]{1,0:T(8,128)(2,1)} custom-call(s32[6]{0:T(128)S(1)} %concatenate.50.refs_0_.at, bf16[256,2048]{1,0:T(8,128)(2,1)} %get-tuple-element.68.refs_0_, bf16[256,2048]{1,0:T(8,128)(2,1)} %get-tuple-element.69.refs_1_, bf16[256,2048]{1,0:T(8,128)(2,1)} %collective-permute-done.27.refs_2_, ...), custom_call_target="tpu_custom_call" | custom-call | flops 1048576 | bytes 4194304 | tf_op jit(solution)/shard_map/assemble/pallas_call | solution.py:240
  231.2 3.9 %collective-permute-done.30 = f32[2048]{0:T(1024)S(1)} collective-permute-done((f32[2048]{0:T(1024)S(1)}, f32[2048]{0:T(1024)S(1)}, u32[]{:S(2)}, u32[]{:S(2)}) %collective-permute-start.30) | collective-permute-done | bytes 8224 | tf_op jit(solution)/shard_map/ppermute | solution.py:499
  (115 shorter events, 55.0 us)
Async XLA Ops:
  7.2 65.1 %all-gather.3.cloned.1.call-start = ((), (), s32[]{:S(2)}) async-start(), calls=%async_computation.2 | async-start | bytes 2621440 | tf_op jit(solution)/shard_map/all_gather | solution.py:420
  7.2 18.7 %collective-permute-start.3 = (bf16[512,2048]{1,0:T(8,128)(2,1)}, bf16[512,2048]{1,0:T(8,128)(2,1)}, u32[]{:S(2)}, u32[]{:S(2)}) collective-permute-start(bf16[512,2048]{1,0:T(8,128)(2,1)} %bitcast.15), channel_id=1, source_target_pairs={{4,6},{5,7},{12,14},{13,15},{20,22},{21,23},{28,30},{29,31}} | collective-permute-start | bytes 6291464 | tf_op jit(solution)/shard_map/ppermute | solution.py:340
  11.3 8.7 %collective-permute-start = (bf16[256,512]{1,0:T(8,128)(2,1)S(1)}, bf16[256,512]{1,0:T(8,128)(2,1)S(1)}, u32[]{:S(2)}, u32[]{:S(2)}) collective-permute-start(bf16[256,512]{1,0:T(8,128)(2,1)S(1)} %get-tuple-element.76), channel_id=1, source_target_pairs={{0,4},{4,0},{1,5},{5,1},{2,6},{6,2},{3,7},{7,3},{8,12},{12,8},{9,1... | collective-permute-start | bytes 786440 | tf_op jit(solution)/shard_map/ppermute | solution.py:339
  20.9 27.2 %collective-permute-start.1 = (bf16[512,2048]{1,0:T(8,128)(2,1)S(1)}, bf16[512,2048]{1,0:T(8,128)(2,1)}, u32[]{:S(2)}, u32[]{:S(2)}) collective-permute-start(bf16[512,2048]{1,0:T(8,128)(2,1)S(1)} %bitcast.16), channel_id=1, source_target_pairs={{0,4},{4,2},{1,5},{5,3},{8,12},{12,10},{9,13},{13,11},{16,20},{20,... | collective-permute-start | bytes 6291464 | tf_op jit(solution)/shard_map/ppermute | solution.py:345
  25.9 92.6 %all-gather.5.cloned.1.call-start = ((), (), s32[]{:S(2)}) async-start(), calls=%async_computation.3 | async-start | bytes 2621440 | tf_op jit(solution)/shard_map/all_gather | solution.py:420
  25.9 24.1 %collective-permute-start.6 = (bf16[512,2048]{1,0:T(8,128)(2,1)}, bf16[512,2048]{1,0:T(8,128)(2,1)S(1)}, u32[]{:S(2)}, u32[]{:S(2)}) collective-permute-start(bf16[512,2048]{1,0:T(8,128)(2,1)} %collective-permute-done.3.refs_2_.refs_5_), channel_id=1, source_target_pairs={{6,7},{7,6},{14,15},{15,14},{22,23},{23,22},{30,31},{31,30}} | collective-permute-start | bytes 6291464 | tf_op jit(solution)/shard_map/ppermute | solution.py:327
  26.7 3.7 %collective-permute-start.4 = (bf16[2048]{0:T(1024)(128)(2,1)S(1)}, bf16[2048]{0:T(1024)(128)(2,1)S(1)}, u32[]{:S(2)}, u32[]{:S(2)}) collective-permute-start(bf16[2048]{0:T(1024)(128)(2,1)S(1)} %copy-done.13), channel_id=1, source_target_pairs={{0,1},{1,0},{2,3},{3,2},{4,5},{5,4},{6,7},{7,6},{8,9},{9,8},{10,11... | collective-permute-start | bytes 12296 | tf_op jit(solution)/shard_map/ppermute | solution.py:342
  30.4 42.0 %collective-permute-start.5 = (bf16[512,2048]{1,0:T(8,128)(2,1)S(1)}, bf16[512,2048]{1,0:T(8,128)(2,1)}, u32[]{:S(2)}, u32[]{:S(2)}) collective-permute-start(bf16[512,2048]{1,0:T(8,128)(2,1)S(1)} %bitcast.17), channel_id=1, source_target_pairs={{0,1},{1,0},{8,9},{9,8},{16,17},{17,16},{24,25},{25,24}} | collective-permute-start | bytes 6291464 | tf_op jit(solution)/shard_map/ppermute | solution.py:327
  48.0 24.4 %collective-permute-start.7 = (bf16[512,2048]{1,0:T(8,128)(2,1)}, bf16[512,2048]{1,0:T(8,128)(2,1)}, u32[]{:S(2)}, u32[]{:S(2)}) collective-permute-start(bf16[512,2048]{1,0:T(8,128)(2,1)} %collective-permute-done.1.refs_3_), channel_id=1, source_target_pairs={{2,3},{3,2},{4,5},{5,4},{10,11},{11,10},{12,13},{13,12},{18,19},{1... | collective-permute-start | bytes 6291464 | tf_op jit(solution)/shard_map/ppermute | solution.py:327
  51.3 13.7 %collective-permute-start.8 = (bf16[256,512]{1,0:T(8,128)(2,1)}, bf16[256,512]{1,0:T(8,128)(2,1)}, u32[]{:S(2)}, u32[]{:S(2)}) collective-permute-start(bf16[256,512]{1,0:T(8,128)(2,1)} %get-tuple-element.42), channel_id=1, source_target_pairs={{0,4},{4,0},{1,5},{5,1},{2,6},{6,2},{3,7},{7,3},{8,12},{12,8},{9,1... | collective-permute-start | bytes 786440 | tf_op jit(solution)/shard_map/ppermute | solution.py:358
  65.0 7.4 %collective-permute-start.10 = (bf16[512,1024]{1,0:T(8,128)(2,1)}, bf16[512,1024]{1,0:T(8,128)(2,1)}, u32[]{:S(2)}, u32[]{:S(2)}) collective-permute-start(bf16[512,1024]{1,0:T(8,128)(2,1)} %get-tuple-element.44), channel_id=1, source_target_pairs={{2,4},{6,2},{3,5},{7,3},{10,12},{14,10},{11,13},{15,11},{18,20},{2... | collective-permute-start | bytes 3145736 | tf_op jit(solution)/shard_map/ppermute | solution.py:370
  66.7 5.7 %collective-permute-start.9 = (bf16[512,1024]{1,0:T(8,128)(2,1)S(1)}, bf16[512,1024]{1,0:T(8,128)(2,1)}, u32[]{:S(2)}, u32[]{:S(2)}) collective-permute-start(bf16[512,1024]{1,0:T(8,128)(2,1)S(1)} %get-tuple-element.43.refs_0_), channel_id=1, source_target_pairs={{2,0},{3,1},{10,8},{11,9},{18,16},{19,17},{26,24},{27,25}} | collective-permute-start | bytes 3145736 | tf_op jit(solution)/shard_map/ppermute | solution.py:369
  69.8 106.9 %reduce-scatter.3.cloned.1.call-start = ((), (), s32[]{:S(2)}) async-start(), calls=%async_computation.4 | async-start | bytes 2621440 | tf_op jit(solution)/shard_map/reduce_scatter | solution.py:439
  72.2 20.2 %collective-permute-start.11 = (bf16[2048,512]{1,0:T(8,128)(2,1)}, bf16[2048,512]{1,0:T(8,128)(2,1)}, u32[]{:S(2)}, u32[]{:S(2)}) collective-permute-start(bf16[2048,512]{1,0:T(8,128)(2,1)} %all-gather.3.cloned.1.call-done.own_0), channel_id=1, source_target_pairs={{0,2},{2,0},{1,3},{3,1},{4,6},{6,4},{5,7},{7,5},{8,10},{10,8},{9,1... | collective-permute-start | bytes 6291464 | tf_op jit(solution)/shard_map/ppermute | solution.py:423
  81.0 24.4 %collective-permute-start.12 = (bf16[512,2048]{1,0:T(8,128)(2,1)}, bf16[512,2048]{1,0:T(8,128)(2,1)S(1)}, u32[]{:S(2)}, u32[]{:S(2)}) collective-permute-start(bf16[512,2048]{1,0:T(8,128)(2,1)} %get-tuple-element.47.enc_other), channel_id=1, source_target_pairs={{0,2},{2,0},{1,3},{3,1},{4,6},{6,4},{5,7},{7,5},{8,10},{10,8},{9,1... | collective-permute-start | bytes 6291464 | tf_op jit(solution)/shard_map/ppermute | solution.py:406
  113.0 101.6 %reduce-scatter.5.cloned.1.call-start = ((), (), s32[]{:S(2)}) async-start(), calls=%async_computation.5 | async-start | bytes 2621440 | tf_op jit(solution)/shard_map/reduce_scatter | solution.py:439
  118.5 4.4 %collective-permute-start.14 = (bf16[2048,512]{1,0:T(8,128)(2,1)}, bf16[2048,512]{1,0:T(8,128)(2,1)S(1)}, u32[]{:S(2)}, u32[]{:S(2)}) collective-permute-start(bf16[2048,512]{1,0:T(8,128)(2,1)} %all-gather.5.cloned.1.call-done.own_1), channel_id=1, source_target_pairs={{0,2},{2,0},{1,3},{3,1},{4,6},{6,4},{5,7},{7,5},{8,10},{10,8},{9,1... | collective-permute-start | bytes 6291464 | tf_op jit(solution)/shard_map/ppermute | solution.py:423
  135.5 7.5 %collective-permute-start.15 = (bf16[512,512]{1,0:T(8,128)(2,1)S(1)}, bf16[512,512]{1,0:T(8,128)(2,1)S(1)}, u32[]{:S(2)}, u32[]{:S(2)}) collective-permute-start(bf16[512,512]{1,0:T(8,128)(2,1)S(1)} %get-tuple-element.51.gkv_1.refs_3_), channel_id=1, source_target_pairs={{0,2},{2,0},{1,3},{3,1},{4,6},{6,4},{5,7},{7,5},{8,10},{10,8},{9,1... | collective-permute-start | bytes 1572872 | tf_op jit(solution)/shard_map/ppermute | solution.py:427
  150.4 16.4 %collective-permute-start.16 = (bf16[256,2048]{1,0:T(8,128)(2,1)}, bf16[256,2048]{1,0:T(8,128)(2,1)S(1)}, u32[]{:S(2)}, u32[]{:S(2)}) collective-permute-start(bf16[256,2048]{1,0:T(8,128)(2,1)} %get-tuple-element.57), channel_id=1, source_target_pairs={{2,3},{3,2},{4,5},{5,4},{10,11},{11,10},{12,13},{13,12},{18,19},{1... | collective-permute-start | bytes 3145736 | tf_op jit(solution)/shard_map/ppermute | solution.py:327
  151.1 18.4 %collective-permute-start.18 = (bf16[512,1024]{1,0:T(8,128)(2,1)}, bf16[512,1024]{1,0:T(8,128)(2,1)}, u32[]{:S(2)}, u32[]{:S(2)}) collective-permute-start(bf16[512,1024]{1,0:T(8,128)(2,1)} %get-tuple-element.58), channel_id=1, source_target_pairs={{4,2},{2,6},{5,3},{3,7},{12,10},{10,14},{13,11},{11,15},{20,18},{1... | collective-permute-start | bytes 3145736 | tf_op jit(solution)/shard_map/ppermute | solution.py:450
  152.8 41.3 %collective-permute-start.21 = (bf16[512,1024]{1,0:T(8,128)(2,1)}, bf16[512,1024]{1,0:T(8,128)(2,1)}, u32[]{:S(2)}, u32[]{:S(2)}) collective-permute-start(bf16[512,1024]{1,0:T(8,128)(2,1)} %get-tuple-element.58), channel_id=1, source_target_pairs={{0,2},{1,3},{8,10},{9,11},{16,18},{17,19},{24,26},{25,27}} | collective-permute-start | bytes 3145736 | tf_op jit(solution)/shard_map/ppermute | solution.py:449
  158.6 19.9 %collective-permute-start.22 = (bf16[256,2048]{1,0:T(8,128)(2,1)}, bf16[256,2048]{1,0:T(8,128)(2,1)}, u32[]{:S(2)}, u32[]{:S(2)}) collective-permute-start(bf16[256,2048]{1,0:T(8,128)(2,1)} %get-tuple-element.63), channel_id=1, source_target_pairs={{2,3},{3,2},{4,5},{5,4},{10,11},{11,10},{12,13},{13,12},{18,19},{1... | collective-permute-start | bytes 3145736 | tf_op jit(solution)/shard_map/ppermute | solution.py:327
  169.6 29.6 %collective-permute-start.19 = (bf16[256,2048]{1,0:T(8,128)(2,1)}, bf16[256,2048]{1,0:T(8,128)(2,1)}, u32[]{:S(2)}, u32[]{:S(2)}) collective-permute-start(bf16[256,2048]{1,0:T(8,128)(2,1)} %add_convert_fusion.1), channel_id=1, source_target_pairs={{4,0},{2,6},{5,1},{3,7},{12,8},{10,14},{13,9},{11,15},{20,16},{18,... | collective-permute-start | bytes 3145736 | tf_op jit(solution)/shard_map/ppermute | solution.py:466
  170.9 28.4 %collective-permute-start.17 = (bf16[256,2048]{1,0:T(8,128)(2,1)}, bf16[256,2048]{1,0:T(8,128)(2,1)}, u32[]{:S(2)}, u32[]{:S(2)}) collective-permute-start(bf16[256,2048]{1,0:T(8,128)(2,1)} %get-tuple-element.57), channel_id=1, source_target_pairs={{0,1},{1,0},{6,7},{7,6},{8,9},{9,8},{14,15},{15,14},{16,17},{17,16... | collective-permute-start | bytes 3145736 | tf_op jit(solution)/shard_map/ppermute | solution.py:327
  173.3 29.9 %collective-permute-start.20 = (bf16[256,2048]{1,0:T(8,128)(2,1)}, bf16[256,2048]{1,0:T(8,128)(2,1)}, u32[]{:S(2)}, u32[]{:S(2)}) collective-permute-start(bf16[256,2048]{1,0:T(8,128)(2,1)} %get-tuple-element.63), channel_id=1, source_target_pairs={{0,1},{1,0},{6,7},{7,6},{8,9},{9,8},{14,15},{15,14},{16,17},{17,16... | collective-permute-start | bytes 3145736 | tf_op jit(solution)/shard_map/ppermute | solution.py:327
  178.5 13.6 %collective-permute-start.23 = (bf16[256,512]{1,0:T(8,128)(2,1)S(1)}, bf16[256,512]{1,0:T(8,128)(2,1)S(1)}, u32[]{:S(2)}, u32[]{:S(2)}) collective-permute-start(bf16[256,512]{1,0:T(8,128)(2,1)S(1)} %get-tuple-element.80), channel_id=1, source_target_pairs={{0,4},{4,0},{1,5},{5,1},{2,6},{6,2},{3,7},{7,3},{8,12},{12,8},{9,1... | collective-permute-start | bytes 786440 | tf_op jit(solution)/shard_map/ppermute | solution.py:448
  192.8 17.0 %collective-permute-start.24 = (bf16[256,2048]{1,0:T(8,128)(2,1)}, bf16[256,2048]{1,0:T(8,128)(2,1)}, u32[]{:S(2)}, u32[]{:S(2)}) collective-permute-start(bf16[256,2048]{1,0:T(8,128)(2,1)} %add_convert_fusion), channel_id=1, source_target_pairs={{4,0},{2,6},{5,1},{3,7},{12,8},{10,14},{13,9},{11,15},{20,16},{18,... | collective-permute-start | bytes 3145736 | tf_op jit(solution)/shard_map/ppermute | solution.py:466
  203.2 23.0 %collective-permute-start.27 = (bf16[256,2048]{1,0:T(8,128)(2,1)}, bf16[256,2048]{1,0:T(8,128)(2,1)}, u32[]{:S(2)}, u32[]{:S(2)}) collective-permute-start(bf16[256,2048]{1,0:T(8,128)(2,1)} %get-tuple-element.68.refs_0_), channel_id=1, source_target_pairs={{6,4},{7,5},{14,12},{15,13},{22,20},{23,21},{30,28},{31,29}} | collective-permute-start | bytes 3145736 | tf_op jit(solution)/shard_map/ppermute | solution.py:486
  213.8 12.4 %collective-permute-start.28 = (bf16[256,2048]{1,0:T(8,128)(2,1)}, bf16[256,2048]{1,0:T(8,128)(2,1)S(1)}, u32[]{:S(2)}, u32[]{:S(2)}) collective-permute-start(bf16[256,2048]{1,0:T(8,128)(2,1)} %get-tuple-element.69.refs_1_), channel_id=1, source_target_pairs={{6,4},{7,5},{14,12},{15,13},{22,20},{23,21},{30,28},{31,29}} | collective-permute-start | bytes 3145736 | tf_op jit(solution)/shard_map/ppermute | solution.py:486
  215.7 21.1 %collective-permute-start.29 = (bf16[256,512]{1,0:T(8,128)(2,1)S(1)}, bf16[256,512]{1,0:T(8,128)(2,1)S(1)}, u32[]{:S(2)}, u32[]{:S(2)}) collective-permute-start(bf16[256,512]{1,0:T(8,128)(2,1)S(1)} %get-tuple-element.82), channel_id=1, source_target_pairs={{0,4},{4,0},{1,5},{5,1},{2,6},{6,2},{3,7},{7,3},{8,12},{12,8},{9,1... | collective-permute-start | bytes 786440 | tf_op jit(solution)/shard_map/ppermute | solution.py:448
  215.9 6.7 %collective-permute-start.25 = (f32[2048]{0:T(1024)S(1)}, f32[2048]{0:T(1024)S(1)}, u32[]{:S(2)}, u32[]{:S(2)}) collective-permute-start(f32[2048]{0:T(1024)S(1)} %add_select_fusion), channel_id=1, source_target_pairs={{0,6},{6,0},{2,4},{4,2},{1,7},{7,1},{3,5},{5,3},{8,14},{14,8},{10,... | collective-permute-start | bytes 24584 | tf_op jit(solution)/shard_map/ppermute | solution.py:494
  230.5 4.5 %collective-permute-start.30 = (f32[2048]{0:T(1024)S(1)}, f32[2048]{0:T(1024)S(1)}, u32[]{:S(2)}, u32[]{:S(2)}) collective-permute-start(f32[2048]{0:T(1024)S(1)} %add.64), channel_id=1, source_target_pairs={{0,16},{8,24},{16,0},{24,8},{1,17},{9,25},{17,1},{25,9},{2,18},{10... | collective-permute-start | bytes 24584 | tf_op jit(solution)/shard_map/ppermute | solution.py:499
  (20 other events, 139.4 us)
Sparse Core Ops, SparseCore 0:
  26.0 46.2 all-gather.2
  73.8 44.6 all-gather.4
  120.8 42.5 reduce-scatter.2
  166.2 43.1 reduce-scatter.4
